TPU v7x, 32 devices: a whole 2x2x4 slice. The times are simulated.
32 devices in a mesh: seabed: 8 (over y, x, core), freq: 4 (over z).
Axes of the slice: x: 2, y: 2, z: 4, core: 2. Of those that a mesh axis runs over, the one named last changes fastest.
Arguments:
- uplift: bfloat16 [128, 32, 40, 128], P('freq', None, 'seabed'), may hold values from -6 to 6
- coefficient: float32 [40, 128], P('seabed'), may hold values from 0.06 to 0.24
- transfer: float32 [4, 2, 600, 5120], P('freq', None, None, 'seabed'), may hold values from -0.0625 to 0.0625
Outputs:
- sensors: float32 [128, 4, 2, 600], P('seabed', 'freq')
All inputs are finite; a program needn't handle non-finite values.
Results may differ from a plain program's by a relative error of at most 0.0003.
Values sent between devices are 32-bit elements; how exact they have to be, the bound alone decides.
No kernel may reach another device: no remote copies, remote signals or barrier semaphores. Data moves between devices by JAX's collectives and lax.ppermute only.
A program may use at most 64 MiB of HBM per device.

v0:
```python
import math

import jax
import jax.numpy as jnp
from jax import lax
from jax.sharding import PartitionSpec as P

FD = 1
PASSES = 3


def with_halo(block, sides, width):
    for axis, dim in sides:
        count = lax.axis_size(axis)
        forward = [(i, i + 1) for i in range(count - 1)]
        backward = [(target, source) for source, target in forward]
        low = lax.ppermute(
            lax.slice_in_dim(block, block.shape[dim] - width, None, axis=dim), axis, forward
        )
        high = lax.ppermute(lax.slice_in_dim(block, 0, width, axis=dim), axis, backward)
        block = jnp.concatenate([low, block, high], axis=dim)
    return block


def dft_table(steps_count, freq_count):
    times = jnp.arange(steps_count, dtype=jnp.int32)
    freqs = jnp.arange(freq_count, dtype=jnp.int32)
    phase = (freqs[:, None] * times[None, :] % steps_count).astype(jnp.float32) * (
        2.0 * math.pi / steps_count
    )
    scale = 1.0 / math.sqrt(steps_count)
    return (
        jnp.stack([jnp.cos(phase), -jnp.sin(phase)], 1).reshape(2 * freq_count, steps_count) * scale
    )


def relax(extended, rows_coefficient):
    centre = extended[:, :, 1:-1]
    padded = jnp.pad(centre, ((0, 0), (0, 0), (0, 0), (1, 1)))
    beside = extended[:, :, 2:] + extended[:, :, :-2] + padded[:, :, :, 2:] + padded[:, :, :, :-2]
    return centre + rows_coefficient * (beside - 4.0 * centre)


def shards(uplift, coefficient, transfer):
    field = uplift.astype(jnp.float32)
    vectors, steps_count, rows, width = field.shape
    extended = with_halo(field, (("seabed", 2),), PASSES)
    coefficient_rim = with_halo(coefficient, (("seabed", 0),), PASSES - 1)
    for step in range(PASSES):
        span = rows + 2 * (PASSES - 1 - step)
        extended = relax(extended, coefficient_rim[step : step + span])
    field = extended
    flat = field.reshape(vectors, steps_count, rows * width)
    freq_count = FD * lax.axis_size("freq")
    table = dft_table(steps_count, freq_count)
    spectrum = jnp.einsum("ft,vtc->fvc", table, flat, precision=lax.Precision.HIGHEST)
    spectrum = spectrum.reshape(freq_count, 2, vectors, rows * width)
    regrouped = lax.all_to_all(spectrum, "freq", split_axis=0, concat_axis=2, tiled=True)
    products = jnp.einsum("kbvc,kasc->vkbas", regrouped, transfer, precision=lax.Precision.HIGHEST)
    real_part = products[:, :, 0, 0] - products[:, :, 1, 1]
    imag_part = products[:, :, 1, 0] + products[:, :, 0, 1]
    return lax.psum_scatter(
        jnp.stack([real_part, imag_part], 2), "seabed", scatter_dimension=0, tiled=True
    )


def solution(mesh):
    placed = (P("freq", None, "seabed", None), P("seabed", None), P("freq", None, None, "seabed"))
    return jax.shard_map(
        shards,
        mesh=mesh,
        in_specs=placed,
        out_specs=P("seabed", "freq", None, None),
        check_vma=False,
    )
```

profile of v0, /device:TPU:0, one launch (start us, length us, event | category | flops | bytes accessed | tf_op | source)
XLA Modules:
  0.0 159.0 jit_solution(17470392824723948402)
XLA Ops:
  6.5 2.0 %fusion.34 = (f32[32,32,3,128]{3,1,2,0:T(8,128)S(1)}, f32[32,32,3,128]{3,1,2,0:T(8,128)S(1)}) fusion(bf16[32,32,5,128]{3,1,2,0:T(8,128)(2,1)} %param.3), kind=kLoop, calls=%fused_computation.51 | loop fusion | bytes 6291456 | tf_op jit(solution)/shard_map/slice | solution.py:18
  8.5 2.5 %collective-permute-start = (f32[32,32,3,128]{3,1,2,0:T(8,128)S(1)}, f32[32,32,3,128]{3,1,2,0:T(8,128)S(1)}, u32[]{:S(2)}, u32[]{:S(2)}) collective-permute-start(f32[32,32,3,128]{3,1,2,0:T(8,128)S(1)} %get-tuple-element.5), channel_id=1, source_target_pairs={{0,4},{4,8},{8,12},{12,16},{16,20},{20,24},{24,28},{1,5},{5,9},{9,... | collective-permute-start | bytes 4718600 | tf_op jit(solution)/shard_map/ppermute | solution.py:17
  11.0 1.3 collective-permute-start.1
  12.3 5.0 %collective-permute-start.2 = (f32[2,128]{1,0:T(2,128)S(1)}, f32[2,128]{1,0:T(2,128)S(1)}, u32[]{:S(2)}, u32[]{:S(2)}) collective-permute-start(f32[2,128]{1,0:T(2,128)S(1)} %get-tuple-element.9), channel_id=1, source_target_pairs={{0,4},{4,8},{8,12},{12,16},{16,20},{20,24},{24,28},{1,5},{5,9},{9,... | collective-permute-start | bytes 3080 | tf_op jit(solution)/shard_map/ppermute | solution.py:17
  17.4 1.3 collective-permute-start.3
  18.7 0.4 convert_element_type.26
  19.1 2.6 %collective-permute-done.3 = f32[2,128]{1,0:T(2,128)S(1)} collective-permute-done((f32[2,128]{1,0:T(2,128)S(1)}, f32[2,128]{1,0:T(2,128)S(1)}, u32[]{:S(2)}, u32[]{:S(2)}) %collective-permute-start.3) | collective-permute-done | bytes 1056 | tf_op jit(solution)/shard_map/ppermute | solution.py:20
  21.7 0.7 pad_maximum_fusion
  22.4 0.5 slice.98
  22.9 2.6 %fusion.4 = f32[32,32,9,128]{3,1,2,0:T(8,128)S(1)} fusion(f32[32,32,9,128]{3,1,2,0:T(8,128)S(1)} %slice.98, f32[32,32,11,128]{3,1,2,0:T(8,128)S(1)} %pad_maximum_fusion, f32[9,128]{1,0:T(8,128)S(1)} %pad_maximum_fusion.2), kind=kLoop, calls=%fused_computation.11 | loop fusion | flops 8257536 | bytes 18878976 | tf_op jit(solution)/shard_map/add | solution.py:41
  25.6 0.4 slice.101
  26.0 2.1 %fusion.9 = f32[32,32,7,128]{3,1,2,0:T(8,128)S(1)} fusion(f32[32,32,7,128]{3,1,2,0:T(8,128)S(1)} %slice.101, f32[32,32,9,128]{3,1,2,0:T(8,128)S(1)} %fusion.4, f32[7,128]{1,0:T(8,128)S(1)} %slice.102), kind=kLoop, calls=%fused_computation.17 | loop fusion | flops 6422528 | bytes 14683648 | tf_op jit(solution)/shard_map/add | solution.py:41
  28.0 0.2 slice.105
  28.3 1.4 fusion.16
  29.7 4.2 %copy.8 = f32[32,32,5,128]{3,2,1,0:T(8,128)} copy(f32[32,32,5,128]{3,1,2,0:T(8,128)S(1)} %fusion.16) | data formatting | bytes 5242880 | tf_op jit(solution)/shard_map/add | solution.py:41
  33.9 4.7 %reshape.136 = f32[32,32,640,1]{2,1,0,3:T(8,128)} reshape(f32[32,32,5,128]{3,2,1,0:T(8,128)} %copy.8) | data formatting | bytes 5242880 | tf_op jit(solution)/shard_map/reshape | solution.py:53
  38.6 3.2 %fusion.23 = f32[4,2,32,640]{3,0,2,1:T(4,128)S(1)} fusion(f32[32,32,640,1]{2,1,0,3:T(8,128)} %reshape.136, f32[4,1,32]{2,0,1:T(4,128)S(1)} %get-tuple-element.11, f32[4,1,32]{2,0,1:T(4,128)S(1)} %get-tuple-element.12), kind=kOutput, calls=%fused_computation.36 | convolution fusion | flops 62915072 | bytes 3277824 | tf_op jit(solution)/shard_map/ft,vtc->fvc/dot_general | solution.py:56
  41.9 16.4 %all_to_all.15 = f32[4,2,32,640]{3,2,1,0:T(8,128)S(1)} all-to-all(f32[4,2,32,640]{3,2,1,0:T(8,128)S(1)} %copy.9), channel_id=1, replica_groups=mesh['seabed'=8,'freq'=4] {'freq'}, dimensions={0} | all-to-all | bytes 1310720 | tf_op jit(solution)/shard_map/all_to_all | solution.py:58
  58.3 3.1 %fusion.17 = f32[128,1,2,2,600]{0,4,3,2,1:T(8,128)S(1)} fusion(f32[2,128,640,1]{2,1,3,0:T(8,128)S(1)} %bitcast.33, f32[1,2,600,640]{3,2,1,0:T(8,128)S(1)} %copy-done), kind=kOutput, calls=%fused_computation.27 | convolution fusion | flops 2359296000 | bytes 4956160 | tf_op jit(solution)/shard_map/kbvc,kasc->vkbas/dot_general | solution.py:59
  61.5 0.9 pad_maximum_fusion.1
  62.4 2.1 %copy.11 = f32[128,1,2,600]{3,2,1,0:T(2,128)} copy(f32[128,1,2,600]{0,3,2,1:T(8,128)} %pad_maximum_fusion.1) | data formatting | bytes 1228800 | tf_op jit(solution)/shard_map/stack | solution.py:63
  64.5 0.6 dynamic-slice
  65.8 84.9 %all-reduce.6.cloned.1.call-done = f32[128,1,2,600]{3,2,1,0:T(2,128)} async-done(((f32[128,1,2,600]{3,2,1,0:T(2,128)}), f32[128,1,2,600]{3,2,1,0:T(2,128)}) %all-reduce.6.cloned.1.call-update) | async-done | bytes 614416
  150.7 1.5 constant_dynamic-slice_fusion
  (20 shorter events, 0.3 us)
Async XLA Ops:
  6.5 51.8 %copy-start = (f32[1,2,600,640]{3,2,1,0:T(8,128)S(1)}, f32[1,2,600,640]{3,2,1,0:T(8,128)}, u32[]{:S(2)}) copy-start(f32[1,2,600,640]{3,2,1,0:T(8,128)} %param.5) | copy-start | bytes 9216004
  6.5 5.8 %copy-start.2 = (f32[5,128]{1,0:T(8,128)S(1)}, f32[5,128]{1,0:T(8,128)}, u32[]{:S(2)}) copy-start(f32[5,128]{1,0:T(8,128)} %param.4) | copy-start | bytes 7684
  6.5 144.1 %all-reduce.6.cloned.1.call-start = ((), (), s32[]{:S(2)}) async-start(), calls=%async_computation.1 | async-start | bytes 1310720
  6.5 12.2 %copy-start.1 = (bf16[32,32,5,128]{3,1,2,0:T(8,128)(2,1)S(1)}, bf16[32,32,5,128]{3,1,2,0:T(8,128)(2,1)}, u32[]{:S(2)}) copy-start(bf16[32,32,5,128]{3,1,2,0:T(8,128)(2,1)} %param.3) | copy-start | bytes 3932164
  8.5 13.2 %collective-permute-start = (f32[32,32,3,128]{3,1,2,0:T(8,128)S(1)}, f32[32,32,3,128]{3,1,2,0:T(8,128)S(1)}, u32[]{:S(2)}, u32[]{:S(2)}) collective-permute-start(f32[32,32,3,128]{3,1,2,0:T(8,128)S(1)} %get-tuple-element.5), channel_id=1, source_target_pairs={{0,4},{4,8},{8,12},{12,16},{16,20},{20,24},{24,28},{1,5},{5,9},{9,... | collective-permute-start | bytes 4718600 | tf_op jit(solution)/shard_map/ppermute | solution.py:17
  11.0 10.7 %collective-permute-start.1 = (f32[32,32,3,128]{3,1,2,0:T(8,128)S(1)}, f32[32,32,3,128]{3,1,2,0:T(8,128)S(1)}, u32[]{:S(2)}, u32[]{:S(2)}) collective-permute-start(f32[32,32,3,128]{3,1,2,0:T(8,128)S(1)} %get-tuple-element.6), channel_id=1, source_target_pairs={{4,0},{8,4},{12,8},{16,12},{20,16},{24,20},{28,24},{5,1},{9,5},{13... | collective-permute-start | bytes 4718600 | tf_op jit(solution)/shard_map/ppermute | solution.py:20
  12.3 6.8 %collective-permute-start.2 = (f32[2,128]{1,0:T(2,128)S(1)}, f32[2,128]{1,0:T(2,128)S(1)}, u32[]{:S(2)}, u32[]{:S(2)}) collective-permute-start(f32[2,128]{1,0:T(2,128)S(1)} %get-tuple-element.9), channel_id=1, source_target_pairs={{0,4},{4,8},{8,12},{12,16},{16,20},{20,24},{24,28},{1,5},{5,9},{9,... | collective-permute-start | bytes 3080 | tf_op jit(solution)/shard_map/ppermute | solution.py:17
  17.4 4.3 %collective-permute-start.3 = (f32[2,128]{1,0:T(2,128)S(1)}, f32[2,128]{1,0:T(2,128)S(1)}, u32[]{:S(2)}, u32[]{:S(2)}) collective-permute-start(f32[2,128]{1,0:T(2,128)S(1)} %get-tuple-element.10), channel_id=1, source_target_pairs={{4,0},{8,4},{12,8},{16,12},{20,16},{24,20},{28,24},{5,1},{9,5},{13... | collective-permute-start | bytes 3080 | tf_op jit(solution)/shard_map/ppermute | solution.py:20
  61.5 3.1 %copy-start.3 = (u32[32]{0:T(128)S(1)}, u32[32]{0:T(128)}, u32[]{:S(2)}) copy-start(u32[32]{0:T(128)} %constant.37) | copy-start | bytes 388
Sparse Core Ops, SparseCore 0:
  64.6 85.9 all-reduce.5
where the time goes:
time: 159 us
  waiting for transfers between devices  87.5 us (55%)
  blocking collectives  16.4 us (10%)
  local copies, waits for them, and re-layouts  16.3 us (10%)
  between operations  14.3 us (9%)
  starting transfers between devices  10.1 us (6%)
  other arithmetic  8.15 us (5%)
  matrix products  6.35 us (4%)
    unnamed x2, waiting for transfers between devices  84.9 us
    all_to_all x1, blocking collectives, shards(): lax.all_to_all(spectrum, 'freq', split_axis=0, concat_axis=2, tiled=True)  16.4 us
    ppermute x2, starting transfers between devices, with_halo(): lax.ppermute(lax.slice_in_dim(block, block.shape[dim] - width, None, axis...  7.52 us
    add x3, other arithmetic, relax(): return centre + rows_coefficient * (beside - 4.0 * centre)  6.11 us
    reshape x1, local copies, waits for them, and re-layouts, shards(): flat = field.reshape(vectors, steps_count, rows * width)  4.7 us
    add x1, local copies, waits for them, and re-layouts, relax(): return centre + rows_coefficient * (beside - 4.0 * centre)  4.19 us
    dot_general x1, matrix products, shards(): jnp.einsum('ft,vtc->fvc', table, flat, precision=lax.Precision.HIGHEST)  3.21 us
  transfers between devices with their start and end apart: 5, of which 2 were waited for; matrix products, arithmetic and copies ran while one was open for 1% of the time, Pallas kernels for 0%

commit v1 on v0

v1 whole, which is shorter than its diff:
```python
import functools
import math

import jax
import jax.numpy as jnp
import numpy as np
from jax import lax
from jax.experimental import pallas as pl
from jax.experimental.pallas import tpu as pltpu
from jax.sharding import PartitionSpec as P

FD = 1
PASSES = 3
LANE_GROUP = 8
PHASES = 1


def dft_table(steps_count, freq_count):
    times = np.arange(steps_count)
    freqs = np.arange(freq_count)
    phase = (freqs[:, None] * times[None, :] % steps_count) * (2.0 * math.pi / steps_count)
    scale = 1.0 / math.sqrt(steps_count)
    return (np.stack([np.cos(phase), -np.sin(phase)], 1) * scale).astype(np.float32)


def split_bf16(values):
    high = values.astype(jnp.bfloat16)
    low = (values - high.astype(values.dtype)).astype(jnp.bfloat16)
    return high, low


def transform_operand(steps_count, freq_count, order):
    table = dft_table(steps_count, freq_count)[order]
    eye = np.eye(LANE_GROUP, dtype=np.float32)
    high, low = split_bf16(table)
    parts = np.stack([high.astype(np.float32), low.astype(np.float32)], 1)
    full = np.einsum("fpkbt,vw->fpkbvwt", parts, eye)
    sources = full.shape[0]
    return jnp.asarray(full.reshape(sources, -1, LANE_GROUP * steps_count), jnp.bfloat16)


def transform_kernel(slots, table_ref, field_ref, *outs):
    table = table_ref[lax.axis_index("freq") if table_ref.shape[0] > 1 else 0]
    group, rows, steps, width = field_ref.shape
    data = jnp.concatenate(
        [field_ref[:, r].reshape(group * steps, width) for r in range(rows)], axis=1
    )
    both = jnp.dot(table, data, preferred_element_type=jnp.float32)
    half = both.shape[0] // 2
    values = both[:half] + both[half:]
    for slot in range(slots):
        ref = outs[slot] if len(outs) > 1 else outs[0].at[slot]
        for b in range(2):
            at = (slot * 2 + b) * group
            for r in range(rows):
                ref[b, r] = values[at : at + group, r * width : (r + 1) * width]


def transform(field, table, slots, blocks, separate):
    vectors, rows, steps, width = field.shape
    group = LANE_GROUP
    count = len(blocks)
    if count > 1:
        step = blocks[1] - blocks[0]
    else:
        step = 1
    first = blocks[0]
    if separate:
        shape = [jax.ShapeDtypeStruct((2, rows, count * group, width), jnp.float32)] * slots
        spec = [pl.BlockSpec((2, rows, group, width), lambda i: (0, 0, i, 0))] * slots
    else:
        shape = [jax.ShapeDtypeStruct((slots, 2, rows, count * group, width), jnp.float32)]
        spec = [pl.BlockSpec((slots, 2, rows, group, width), lambda i: (0, 0, 0, i, 0))]
    return pl.pallas_call(
        functools.partial(transform_kernel, slots),
        out_shape=shape,
        grid=(count,),
        in_specs=[
            pl.BlockSpec(table.shape, lambda i: (0, 0, 0)),
            pl.BlockSpec((group, rows, steps, width), lambda i: (first + step * i, 0, 0, 0)),
        ],
        out_specs=spec,
        cost_estimate=pl.CostEstimate(
            flops=2 * table.shape[1] * table.shape[2] * rows * width * count,
            bytes_accessed=count * group * rows * width * (2 * steps + 8 * slots),
            transcendentals=0,
        ),
        name="transform",
    )(table, field)


def split_kernel(x_ref, high_ref, low_ref):
    high, low = split_bf16(x_ref[...])
    high_ref[...] = high
    low_ref[...] = low


def split_transfer(transfer):
    parts, sensors, cells = transfer.shape
    block = pl.BlockSpec((1, sensors, cells), lambda a: (a, 0, 0))
    return pl.pallas_call(
        split_kernel,
        out_shape=[jax.ShapeDtypeStruct(transfer.shape, jnp.bfloat16)] * 2,
        grid=(parts,),
        in_specs=[block],
        out_specs=[block, block],
        cost_estimate=pl.CostEstimate(
            flops=2 * transfer.size, bytes_accessed=8 * transfer.size, transcendentals=0
        ),
        name="split_transfer",
    )(transfer)


def relaxed_rows(rows, coefficients):
    width = rows[0].shape[-1]
    lane = lax.broadcasted_iota(jnp.int32, rows[0].shape, 1)
    first, last = lane == 0, lane == width - 1
    out = []
    for i in range(1, len(rows) - 1):
        centre = rows[i]
        left = jnp.where(first, 0.0, pltpu.roll(centre, 1, 1))
        right = jnp.where(last, 0.0, pltpu.roll(centre, width - 1, 1))
        beside = (rows[i + 1] + rows[i - 1]) + (left + right)
        out.append(centre + coefficients[i - 1] * (beside - 4.0 * centre))
    return out


def smoothed(rows, coefficients):
    count = len(coefficients)
    for step in range(PASSES):
        rows = relaxed_rows(rows, coefficients[step : count - step])
    return rows


def coefficient_rows(low_ref, own_ref, high_ref):
    rim = PASSES - 1
    rows = [low_ref[i : i + 1] for i in range(rim)]
    rows += [own_ref[i : i + 1] for i in range(own_ref.shape[0])]
    return rows + [high_ref[i : i + 1] for i in range(rim)]


def finish_kernel(sources, paired, owners_in, smooth, *refs):
    refs = list(refs)
    chunks = [refs.pop(0) for _ in range(sources)]
    if smooth:
        low, high, own_c, low_c, high_c = (refs.pop(0) for _ in range(5))
        coefficients = coefficient_rows(low_c, own_c, high_c)
    t_high, t_low = refs.pop(0), refs.pop(0)
    outs, held = refs[:-1], refs[-1]
    flat = [(c, None) for c in chunks] if paired else [(chunks[0], g) for g in range(chunks[0].shape[0])]
    width = held.shape[-1] // flat_rows(chunks, paired)
    rows = flat_rows(chunks, paired)
    for index, (ref, at) in enumerate(flat):
        ref = ref if at is None else ref.at[at]
        vectors = ref.shape[2]
        each = vectors // owners_in
        for b in range(2):
            for o in range(owners_in):
                span = slice(o * each, (o + 1) * each)
                values = [ref[b, r, span] for r in range(rows)]
                if smooth:
                    before = [low[index, b, r, span] for r in range(PASSES)]
                    after = [high[index, b, r, span] for r in range(PASSES)]
                    values = smoothed(before + values + after, coefficients)
                if paired:
                    group = lax.axis_index("freq") ^ index
                    apart = (group * owners_in + o) ^ lax.axis_index("seabed")
                    place = (apart & 1) * (held.shape[1] // 2) + (apart >> 1)
                else:
                    place = index * owners_in + o
                for r in range(rows):
                    held[b, place, :, r * width : (r + 1) * width] = values[r]
    places, each, cells = held.shape[1:]
    lhs = held[...].reshape(2 * places * each, cells)
    lhs_high, lhs_low = split_bf16(lhs)

    def times(a):
        def dot(x, w):
            return lax.dot_general(
                x, w, (((1,), (1,)), ((), ())), preferred_element_type=jnp.float32
            )

        return (
            dot(lhs_low, t_high[a]) + dot(lhs_high, t_low[a])
        ) + dot(lhs_high, t_high[a])

    half = places * each
    by_real, by_imag = times(0), times(1)
    real = by_real[:half] - by_imag[half:]
    imag = by_imag[:half] + by_real[half:]
    sensors = real.shape[-1]
    if paired:
        for e in range(2):
            at = slice(e * half // 2, (e + 1) * half // 2)
            outs[e][:, 0] = real[at].reshape(places // 2, each, sensors)
            outs[e][:, 1] = imag[at].reshape(places // 2, each, sensors)
    else:
        outs[0][0] = real
        outs[0][1] = imag


def flat_rows(chunks, paired):
    return chunks[0].shape[1] if paired else chunks[0].shape[2]


def finish(chunks, rims, split, owners_in, paired):
    t_high, t_low = split
    sensors, cells = t_high.shape[1:]
    shape = chunks[0].shape if paired else chunks[0].shape[1:]
    count = len(chunks) if paired else chunks[0].shape[0]
    vectors = count * shape[2]
    places = count * owners_in
    each = vectors // places
    if paired:
        out = [jax.ShapeDtypeStruct((places // 2, 2, each, sensors), jnp.float32)] * 2
    else:
        out = [jax.ShapeDtypeStruct((2, vectors, sensors), jnp.float32)]
    return pl.pallas_call(
        functools.partial(finish_kernel, len(chunks), paired, owners_in, rims is not None),
        out_shape=out,
        scratch_shapes=[pltpu.VMEM((2, places, each, cells), jnp.float32)],
        cost_estimate=pl.CostEstimate(
            flops=24 * vectors * sensors * cells,
            bytes_accessed=8 * sensors * cells + 12 * vectors * cells + 8 * vectors * sensors,
            transcendentals=0,
        ),
        name="finish",
    )(*chunks, *(rims or ()), t_high, t_low)


def chain(count):
    up = [(i, i + 1) for i in range(count - 1)]
    return up, [(b, a) for a, b in up]


def xor_pairs(count, apart):
    return [(i, i ^ apart) for i in range(count)]


def shards(uplift, coefficient, transfer):
    vectors, steps, rows, width = uplift.shape
    freq_count, strips = lax.axis_size("freq"), lax.axis_size("seabed")
    owned = vectors * freq_count // strips
    owners_in = max(1, vectors // owned)
    field = jnp.transpose(uplift, (0, 2, 1, 3))
    up, down = chain(strips)
    paired = (
        owners_in == 2
        and strips == 2 * freq_count
        and strips & (strips - 1) == 0
        and owned % (LANE_GROUP * PHASES) == 0
    )
    rim = PASSES - 1
    low_c = lax.ppermute(coefficient[rows - rim :], "seabed", up)
    high_c = lax.ppermute(coefficient[:rim], "seabed", down)
    split = split_transfer(transfer[0])
    if paired:
        order = np.arange(freq_count)[:, None] ^ np.arange(freq_count)[None, :]
    else:
        order = np.arange(freq_count)[None, :]
    table = transform_operand(steps, freq_count, order)
    blocks = list(range(vectors // LANE_GROUP))
    spectrum = transform(field, table, freq_count, blocks, paired)
    if paired:
        chunks = [spectrum[0]] + [
            lax.ppermute(spectrum[m], "freq", xor_pairs(freq_count, m))
            for m in range(1, freq_count)
        ]
        stacked_low = jnp.stack([c[:, rows - PASSES :] for c in chunks])
        stacked_high = jnp.stack([c[:, :PASSES] for c in chunks])
    else:
        chunks = [lax.all_to_all(spectrum[0], "freq", split_axis=0, concat_axis=0, tiled=True)]
        stacked_low = chunks[0][:, :, rows - PASSES :]
        stacked_high = chunks[0][:, :, :PASSES]
    low = lax.ppermute(stacked_low, "seabed", up)
    high = lax.ppermute(stacked_high, "seabed", down)
    partial = finish(chunks, (low, high, coefficient, low_c, high_c), split, owners_in, paired)
    if paired:
        keep, send = partial
        pair = keep + lax.ppermute(send, "seabed", xor_pairs(strips, 1))
        total = pair[0]
        for d in range(1, strips // 2):
            total = total + lax.ppermute(pair[d], "seabed", xor_pairs(strips, 2 * d))
    else:
        spread = partial[0].reshape(2, strips, owned, -1)
        got = lax.all_to_all(spread, "seabed", split_axis=1, concat_axis=1, tiled=True)
        total = got.sum(1)
    return jnp.transpose(total, (1, 0, 2))[:, None]


def solution(mesh):
    placed = (P("freq", None, "seabed", None), P("seabed", None), P("freq", None, None, "seabed"))
    return jax.shard_map(
        shards,
        mesh=mesh,
        in_specs=placed,
        out_specs=P("seabed", "freq", None, None),
        check_vma=False,
    )
```

time: 159 us -> 56.8 us (0.36)
  waiting for transfers between devices: 87.5 us -> 18.2 us
  blocking collectives: 16.4 us -> 0 us
  between operations: 14.3 us -> 0.19 us
  local copies, waits for them, and re-layouts: 16.3 us -> 2.59 us
  Pallas kernels: 0 us -> 13.7 us
  starting transfers between devices: 10.1 us -> 20.6 us
  other arithmetic: 8.15 us -> 1.1 us
  matrix products: 6.35 us -> 0 us
    unnamed x2 -> x0, waiting for transfers between devices: 84.9 us -> none
    all_to_all x1 -> x0, blocking collectives: 16.4 us -> none  [shards(): lax.all_to_all(spectrum, 'freq', split_axis=0, concat_axis=2, tiled=True)]
    ppermute x4 -> x11, waiting for transfers between devices: 2.57 us -> 18.2 us  [the longest x3 11.6 us: shards(): lax.ppermute(spectrum[m], 'freq', xor_pairs(freq_count, m))]
    pallas_call x0 -> x3, Pallas kernels: none -> 13.7 us  [the longest x1 6.79 us: finish(): pl.pallas_call(functools.partial(finish_kernel, len(chunks), paired, owne...]
    ppermute x4 -> x11, starting transfers between devices: 10.1 us -> 20.6 us  [the longest x3 5.65 us: shards(): lax.ppermute(spectrum[m], 'freq', xor_pairs(freq_count, m))]
    dot_general x2 -> x0, matrix products: 6.35 us -> none  [the longest x1 3.21 us: shards(): jnp.einsum('ft,vtc->fvc', table, flat, precision=lax.Precision.HIGHEST)]
    add x3 -> x1, other arithmetic: 6.11 us -> 1.02 us  [shards(): pair = keep + lax.ppermute(send, 'seabed', xor_pairs(strips, 1))]
    reshape x1 -> x0, local copies, waits for them, and re-layouts: 4.7 us -> none  [shards(): flat = field.reshape(vectors, steps_count, rows * width)]
  transfers between devices with their start and end apart: 5 -> 11, of which waited for: 2 -> 6; matrix products, arithmetic and copies ran while one was open for 1% -> 2% of each run, Pallas kernels for 0% -> 6%
where the time goes in v1:
time: 56.8 us; the launch traced here: 56.4 us
  starting transfers between devices  20.6 us (36%)
  waiting for transfers between devices  18.2 us (32%)
  Pallas kernels  13.7 us (24%)
  local copies, waits for them, and re-layouts  2.59 us (5%)
  other arithmetic  1.1 us (2%)
    ppermute x3, waiting for transfers between devices, shards(): lax.ppermute(spectrum[m], 'freq', xor_pairs(freq_count, m))  11.6 us
    pallas_call x1, Pallas kernels, finish(): pl.pallas_call(functools.partial(finish_kernel, len(chunks), paired, owne...  6.79 us
    ppermute x3, starting transfers between devices, shards(): lax.ppermute(spectrum[m], 'freq', xor_pairs(freq_count, m))  5.65 us
    ppermute x1, starting transfers between devices, shards(): low_c = lax.ppermute(coefficient[rows - rim:], 'seabed', up)  5.36 us
    ppermute x3, waiting for transfers between devices, shards(): total = total + lax.ppermute(pair[d], 'seabed', xor_pairs(strips, 2 * d))  5.08 us
    ppermute x3, starting transfers between devices, shards(): total = total + lax.ppermute(pair[d], 'seabed', xor_pairs(strips, 2 * d))  4 us
    pallas_call x1, Pallas kernels, transform(): pl.pallas_call(functools.partial(transform_kernel, slots), out_shape=shap...  3.8 us
    pallas_call x1, Pallas kernels, split_transfer(): pl.pallas_call(split_kernel, out_shape=[jax.ShapeDtypeStruct(transfer.sha...  3.13 us
  transfers between devices with their start and end apart: 11, of which 6 were waited for; matrix products, arithmetic and copies ran while one was open for 2% of the time, Pallas kernels for 6%

profile of v1, /device:TPU:0, one launch (start us, length us, event | category | flops | bytes accessed | tf_op | source)
XLA Modules:
  0.0 56.4 jit_solution(7865892484881777393)
XLA Ops:
  0.0 3.8 %transform.1 = (f32[2,5,32,128]{3,2,1,0:T(8,128)}, f32[2,5,32,128]{3,2,1,0:T(8,128)}, f32[2,5,32,128]{3,2,1,0:T(8,128)}, f32[2,5,32,128]{3,2,1,0:T(8,128)}) custom-call(bf16[4,128,256]{2,1,0:T(8,128)(2,1)} %constant.2.clone.table_ref, bf16[32,5,32,128]{3,2,1,0:T(8,128)(2,1)} %bitcast.39), custom_call_target="tpu_custom_call" | custom-call | flops 167772160 | bytes 1966080 | tf_op jit(solution)/shard_map/transform/pallas_call | solution.py:74
  3.8 3.1 %collective-permute-start = (f32[2,5,32,128]{3,2,1,0:T(8,128)}, f32[2,5,32,128]{3,2,1,0:T(8,128)S(1)}, u32[]{:S(2)}, u32[]{:S(2)}) collective-permute-start(f32[2,5,32,128]{3,2,1,0:T(8,128)} %get-tuple-element.14), channel_id=1, source_target_pairs={{0,1},{1,0},{2,3},{3,2},{4,5},{5,4},{6,7},{7,6},{8,9},{9,8},{10,11... | collective-permute-start | bytes 491528 | tf_op jit(solution)/shard_map/ppermute | solution.py:266
  6.9 2.6 %collective-permute-start.1 = (f32[2,5,32,128]{3,2,1,0:T(8,128)}, f32[2,5,32,128]{3,2,1,0:T(8,128)S(1)}, u32[]{:S(2)}, u32[]{:S(2)}) collective-permute-start(f32[2,5,32,128]{3,2,1,0:T(8,128)} %get-tuple-element.15), channel_id=1, source_target_pairs={{0,2},{1,3},{2,0},{3,1},{4,6},{5,7},{6,4},{7,5},{8,10},{9,11},{10,... | collective-permute-start | bytes 491528 | tf_op jit(solution)/shard_map/ppermute | solution.py:266
  9.5 1.0 %slice_bitcast_fusion.6 = (f32[1,2,3,32,128]{4,3,2,1,0:T(8,128)S(1)}, f32[1,2,3,32,128]{4,3,2,1,0:T(8,128)S(1)}) fusion(f32[2,5,32,128]{3,2,1,0:T(8,128)} %get-tuple-element.13.refs_0_), kind=kLoop, calls=%fused_computation.8 | loop fusion | bytes 393216 | tf_op jit(solution)/shard_map/stack | solution.py:270
  10.4 10.1 %collective-permute-done.2.refs_3_ = f32[2,5,32,128]{3,2,1,0:T(8,128)S(1)} collective-permute-done((f32[2,5,32,128]{3,2,1,0:T(8,128)}, f32[2,5,32,128]{3,2,1,0:T(8,128)S(1)}, u32[]{:S(2)}, u32[]{:S(2)}) %collective-permute-start.2) | collective-permute-done | bytes 163872 | tf_op jit(solution)/shard_map/ppermute | solution.py:266
  20.6 1.5 %collective-permute-done.1.refs_2_ = f32[2,5,32,128]{3,2,1,0:T(8,128)S(1)} collective-permute-done((f32[2,5,32,128]{3,2,1,0:T(8,128)}, f32[2,5,32,128]{3,2,1,0:T(8,128)S(1)}, u32[]{:S(2)}, u32[]{:S(2)}) %collective-permute-start.1) | collective-permute-done | bytes 163872 | tf_op jit(solution)/shard_map/ppermute | solution.py:266
  22.2 1.3 %collective-permute-start.3 = (f32[4,2,3,32,128]{4,3,2,1,0:T(8,128)S(1)}, f32[4,2,3,32,128]{4,3,2,1,0:T(8,128)S(1)}, u32[]{:S(2)}, u32[]{:S(2)}) collective-permute-start(f32[4,2,3,32,128]{4,3,2,1,0:T(8,128)S(1)} %pad_maximum_fusion), channel_id=1, source_target_pairs={{0,4},{4,8},{8,12},{12,16},{16,20},{20,24},{24,28},{1,5},{5,9},{9,... | collective-permute-start | bytes 1179656 | tf_op jit(solution)/shard_map/ppermute | solution.py:275
  23.5 1.3 %collective-permute-start.4 = (f32[4,2,3,32,128]{4,3,2,1,0:T(8,128)S(1)}, f32[4,2,3,32,128]{4,3,2,1,0:T(8,128)S(1)}, u32[]{:S(2)}, u32[]{:S(2)}) collective-permute-start(f32[4,2,3,32,128]{4,3,2,1,0:T(8,128)S(1)} %pad_maximum_fusion.1), channel_id=1, source_target_pairs={{4,0},{8,4},{12,8},{16,12},{20,16},{24,20},{28,24},{5,1},{9,5},{13... | collective-permute-start | bytes 1179656 | tf_op jit(solution)/shard_map/ppermute | solution.py:276
  24.8 1.3 %collective-permute-start.6 = (f32[2,128]{1,0:T(2,128)S(1)}, f32[2,128]{1,0:T(2,128)S(1)}, u32[]{:S(2)}, u32[]{:S(2)}) collective-permute-start(f32[2,128]{1,0:T(2,128)S(1)} %get-tuple-element.32), channel_id=1, source_target_pairs={{4,0},{8,4},{12,8},{16,12},{20,16},{24,20},{28,24},{5,1},{9,5},{13... | collective-permute-start | bytes 3080 | tf_op jit(solution)/shard_map/ppermute | solution.py:255
  26.1 5.4 %collective-permute-start.5 = (f32[2,128]{1,0:T(2,128)S(1)}, f32[2,128]{1,0:T(2,128)S(1)}, u32[]{:S(2)}, u32[]{:S(2)}) collective-permute-start(f32[2,128]{1,0:T(2,128)S(1)} %get-tuple-element.33), channel_id=1, source_target_pairs={{0,4},{4,8},{8,12},{12,16},{16,20},{20,24},{24,28},{1,5},{5,9},{9,... | collective-permute-start | bytes 3080 | tf_op jit(solution)/shard_map/ppermute | solution.py:254
  31.5 3.1 %split_transfer.1 = (bf16[2,600,640]{2,1,0:T(8,128)(2,1)}, bf16[2,600,640]{2,1,0:T(8,128)(2,1)}) custom-call(f32[2,600,640]{2,1,0:T(8,128)} %bitcast.38), custom_call_target="tpu_custom_call" | custom-call | flops 1536000 | bytes 6144000 | tf_op jit(solution)/shard_map/split_transfer/pallas_call | solution.py:101
  34.7 0.5 copy-done.6
  35.3 0.2 copy-done.3
  35.6 6.8 %finish.1 = (f32[4,2,16,600]{3,2,1,0:T(8,128)}, f32[4,2,16,600]{3,2,1,0:T(8,128)}) custom-call(f32[2,5,32,128]{3,2,1,0:T(8,128)} %get-tuple-element.13.refs_0_, f32[2,5,32,128]{3,2,1,0:T(8,128)} %copy-done, f32[2,5,32,128]{3,2,1,0:T(8,128)} %copy-done.1, f32[2,5,32,128]{3,2,1,0:T(8,128)} %copy-done.2, f32[4,2,3,32,128]{4,3,2,1,0:T(8,128)} %copy-done.3, ...), custom_call_target="tpu_custom_call" | custom-call | flops 1179648000 | bytes 4669440 | tf_op jit(solution)/shard_map/finish/pallas_call | solution.py:218
  42.4 1.7 %collective-permute-start.7 = (f32[4,2,16,600]{3,2,1,0:T(8,128)}, f32[4,2,16,600]{3,2,1,0:T(8,128)S(1)}, u32[]{:S(2)}, u32[]{:S(2)}) collective-permute-start(f32[4,2,16,600]{3,2,1,0:T(8,128)} %get-tuple-element.20), channel_id=1, source_target_pairs={{0,4},{4,0},{8,12},{12,8},{16,20},{20,16},{24,28},{28,24},{1,5},{5... | collective-permute-start | bytes 921608 | tf_op jit(solution)/shard_map/ppermute | solution.py:280
  44.1 1.5 %collective-permute-done.7 = f32[4,2,16,600]{3,2,1,0:T(8,128)S(1)} collective-permute-done((f32[4,2,16,600]{3,2,1,0:T(8,128)}, f32[4,2,16,600]{3,2,1,0:T(8,128)S(1)}, u32[]{:S(2)}, u32[]{:S(2)}) %collective-permute-start.7) | collective-permute-done | bytes 307232 | tf_op jit(solution)/shard_map/ppermute | solution.py:280
  45.6 1.0 %add.12 = f32[4,2,16,600]{3,2,1,0:T(8,128)S(1)} add(f32[4,2,16,600]{3,2,1,0:T(8,128)} %get-tuple-element.19, f32[4,2,16,600]{3,2,1,0:T(8,128)S(1)} %collective-permute-done.7) | non-fusion elementwise | flops 76800 | bytes 921600 | tf_op jit(solution)/shard_map/add | solution.py:280
  46.6 2.5 %collective-permute-start.8 = (f32[2,16,600]{2,1,0:T(8,128)S(1)}, f32[2,16,600]{2,1,0:T(8,128)S(1)}, u32[]{:S(2)}, u32[]{:S(2)}) collective-permute-start(f32[2,16,600]{2,1,0:T(8,128)S(1)} %get-tuple-element.21), channel_id=1, source_target_pairs={{0,8},{4,12},{8,0},{12,4},{16,24},{20,28},{24,16},{28,20},{1,9},{5... | collective-permute-start | bytes 230408 | tf_op jit(solution)/shard_map/ppermute | solution.py:283
  49.1 0.9 %collective-permute-start.10 = (f32[2,16,600]{2,1,0:T(8,128)S(1)}, f32[2,16,600]{2,1,0:T(8,128)S(1)}, u32[]{:S(2)}, u32[]{:S(2)}) collective-permute-start(f32[2,16,600]{2,1,0:T(8,128)S(1)} %get-tuple-element.22), channel_id=1, source_target_pairs={{0,24},{4,28},{8,16},{12,20},{16,8},{20,12},{24,0},{28,4},{1,25},{... | collective-permute-start | bytes 230408 | tf_op jit(solution)/shard_map/ppermute | solution.py:283
  50.0 0.6 %collective-permute-start.9 = (f32[2,16,600]{2,1,0:T(8,128)S(1)}, f32[2,16,600]{2,1,0:T(8,128)S(1)}, u32[]{:S(2)}, u32[]{:S(2)}) collective-permute-start(f32[2,16,600]{2,1,0:T(8,128)S(1)} %get-tuple-element.23), channel_id=1, source_target_pairs={{0,16},{4,20},{8,24},{12,28},{16,0},{20,4},{24,8},{28,12},{1,17},{... | collective-permute-start | bytes 230408 | tf_op jit(solution)/shard_map/ppermute | solution.py:283
  50.6 1.8 %collective-permute-done.8 = f32[2,16,600]{2,1,0:T(8,128)S(1)} collective-permute-done((f32[2,16,600]{2,1,0:T(8,128)S(1)}, f32[2,16,600]{2,1,0:T(8,128)S(1)}, u32[]{:S(2)}, u32[]{:S(2)}) %collective-permute-start.8) | collective-permute-done | bytes 76832 | tf_op jit(solution)/shard_map/ppermute | solution.py:283
  52.4 2.1 %collective-permute-done.10 = f32[2,16,600]{2,1,0:T(8,128)S(1)} collective-permute-done((f32[2,16,600]{2,1,0:T(8,128)S(1)}, f32[2,16,600]{2,1,0:T(8,128)S(1)}, u32[]{:S(2)}, u32[]{:S(2)}) %collective-permute-start.10) | collective-permute-done | bytes 76832 | tf_op jit(solution)/shard_map/ppermute | solution.py:283
  54.5 1.2 %collective-permute-done.9 = f32[2,16,600]{2,1,0:T(8,128)S(1)} collective-permute-done((f32[2,16,600]{2,1,0:T(8,128)S(1)}, f32[2,16,600]{2,1,0:T(8,128)S(1)}, u32[]{:S(2)}, u32[]{:S(2)}) %collective-permute-start.9) | collective-permute-done | bytes 76832 | tf_op jit(solution)/shard_map/ppermute | solution.py:283
  55.7 0.7 %copy.5 = f32[16,1,2,600]{3,2,1,0:T(2,128)} copy(f32[16,1,2,600]{3,0,2,1:T(8,128)S(1)} %fusion.3) | data formatting | bytes 153600 | tf_op jit(solution)/shard_map/broadcast_in_dim | solution.py:288
  (28 shorter events, 0.3 us)
Async XLA Ops:
  3.8 18.3 %collective-permute-start = (f32[2,5,32,128]{3,2,1,0:T(8,128)}, f32[2,5,32,128]{3,2,1,0:T(8,128)S(1)}, u32[]{:S(2)}, u32[]{:S(2)}) collective-permute-start(f32[2,5,32,128]{3,2,1,0:T(8,128)} %get-tuple-element.14), channel_id=1, source_target_pairs={{0,1},{1,0},{2,3},{3,2},{4,5},{5,4},{6,7},{7,6},{8,9},{9,8},{10,11... | collective-permute-start | bytes 491528 | tf_op jit(solution)/shard_map/ppermute | solution.py:266
  6.9 15.2 %collective-permute-start.1 = (f32[2,5,32,128]{3,2,1,0:T(8,128)}, f32[2,5,32,128]{3,2,1,0:T(8,128)S(1)}, u32[]{:S(2)}, u32[]{:S(2)}) collective-permute-start(f32[2,5,32,128]{3,2,1,0:T(8,128)} %get-tuple-element.15), channel_id=1, source_target_pairs={{0,2},{1,3},{2,0},{3,1},{4,6},{5,7},{6,4},{7,5},{8,10},{9,11},{10,... | collective-permute-start | bytes 491528 | tf_op jit(solution)/shard_map/ppermute | solution.py:266
  9.5 11.1 %collective-permute-start.2 = (f32[2,5,32,128]{3,2,1,0:T(8,128)}, f32[2,5,32,128]{3,2,1,0:T(8,128)S(1)}, u32[]{:S(2)}, u32[]{:S(2)}) collective-permute-start(f32[2,5,32,128]{3,2,1,0:T(8,128)} %get-tuple-element.16), channel_id=1, source_target_pairs={{0,3},{1,2},{2,1},{3,0},{4,7},{5,6},{6,5},{7,4},{8,11},{9,10},{10,... | collective-permute-start | bytes 491528 | tf_op jit(solution)/shard_map/ppermute | solution.py:266
  9.5 15.4 %copy-start.5 = (f32[5,128]{1,0:T(8,128)S(1)}, f32[5,128]{1,0:T(8,128)}, u32[]{:S(2)}) copy-start(f32[5,128]{1,0:T(8,128)} %refs_6_.1) | copy-start | bytes 7684
  20.6 14.1 %copy-start.2 = (f32[2,5,32,128]{3,2,1,0:T(8,128)}, f32[2,5,32,128]{3,2,1,0:T(8,128)S(1)}, u32[]{:S(2)}) copy-start(f32[2,5,32,128]{3,2,1,0:T(8,128)S(1)} %collective-permute-done.2.refs_3_) | copy-start | bytes 491524
  22.1 12.6 %copy-start.1 = (f32[2,5,32,128]{3,2,1,0:T(8,128)}, f32[2,5,32,128]{3,2,1,0:T(8,128)S(1)}, u32[]{:S(2)}) copy-start(f32[2,5,32,128]{3,2,1,0:T(8,128)S(1)} %collective-permute-done.1.refs_2_) | copy-start | bytes 491524
  22.1 12.6 %copy-start = (f32[2,5,32,128]{3,2,1,0:T(8,128)}, f32[2,5,32,128]{3,2,1,0:T(8,128)S(1)}, u32[]{:S(2)}) copy-start(f32[2,5,32,128]{3,2,1,0:T(8,128)S(1)} %collective-permute-done.refs_1_) | copy-start | bytes 491524
  22.2 12.5 %collective-permute-start.3 = (f32[4,2,3,32,128]{4,3,2,1,0:T(8,128)S(1)}, f32[4,2,3,32,128]{4,3,2,1,0:T(8,128)S(1)}, u32[]{:S(2)}, u32[]{:S(2)}) collective-permute-start(f32[4,2,3,32,128]{4,3,2,1,0:T(8,128)S(1)} %pad_maximum_fusion), channel_id=1, source_target_pairs={{0,4},{4,8},{8,12},{12,16},{16,20},{20,24},{24,28},{1,5},{5,9},{9,... | collective-permute-start | bytes 1179656 | tf_op jit(solution)/shard_map/ppermute | solution.py:275
  23.5 11.2 %collective-permute-start.4 = (f32[4,2,3,32,128]{4,3,2,1,0:T(8,128)S(1)}, f32[4,2,3,32,128]{4,3,2,1,0:T(8,128)S(1)}, u32[]{:S(2)}, u32[]{:S(2)}) collective-permute-start(f32[4,2,3,32,128]{4,3,2,1,0:T(8,128)S(1)} %pad_maximum_fusion.1), channel_id=1, source_target_pairs={{4,0},{8,4},{12,8},{16,12},{20,16},{24,20},{28,24},{5,1},{9,5},{13... | collective-permute-start | bytes 1179656 | tf_op jit(solution)/shard_map/ppermute | solution.py:276
  24.8 9.8 %collective-permute-start.6 = (f32[2,128]{1,0:T(2,128)S(1)}, f32[2,128]{1,0:T(2,128)S(1)}, u32[]{:S(2)}, u32[]{:S(2)}) collective-permute-start(f32[2,128]{1,0:T(2,128)S(1)} %get-tuple-element.32), channel_id=1, source_target_pairs={{4,0},{8,4},{12,8},{16,12},{20,16},{24,20},{28,24},{5,1},{9,5},{13... | collective-permute-start | bytes 3080 | tf_op jit(solution)/shard_map/ppermute | solution.py:255
  26.1 8.5 %collective-permute-start.5 = (f32[2,128]{1,0:T(2,128)S(1)}, f32[2,128]{1,0:T(2,128)S(1)}, u32[]{:S(2)}, u32[]{:S(2)}) collective-permute-start(f32[2,128]{1,0:T(2,128)S(1)} %get-tuple-element.33), channel_id=1, source_target_pairs={{0,4},{4,8},{8,12},{12,16},{16,20},{20,24},{24,28},{1,5},{5,9},{9,... | collective-permute-start | bytes 3080 | tf_op jit(solution)/shard_map/ppermute | solution.py:254
  34.7 0.6 %copy-start.6 = (f32[2,128]{1,0:T(2,128)}, f32[2,128]{1,0:T(2,128)S(1)}, u32[]{:S(2)}) copy-start(f32[2,128]{1,0:T(2,128)S(1)} %collective-permute-done.6.refs_8_) | copy-start | bytes 3076
  34.7 0.6 %copy-start.7 = (f32[2,128]{1,0:T(2,128)}, f32[2,128]{1,0:T(2,128)S(1)}, u32[]{:S(2)}) copy-start(f32[2,128]{1,0:T(2,128)S(1)} %collective-permute-done.5.refs_7_) | copy-start | bytes 3076
  34.7 0.7 %copy-start.3 = (f32[4,2,3,32,128]{4,3,2,1,0:T(8,128)}, f32[4,2,3,32,128]{4,3,2,1,0:T(8,128)S(1)}, u32[]{:S(2)}) copy-start(f32[4,2,3,32,128]{4,3,2,1,0:T(8,128)S(1)} %collective-permute-done.3.refs_4_) | copy-start | bytes 1179652
  34.7 0.8 %copy-start.4 = (f32[4,2,3,32,128]{4,3,2,1,0:T(8,128)}, f32[4,2,3,32,128]{4,3,2,1,0:T(8,128)S(1)}, u32[]{:S(2)}) copy-start(f32[4,2,3,32,128]{4,3,2,1,0:T(8,128)S(1)} %collective-permute-done.4.refs_5_) | copy-start | bytes 1179652
  42.4 3.2 %collective-permute-start.7 = (f32[4,2,16,600]{3,2,1,0:T(8,128)}, f32[4,2,16,600]{3,2,1,0:T(8,128)S(1)}, u32[]{:S(2)}, u32[]{:S(2)}) collective-permute-start(f32[4,2,16,600]{3,2,1,0:T(8,128)} %get-tuple-element.20), channel_id=1, source_target_pairs={{0,4},{4,0},{8,12},{12,8},{16,20},{20,16},{24,28},{28,24},{1,5},{5... | collective-permute-start | bytes 921608 | tf_op jit(solution)/shard_map/ppermute | solution.py:280
  46.6 5.8 %collective-permute-start.8 = (f32[2,16,600]{2,1,0:T(8,128)S(1)}, f32[2,16,600]{2,1,0:T(8,128)S(1)}, u32[]{:S(2)}, u32[]{:S(2)}) collective-permute-start(f32[2,16,600]{2,1,0:T(8,128)S(1)} %get-tuple-element.21), channel_id=1, source_target_pairs={{0,8},{4,12},{8,0},{12,4},{16,24},{20,28},{24,16},{28,20},{1,9},{5... | collective-permute-start | bytes 230408 | tf_op jit(solution)/shard_map/ppermute | solution.py:283
  49.1 5.4 %collective-permute-start.10 = (f32[2,16,600]{2,1,0:T(8,128)S(1)}, f32[2,16,600]{2,1,0:T(8,128)S(1)}, u32[]{:S(2)}, u32[]{:S(2)}) collective-permute-start(f32[2,16,600]{2,1,0:T(8,128)S(1)} %get-tuple-element.22), channel_id=1, source_target_pairs={{0,24},{4,28},{8,16},{12,20},{16,8},{20,12},{24,0},{28,4},{1,25},{... | collective-permute-start | bytes 230408 | tf_op jit(solution)/shard_map/ppermute | solution.py:283
  50.0 5.7 %collective-permute-start.9 = (f32[2,16,600]{2,1,0:T(8,128)S(1)}, f32[2,16,600]{2,1,0:T(8,128)S(1)}, u32[]{:S(2)}, u32[]{:S(2)}) collective-permute-start(f32[2,16,600]{2,1,0:T(8,128)S(1)} %get-tuple-element.23), channel_id=1, source_target_pairs={{0,16},{4,20},{8,24},{12,28},{16,0},{20,4},{24,8},{28,12},{1,17},{... | collective-permute-start | bytes 230408 | tf_op jit(solution)/shard_map/ppermute | solution.py:283

commit v2 on v0

v2 whole, which is shorter than its diff:
```python
import functools
import math

import jax
import jax.numpy as jnp
import numpy as np
from jax import lax
from jax.experimental import pallas as pl
from jax.experimental.pallas import tpu as pltpu
from jax.sharding import PartitionSpec as P


FD = 1
PASSES = 3
GROUP = 8
GRANT = 16 * 1024 * 1024


def params():
    return pltpu.CompilerParams(vmem_limit_bytes=GRANT)


def cost(flops, moved):
    return pl.CostEstimate(flops=flops, bytes_accessed=moved, transcendentals=0)


def dft_table(steps_count, freq_count):
    times = np.arange(steps_count)
    freqs = np.arange(freq_count)
    phase = (freqs[:, None] * times[None, :] % steps_count) * (2.0 * math.pi / steps_count)
    scale = 1.0 / math.sqrt(steps_count)
    return (np.stack([np.cos(phase), -np.sin(phase)], 1) * scale).astype(np.float32)


def split_bf16(values):
    high = values.astype(jnp.bfloat16)
    low = (values - high.astype(values.dtype)).astype(jnp.bfloat16)
    return high, low


def transform_operand(steps_count, freq_count, order):
    table = dft_table(steps_count, freq_count)[order]
    eye = np.eye(GROUP, dtype=np.float32)
    high, low = split_bf16(table)
    parts = np.stack([high.astype(np.float32), low.astype(np.float32)], 1)
    full = np.einsum("fpkbt,vw->fpkbvwt", parts, eye)
    return jnp.asarray(full.reshape(full.shape[0], -1, GROUP * steps_count), jnp.bfloat16)


def transform_kernel(slots, edges, table_ref, field_ref, *outs):
    at_table = lax.axis_index("freq") if table_ref.shape[0] > 1 else 0
    group, rows, steps, width = field_ref.shape
    data = jnp.concatenate(
        [field_ref[:, r].reshape(group * steps, width) for r in range(rows)], axis=1
    )
    both = jnp.dot(table_ref[at_table], data, preferred_element_type=jnp.float32)
    half = both.shape[0] // 2
    values = both[:half] + both[half:]
    i = pl.program_id(0)
    for slot in range(slots):
        for b in range(2):
            at = (slot * 2 + b) * group
            for r in range(rows):
                piece = values[at : at + group, r * width : (r + 1) * width]
                outs[slot][b, r] = piece
                if edges:
                    low, high = outs[slots:]
                    if r >= rows - PASSES:
                        low[slot * 2 + b, r - rows + PASSES, i] = piece
                    if r < PASSES:
                        high[slot * 2 + b, r, i] = piece


def transform(field, table, slots, blocks, edges):
    _, rows, steps, width = field.shape
    count = len(blocks)
    first = blocks[0]
    stride = blocks[1] - first if count > 1 else 1
    shape = [jax.ShapeDtypeStruct((2, rows, count * GROUP, width), jnp.float32)] * slots
    spec = [pl.BlockSpec((2, rows, GROUP, width), lambda i: (0, 0, i, 0))] * slots
    if edges:
        rim = (slots * 2, PASSES, count, GROUP, width)
        shape = shape + [jax.ShapeDtypeStruct(rim, jnp.float32)] * 2
        spec = spec + [pl.BlockSpec(rim, lambda i: (0, 0, 0, 0, 0))] * 2
    return pl.pallas_call(
        functools.partial(transform_kernel, slots, edges),
        out_shape=shape,
        grid=(count,),
        in_specs=[
            pl.BlockSpec(table.shape, lambda i: (0, 0, 0)),
            pl.BlockSpec((GROUP, rows, steps, width), lambda i: (first + stride * i, 0, 0, 0)),
        ],
        out_specs=spec,
        compiler_params=params(),
        cost_estimate=cost(
            2 * table.shape[1] * table.shape[2] * rows * width * count,
            count * GROUP * rows * width * (2 * steps + 8 * slots),
        ),
        name="transform",
    )(table, field)


def split_kernel(x_ref, high_ref, low_ref):
    high, low = split_bf16(x_ref[...])
    high_ref[...] = high
    low_ref[...] = low


def split_transfer(transfer):
    parts, sensors, cells = transfer.shape
    block = pl.BlockSpec((1, sensors, cells), lambda a: (a, 0, 0))
    return pl.pallas_call(
        split_kernel,
        out_shape=[jax.ShapeDtypeStruct(transfer.shape, jnp.bfloat16)] * 2,
        grid=(parts,),
        in_specs=[block],
        out_specs=[block, block],
        compiler_params=params(),
        cost_estimate=cost(2 * transfer.size, 8 * transfer.size),
        name="split_transfer",
    )(transfer)


def relaxed_rows(rows, coefficients):
    width = rows[0].shape[-1]
    lane = lax.broadcasted_iota(jnp.int32, rows[0].shape, 1)
    first, last = lane == 0, lane == width - 1
    out = []
    for i in range(1, len(rows) - 1):
        centre = rows[i]
        left = jnp.where(first, 0.0, pltpu.roll(centre, 1, 1))
        right = jnp.where(last, 0.0, pltpu.roll(centre, width - 1, 1))
        beside = (rows[i + 1] + rows[i - 1]) + (left + right)
        out.append(centre + coefficients[i - 1] * (beside - 4.0 * centre))
    return out


def smooth_kernel(count, *refs):
    chunks, (low, high, own_c, low_c, high_c) = refs[:count], refs[count : count + 5]
    outs = refs[count + 5 :]
    rows, vectors, width = chunks[0].shape[1:]
    rim = PASSES - 1
    coefficients = [low_c[i : i + 1] for i in range(rim)]
    coefficients += [own_c[i : i + 1] for i in range(rows)]
    coefficients += [high_c[i : i + 1] for i in range(rim)]
    coefficients = [jnp.broadcast_to(c, (vectors, width)) for c in coefficients]
    for index in range(count):
        for b in range(2):
            values = [low[index * 2 + b, r] for r in range(PASSES)]
            values += [chunks[index][b, r] for r in range(rows)]
            values += [high[index * 2 + b, r] for r in range(PASSES)]
            for step in range(PASSES):
                values = relaxed_rows(values, coefficients[step : len(coefficients) - step])
            for r in range(rows):
                outs[index][b, r] = values[r]


def smooth(chunks, low, high, coefficients):
    shape = chunks[0].shape
    size = len(chunks) * math.prod(shape)
    return pl.pallas_call(
        functools.partial(smooth_kernel, len(chunks)),
        out_shape=[jax.ShapeDtypeStruct(shape, jnp.float32)] * len(chunks),
        compiler_params=params(),
        cost_estimate=cost(30 * size, 10 * size),
        name="smooth",
    )(*chunks, low, high, *coefficients)


def combine_kernel(chunks_in, owners_in, paired, *refs):
    refs = list(refs)
    phases = [[refs.pop(0) for _ in range(count)] for count in chunks_in]
    t_high, t_low = refs.pop(0), refs.pop(0)
    outs, held = refs[:-1], refs[-1]
    rows, vectors, width = phases[0][0].shape[1:]
    each = vectors // owners_in
    for phase, chunks in enumerate(phases):
        inner = slice(phase * each, (phase + 1) * each)
        for index, ref in enumerate(chunks):
            for o in range(owners_in):
                if paired:
                    owner = (lax.axis_index("freq") ^ index) * owners_in + o
                    apart = owner ^ lax.axis_index("seabed")
                    place = (apart & 1) * (held.shape[1] // 2) + (apart >> 1)
                else:
                    place = index * owners_in + o
                for b in range(2):
                    for r in range(rows):
                        held[b, place, inner, r * width : (r + 1) * width] = ref[
                            b, r, o * each : (o + 1) * each
                        ]
    places, owned, cells = held.shape[1:]
    lhs_high, lhs_low = split_bf16(held[...].reshape(2 * places * owned, cells))

    def times(a):
        def dot(x, w):
            return lax.dot_general(
                x, w, (((1,), (1,)), ((), ())), preferred_element_type=jnp.float32
            )

        return (dot(lhs_low, t_high[a]) + dot(lhs_high, t_low[a])) + dot(lhs_high, t_high[a])

    half = places * owned
    by_real, by_imag = times(0), times(1)
    real = by_real[:half] - by_imag[half:]
    imag = by_imag[:half] + by_real[half:]
    sensors = real.shape[-1]
    share = places // len(outs)
    for e, out in enumerate(outs):
        at = slice(e * share * owned, (e + 1) * share * owned)
        out[:, 0] = real[at].reshape(share, owned, sensors)
        out[:, 1] = imag[at].reshape(share, owned, sensors)


def combine(phases, split, owners_in, paired):
    t_high, t_low = split
    sensors, cells = t_high.shape[1:]
    places = len(phases[0]) * owners_in
    owned = sum(p[0].shape[2] for p in phases) // owners_in
    vectors = places * owned
    outs = 2 if paired else 1
    return pl.pallas_call(
        functools.partial(combine_kernel, [len(p) for p in phases], owners_in, paired),
        out_shape=[jax.ShapeDtypeStruct((places // outs, 2, owned, sensors), jnp.float32)] * outs,
        scratch_shapes=[pltpu.VMEM((2, places, owned, cells), jnp.float32)],
        compiler_params=params(),
        cost_estimate=cost(
            24 * vectors * sensors * cells,
            8 * sensors * cells + 8 * vectors * cells + 16 * vectors * sensors,
        ),
        name="combine",
    )(*[c for p in phases for c in p], t_high, t_low)


def chain(count):
    up = [(i, i + 1) for i in range(count - 1)]
    return up, [(b, a) for a, b in up]


def xor_pairs(count, apart):
    return [(i, i ^ apart) for i in range(count)]


def halo_of(chunks):
    rows, vectors, width = chunks[0].shape[1:]
    last = jnp.stack([c[:, rows - PASSES :] for c in chunks])
    first = jnp.stack([c[:, :PASSES] for c in chunks])
    return [x.reshape(-1, PASSES, vectors, width) for x in (last, first)]


def paired_shards(field, coefficient, split_of, table, freq_count, strips, owned):
    vectors, rows, _, width = field.shape
    rim = PASSES - 1
    up, down = chain(strips)
    blocks = np.arange(vectors // GROUP).reshape(2, 2).T.tolist()

    def exchange(chunks):
        moved = {
            m: lax.ppermute(chunks[m], "freq", xor_pairs(freq_count, m))
            for m in reversed(range(1, freq_count))
        }
        return [chunks[0]] + [moved[m] for m in range(1, freq_count)]

    first = transform(field, table, freq_count, blocks[0], False)
    first = exchange(first)
    *second, last_rows, first_rows = transform(field, table, freq_count, blocks[1], True)
    pad = ((0, GROUP - rim), (0, 0))

    def with_rim(edge, rim_rows):
        flat = edge.reshape(-1, width)
        return jnp.concatenate([flat, jnp.pad(rim_rows, pad)], 0)

    def without_rim(moved):
        edge = moved[:-GROUP].reshape(2 * freq_count, PASSES, -1, width)
        return edge, moved[-GROUP : -GROUP + rim]

    last_rows = with_rim(last_rows, coefficient[rows - rim :])
    first_rows = with_rim(first_rows, coefficient[:rim])
    low = lax.ppermute(last_rows, "seabed", up)
    high = lax.ppermute(first_rows, "seabed", down)
    low, low_c = without_rim(low)
    high, high_c = without_rim(high)
    coefficients = (coefficient, low_c, high_c)
    split = split_of()
    second = smooth(second, low, high, coefficients)
    second = exchange(second)
    last_rows, first_rows = halo_of(first)
    low = lax.ppermute(last_rows, "seabed", up)
    high = lax.ppermute(first_rows, "seabed", down)
    first = smooth(first, low, high, coefficients)
    keep, send = combine([first, second], split, 2, True)
    pair = keep + lax.ppermute(send, "seabed", xor_pairs(strips, 1))
    total = pair[0]
    for d in range(1, strips // 2):
        total = total + lax.ppermute(pair[d], "seabed", xor_pairs(strips, 2 * d))
    return total


def plain_shards(field, coefficient, split_of, table, freq_count, strips, owned):
    vectors, rows, _, _ = field.shape
    rim = PASSES - 1
    up, down = chain(strips)
    blocks = list(range(vectors // GROUP))
    spectrum = jnp.stack(transform(field, table, freq_count, blocks, False))
    spectrum = lax.all_to_all(spectrum, "freq", split_axis=0, concat_axis=0, tiled=True)
    chunks = list(spectrum)
    last_rows, first_rows = halo_of(chunks)
    low = lax.ppermute(last_rows, "seabed", up)
    high = lax.ppermute(first_rows, "seabed", down)
    low_c = lax.ppermute(coefficient[rows - rim :], "seabed", up)
    high_c = lax.ppermute(coefficient[:rim], "seabed", down)
    chunks = smooth(chunks, low, high, (coefficient, low_c, high_c))
    (partial,) = combine([chunks], split_of(), vectors // owned, False)
    got = lax.all_to_all(partial, "seabed", split_axis=0, concat_axis=0, tiled=True)
    return got.sum(0)


def shards(uplift, coefficient, transfer):
    vectors, steps, _, _ = uplift.shape
    freq_count, strips = FD * lax.axis_size("freq"), lax.axis_size("seabed")
    owned = vectors * freq_count // strips
    paired = (
        strips == 2 * freq_count
        and strips & (strips - 1) == 0
        and vectors == 2 * owned
        and owned == 2 * GROUP
    )
    slots = np.arange(freq_count)
    order = slots[:, None] ^ slots[None, :] if paired else slots[None, :]
    table = transform_operand(steps, freq_count, order)
    field = jnp.transpose(uplift, (0, 2, 1, 3))
    run = paired_shards if paired else plain_shards
    total = run(
        field,
        coefficient,
        lambda: split_transfer(transfer[0]),
        table,
        freq_count,
        strips,
        owned,
    )
    return jnp.transpose(total, (1, 0, 2))[:, None]


def solution(mesh):
    placed = (P("freq", None, "seabed", None), P("seabed", None), P("freq", None, None, "seabed"))
    return jax.shard_map(
        shards,
        mesh=mesh,
        in_specs=placed,
        out_specs=P("seabed", "freq", None, None),
        check_vma=False,
    )
```

time: 159 us -> 47.8 us (0.30)
  waiting for transfers between devices: 87.5 us -> 14.3 us
  blocking collectives: 16.4 us -> 0 us
  between operations: 14.3 us -> 0.25 us
  starting transfers between devices: 10.1 us -> 23.5 us
  local copies, waits for them, and re-layouts: 16.3 us -> 3.04 us
  other arithmetic: 8.15 us -> 0.13 us
  matrix products: 6.35 us -> 0 us
  Pallas kernels: 0 us -> 6.27 us
    unnamed x2 -> x0, waiting for transfers between devices: 84.9 us -> none
    all_to_all x1 -> x0, blocking collectives: 16.4 us -> none  [shards(): lax.all_to_all(spectrum, 'freq', split_axis=0, concat_axis=2, tiled=True)]
    ppermute x4 -> x14, starting transfers between devices: 10.1 us -> 23.5 us  [the longest x6 10.2 us: exchange(): lax.ppermute(chunks[m], 'freq', xor_pairs(freq_count, m))]
    ppermute x4 -> x14, waiting for transfers between devices: 2.57 us -> 14.3 us  [the longest x6 7.67 us: exchange(): lax.ppermute(chunks[m], 'freq', xor_pairs(freq_count, m))]
    dot_general x2 -> x0, matrix products: 6.35 us -> none  [the longest x1 3.21 us: shards(): jnp.einsum('ft,vtc->fvc', table, flat, precision=lax.Precision.HIGHEST)]
    pallas_call x0 -> x6, Pallas kernels: none -> 6.27 us  [the longest x2 2.76 us: smooth(): pl.pallas_call(functools.partial(smooth_kernel, len(chunks)), out_shape=[...]
    add x3 -> x1, other arithmetic: 6.11 us -> 0.04 us  [paired_shards(): pair = keep + lax.ppermute(send, 'seabed', xor_pairs(strips, 1))]
    reshape x1 -> x0, local copies, waits for them, and re-layouts: 4.7 us -> none  [shards(): flat = field.reshape(vectors, steps_count, rows * width)]
  transfers between devices with their start and end apart: 5 -> 14, of which waited for: 2 -> 8; matrix products, arithmetic and copies ran while one was open for 1% -> 0% of each run, Pallas kernels for 0% -> 8%
where the time goes in v2:
time: 47.8 us; the launch traced here: 47.6 us
  starting transfers between devices  23.5 us (49%)
  waiting for transfers between devices  14.3 us (30%)
  Pallas kernels  6.27 us (13%)
  local copies, waits for them, and re-layouts  3.04 us (6%)
    ppermute x6, starting transfers between devices, exchange(): lax.ppermute(chunks[m], 'freq', xor_pairs(freq_count, m))  10.2 us
    ppermute x6, waiting for transfers between devices, exchange(): lax.ppermute(chunks[m], 'freq', xor_pairs(freq_count, m))  7.67 us
    ppermute x3, starting transfers between devices, paired_shards(): total = total + lax.ppermute(pair[d], 'seabed', xor_pairs(strips, 2 * d))  6.8 us
    ppermute x3, waiting for transfers between devices, paired_shards(): total = total + lax.ppermute(pair[d], 'seabed', xor_pairs(strips, 2 * d))  5.41 us
    ppermute x2, starting transfers between devices, paired_shards(): low = lax.ppermute(last_rows, 'seabed', up)  3.18 us
    pallas_call x2, Pallas kernels, smooth(): pl.pallas_call(functools.partial(smooth_kernel, len(chunks)), out_shape=[...  2.76 us
    ppermute x2, starting transfers between devices, paired_shards(): high = lax.ppermute(first_rows, 'seabed', down)  2.58 us
    unnamed x8, local copies, waits for them, and re-layouts  2.28 us
  transfers between devices with their start and end apart: 14, of which 8 were waited for; matrix products, arithmetic and copies ran while one was open for 0% of the time, Pallas kernels for 8%

profile of v2, /device:TPU:0, one launch (start us, length us, event | category | flops | bytes accessed | tf_op | source)
XLA Modules:
  0.0 47.6 jit_solution(1991698660103419449)
XLA Ops:
  0.0 1.3 %copy-done = bf16[32,32,5,128]{3,1,2,0:T(8,128)(2,1)S(1)} copy-done((bf16[32,32,5,128]{3,1,2,0:T(8,128)(2,1)S(1)}, bf16[32,32,5,128]{3,1,2,0:T(8,128)(2,1)}, u32[]{:S(2)}) %copy-start) | copy-done | bytes 1310744
  1.3 0.9 %copy-done.2 = bf16[4,128,256]{2,1,0:T(8,128)(2,1)S(1)} copy-done((bf16[4,128,256]{2,1,0:T(8,128)(2,1)S(1)}, bf16[4,128,256]{2,1,0:T(8,128)(2,1)}, u32[]{:S(2)}) %copy-start.2) | copy-done | bytes 262168
  2.3 0.5 %transform.2 = (f32[2,5,16,128]{3,2,1,0:T(8,128)S(1)}, f32[2,5,16,128]{3,2,1,0:T(8,128)S(1)}, f32[2,5,16,128]{3,2,1,0:T(8,128)S(1)}, f32[2,5,16,128]{3,2,1,0:T(8,128)S(1)}) custom-call(bf16[4,128,256]{2,1,0:T(8,128)(2,1)S(1)} %copy-done.2, bf16[32,5,32,128]{3,2,1,0:T(8,128)(2,1)S(1)} %bitcast.44), custom_call_target="tpu_custom_call" | custom-call | flops 83886080 | bytes 983040 | tf_op jit(solution)/shard_map/transform/pallas_call | solution.py:85
  2.8 3.1 %collective-permute-start = (f32[2,5,16,128]{3,2,1,0:T(8,128)S(1)}, f32[2,5,16,128]{3,2,1,0:T(8,128)S(1)}, u32[]{:S(2)}, u32[]{:S(2)}) collective-permute-start(f32[2,5,16,128]{3,2,1,0:T(8,128)S(1)} %get-tuple-element.28), channel_id=1, source_target_pairs={{0,1},{1,0},{2,3},{3,2},{4,5},{5,4},{6,7},{7,6},{8,9},{9,8},{10,11... | collective-permute-start | bytes 245768 | tf_op jit(solution)/shard_map/ppermute | solution.py:259
  5.9 2.6 %collective-permute-start.1 = (f32[2,5,16,128]{3,2,1,0:T(8,128)S(1)}, f32[2,5,16,128]{3,2,1,0:T(8,128)S(1)}, u32[]{:S(2)}, u32[]{:S(2)}) collective-permute-start(f32[2,5,16,128]{3,2,1,0:T(8,128)S(1)} %get-tuple-element.29), channel_id=1, source_target_pairs={{0,2},{1,3},{2,0},{3,1},{4,6},{5,7},{6,4},{7,5},{8,10},{9,11},{10,... | collective-permute-start | bytes 245768 | tf_op jit(solution)/shard_map/ppermute | solution.py:259
  9.0 1.3 %collective-permute-start.5 = (f32[392,128]{1,0:T(8,128)S(1)}, f32[392,128]{1,0:T(8,128)S(1)}, u32[]{:S(2)}, u32[]{:S(2)}) collective-permute-start(f32[392,128]{1,0:T(8,128)S(1)} %select_maximum_fusion.1), channel_id=1, source_target_pairs={{0,4},{4,8},{8,12},{12,16},{16,20},{20,24},{24,28},{1,5},{5,9},{9,... | collective-permute-start | bytes 602120 | tf_op jit(solution)/shard_map/ppermute | solution.py:279
  10.3 1.3 %collective-permute-start.6 = (f32[392,128]{1,0:T(8,128)S(1)}, f32[392,128]{1,0:T(8,128)S(1)}, u32[]{:S(2)}, u32[]{:S(2)}) collective-permute-start(f32[392,128]{1,0:T(8,128)S(1)} %select_maximum_fusion), channel_id=1, source_target_pairs={{4,0},{8,4},{12,8},{16,12},{20,16},{24,20},{28,24},{5,1},{9,5},{13... | collective-permute-start | bytes 602120 | tf_op jit(solution)/shard_map/ppermute | solution.py:280
  11.7 3.1 %collective-permute-done.2.refs_3_ = f32[2,5,16,128]{3,2,1,0:T(8,128)S(1)} collective-permute-done((f32[2,5,16,128]{3,2,1,0:T(8,128)S(1)}, f32[2,5,16,128]{3,2,1,0:T(8,128)S(1)}, u32[]{:S(2)}, u32[]{:S(2)}) %collective-permute-start.2) | collective-permute-done | bytes 81952 | tf_op jit(solution)/shard_map/ppermute | solution.py:259
  15.1 1.9 %collective-permute-start.3 = (f32[8,3,16,128]{3,2,1,0:T(8,128)S(1)}, f32[8,3,16,128]{3,2,1,0:T(8,128)S(1)}, u32[]{:S(2)}, u32[]{:S(2)}) collective-permute-start(f32[8,3,16,128]{3,2,1,0:T(8,128)S(1)} %bitcast.51), channel_id=1, source_target_pairs={{0,4},{4,8},{8,12},{12,16},{16,20},{20,24},{24,28},{1,5},{5,9},{9,... | collective-permute-start | bytes 589832 | tf_op jit(solution)/shard_map/ppermute | solution.py:288
  17.0 1.3 %collective-permute-start.4 = (f32[8,3,16,128]{3,2,1,0:T(8,128)S(1)}, f32[8,3,16,128]{3,2,1,0:T(8,128)S(1)}, u32[]{:S(2)}, u32[]{:S(2)}) collective-permute-start(f32[8,3,16,128]{3,2,1,0:T(8,128)S(1)} %bitcast.52), channel_id=1, source_target_pairs={{4,0},{8,4},{12,8},{16,12},{20,16},{24,20},{28,24},{5,1},{9,5},{13... | collective-permute-start | bytes 589832 | tf_op jit(solution)/shard_map/ppermute | solution.py:289
  18.4 1.4 %smooth.3 = (f32[2,5,16,128]{3,2,1,0:T(8,128)S(1)}, f32[2,5,16,128]{3,2,1,0:T(8,128)S(1)}, f32[2,5,16,128]{3,2,1,0:T(8,128)S(1)}, f32[2,5,16,128]{3,2,1,0:T(8,128)S(1)}) custom-call(f32[2,5,16,128]{3,2,1,0:T(8,128)S(1)} %get-tuple-element.37.refs_0_, f32[2,5,16,128]{3,2,1,0:T(8,128)S(1)} %get-tuple-element.38.refs_1_, ...), custom_call_target="tpu_custom_call" | custom-call | flops 2457600 | bytes 819200 | tf_op jit(solution)/shard_map/smooth/pallas_call | solution.py:161
  19.8 1.0 %collective-permute-start.7 = (f32[2,5,16,128]{3,2,1,0:T(8,128)S(1)}, f32[2,5,16,128]{3,2,1,0:T(8,128)S(1)}, u32[]{:S(2)}, u32[]{:S(2)}) collective-permute-start(f32[2,5,16,128]{3,2,1,0:T(8,128)S(1)} %get-tuple-element.42), channel_id=1, source_target_pairs={{0,1},{1,0},{2,3},{3,2},{4,5},{5,4},{6,7},{7,6},{8,9},{9,8},{10,11... | collective-permute-start | bytes 245768 | tf_op jit(solution)/shard_map/ppermute | solution.py:259
  20.8 3.3 %collective-permute-start.8 = (f32[2,5,16,128]{3,2,1,0:T(8,128)S(1)}, f32[2,5,16,128]{3,2,1,0:T(8,128)S(1)}, u32[]{:S(2)}, u32[]{:S(2)}) collective-permute-start(f32[2,5,16,128]{3,2,1,0:T(8,128)S(1)} %get-tuple-element.43), channel_id=1, source_target_pairs={{0,2},{1,3},{2,0},{3,1},{4,6},{5,7},{6,4},{7,5},{8,10},{9,11},{10,... | collective-permute-start | bytes 245768 | tf_op jit(solution)/shard_map/ppermute | solution.py:259
  24.8 1.4 %smooth.2 = (f32[2,5,16,128]{3,2,1,0:T(8,128)S(1)}, f32[2,5,16,128]{3,2,1,0:T(8,128)S(1)}, f32[2,5,16,128]{3,2,1,0:T(8,128)S(1)}, f32[2,5,16,128]{3,2,1,0:T(8,128)S(1)}) custom-call(f32[2,5,16,128]{3,2,1,0:T(8,128)S(1)} %get-tuple-element.27.refs_0_, f32[2,5,16,128]{3,2,1,0:T(8,128)S(1)} %collective-permute-done.refs_1_, ...), custom_call_target="tpu_custom_call" | custom-call | flops 2457600 | bytes 819200 | tf_op jit(solution)/shard_map/smooth/pallas_call | solution.py:161
  26.2 1.6 %collective-permute-done.8.refs_6_ = f32[2,5,16,128]{3,2,1,0:T(8,128)S(1)} collective-permute-done((f32[2,5,16,128]{3,2,1,0:T(8,128)S(1)}, f32[2,5,16,128]{3,2,1,0:T(8,128)S(1)}, u32[]{:S(2)}, u32[]{:S(2)}) %collective-permute-start.8) | collective-permute-done | bytes 81952 | tf_op jit(solution)/shard_map/ppermute | solution.py:259
  27.7 2.7 %collective-permute-done.9.refs_7_ = f32[2,5,16,128]{3,2,1,0:T(8,128)S(1)} collective-permute-done((f32[2,5,16,128]{3,2,1,0:T(8,128)S(1)}, f32[2,5,16,128]{3,2,1,0:T(8,128)S(1)}, u32[]{:S(2)}, u32[]{:S(2)}) %collective-permute-start.9) | collective-permute-done | bytes 81952 | tf_op jit(solution)/shard_map/ppermute | solution.py:259
  30.4 2.1 %combine.1 = (f32[4,2,16,600]{3,2,1,0:T(8,128)S(1)}, f32[4,2,16,600]{3,2,1,0:T(8,128)S(1)}) custom-call(f32[2,5,16,128]{3,2,1,0:T(8,128)S(1)} %get-tuple-element.33.refs_0_, f32[2,5,16,128]{3,2,1,0:T(8,128)S(1)} %get-tuple-element.34.refs_1_, f32[2,5,16,128]{3,2,1,0:T(8,128)S(1)} %get-tuple-element.35.refs_2_, ...), custom_call_target="tpu_custom_call" | custom-call | flops 1179648000 | bytes 4956160 | tf_op jit(solution)/shard_map/combine/pallas_call | solution.py:222
  32.5 0.8 %collective-permute-start.10 = (f32[4,2,16,600]{3,2,1,0:T(8,128)S(1)}, f32[4,2,16,600]{3,2,1,0:T(8,128)S(1)}, u32[]{:S(2)}, u32[]{:S(2)}) collective-permute-start(f32[4,2,16,600]{3,2,1,0:T(8,128)S(1)} %get-tuple-element.48), channel_id=1, source_target_pairs={{0,4},{4,0},{8,12},{12,8},{16,20},{20,16},{24,28},{28,24},{1,5},{5... | collective-permute-start | bytes 921608 | tf_op jit(solution)/shard_map/ppermute | solution.py:292
  33.3 1.3 %collective-permute-done.10 = f32[4,2,16,600]{3,2,1,0:T(8,128)S(1)} collective-permute-done((f32[4,2,16,600]{3,2,1,0:T(8,128)S(1)}, f32[4,2,16,600]{3,2,1,0:T(8,128)S(1)}, u32[]{:S(2)}, u32[]{:S(2)}) %collective-permute-start.10) | collective-permute-done | bytes 307232 | tf_op jit(solution)/shard_map/ppermute | solution.py:292
  34.7 4.2 %collective-permute-start.11 = (f32[2,16,600]{2,1,0:T(8,128)S(1)}, f32[2,16,600]{2,1,0:T(8,128)S(1)}, u32[]{:S(2)}, u32[]{:S(2)}) collective-permute-start(f32[2,16,600]{2,1,0:T(8,128)S(1)} %get-tuple-element.49), channel_id=1, source_target_pairs={{0,8},{4,12},{8,0},{12,4},{16,24},{20,28},{24,16},{28,20},{1,9},{5... | collective-permute-start | bytes 230408 | tf_op jit(solution)/shard_map/ppermute | solution.py:295
  38.9 2.6 %collective-permute-start.13 = (f32[2,16,600]{2,1,0:T(8,128)S(1)}, f32[2,16,600]{2,1,0:T(8,128)S(1)}, u32[]{:S(2)}, u32[]{:S(2)}) collective-permute-start(f32[2,16,600]{2,1,0:T(8,128)S(1)} %get-tuple-element.50), channel_id=1, source_target_pairs={{0,24},{4,28},{8,16},{12,20},{16,8},{20,12},{24,0},{28,4},{1,25},{... | collective-permute-start | bytes 230408 | tf_op jit(solution)/shard_map/ppermute | solution.py:295
  41.6 4.2 %collective-permute-done.13 = f32[2,16,600]{2,1,0:T(8,128)S(1)} collective-permute-done((f32[2,16,600]{2,1,0:T(8,128)S(1)}, f32[2,16,600]{2,1,0:T(8,128)S(1)}, u32[]{:S(2)}, u32[]{:S(2)}) %collective-permute-start.13) | collective-permute-done | bytes 76832 | tf_op jit(solution)/shard_map/ppermute | solution.py:295
  45.8 1.1 %collective-permute-done.12 = f32[2,16,600]{2,1,0:T(8,128)S(1)} collective-permute-done((f32[2,16,600]{2,1,0:T(8,128)S(1)}, f32[2,16,600]{2,1,0:T(8,128)S(1)}, u32[]{:S(2)}, u32[]{:S(2)}) %collective-permute-start.12) | collective-permute-done | bytes 76832 | tf_op jit(solution)/shard_map/ppermute | solution.py:295
  46.9 0.7 %copy.5 = f32[16,1,2,600]{3,2,1,0:T(2,128)} copy(f32[16,1,2,600]{3,0,2,1:T(8,128)S(1)} %fusion.3) | data formatting | bytes 153600 | tf_op jit(solution)/shard_map/broadcast_in_dim | solution.py:342
  (35 shorter events, 1.8 us)
Async XLA Ops:
  0.0 1.3 %copy-start = (bf16[32,32,5,128]{3,1,2,0:T(8,128)(2,1)S(1)}, bf16[32,32,5,128]{3,1,2,0:T(8,128)(2,1)}, u32[]{:S(2)}) copy-start(bf16[32,32,5,128]{3,1,2,0:T(8,128)(2,1)} %param.4) | copy-start | bytes 3932164
  1.3 0.9 %copy-start.2 = (bf16[4,128,256]{2,1,0:T(8,128)(2,1)S(1)}, bf16[4,128,256]{2,1,0:T(8,128)(2,1)}, u32[]{:S(2)}) copy-start(bf16[4,128,256]{2,1,0:T(8,128)(2,1)} %constant.5.clone.table_ref) | copy-start | bytes 786436
  2.3 6.7 %copy-start.3 = (f32[5,128]{1,0:T(8,128)S(1)}, f32[5,128]{1,0:T(8,128)}, u32[]{:S(2)}) copy-start(f32[5,128]{1,0:T(8,128)} %refs_6_.3) | copy-start | bytes 7684
  2.8 12.3 %collective-permute-start = (f32[2,5,16,128]{3,2,1,0:T(8,128)S(1)}, f32[2,5,16,128]{3,2,1,0:T(8,128)S(1)}, u32[]{:S(2)}, u32[]{:S(2)}) collective-permute-start(f32[2,5,16,128]{3,2,1,0:T(8,128)S(1)} %get-tuple-element.28), channel_id=1, source_target_pairs={{0,1},{1,0},{2,3},{3,2},{4,5},{5,4},{6,7},{7,6},{8,9},{9,8},{10,11... | collective-permute-start | bytes 245768 | tf_op jit(solution)/shard_map/ppermute | solution.py:259
  5.9 9.2 %collective-permute-start.1 = (f32[2,5,16,128]{3,2,1,0:T(8,128)S(1)}, f32[2,5,16,128]{3,2,1,0:T(8,128)S(1)}, u32[]{:S(2)}, u32[]{:S(2)}) collective-permute-start(f32[2,5,16,128]{3,2,1,0:T(8,128)S(1)} %get-tuple-element.29), channel_id=1, source_target_pairs={{0,2},{1,3},{2,0},{3,1},{4,6},{5,7},{6,4},{7,5},{8,10},{9,11},{10,... | collective-permute-start | bytes 245768 | tf_op jit(solution)/shard_map/ppermute | solution.py:259
  8.5 6.3 %collective-permute-start.2 = (f32[2,5,16,128]{3,2,1,0:T(8,128)S(1)}, f32[2,5,16,128]{3,2,1,0:T(8,128)S(1)}, u32[]{:S(2)}, u32[]{:S(2)}) collective-permute-start(f32[2,5,16,128]{3,2,1,0:T(8,128)S(1)} %get-tuple-element.30), channel_id=1, source_target_pairs={{0,3},{1,2},{2,1},{3,0},{4,7},{5,6},{6,5},{7,4},{8,11},{9,10},{10,... | collective-permute-start | bytes 245768 | tf_op jit(solution)/shard_map/ppermute | solution.py:259
  9.0 9.3 %collective-permute-start.5 = (f32[392,128]{1,0:T(8,128)S(1)}, f32[392,128]{1,0:T(8,128)S(1)}, u32[]{:S(2)}, u32[]{:S(2)}) collective-permute-start(f32[392,128]{1,0:T(8,128)S(1)} %select_maximum_fusion.1), channel_id=1, source_target_pairs={{0,4},{4,8},{8,12},{12,16},{16,20},{20,24},{24,28},{1,5},{5,9},{9,... | collective-permute-start | bytes 602120 | tf_op jit(solution)/shard_map/ppermute | solution.py:279
  10.3 8.1 %collective-permute-start.6 = (f32[392,128]{1,0:T(8,128)S(1)}, f32[392,128]{1,0:T(8,128)S(1)}, u32[]{:S(2)}, u32[]{:S(2)}) collective-permute-start(f32[392,128]{1,0:T(8,128)S(1)} %select_maximum_fusion), channel_id=1, source_target_pairs={{4,0},{8,4},{12,8},{16,12},{20,16},{24,20},{28,24},{5,1},{9,5},{13... | collective-permute-start | bytes 602120 | tf_op jit(solution)/shard_map/ppermute | solution.py:280
  11.6 12.6 %copy-start.1 = (f32[1,2,600,640]{3,2,1,0:T(8,128)S(1)}, f32[1,2,600,640]{3,2,1,0:T(8,128)}, u32[]{:S(2)}) copy-start(f32[1,2,600,640]{3,2,1,0:T(8,128)} %param.6) | copy-start | bytes 9216004
  15.1 9.6 %collective-permute-start.3 = (f32[8,3,16,128]{3,2,1,0:T(8,128)S(1)}, f32[8,3,16,128]{3,2,1,0:T(8,128)S(1)}, u32[]{:S(2)}, u32[]{:S(2)}) collective-permute-start(f32[8,3,16,128]{3,2,1,0:T(8,128)S(1)} %bitcast.51), channel_id=1, source_target_pairs={{0,4},{4,8},{8,12},{12,16},{16,20},{20,24},{24,28},{1,5},{5,9},{9,... | collective-permute-start | bytes 589832 | tf_op jit(solution)/shard_map/ppermute | solution.py:288
  17.0 7.7 %collective-permute-start.4 = (f32[8,3,16,128]{3,2,1,0:T(8,128)S(1)}, f32[8,3,16,128]{3,2,1,0:T(8,128)S(1)}, u32[]{:S(2)}, u32[]{:S(2)}) collective-permute-start(f32[8,3,16,128]{3,2,1,0:T(8,128)S(1)} %bitcast.52), channel_id=1, source_target_pairs={{4,0},{8,4},{12,8},{16,12},{20,16},{24,20},{28,24},{5,1},{9,5},{13... | collective-permute-start | bytes 589832 | tf_op jit(solution)/shard_map/ppermute | solution.py:289
  19.8 6.3 %collective-permute-start.7 = (f32[2,5,16,128]{3,2,1,0:T(8,128)S(1)}, f32[2,5,16,128]{3,2,1,0:T(8,128)S(1)}, u32[]{:S(2)}, u32[]{:S(2)}) collective-permute-start(f32[2,5,16,128]{3,2,1,0:T(8,128)S(1)} %get-tuple-element.42), channel_id=1, source_target_pairs={{0,1},{1,0},{2,3},{3,2},{4,5},{5,4},{6,7},{7,6},{8,9},{9,8},{10,11... | collective-permute-start | bytes 245768 | tf_op jit(solution)/shard_map/ppermute | solution.py:259
  20.8 7.0 %collective-permute-start.8 = (f32[2,5,16,128]{3,2,1,0:T(8,128)S(1)}, f32[2,5,16,128]{3,2,1,0:T(8,128)S(1)}, u32[]{:S(2)}, u32[]{:S(2)}) collective-permute-start(f32[2,5,16,128]{3,2,1,0:T(8,128)S(1)} %get-tuple-element.43), channel_id=1, source_target_pairs={{0,2},{1,3},{2,0},{3,1},{4,6},{5,7},{6,4},{7,5},{8,10},{9,11},{10,... | collective-permute-start | bytes 245768 | tf_op jit(solution)/shard_map/ppermute | solution.py:259
  24.1 6.4 %collective-permute-start.9 = (f32[2,5,16,128]{3,2,1,0:T(8,128)S(1)}, f32[2,5,16,128]{3,2,1,0:T(8,128)S(1)}, u32[]{:S(2)}, u32[]{:S(2)}) collective-permute-start(f32[2,5,16,128]{3,2,1,0:T(8,128)S(1)} %get-tuple-element.44), channel_id=1, source_target_pairs={{0,3},{1,2},{2,1},{3,0},{4,7},{5,6},{6,5},{7,4},{8,11},{9,10},{10,... | collective-permute-start | bytes 245768 | tf_op jit(solution)/shard_map/ppermute | solution.py:259
  32.5 2.1 %collective-permute-start.10 = (f32[4,2,16,600]{3,2,1,0:T(8,128)S(1)}, f32[4,2,16,600]{3,2,1,0:T(8,128)S(1)}, u32[]{:S(2)}, u32[]{:S(2)}) collective-permute-start(f32[4,2,16,600]{3,2,1,0:T(8,128)S(1)} %get-tuple-element.48), channel_id=1, source_target_pairs={{0,4},{4,0},{8,12},{12,8},{16,20},{20,16},{24,28},{28,24},{1,5},{5... | collective-permute-start | bytes 921608 | tf_op jit(solution)/shard_map/ppermute | solution.py:292
  34.7 7.0 %collective-permute-start.11 = (f32[2,16,600]{2,1,0:T(8,128)S(1)}, f32[2,16,600]{2,1,0:T(8,128)S(1)}, u32[]{:S(2)}, u32[]{:S(2)}) collective-permute-start(f32[2,16,600]{2,1,0:T(8,128)S(1)} %get-tuple-element.49), channel_id=1, source_target_pairs={{0,8},{4,12},{8,0},{12,4},{16,24},{20,28},{24,16},{28,20},{1,9},{5... | collective-permute-start | bytes 230408 | tf_op jit(solution)/shard_map/ppermute | solution.py:295
  38.9 6.9 %collective-permute-start.13 = (f32[2,16,600]{2,1,0:T(8,128)S(1)}, f32[2,16,600]{2,1,0:T(8,128)S(1)}, u32[]{:S(2)}, u32[]{:S(2)}) collective-permute-start(f32[2,16,600]{2,1,0:T(8,128)S(1)} %get-tuple-element.50), channel_id=1, source_target_pairs={{0,24},{4,28},{8,16},{12,20},{16,8},{20,12},{24,0},{28,4},{1,25},{... | collective-permute-start | bytes 230408 | tf_op jit(solution)/shard_map/ppermute | solution.py:295
  41.5 5.4 %collective-permute-start.12 = (f32[2,16,600]{2,1,0:T(8,128)S(1)}, f32[2,16,600]{2,1,0:T(8,128)S(1)}, u32[]{:S(2)}, u32[]{:S(2)}) collective-permute-start(f32[2,16,600]{2,1,0:T(8,128)S(1)} %get-tuple-element.51), channel_id=1, source_target_pairs={{0,16},{4,20},{8,24},{12,28},{16,0},{20,4},{24,8},{28,12},{1,17},{... | collective-permute-start | bytes 230408 | tf_op jit(solution)/shard_map/ppermute | solution.py:295

commit v3 on v2

v3 whole, which is shorter than its diff:
```python
import functools
import math

import jax
import jax.numpy as jnp
import numpy as np
from jax import lax
from jax.experimental import pallas as pl
from jax.experimental.pallas import tpu as pltpu
from jax.sharding import PartitionSpec as P


FD = 1
PASSES = 3
GROUP = 8
GRANT = 16 * 1024 * 1024


def params():
    return pltpu.CompilerParams(vmem_limit_bytes=GRANT)


def cost(flops, moved):
    return pl.CostEstimate(flops=flops, bytes_accessed=moved, transcendentals=0)


def dft_table(steps_count, freq_count):
    times = np.arange(steps_count)
    freqs = np.arange(freq_count)
    phase = (freqs[:, None] * times[None, :] % steps_count) * (2.0 * math.pi / steps_count)
    scale = 1.0 / math.sqrt(steps_count)
    return (np.stack([np.cos(phase), -np.sin(phase)], 1) * scale).astype(np.float32)


def split_bf16(values):
    high = values.astype(jnp.bfloat16)
    low = (values - high.astype(values.dtype)).astype(jnp.bfloat16)
    return high, low


def transform_operand(steps_count, freq_count, order):
    table = dft_table(steps_count, freq_count)[order]
    parts = np.stack([x.astype(np.float32) for x in split_bf16(table)], 1)
    sources = parts.shape[0]
    wide = np.broadcast_to(parts[..., None, :], (*parts.shape[:-1], GROUP, steps_count))
    return jnp.asarray(wide.reshape(sources, -1, GROUP * steps_count), jnp.float32)


def edge_base(slot, b, r, vectors):
    return ((slot * 2 + b) * PASSES + r) * vectors


def transform_kernel(slots, edged, field_hbm, table_hbm, own_hbm, *refs):
    outs, (low, high) = refs[:slots], refs[slots : slots + 2]
    field, table, own_c, field_sem, table_sem, own_sem = refs[slots + 2 :]
    vectors, rows, steps, width = field.shape
    blocks = vectors // GROUP
    source = lax.axis_index("freq") if table_hbm.shape[0] > 1 else 0
    get_table = pltpu.make_async_copy(table_hbm.at[source], table, table_sem)
    get_table.start()
    get_own = pltpu.make_async_copy(own_hbm, own_c, own_sem)
    get_own.start()

    def get(i):
        at = pl.ds(i * GROUP, GROUP)
        return pltpu.make_async_copy(field_hbm.at[at], field.at[at], field_sem.at[i])

    for i in range(blocks):
        get(i).start()
    get_own.wait()
    rim = PASSES - 1
    base = edge_base(edged, 0, 0, vectors)
    low[base : base + rim] = own_c[rows - rim :]
    high[base : base + rim] = own_c[:rim]
    low[base + rim :] = jnp.zeros((low.shape[0] - base - rim, width), jnp.float32)
    high[base + rim :] = jnp.zeros((low.shape[0] - base - rim, width), jnp.float32)
    get_table.wait()
    short = table[...]
    shape = (short.shape[0], GROUP, short.shape[1])
    mine = lax.broadcasted_iota(jnp.int32, shape, 1)
    column = lax.broadcasted_iota(jnp.int32, shape, 2)
    full = jnp.where(
        (column >= mine * steps) & (column < (mine + 1) * steps), short[:, None], 0.0
    )
    full = full.reshape(-1, short.shape[1]).astype(jnp.bfloat16)
    for i in range(blocks):
        get(i).wait()
        span = slice(i * GROUP, (i + 1) * GROUP)
        data = jnp.concatenate(
            [field[span, r].reshape(GROUP * steps, width) for r in range(rows)], axis=1
        )
        both = jnp.dot(full, data, preferred_element_type=jnp.float32)
        half = both.shape[0] // 2
        values = both[:half] + both[half:]
        for slot in range(slots):
            for b in range(2):
                at = (slot * 2 + b) * GROUP
                for r in range(rows):
                    piece = values[at : at + GROUP, r * width : (r + 1) * width]
                    outs[slot][b, r, span] = piece
                    if slot >= edged:
                        continue
                    if r >= rows - PASSES:
                        to = edge_base(slot, b, r - rows + PASSES, vectors) + i * GROUP
                        low[to : to + GROUP] = piece
                    if r < PASSES:
                        to = edge_base(slot, b, r, vectors) + i * GROUP
                        high[to : to + GROUP] = piece


def transform(field, table, coefficient, slots, edged):
    vectors, rows, steps, width = field.shape
    chunk = jax.ShapeDtypeStruct((2, rows, vectors, width), jnp.float32)
    edge = jax.ShapeDtypeStruct((edge_base(edged, 0, 0, vectors) + GROUP, width), jnp.float32)
    hbm = pl.BlockSpec(memory_space=pltpu.HBM)
    vmem = pl.BlockSpec(memory_space=pltpu.VMEM)
    *chunks, low, high = pl.pallas_call(
        functools.partial(transform_kernel, slots, edged),
        out_shape=[chunk] * slots + [edge] * 2,
        in_specs=[hbm, hbm, hbm],
        out_specs=[vmem] * (slots + 2),
        scratch_shapes=[
            pltpu.VMEM(field.shape, field.dtype),
            pltpu.VMEM(table.shape[1:], table.dtype),
            pltpu.VMEM(coefficient.shape, coefficient.dtype),
            pltpu.SemaphoreType.DMA((vectors // GROUP,)),
            pltpu.SemaphoreType.DMA(()),
            pltpu.SemaphoreType.DMA(()),
        ],
        compiler_params=params(),
        cost_estimate=cost(
            2 * table.shape[1] * table.shape[2] * rows * width * vectors,
            vectors * rows * width * (2 * steps + 8 * slots),
        ),
        name="transform",
    )(*(pltpu.with_memory_space_constraint(x, pltpu.HBM) for x in (field, table, coefficient)))
    return chunks, low, high


def split_kernel(x_ref, high_ref, low_ref):
    high, low = split_bf16(x_ref[...])
    high_ref[...] = high
    low_ref[...] = low


def split_transfer(transfer):
    parts, sensors, cells = transfer.shape
    block = pl.BlockSpec((1, sensors, cells), lambda a: (a, 0, 0))
    return pl.pallas_call(
        split_kernel,
        out_shape=[jax.ShapeDtypeStruct(transfer.shape, jnp.bfloat16)] * 2,
        grid=(parts,),
        in_specs=[block],
        out_specs=[block, block],
        compiler_params=params(),
        cost_estimate=cost(2 * transfer.size, 8 * transfer.size),
        name="split_transfer",
    )(transfer)


def relaxed_rows(rows, coefficients):
    width = rows[0].shape[-1]
    lane = lax.broadcasted_iota(jnp.int32, rows[0].shape, 1)
    first, last = lane == 0, lane == width - 1
    out = []
    for i in range(1, len(rows) - 1):
        centre = rows[i]
        left = jnp.where(first, 0.0, pltpu.roll(centre, 1, 1))
        right = jnp.where(last, 0.0, pltpu.roll(centre, width - 1, 1))
        beside = (rows[i + 1] + rows[i - 1]) + (left + right)
        out.append(centre + coefficients[i - 1] * (beside - 4.0 * centre))
    return out


def smooth_kernel(base, rim_base, chunk, low, high, own_c, low_c, high_c, out):
    _, rows, vectors, width = chunk.shape
    rim = PASSES - 1
    coefficients = [low_c[rim_base + i : rim_base + i + 1] for i in range(rim)]
    coefficients += [own_c[i : i + 1] for i in range(rows)]
    coefficients += [high_c[rim_base + i : rim_base + i + 1] for i in range(rim)]
    part = math.gcd(vectors, 2 * GROUP)
    coefficients = [jnp.broadcast_to(c, (part, width)) for c in coefficients]
    for b in range(2):
        for start in range(0, vectors, part):
            span = slice(start, start + part)

            def edge(ref, r):
                at = base + edge_base(0, b, r, vectors) + start
                return ref[at : at + part]

            values = [edge(low, r) for r in range(PASSES)]
            values += [chunk[b, r, span] for r in range(rows)]
            values += [edge(high, r) for r in range(PASSES)]
            for step in range(PASSES):
                values = relaxed_rows(values, coefficients[step : len(coefficients) - step])
            for r in range(rows):
                out[b, r, span] = values[r]


def smooth(chunk, low, high, slot, coefficients, rim_base):
    base = edge_base(slot, 0, 0, chunk.shape[2])
    return pl.pallas_call(
        functools.partial(smooth_kernel, base, rim_base),
        out_shape=jax.ShapeDtypeStruct(chunk.shape, jnp.float32),
        compiler_params=params(),
        cost_estimate=cost(30 * chunk.size, 10 * chunk.size),
        name="smooth",
    )(chunk, low, high, *coefficients)


def combine_kernel(chunks_in, owners_in, paired, *refs):
    refs = list(refs)
    phases = [[refs.pop(0) for _ in range(count)] for count in chunks_in]
    t_high, t_low = refs.pop(0), refs.pop(0)
    outs, held = refs[:-1], refs[-1]
    rows, vectors, width = phases[0][0].shape[1:]
    each = vectors // owners_in
    for phase, chunks in enumerate(phases):
        inner = slice(phase * each, (phase + 1) * each)
        for index, ref in enumerate(chunks):
            for o in range(owners_in):
                if paired:
                    owner = (lax.axis_index("freq") ^ index) * owners_in + o
                    apart = owner ^ lax.axis_index("seabed")
                    place = (apart & 1) * (held.shape[1] // 2) + (apart >> 1)
                else:
                    place = index * owners_in + o
                for b in range(2):
                    for r in range(rows):
                        held[b, place, inner, r * width : (r + 1) * width] = ref[
                            b, r, o * each : (o + 1) * each
                        ]
    places, owned, cells = held.shape[1:]
    lhs_high, lhs_low = split_bf16(held[...].reshape(2 * places * owned, cells))

    def times(a):
        def dot(x, w):
            return lax.dot_general(
                x, w, (((1,), (1,)), ((), ())), preferred_element_type=jnp.float32
            )

        return (dot(lhs_low, t_high[a]) + dot(lhs_high, t_low[a])) + dot(lhs_high, t_high[a])

    half = places * owned
    by_real, by_imag = times(0), times(1)
    real = by_real[:half] - by_imag[half:]
    imag = by_imag[:half] + by_real[half:]
    sensors = real.shape[-1]
    share = places // len(outs)
    for e, out in enumerate(outs):
        at = slice(e * share * owned, (e + 1) * share * owned)
        out[:, 0] = real[at].reshape(share, owned, sensors)
        out[:, 1] = imag[at].reshape(share, owned, sensors)


def combine(phases, split, owners_in, paired):
    t_high, t_low = split
    sensors, cells = t_high.shape[1:]
    places = len(phases[0]) * owners_in
    owned = sum(p[0].shape[2] for p in phases) // owners_in
    vectors = places * owned
    outs = 2 if paired else 1
    return pl.pallas_call(
        functools.partial(combine_kernel, [len(p) for p in phases], owners_in, paired),
        out_shape=[jax.ShapeDtypeStruct((places // outs, 2, owned, sensors), jnp.float32)] * outs,
        scratch_shapes=[pltpu.VMEM((2, places, owned, cells), jnp.float32)],
        compiler_params=params(),
        cost_estimate=cost(
            24 * vectors * sensors * cells,
            8 * sensors * cells + 8 * vectors * cells + 16 * vectors * sensors,
        ),
        name="combine",
    )(*[c for p in phases for c in p], t_high, t_low)


def chain(count):
    up = [(i, i + 1) for i in range(count - 1)]
    return up, [(b, a) for a, b in up]


def xor_pairs(count, apart):
    return [(i, i ^ apart) for i in range(count)]


def edges_of(chunk):
    _, rows, _, width = chunk.shape
    return [x.reshape(-1, width) for x in (chunk[:, rows - PASSES :], chunk[:, :PASSES])]


def shifted(low, high, strips):
    up, down = chain(strips)
    return lax.ppermute(low, "seabed", up), lax.ppermute(high, "seabed", down)


def paired_shards(field, coefficient, split_of, table, freq_count, strips, owned):
    vectors = field.shape[0]
    last = freq_count - 1
    chunks, low, high = transform(field, table, coefficient, freq_count, last)
    low, high = shifted(low, high, strips)

    def exchange(m, chunk):
        return lax.ppermute(chunk, "freq", xor_pairs(freq_count, m))

    moved = {last: exchange(last, chunks[last])}
    split = split_of()
    coefficients = (coefficient, low, high)
    rim_base = edge_base(last, 0, 0, vectors)
    for m in reversed(range(last)):
        chunk = smooth(chunks[m], low, high, m, coefficients, rim_base)
        moved[m] = exchange(m, chunk) if m else chunk
    low, high = shifted(*edges_of(moved[last]), strips)
    moved[last] = smooth(moved[last], low, high, 0, coefficients, rim_base)
    keep, send = combine([[moved[m] for m in range(freq_count)]], split, 2, True)
    pair = keep + lax.ppermute(send, "seabed", xor_pairs(strips, 1))
    total = pair[0]
    for d in reversed(range(1, strips // 2)):
        total = total + lax.ppermute(pair[d], "seabed", xor_pairs(strips, 2 * d))
    return total


def plain_shards(field, coefficient, split_of, table, freq_count, strips, owned):
    vectors, rows = field.shape[:2]
    spectrum, _, _ = transform(field, table, coefficient, freq_count, 0)
    spectrum = jnp.stack(spectrum)
    spectrum = lax.all_to_all(spectrum, "freq", split_axis=0, concat_axis=0, tiled=True)
    chunks = list(spectrum)
    edges = [jnp.concatenate(e) for e in zip(*[edges_of(c) for c in chunks])]
    low, high = shifted(*edges, strips)
    rim = PASSES - 1
    coefficients = (
        coefficient,
        *shifted(coefficient[rows - rim :], coefficient[:rim], strips),
    )
    chunks = [smooth(c, low, high, i, coefficients, 0) for i, c in enumerate(chunks)]
    (partial,) = combine([chunks], split_of(), vectors // owned, False)
    got = lax.all_to_all(partial, "seabed", split_axis=0, concat_axis=0, tiled=True)
    return got.sum(0)


def shards(uplift, coefficient, transfer):
    vectors, steps, _, _ = uplift.shape
    freq_count, strips = FD * lax.axis_size("freq"), lax.axis_size("seabed")
    owned = vectors * freq_count // strips
    paired = (
        strips == 2 * freq_count
        and strips & (strips - 1) == 0
        and vectors == 2 * owned
        and owned == 2 * GROUP
    )
    slots = np.arange(freq_count)
    order = slots[:, None] ^ slots[None, :] if paired else slots[None, :]
    table = transform_operand(steps, freq_count, order)
    field = jnp.transpose(uplift, (0, 2, 1, 3))
    run = paired_shards if paired else plain_shards
    total = run(
        field,
        coefficient,
        lambda: split_transfer(transfer[0]),
        table,
        freq_count,
        strips,
        owned,
    )
    return jnp.transpose(total, (1, 0, 2))[:, None]


def solution(mesh):
    placed = (P("freq", None, "seabed", None), P("seabed", None), P("freq", None, None, "seabed"))
    return jax.shard_map(
        shards,
        mesh=mesh,
        in_specs=placed,
        out_specs=P("seabed", "freq", None, None),
        check_vma=False,
    )
```

time: 47.8 us -> 42.4 us (0.89)
  waiting for transfers between devices: 14.3 us -> 5.26 us
  starting transfers between devices: 23.5 us -> 28 us
  local copies, waits for them, and re-layouts: 3.04 us -> 1.4 us
  Pallas kernels: 6.27 us -> 7.24 us
    ppermute x10 -> x7, waiting for transfers between devices: 7.68 us -> 0.71 us  [the longest x4 0.71 us: shifted(): return (lax.ppermute(low, 'seabed', up), lax.ppermute(high, 'seabed', down))]
    ppermute x10 -> x7, starting transfers between devices: 15.9 us -> 20.8 us  [the longest x4 12.2 us: shifted(): return (lax.ppermute(low, 'seabed', up), lax.ppermute(high, 'seabed', down))]
    ppermute x3, starting transfers between devices: 6.8 us -> 4.15 us  [paired_shards(): total = total + lax.ppermute(pair[d], 'seabed', xor_pairs(strips, 2 * d))]
    ppermute x1, starting transfers between devices: 0.81 us -> 3.12 us  [paired_shards(): pair = keep + lax.ppermute(send, 'seabed', xor_pairs(strips, 1))]
    ppermute x3, waiting for transfers between devices: 5.41 us -> 3.29 us  [paired_shards(): total = total + lax.ppermute(pair[d], 'seabed', xor_pairs(strips, 2 * d))]
    unnamed x8 -> x4, local copies, waits for them, and re-layouts: 2.28 us -> 0.69 us
    pallas_call x4 -> x5, Pallas kernels: 3.72 us -> 4.67 us  [the longest x4 2.62 us: smooth(): pl.pallas_call(functools.partial(smooth_kernel, base, rim_base), out_shap...]
  transfers between devices with their start and end apart: 14 -> 11, of which waited for: 8 -> 4; matrix products, arithmetic and copies ran while one was open for 0% -> 0% of each run, Pallas kernels for 8% -> 7%
where the time goes in v3:
time: 42.4 us; the launch traced here: 42.1 us
  starting transfers between devices  28 us (66%)
  Pallas kernels  7.24 us (17%)
  waiting for transfers between devices  5.26 us (12%)
  local copies, waits for them, and re-layouts  1.4 us (3%)
    ppermute x4, starting transfers between devices, shifted(): return (lax.ppermute(low, 'seabed', up), lax.ppermute(high, 'seabed', down))  12.2 us
    ppermute x3, starting transfers between devices, exchange(): return lax.ppermute(chunk, 'freq', xor_pairs(freq_count, m))  8.57 us
    ppermute x3, starting transfers between devices, paired_shards(): total = total + lax.ppermute(pair[d], 'seabed', xor_pairs(strips, 2 * d))  4.15 us
    ppermute x3, waiting for transfers between devices, paired_shards(): total = total + lax.ppermute(pair[d], 'seabed', xor_pairs(strips, 2 * d))  3.29 us
    ppermute x1, starting transfers between devices, paired_shards(): pair = keep + lax.ppermute(send, 'seabed', xor_pairs(strips, 1))  3.12 us
    pallas_call x4, Pallas kernels, smooth(): pl.pallas_call(functools.partial(smooth_kernel, base, rim_base), out_shap...  2.62 us
    pallas_call x1, Pallas kernels, combine(): pl.pallas_call(functools.partial(combine_kernel, [len(p) for p in phases]...  2.06 us
    pallas_call x1, Pallas kernels, transform(): pl.pallas_call(functools.partial(transform_kernel, slots, edged), out_sha...  2.05 us
  transfers between devices with their start and end apart: 11, of which 4 were waited for; matrix products, arithmetic and copies ran while one was open for 0% of the time, Pallas kernels for 7%

profile of v3, /device:TPU:0, one launch (start us, length us, event | category | flops | bytes accessed | tf_op | source)
XLA Modules:
  0.0 42.1 jit_solution(3203889091042484977)
XLA Ops:
  0.0 2.0 %transform.1 = (f32[2,5,32,128]{3,2,1,0:T(8,128)S(1)}, f32[2,5,32,128]{3,2,1,0:T(8,128)S(1)}, f32[2,5,32,128]{3,2,1,0:T(8,128)S(1)}, f32[2,5,32,128]{3,2,1,0:T(8...) custom-call(bf16[32,5,32,128]{3,2,1,0:T(8,128)(2,1)} %bitcast.25, f32[4,16,256]{2,1,0:T(8,128)} %constant.2.clone.table_hbm, ...), custom_call_target="tpu_custom_call" | custom-call | flops 167772160 | bytes 1966080 | tf_op jit(solution)/shard_map/transform/pallas_call | solution.py:117
  2.1 2.4 %collective-permute-start = (f32[584,128]{1,0:T(8,128)S(1)}, f32[584,128]{1,0:T(8,128)S(1)}, u32[]{:S(2)}, u32[]{:S(2)}) collective-permute-start(f32[584,128]{1,0:T(8,128)S(1)} %get-tuple-element.16), channel_id=1, source_target_pairs={{0,4},{4,8},{8,12},{12,16},{16,20},{20,24},{24,28},{1,5},{5,9},{9,... | collective-permute-start | bytes 897032 | tf_op jit(solution)/shard_map/ppermute | solution.py:292
  4.5 1.3 %collective-permute-start.1 = (f32[584,128]{1,0:T(8,128)S(1)}, f32[584,128]{1,0:T(8,128)S(1)}, u32[]{:S(2)}, u32[]{:S(2)}) collective-permute-start(f32[584,128]{1,0:T(8,128)S(1)} %get-tuple-element.17), channel_id=1, source_target_pairs={{4,0},{8,4},{12,8},{16,12},{20,16},{24,20},{28,24},{5,1},{9,5},{13... | collective-permute-start | bytes 897032 | tf_op jit(solution)/shard_map/ppermute | solution.py:292
  5.8 4.5 %collective-permute-start.4 = (f32[2,5,32,128]{3,2,1,0:T(8,128)S(1)}, f32[2,5,32,128]{3,2,1,0:T(8,128)S(1)}, u32[]{:S(2)}, u32[]{:S(2)}) collective-permute-start(f32[2,5,32,128]{3,2,1,0:T(8,128)S(1)} %get-tuple-element.20), channel_id=1, source_target_pairs={{0,3},{1,2},{2,1},{3,0},{4,7},{5,6},{6,5},{7,4},{8,11},{9,10},{10,... | collective-permute-start | bytes 491528 | tf_op jit(solution)/shard_map/ppermute | solution.py:302
  10.3 0.7 %copy-done.1 = f32[5,128]{1,0:T(8,128)S(1)} copy-done((f32[5,128]{1,0:T(8,128)S(1)}, f32[5,128]{1,0:T(8,128)}, u32[]{:S(2)}) %copy-start.1) | copy-done | bytes 2584
  11.0 0.7 %smooth.5 = f32[2,5,32,128]{3,2,1,0:T(8,128)S(1)} custom-call(f32[2,5,32,128]{3,2,1,0:T(8,128)S(1)} %get-tuple-element.18.chunk, f32[584,128]{1,0:T(8,128)S(1)} %collective-permute-done.low.low_c, f32[584,128]{1,0:T(8,128)S(1)} %collective-permute-done.1.high.high_c, f32[5,128]{1,0:T(8,128)S(1)} %copy-done.1, f32[584,128]{1,0:T(8,128)S(1)} %collective-permute-done.low.low_c, ...), custom_call_target="tpu_custom_call" | custom-call | flops 1228800 | bytes 409600 | tf_op jit(solution)/shard_map/smooth/pallas_call | solution.py:202
  11.6 1.4 %collective-permute-start.2 = (f32[2,5,32,128]{3,2,1,0:T(8,128)S(1)}, f32[2,5,32,128]{3,2,1,0:T(8,128)S(1)}, u32[]{:S(2)}, u32[]{:S(2)}) collective-permute-start(f32[2,5,32,128]{3,2,1,0:T(8,128)S(1)} %smooth.5), channel_id=1, source_target_pairs={{0,1},{1,0},{2,3},{3,2},{4,5},{5,4},{6,7},{7,6},{8,9},{9,8},{10,11... | collective-permute-start | bytes 491528 | tf_op jit(solution)/shard_map/ppermute | solution.py:302
  13.0 0.7 %smooth.6 = f32[2,5,32,128]{3,2,1,0:T(8,128)S(1)} custom-call(f32[2,5,32,128]{3,2,1,0:T(8,128)S(1)} %get-tuple-element.19.chunk, f32[584,128]{1,0:T(8,128)S(1)} %collective-permute-done.low.low_c, f32[584,128]{1,0:T(8,128)S(1)} %collective-permute-done.1.high.high_c, f32[5,128]{1,0:T(8,128)S(1)} %copy-done.1, f32[584,128]{1,0:T(8,128)S(1)} %collective-permute-done.low.low_c, ...), custom_call_target="tpu_custom_call" | custom-call | flops 1228800 | bytes 409600 | tf_op jit(solution)/shard_map/smooth/pallas_call | solution.py:202
  13.7 2.7 %collective-permute-start.3 = (f32[2,5,32,128]{3,2,1,0:T(8,128)S(1)}, f32[2,5,32,128]{3,2,1,0:T(8,128)S(1)}, u32[]{:S(2)}, u32[]{:S(2)}) collective-permute-start(f32[2,5,32,128]{3,2,1,0:T(8,128)S(1)} %smooth.6), channel_id=1, source_target_pairs={{0,2},{1,3},{2,0},{3,1},{4,6},{5,7},{6,4},{7,5},{8,10},{9,11},{10,... | collective-permute-start | bytes 491528 | tf_op jit(solution)/shard_map/ppermute | solution.py:302
  16.4 7.2 %collective-permute-start.5 = (f32[192,128]{1,0:T(8,128)S(1)}, f32[192,128]{1,0:T(8,128)S(1)}, u32[]{:S(2)}, u32[]{:S(2)}) collective-permute-start(f32[192,128]{1,0:T(8,128)S(1)} %bitcast.27), channel_id=1, source_target_pairs={{0,4},{4,8},{8,12},{12,16},{16,20},{20,24},{24,28},{1,5},{5,9},{9,... | collective-permute-start | bytes 294920 | tf_op jit(solution)/shard_map/ppermute | solution.py:292
  23.6 1.3 %collective-permute-start.6 = (f32[192,128]{1,0:T(8,128)S(1)}, f32[192,128]{1,0:T(8,128)S(1)}, u32[]{:S(2)}, u32[]{:S(2)}) collective-permute-start(f32[192,128]{1,0:T(8,128)S(1)} %bitcast.26), channel_id=1, source_target_pairs={{4,0},{8,4},{12,8},{16,12},{20,16},{24,20},{28,24},{5,1},{9,5},{13... | collective-permute-start | bytes 294920 | tf_op jit(solution)/shard_map/ppermute | solution.py:292
  24.9 0.5 %split_transfer.1 = (bf16[2,600,640]{2,1,0:T(8,128)(2,1)S(1)}, bf16[2,600,640]{2,1,0:T(8,128)(2,1)S(1)}) custom-call(f32[2,600,640]{2,1,0:T(8,128)S(1)} %bitcast.24), custom_call_target="tpu_custom_call" | custom-call | flops 1536000 | bytes 6144000 | tf_op jit(solution)/shard_map/split_transfer/pallas_call | solution.py:149
  25.4 0.7 %smooth.4.refs_0_ = f32[2,5,32,128]{3,2,1,0:T(8,128)S(1)} custom-call(f32[2,5,32,128]{3,2,1,0:T(8,128)S(1)} %get-tuple-element.15.chunk, f32[584,128]{1,0:T(8,128)S(1)} %collective-permute-done.low.low_c, f32[584,128]{1,0:T(8,128)S(1)} %collective-permute-done.1.high.high_c, f32[5,128]{1,0:T(8,128)S(1)} %copy-done.1, ...), custom_call_target="tpu_custom_call" | custom-call | flops 1228800 | bytes 409600 | tf_op jit(solution)/shard_map/smooth/pallas_call | solution.py:202
  26.1 0.7 %collective-permute-done.6.high = f32[192,128]{1,0:T(8,128)S(1)} collective-permute-done((f32[192,128]{1,0:T(8,128)S(1)}, f32[192,128]{1,0:T(8,128)S(1)}, u32[]{:S(2)}, u32[]{:S(2)}) %collective-permute-start.6) | collective-permute-done | bytes 98336 | tf_op jit(solution)/shard_map/ppermute | solution.py:292
  26.8 0.7 %smooth.7.refs_3_ = f32[2,5,32,128]{3,2,1,0:T(8,128)S(1)} custom-call(f32[2,5,32,128]{3,2,1,0:T(8,128)S(1)} %collective-permute-done.4.chunk, f32[192,128]{1,0:T(8,128)S(1)} %collective-permute-done.5.low, f32[192,128]{1,0:T(8,128)S(1)} %collective-permute-done.6.high, f32[5,128]{1,0:T(8,128)S(1)} %copy-done.1, ...), custom_call_target="tpu_custom_call" | custom-call | flops 1228800 | bytes 409600 | tf_op jit(solution)/shard_map/smooth/pallas_call | solution.py:202
  27.5 2.1 %combine.1 = (f32[4,2,16,600]{3,2,1,0:T(8,128)S(1)}, f32[4,2,16,600]{3,2,1,0:T(8,128)S(1)}) custom-call(f32[2,5,32,128]{3,2,1,0:T(8,128)S(1)} %smooth.4.refs_0_, f32[2,5,32,128]{3,2,1,0:T(8,128)S(1)} %collective-permute-done.2.refs_1_, f32[2,5,32,128]{3,2,1,0:T(8,128)S(1)} %collective-permute-done.3.refs_2_, f32[2,5,32,128]{3,2,1,0:T(8,128)S(1)} %smooth.7.refs_3_, ...), custom_call_target="tpu_custom_call" | custom-call | flops 1179648000 | bytes 4956160 | tf_op jit(solution)/shard_map/combine/pallas_call | solution.py:263
  29.5 3.1 %collective-permute-start.7 = (f32[4,2,16,600]{3,2,1,0:T(8,128)S(1)}, f32[4,2,16,600]{3,2,1,0:T(8,128)S(1)}, u32[]{:S(2)}, u32[]{:S(2)}) collective-permute-start(f32[4,2,16,600]{3,2,1,0:T(8,128)S(1)} %get-tuple-element.24), channel_id=1, source_target_pairs={{0,4},{4,0},{8,12},{12,8},{16,20},{20,16},{24,28},{28,24},{1,5},{5... | collective-permute-start | bytes 921608 | tf_op jit(solution)/shard_map/ppermute | solution.py:314
  32.7 1.3 %collective-permute-done.7 = f32[4,2,16,600]{3,2,1,0:T(8,128)S(1)} collective-permute-done((f32[4,2,16,600]{3,2,1,0:T(8,128)S(1)}, f32[4,2,16,600]{3,2,1,0:T(8,128)S(1)}, u32[]{:S(2)}, u32[]{:S(2)}) %collective-permute-start.7) | collective-permute-done | bytes 307232 | tf_op jit(solution)/shard_map/ppermute | solution.py:314
  34.0 0.5 %collective-permute-start.8 = (f32[2,16,600]{2,1,0:T(8,128)S(1)}, f32[2,16,600]{2,1,0:T(8,128)S(1)}, u32[]{:S(2)}, u32[]{:S(2)}) collective-permute-start(f32[2,16,600]{2,1,0:T(8,128)S(1)} %get-tuple-element.25), channel_id=1, source_target_pairs={{0,24},{4,28},{8,16},{12,20},{16,8},{20,12},{24,0},{28,4},{1,25},{... | collective-permute-start | bytes 230408 | tf_op jit(solution)/shard_map/ppermute | solution.py:317
  34.5 2.3 %collective-permute-start.10 = (f32[2,16,600]{2,1,0:T(8,128)S(1)}, f32[2,16,600]{2,1,0:T(8,128)S(1)}, u32[]{:S(2)}, u32[]{:S(2)}) collective-permute-start(f32[2,16,600]{2,1,0:T(8,128)S(1)} %get-tuple-element.26), channel_id=1, source_target_pairs={{0,8},{4,12},{8,0},{12,4},{16,24},{20,28},{24,16},{28,20},{1,9},{5... | collective-permute-start | bytes 230408 | tf_op jit(solution)/shard_map/ppermute | solution.py:317
  36.9 1.3 %collective-permute-start.9 = (f32[2,16,600]{2,1,0:T(8,128)S(1)}, f32[2,16,600]{2,1,0:T(8,128)S(1)}, u32[]{:S(2)}, u32[]{:S(2)}) collective-permute-start(f32[2,16,600]{2,1,0:T(8,128)S(1)} %get-tuple-element.27), channel_id=1, source_target_pairs={{0,16},{4,20},{8,24},{12,28},{16,0},{20,4},{24,8},{28,12},{1,17},{... | collective-permute-start | bytes 230408 | tf_op jit(solution)/shard_map/ppermute | solution.py:317
  38.1 1.6 %collective-permute-done.8 = f32[2,16,600]{2,1,0:T(8,128)S(1)} collective-permute-done((f32[2,16,600]{2,1,0:T(8,128)S(1)}, f32[2,16,600]{2,1,0:T(8,128)S(1)}, u32[]{:S(2)}, u32[]{:S(2)}) %collective-permute-start.8) | collective-permute-done | bytes 76832 | tf_op jit(solution)/shard_map/ppermute | solution.py:317
  39.7 1.7 %collective-permute-done.10 = f32[2,16,600]{2,1,0:T(8,128)S(1)} collective-permute-done((f32[2,16,600]{2,1,0:T(8,128)S(1)}, f32[2,16,600]{2,1,0:T(8,128)S(1)}, u32[]{:S(2)}, u32[]{:S(2)}) %collective-permute-start.10) | collective-permute-done | bytes 76832 | tf_op jit(solution)/shard_map/ppermute | solution.py:317
  41.5 0.7 %copy.5 = f32[16,1,2,600]{3,2,1,0:T(2,128)} copy(f32[16,1,2,600]{3,0,2,1:T(8,128)S(1)} %fusion.3) | data formatting | bytes 153600 | tf_op jit(solution)/shard_map/broadcast_in_dim | solution.py:364
  (14 shorter events, 0.1 us)
Async XLA Ops:
  2.1 8.2 %collective-permute-start = (f32[584,128]{1,0:T(8,128)S(1)}, f32[584,128]{1,0:T(8,128)S(1)}, u32[]{:S(2)}, u32[]{:S(2)}) collective-permute-start(f32[584,128]{1,0:T(8,128)S(1)} %get-tuple-element.16), channel_id=1, source_target_pairs={{0,4},{4,8},{8,12},{12,16},{16,20},{20,24},{24,28},{1,5},{5,9},{9,... | collective-permute-start | bytes 897032 | tf_op jit(solution)/shard_map/ppermute | solution.py:292
  4.5 5.8 %collective-permute-start.1 = (f32[584,128]{1,0:T(8,128)S(1)}, f32[584,128]{1,0:T(8,128)S(1)}, u32[]{:S(2)}, u32[]{:S(2)}) collective-permute-start(f32[584,128]{1,0:T(8,128)S(1)} %get-tuple-element.17), channel_id=1, source_target_pairs={{4,0},{8,4},{12,8},{16,12},{20,16},{24,20},{28,24},{5,1},{9,5},{13... | collective-permute-start | bytes 897032 | tf_op jit(solution)/shard_map/ppermute | solution.py:292
  5.8 10.6 %collective-permute-start.4 = (f32[2,5,32,128]{3,2,1,0:T(8,128)S(1)}, f32[2,5,32,128]{3,2,1,0:T(8,128)S(1)}, u32[]{:S(2)}, u32[]{:S(2)}) collective-permute-start(f32[2,5,32,128]{3,2,1,0:T(8,128)S(1)} %get-tuple-element.20), channel_id=1, source_target_pairs={{0,3},{1,2},{2,1},{3,0},{4,7},{5,6},{6,5},{7,4},{8,11},{9,10},{10,... | collective-permute-start | bytes 491528 | tf_op jit(solution)/shard_map/ppermute | solution.py:302
  10.3 0.7 %copy-start.1 = (f32[5,128]{1,0:T(8,128)S(1)}, f32[5,128]{1,0:T(8,128)}, u32[]{:S(2)}) copy-start(f32[5,128]{1,0:T(8,128)} %own_c.7) | copy-start | bytes 7684
  11.0 13.9 %copy-start = (f32[1,2,600,640]{3,2,1,0:T(8,128)S(1)}, f32[1,2,600,640]{3,2,1,0:T(8,128)}, u32[]{:S(2)}) copy-start(f32[1,2,600,640]{3,2,1,0:T(8,128)} %param.6) | copy-start | bytes 9216004
  11.6 15.8 %collective-permute-start.2 = (f32[2,5,32,128]{3,2,1,0:T(8,128)S(1)}, f32[2,5,32,128]{3,2,1,0:T(8,128)S(1)}, u32[]{:S(2)}, u32[]{:S(2)}) collective-permute-start(f32[2,5,32,128]{3,2,1,0:T(8,128)S(1)} %smooth.5), channel_id=1, source_target_pairs={{0,1},{1,0},{2,3},{3,2},{4,5},{5,4},{6,7},{7,6},{8,9},{9,8},{10,11... | collective-permute-start | bytes 491528 | tf_op jit(solution)/shard_map/ppermute | solution.py:302
  13.7 13.8 %collective-permute-start.3 = (f32[2,5,32,128]{3,2,1,0:T(8,128)S(1)}, f32[2,5,32,128]{3,2,1,0:T(8,128)S(1)}, u32[]{:S(2)}, u32[]{:S(2)}) collective-permute-start(f32[2,5,32,128]{3,2,1,0:T(8,128)S(1)} %smooth.6), channel_id=1, source_target_pairs={{0,2},{1,3},{2,0},{3,1},{4,6},{5,7},{6,4},{7,5},{8,10},{9,11},{10,... | collective-permute-start | bytes 491528 | tf_op jit(solution)/shard_map/ppermute | solution.py:302
  16.4 9.7 %collective-permute-start.5 = (f32[192,128]{1,0:T(8,128)S(1)}, f32[192,128]{1,0:T(8,128)S(1)}, u32[]{:S(2)}, u32[]{:S(2)}) collective-permute-start(f32[192,128]{1,0:T(8,128)S(1)} %bitcast.27), channel_id=1, source_target_pairs={{0,4},{4,8},{8,12},{12,16},{16,20},{20,24},{24,28},{1,5},{5,9},{9,... | collective-permute-start | bytes 294920 | tf_op jit(solution)/shard_map/ppermute | solution.py:292
  23.6 3.2 %collective-permute-start.6 = (f32[192,128]{1,0:T(8,128)S(1)}, f32[192,128]{1,0:T(8,128)S(1)}, u32[]{:S(2)}, u32[]{:S(2)}) collective-permute-start(f32[192,128]{1,0:T(8,128)S(1)} %bitcast.26), channel_id=1, source_target_pairs={{4,0},{8,4},{12,8},{16,12},{20,16},{24,20},{28,24},{5,1},{9,5},{13... | collective-permute-start | bytes 294920 | tf_op jit(solution)/shard_map/ppermute | solution.py:292
  29.5 4.4 %collective-permute-start.7 = (f32[4,2,16,600]{3,2,1,0:T(8,128)S(1)}, f32[4,2,16,600]{3,2,1,0:T(8,128)S(1)}, u32[]{:S(2)}, u32[]{:S(2)}) collective-permute-start(f32[4,2,16,600]{3,2,1,0:T(8,128)S(1)} %get-tuple-element.24), channel_id=1, source_target_pairs={{0,4},{4,0},{8,12},{12,8},{16,20},{20,16},{24,28},{28,24},{1,5},{5... | collective-permute-start | bytes 921608 | tf_op jit(solution)/shard_map/ppermute | solution.py:314
  34.0 5.7 %collective-permute-start.8 = (f32[2,16,600]{2,1,0:T(8,128)S(1)}, f32[2,16,600]{2,1,0:T(8,128)S(1)}, u32[]{:S(2)}, u32[]{:S(2)}) collective-permute-start(f32[2,16,600]{2,1,0:T(8,128)S(1)} %get-tuple-element.25), channel_id=1, source_target_pairs={{0,24},{4,28},{8,16},{12,20},{16,8},{20,12},{24,0},{28,4},{1,25},{... | collective-permute-start | bytes 230408 | tf_op jit(solution)/shard_map/ppermute | solution.py:317
  34.5 6.9 %collective-permute-start.10 = (f32[2,16,600]{2,1,0:T(8,128)S(1)}, f32[2,16,600]{2,1,0:T(8,128)S(1)}, u32[]{:S(2)}, u32[]{:S(2)}) collective-permute-start(f32[2,16,600]{2,1,0:T(8,128)S(1)} %get-tuple-element.26), channel_id=1, source_target_pairs={{0,8},{4,12},{8,0},{12,4},{16,24},{20,28},{24,16},{28,20},{1,9},{5... | collective-permute-start | bytes 230408 | tf_op jit(solution)/shard_map/ppermute | solution.py:317
  36.9 4.6 %collective-permute-start.9 = (f32[2,16,600]{2,1,0:T(8,128)S(1)}, f32[2,16,600]{2,1,0:T(8,128)S(1)}, u32[]{:S(2)}, u32[]{:S(2)}) collective-permute-start(f32[2,16,600]{2,1,0:T(8,128)S(1)} %get-tuple-element.27), channel_id=1, source_target_pairs={{0,16},{4,20},{8,24},{12,28},{16,0},{20,4},{24,8},{28,12},{1,17},{... | collective-permute-start | bytes 230408 | tf_op jit(solution)/shard_map/ppermute | solution.py:317

commit v4 on v3

--- a/solution.py
+++ b/solution.py
@@ -24,6 +24,18 @@
     return pl.CostEstimate(flops=flops, bytes_accessed=moved, transcendentals=0)
 
 
+def in_hbm(array):
+    return pltpu.with_memory_space_constraint(array, pltpu.HBM)
+
+
+def even_strip():
+    return lax.rem(lax.axis_index("seabed"), 2) == 0
+
+
+def pick(flag, one, other):
+    return jnp.where(jnp.full(one.shape, flag), one, other)
+
+
 def dft_table(steps_count, freq_count):
     times = np.arange(steps_count)
     freqs = np.arange(freq_count)
@@ -51,10 +63,11 @@
 
 
 def transform_kernel(slots, edged, field_hbm, table_hbm, own_hbm, *refs):
-    outs, (low, high) = refs[:slots], refs[slots : slots + 2]
+    outs, (pair, cross) = refs[:slots], refs[slots : slots + 2]
     field, table, own_c, field_sem, table_sem, own_sem = refs[slots + 2 :]
     vectors, rows, steps, width = field.shape
     blocks = vectors // GROUP
+    even = even_strip()
     source = lax.axis_index("freq") if table_hbm.shape[0] > 1 else 0
     get_table = pltpu.make_async_copy(table_hbm.at[source], table, table_sem)
     get_table.start()
@@ -69,11 +82,12 @@
         get(i).start()
     get_own.wait()
     rim = PASSES - 1
-    base = edge_base(edged, 0, 0, vectors)
-    low[base : base + rim] = own_c[rows - rim :]
-    high[base : base + rim] = own_c[:rim]
-    low[base + rim :] = jnp.zeros((low.shape[0] - base - rim, width), jnp.float32)
-    high[base + rim :] = jnp.zeros((low.shape[0] - base - rim, width), jnp.float32)
+    base = edge_base(len(edged), 0, 0, vectors)
+    last_c, first_c = own_c[rows - rim :], own_c[:rim]
+    pad = jnp.zeros((pair.shape[0] - base - rim, width), jnp.float32)
+    for ref, one, other in ((pair, last_c, first_c), (cross, first_c, last_c)):
+        ref[base : base + rim] = pick(even, one, other)
+        ref[base + rim :] = pad
     get_table.wait()
     short = table[...]
     shape = (short.shape[0], GROUP, short.shape[1])
@@ -98,23 +112,24 @@
                 for r in range(rows):
                     piece = values[at : at + GROUP, r * width : (r + 1) * width]
                     outs[slot][b, r, span] = piece
-                    if slot >= edged:
-                        continue
-                    if r >= rows - PASSES:
-                        to = edge_base(slot, b, r - rows + PASSES, vectors) + i * GROUP
-                        low[to : to + GROUP] = piece
-                    if r < PASSES:
-                        to = edge_base(slot, b, r, vectors) + i * GROUP
-                        high[to : to + GROUP] = piece
+                if slot not in edged:
+                    continue
+                for r in range(PASSES):
+                    row = (rows - PASSES + r) * width
+                    last = values[at : at + GROUP, row : row + width]
+                    first = values[at : at + GROUP, r * width : (r + 1) * width]
+                    to = edge_base(edged.index(slot), b, r, vectors) + i * GROUP
+                    pair[to : to + GROUP] = pick(even, last, first)
+                    cross[to : to + GROUP] = pick(even, first, last)
 
 
 def transform(field, table, coefficient, slots, edged):
     vectors, rows, steps, width = field.shape
     chunk = jax.ShapeDtypeStruct((2, rows, vectors, width), jnp.float32)
-    edge = jax.ShapeDtypeStruct((edge_base(edged, 0, 0, vectors) + GROUP, width), jnp.float32)
+    edge = jax.ShapeDtypeStruct((edge_base(len(edged), 0, 0, vectors) + GROUP, width), jnp.float32)
     hbm = pl.BlockSpec(memory_space=pltpu.HBM)
     vmem = pl.BlockSpec(memory_space=pltpu.VMEM)
-    *chunks, low, high = pl.pallas_call(
+    *chunks, pair, cross = pl.pallas_call(
         functools.partial(transform_kernel, slots, edged),
         out_shape=[chunk] * slots + [edge] * 2,
         in_specs=[hbm, hbm, hbm],
@@ -133,8 +148,8 @@
             vectors * rows * width * (2 * steps + 8 * slots),
         ),
         name="transform",
-    )(*(pltpu.with_memory_space_constraint(x, pltpu.HBM) for x in (field, table, coefficient)))
-    return chunks, low, high
+    )(*map(in_hbm, (field, table, coefficient)))
+    return chunks, pair, cross
 
 
 def split_kernel(x_ref, high_ref, low_ref):
@@ -155,7 +170,7 @@
         compiler_params=params(),
         cost_estimate=cost(2 * transfer.size, 8 * transfer.size),
         name="split_transfer",
-    )(transfer)
+    )(in_hbm(transfer))
 
 
 def relaxed_rows(rows, coefficients):
@@ -172,32 +187,62 @@
     return out
 
 
-def smooth_kernel(base, rim_base, chunk, low, high, own_c, low_c, high_c, out):
+def edges_kernel(count, *refs):
+    chunks, (pair, cross) = refs[:count], refs[count:]
+    _, rows, vectors, _ = chunks[0].shape
+    even = even_strip().astype(jnp.int32)
+    for index, chunk in enumerate(chunks):
+        for ref, start in ((pair, even), (cross, 1 - even)):
+            for b in range(2):
+                for r in range(PASSES):
+                    at = edge_base(index, b, r, vectors)
+                    ref[at : at + vectors] = chunk[b, start * (rows - PASSES) + r]
+
+
+def edges(chunks):
+    _, _, vectors, width = chunks[0].shape
+    shape = (edge_base(len(chunks), 0, 0, vectors), width)
+    return pl.pallas_call(
+        functools.partial(edges_kernel, len(chunks)),
+        out_shape=[jax.ShapeDtypeStruct(shape, jnp.float32)] * 2,
+        compiler_params=params(),
+        cost_estimate=cost(0, 16 * shape[0] * width),
+        name="edges",
+    )(*chunks)
+
+
+def smooth_kernel(base, rim_base, chunk, pair, cross, own_c, pair_c, cross_c, out):
     _, rows, vectors, width = chunk.shape
     rim = PASSES - 1
-    coefficients = [low_c[rim_base + i : rim_base + i + 1] for i in range(rim)]
+    even = even_strip()
+    part = math.gcd(vectors, 2 * GROUP)
+
+    def rims(one, other):
+        return pick(even, one, other), pick(even, other, one)
+
+    at_c = slice(rim_base, rim_base + rim)
+    high_c, low_c = rims(pair_c[at_c], cross_c[at_c])
+    coefficients = [low_c[i : i + 1] for i in range(rim)]
     coefficients += [own_c[i : i + 1] for i in range(rows)]
-    coefficients += [high_c[rim_base + i : rim_base + i + 1] for i in range(rim)]
-    part = math.gcd(vectors, 2 * GROUP)
+    coefficients += [high_c[i : i + 1] for i in range(rim)]
     coefficients = [jnp.broadcast_to(c, (part, width)) for c in coefficients]
     for b in range(2):
         for start in range(0, vectors, part):
             span = slice(start, start + part)
-
-            def edge(ref, r):
+            low, high = [], []
+            for r in range(PASSES):
                 at = base + edge_base(0, b, r, vectors) + start
-                return ref[at : at + part]
-
-            values = [edge(low, r) for r in range(PASSES)]
-            values += [chunk[b, r, span] for r in range(rows)]
-            values += [edge(high, r) for r in range(PASSES)]
+                above, below = rims(pair[at : at + part], cross[at : at + part])
+                high.append(above)
+                low.append(below)
+            values = low + [chunk[b, r, span] for r in range(rows)] + high
             for step in range(PASSES):
                 values = relaxed_rows(values, coefficients[step : len(coefficients) - step])
             for r in range(rows):
                 out[b, r, span] = values[r]
 
 
-def smooth(chunk, low, high, slot, coefficients, rim_base):
+def smooth(chunk, pair, cross, slot, coefficients, rim_base):
     base = edge_base(slot, 0, 0, chunk.shape[2])
     return pl.pallas_call(
         functools.partial(smooth_kernel, base, rim_base),
@@ -205,7 +250,7 @@
         compiler_params=params(),
         cost_estimate=cost(30 * chunk.size, 10 * chunk.size),
         name="smooth",
-    )(chunk, low, high, *coefficients)
+    )(chunk, pair, cross, *coefficients)
 
 
 def combine_kernel(chunks_in, owners_in, paired, *refs):
@@ -222,7 +267,9 @@
                 if paired:
                     owner = (lax.axis_index("freq") ^ index) * owners_in + o
                     apart = owner ^ lax.axis_index("seabed")
-                    place = (apart & 1) * (held.shape[1] // 2) + (apart >> 1)
+                    x, y = (apart >> 1) & 1, apart >> 2
+                    early, late = jnp.where(owner % 2 == 0, x, y), jnp.where(owner % 2 == 0, y, x)
+                    place = (apart & 1) * 4 + early * 2 + late
                 else:
                     place = index * owners_in + o
                 for b in range(2):
@@ -273,66 +320,63 @@
     )(*[c for p in phases for c in p], t_high, t_low)
 
 
-def chain(count):
-    up = [(i, i + 1) for i in range(count - 1)]
-    return up, [(b, a) for a, b in up]
-
-
 def xor_pairs(count, apart):
     return [(i, i ^ apart) for i in range(count)]
 
 
-def edges_of(chunk):
-    _, rows, _, width = chunk.shape
-    return [x.reshape(-1, width) for x in (chunk[:, rows - PASSES :], chunk[:, :PASSES])]
-
-
-def shifted(low, high, strips):
-    up, down = chain(strips)
-    return lax.ppermute(low, "seabed", up), lax.ppermute(high, "seabed", down)
-
-
-def paired_shards(field, coefficient, split_of, table, freq_count, strips, owned):
+def neighbours(pair, cross, strips):
+    inner = [(i, i + 1) for i in range(1, strips - 1, 2)]
+    inner = inner + [(b, a) for a, b in inner]
+    cross = lax.ppermute(cross, "seabed", inner)
+    pair = lax.ppermute(pair, "seabed", xor_pairs(strips, 1))
+    return pair, cross
+
+
+def paired_shards(field, coefficient, split_of, table, freq_count, strips):
     vectors = field.shape[0]
-    last = freq_count - 1
-    chunks, low, high = transform(field, table, coefficient, freq_count, last)
-    low, high = shifted(low, high, strips)
-
-    def exchange(m, chunk):
+    chunks, pair, cross = transform(field, table, coefficient, freq_count, (2, 0))
+
+    def swap(m, chunk):
         return lax.ppermute(chunk, "freq", xor_pairs(freq_count, m))
 
-    moved = {last: exchange(last, chunks[last])}
+    def relax(chunk, edge, slot):
+        return smooth(chunk, *edge, slot, coefficients, rim_base)
+
+    third = swap(3, chunks[3])
+    edge = neighbours(pair, cross, strips)
+    first = swap(1, chunks[1])
     split = split_of()
-    coefficients = (coefficient, low, high)
-    rim_base = edge_base(last, 0, 0, vectors)
-    for m in reversed(range(last)):
-        chunk = smooth(chunks[m], low, high, m, coefficients, rim_base)
-        moved[m] = exchange(m, chunk) if m else chunk
-    low, high = shifted(*edges_of(moved[last]), strips)
-    moved[last] = smooth(moved[last], low, high, 0, coefficients, rim_base)
-    keep, send = combine([[moved[m] for m in range(freq_count)]], split, 2, True)
-    pair = keep + lax.ppermute(send, "seabed", xor_pairs(strips, 1))
-    total = pair[0]
-    for d in reversed(range(1, strips // 2)):
-        total = total + lax.ppermute(pair[d], "seabed", xor_pairs(strips, 2 * d))
-    return total
-
-
-def plain_shards(field, coefficient, split_of, table, freq_count, strips, owned):
+    coefficients = (coefficient, *edge)
+    rim_base = edge_base(2, 0, 0, vectors)
+    second = swap(2, relax(chunks[2], edge, 0))
+    own = relax(chunks[0], edge, 1)
+    edge = neighbours(*edges([third, first]), strips)
+    third = relax(third, edge, 0)
+    first = relax(first, edge, 1)
+    keep, send = combine([[own, first, second, third]], split, 2, True)
+    total = keep + lax.ppermute(send, "seabed", xor_pairs(strips, 1))
+    for hop in range(2):
+        half = total.shape[0] // 2
+        apart = [(i, i ^ (2 if i % 2 == hop else 4)) for i in range(strips)]
+        total = total[:half] + lax.ppermute(total[half:], "seabed", apart)
+    return total[0]
+
+
+def plain_shards(field, coefficient, split_of, table, freq_count, strips):
     vectors, rows = field.shape[:2]
-    spectrum, _, _ = transform(field, table, coefficient, freq_count, 0)
+    spectrum, _, _ = transform(field, table, coefficient, freq_count, ())
     spectrum = jnp.stack(spectrum)
     spectrum = lax.all_to_all(spectrum, "freq", split_axis=0, concat_axis=0, tiled=True)
     chunks = list(spectrum)
-    edges = [jnp.concatenate(e) for e in zip(*[edges_of(c) for c in chunks])]
-    low, high = shifted(*edges, strips)
     rim = PASSES - 1
-    coefficients = (
-        coefficient,
-        *shifted(coefficient[rows - rim :], coefficient[:rim], strips),
-    )
-    chunks = [smooth(c, low, high, i, coefficients, 0) for i, c in enumerate(chunks)]
-    (partial,) = combine([chunks], split_of(), vectors // owned, False)
+    even = even_strip()
+    first_c, last_c = coefficient[:rim], coefficient[rows - rim :]
+    pair_c, cross_c = pick(even, last_c, first_c), pick(even, first_c, last_c)
+    coefficients = (coefficient, *neighbours(pair_c, cross_c, strips))
+    edge = neighbours(*edges(chunks), strips)
+    chunks = [smooth(c, *edge, i, coefficients, 0) for i, c in enumerate(chunks)]
+    owners_in = vectors * freq_count // strips
+    (partial,) = combine([chunks], split_of(), vectors // owners_in, False)
     got = lax.all_to_all(partial, "seabed", split_axis=0, concat_axis=0, tiled=True)
     return got.sum(0)
 
@@ -342,8 +386,8 @@
     freq_count, strips = FD * lax.axis_size("freq"), lax.axis_size("seabed")
     owned = vectors * freq_count // strips
     paired = (
-        strips == 2 * freq_count
-        and strips & (strips - 1) == 0
+        strips == 8
+        and freq_count == 4
         and vectors == 2 * owned
         and owned == 2 * GROUP
     )
@@ -359,7 +403,6 @@
         table,
         freq_count,
         strips,
-        owned,
     )
     return jnp.transpose(total, (1, 0, 2))[:, None]
 

time: 42.4 us -> 47.1 us (1.11)
  waiting for transfers between devices: 5.26 us -> 15.6 us
  starting transfers between devices: 28 us -> 21.5 us
  Pallas kernels: 7.24 us -> 8.91 us
  local copies, waits for them, and re-layouts: 1.4 us -> 0.7 us
    ppermute x11 -> x10, waiting for transfers between devices: 5.26 us -> 15.6 us  [the longest x3 8.42 us: swap(): return lax.ppermute(chunk, 'freq', xor_pairs(freq_count, m))]
    ppermute x11 -> x10, starting transfers between devices: 28 us -> 21.5 us  [the longest x3 7.33 us: swap(): return lax.ppermute(chunk, 'freq', xor_pairs(freq_count, m))]
    pallas_call x1, Pallas kernels: 0.51 us -> 2.09 us  [split_transfer(): pl.pallas_call(split_kernel, out_shape=[jax.ShapeDtypeStruct(transfer.sha...]
    unnamed x4 -> x2, local copies, waits for them, and re-layouts: 0.69 us -> 0.01 us
  transfers between devices with their start and end apart: 11 -> 10, of which waited for: 4 -> 6; matrix products, arithmetic and copies ran while one was open for 0% -> 0% of each run, Pallas kernels for 7% -> 10%
where the time goes in v4:
time: 47.1 us; the launch traced here: 47 us
  starting transfers between devices  21.5 us (46%)
  waiting for transfers between devices  15.6 us (33%)
  Pallas kernels  8.91 us (19%)
  local copies, waits for them, and re-layouts  0.7 us (1%)
    ppermute x3, waiting for transfers between devices, swap(): return lax.ppermute(chunk, 'freq', xor_pairs(freq_count, m))  8.42 us
    ppermute x3, starting transfers between devices, swap(): return lax.ppermute(chunk, 'freq', xor_pairs(freq_count, m))  7.33 us
    ppermute x2, starting transfers between devices, paired_shards(): total = total[:half] + lax.ppermute(total[half:], 'seabed', apart)  6.83 us
    ppermute x2, waiting for transfers between devices, paired_shards(): total = total[:half] + lax.ppermute(total[half:], 'seabed', apart)  5.92 us
    ppermute x1, starting transfers between devices, paired_shards(): total = keep + lax.ppermute(send, 'seabed', xor_pairs(strips, 1))  3.73 us
    pallas_call x4, Pallas kernels, smooth(): pl.pallas_call(functools.partial(smooth_kernel, base, rim_base), out_shap...  2.62 us
    ppermute x2, starting transfers between devices, neighbours(): pair = lax.ppermute(pair, 'seabed', xor_pairs(strips, 1))  2.32 us
    pallas_call x1, Pallas kernels, transform(): pl.pallas_call(functools.partial(transform_kernel, slots, edged), out_sha...  2.1 us
  transfers between devices with their start and end apart: 10, of which 6 were waited for; matrix products, arithmetic and copies ran while one was open for 0% of the time, Pallas kernels for 10%

profile of v4, /device:TPU:0, one launch (start us, length us, event | category | flops | bytes accessed | tf_op | source)
XLA Modules:
  0.0 47.0 jit_solution(17295458617956991837)
XLA Ops:
  0.0 2.1 %transform.1 = (f32[2,5,32,128]{3,2,1,0:T(8,128)S(1)}, f32[2,5,32,128]{3,2,1,0:T(8,128)S(1)}, f32[2,5,32,128]{3,2,1,0:T(8,128)S(1)}, f32[2,5,32,128]{3,2,1,0:T(8...) custom-call(bf16[32,5,32,128]{3,2,1,0:T(8,128)(2,1)} %bitcast.9, f32[4,16,256]{2,1,0:T(8,128)} %constant.2.clone.table_hbm, ...), custom_call_target="tpu_custom_call" | custom-call | flops 167772160 | bytes 1966080 | tf_op jit(solution)/shard_map/transform/pallas_call | solution.py:132
  2.1 0.6 %collective-permute-start = (f32[392,128]{1,0:T(8,128)S(1)}, f32[392,128]{1,0:T(8,128)S(1)}, u32[]{:S(2)}, u32[]{:S(2)}) collective-permute-start(f32[392,128]{1,0:T(8,128)S(1)} %get-tuple-element.18), channel_id=1, source_target_pairs={{0,4},{4,0},{8,12},{12,8},{16,20},{20,16},{24,28},{28,24},{1,5},{5... | collective-permute-start | bytes 602120 | tf_op jit(solution)/shard_map/ppermute | solution.py:331
  2.7 0.7 %collective-permute-start.1 = (f32[392,128]{1,0:T(8,128)S(1)}, f32[392,128]{1,0:T(8,128)S(1)}, u32[]{:S(2)}, u32[]{:S(2)}) collective-permute-start(f32[392,128]{1,0:T(8,128)S(1)} %get-tuple-element.19), channel_id=1, source_target_pairs={{4,8},{12,16},{20,24},{8,4},{16,12},{24,20},{5,9},{13,17},{21,25},... | collective-permute-start | bytes 602120 | tf_op jit(solution)/shard_map/ppermute | solution.py:330
  3.3 2.7 %collective-permute-start.2 = (f32[2,5,32,128]{3,2,1,0:T(8,128)S(1)}, f32[2,5,32,128]{3,2,1,0:T(8,128)S(1)}, u32[]{:S(2)}, u32[]{:S(2)}) collective-permute-start(f32[2,5,32,128]{3,2,1,0:T(8,128)S(1)} %get-tuple-element.20), channel_id=1, source_target_pairs={{0,1},{1,0},{2,3},{3,2},{4,5},{5,4},{6,7},{7,6},{8,9},{9,8},{10,11... | collective-permute-start | bytes 491528 | tf_op jit(solution)/shard_map/ppermute | solution.py:340
  6.0 2.5 %collective-permute-start.3 = (f32[2,5,32,128]{3,2,1,0:T(8,128)S(1)}, f32[2,5,32,128]{3,2,1,0:T(8,128)S(1)}, u32[]{:S(2)}, u32[]{:S(2)}) collective-permute-start(f32[2,5,32,128]{3,2,1,0:T(8,128)S(1)} %get-tuple-element.21), channel_id=1, source_target_pairs={{0,3},{1,2},{2,1},{3,0},{4,7},{5,6},{6,5},{7,4},{8,11},{9,10},{10,... | collective-permute-start | bytes 491528 | tf_op jit(solution)/shard_map/ppermute | solution.py:340
  8.5 0.8 %collective-permute-done.2.refs_1_.chunk = f32[2,5,32,128]{3,2,1,0:T(8,128)S(1)} collective-permute-done((f32[2,5,32,128]{3,2,1,0:T(8,128)S(1)}, f32[2,5,32,128]{3,2,1,0:T(8,128)S(1)}, u32[]{:S(2)}, u32[]{:S(2)}) %collective-permute-start.2) | collective-permute-done | bytes 163872 | tf_op jit(solution)/shard_map/ppermute | solution.py:340
  9.3 5.9 %collective-permute-done.3.refs_0_.chunk = f32[2,5,32,128]{3,2,1,0:T(8,128)S(1)} collective-permute-done((f32[2,5,32,128]{3,2,1,0:T(8,128)S(1)}, f32[2,5,32,128]{3,2,1,0:T(8,128)S(1)}, u32[]{:S(2)}, u32[]{:S(2)}) %collective-permute-start.3) | collective-permute-done | bytes 163872 | tf_op jit(solution)/shard_map/ppermute | solution.py:340
  15.2 1.8 %collective-permute-start.4 = (f32[384,128]{1,0:T(8,128)S(1)}, f32[384,128]{1,0:T(8,128)S(1)}, u32[]{:S(2)}, u32[]{:S(2)}) collective-permute-start(f32[384,128]{1,0:T(8,128)S(1)} %get-tuple-element.22), channel_id=1, source_target_pairs={{0,4},{4,0},{8,12},{12,8},{16,20},{20,16},{24,28},{28,24},{1,5},{5... | collective-permute-start | bytes 589832 | tf_op jit(solution)/shard_map/ppermute | solution.py:331
  16.9 0.7 %collective-permute-start.5 = (f32[384,128]{1,0:T(8,128)S(1)}, f32[384,128]{1,0:T(8,128)S(1)}, u32[]{:S(2)}, u32[]{:S(2)}) collective-permute-start(f32[384,128]{1,0:T(8,128)S(1)} %get-tuple-element.23), channel_id=1, source_target_pairs={{4,8},{12,16},{20,24},{8,4},{16,12},{24,20},{5,9},{13,17},{21,25},... | collective-permute-start | bytes 589832 | tf_op jit(solution)/shard_map/ppermute | solution.py:330
  17.6 0.7 %smooth.6 = f32[2,5,32,128]{3,2,1,0:T(8,128)S(1)} custom-call(f32[2,5,32,128]{3,2,1,0:T(8,128)S(1)} %get-tuple-element.24.chunk, f32[392,128]{1,0:T(8,128)S(1)} %collective-permute-done.pair.pair_c, f32[392,128]{1,0:T(8,128)S(1)} %collective-permute-done.1.cross.cross_c, f32[5,128]{1,0:T(8,128)S(1)} %copy-done, ...), custom_call_target="tpu_custom_call" | custom-call | flops 1228800 | bytes 409600 | tf_op jit(solution)/shard_map/smooth/pallas_call | solution.py:247
  18.3 2.2 %collective-permute-start.6 = (f32[2,5,32,128]{3,2,1,0:T(8,128)S(1)}, f32[2,5,32,128]{3,2,1,0:T(8,128)S(1)}, u32[]{:S(2)}, u32[]{:S(2)}) collective-permute-start(f32[2,5,32,128]{3,2,1,0:T(8,128)S(1)} %smooth.6), channel_id=1, source_target_pairs={{0,2},{1,3},{2,0},{3,1},{4,6},{5,7},{6,4},{7,5},{8,10},{9,11},{10,... | collective-permute-start | bytes 491528 | tf_op jit(solution)/shard_map/ppermute | solution.py:340
  20.5 2.1 %split_transfer.1 = (bf16[2,600,640]{2,1,0:T(8,128)(2,1)S(1)}, bf16[2,600,640]{2,1,0:T(8,128)(2,1)S(1)}) custom-call(f32[2,600,640]{2,1,0:T(8,128)} %bitcast.8), custom_call_target="tpu_custom_call" | custom-call | flops 1536000 | bytes 6144000 | tf_op jit(solution)/shard_map/split_transfer/pallas_call | solution.py:164
  22.6 0.7 %smooth.4.refs_0_ = f32[2,5,32,128]{3,2,1,0:T(8,128)S(1)} custom-call(f32[2,5,32,128]{3,2,1,0:T(8,128)S(1)} %get-tuple-element.17.chunk, f32[392,128]{1,0:T(8,128)S(1)} %collective-permute-done.pair.pair_c, f32[392,128]{1,0:T(8,128)S(1)} %collective-permute-done.1.cross.cross_c, f32[5,128]{1,0:T(8,128)S(1)} %copy-done, ...), custom_call_target="tpu_custom_call" | custom-call | flops 1228800 | bytes 409600 | tf_op jit(solution)/shard_map/smooth/pallas_call | solution.py:247
  23.3 0.7 %smooth.7.refs_3_ = f32[2,5,32,128]{3,2,1,0:T(8,128)S(1)} custom-call(f32[2,5,32,128]{3,2,1,0:T(8,128)S(1)} %collective-permute-done.3.refs_0_.chunk, f32[384,128]{1,0:T(8,128)S(1)} %collective-permute-done.4.pair, f32[384,128]{1,0:T(8,128)S(1)} %collective-permute-done.5.cross, f32[5,128]{1,0:T(8,128)S(1)} %copy-done, ...), custom_call_target="tpu_custom_call" | custom-call | flops 1228800 | bytes 409600 | tf_op jit(solution)/shard_map/smooth/pallas_call | solution.py:247
  24.0 0.7 %smooth.5.refs_1_ = f32[2,5,32,128]{3,2,1,0:T(8,128)S(1)} custom-call(f32[2,5,32,128]{3,2,1,0:T(8,128)S(1)} %collective-permute-done.2.refs_1_.chunk, f32[384,128]{1,0:T(8,128)S(1)} %collective-permute-done.4.pair, f32[384,128]{1,0:T(8,128)S(1)} %collective-permute-done.5.cross, f32[5,128]{1,0:T(8,128)S(1)} %copy-done, ...), custom_call_target="tpu_custom_call" | custom-call | flops 1228800 | bytes 409600 | tf_op jit(solution)/shard_map/smooth/pallas_call | solution.py:247
  24.6 1.7 %collective-permute-done.6.refs_2_ = f32[2,5,32,128]{3,2,1,0:T(8,128)S(1)} collective-permute-done((f32[2,5,32,128]{3,2,1,0:T(8,128)S(1)}, f32[2,5,32,128]{3,2,1,0:T(8,128)S(1)}, u32[]{:S(2)}, u32[]{:S(2)}) %collective-permute-start.6) | collective-permute-done | bytes 163872 | tf_op jit(solution)/shard_map/ppermute | solution.py:340
  26.3 2.1 %combine.1 = (f32[4,2,16,600]{3,2,1,0:T(8,128)S(1)}, f32[4,2,16,600]{3,2,1,0:T(8,128)S(1)}) custom-call(f32[2,5,32,128]{3,2,1,0:T(8,128)S(1)} %smooth.4.refs_0_, f32[2,5,32,128]{3,2,1,0:T(8,128)S(1)} %smooth.5.refs_1_, f32[2,5,32,128]{3,2,1,0:T(8,128)S(1)} %collective-permute-done.6.refs_2_, f32[2,5,32,128]{3,2,1,0:T(8,128)S(1)} %smooth.7.refs_3_, ...), custom_call_target="tpu_custom_call" | custom-call | flops 1179648000 | bytes 4956160 | tf_op jit(solution)/shard_map/combine/pallas_call | solution.py:310
  28.4 3.7 %collective-permute-start.7 = (f32[4,2,16,600]{3,2,1,0:T(8,128)S(1)}, f32[4,2,16,600]{3,2,1,0:T(8,128)S(1)}, u32[]{:S(2)}, u32[]{:S(2)}) collective-permute-start(f32[4,2,16,600]{3,2,1,0:T(8,128)S(1)} %get-tuple-element.28), channel_id=1, source_target_pairs={{0,4},{4,0},{8,12},{12,8},{16,20},{20,16},{24,28},{28,24},{1,5},{5... | collective-permute-start | bytes 921608 | tf_op jit(solution)/shard_map/ppermute | solution.py:357
  32.2 1.3 %collective-permute-done.7 = f32[4,2,16,600]{3,2,1,0:T(8,128)S(1)} collective-permute-done((f32[4,2,16,600]{3,2,1,0:T(8,128)S(1)}, f32[4,2,16,600]{3,2,1,0:T(8,128)S(1)}, u32[]{:S(2)}, u32[]{:S(2)}) %collective-permute-start.7) | collective-permute-done | bytes 307232 | tf_op jit(solution)/shard_map/ppermute | solution.py:357
  33.5 4.9 %collective-permute-start.8 = (f32[2,2,16,600]{3,2,1,0:T(8,128)S(1)}, f32[2,2,16,600]{3,2,1,0:T(8,128)S(1)}, u32[]{:S(2)}, u32[]{:S(2)}) collective-permute-start(f32[2,2,16,600]{3,2,1,0:T(8,128)S(1)} %slice.17), channel_id=1, source_target_pairs={{0,8},{4,20},{8,0},{12,28},{16,24},{20,4},{24,16},{28,12},{1,9},{5... | collective-permute-start | bytes 460808 | tf_op jit(solution)/shard_map/ppermute | solution.py:361
  38.4 3.3 %collective-permute-done.8 = f32[2,2,16,600]{3,2,1,0:T(8,128)S(1)} collective-permute-done((f32[2,2,16,600]{3,2,1,0:T(8,128)S(1)}, f32[2,2,16,600]{3,2,1,0:T(8,128)S(1)}, u32[]{:S(2)}, u32[]{:S(2)}) %collective-permute-start.8) | collective-permute-done | bytes 153632 | tf_op jit(solution)/shard_map/ppermute | solution.py:361
  41.8 1.9 %collective-permute-start.9 = (f32[1,2,16,600]{3,2,1,0:T(8,128)S(1)}, f32[1,2,16,600]{3,2,1,0:T(8,128)S(1)}, u32[]{:S(2)}, u32[]{:S(2)}) collective-permute-start(f32[1,2,16,600]{3,2,1,0:T(8,128)S(1)} %slice.19), channel_id=1, source_target_pairs={{0,16},{4,12},{8,24},{12,4},{16,0},{20,28},{24,8},{28,20},{1,17},{... | collective-permute-start | bytes 230408 | tf_op jit(solution)/shard_map/ppermute | solution.py:361
  43.6 2.6 %collective-permute-done.9 = f32[1,2,16,600]{3,2,1,0:T(8,128)S(1)} collective-permute-done((f32[1,2,16,600]{3,2,1,0:T(8,128)S(1)}, f32[1,2,16,600]{3,2,1,0:T(8,128)S(1)}, u32[]{:S(2)}, u32[]{:S(2)}) %collective-permute-start.9) | collective-permute-done | bytes 76832 | tf_op jit(solution)/shard_map/ppermute | solution.py:361
  46.3 0.7 %copy.5 = f32[16,1,2,600]{3,2,1,0:T(2,128)} copy(f32[16,1,2,600]{3,0,2,1:T(8,128)S(1)} %fusion) | data formatting | bytes 153600 | tf_op jit(solution)/shard_map/broadcast_in_dim | solution.py:407
  (12 shorter events, 0.1 us)
Async XLA Ops:
  0.0 17.6 %copy-start = (f32[5,128]{1,0:T(8,128)S(1)}, f32[5,128]{1,0:T(8,128)}, u32[]{:S(2)}) copy-start(f32[5,128]{1,0:T(8,128)} %own_c.7) | copy-start | bytes 7684
  2.1 15.5 %collective-permute-start = (f32[392,128]{1,0:T(8,128)S(1)}, f32[392,128]{1,0:T(8,128)S(1)}, u32[]{:S(2)}, u32[]{:S(2)}) collective-permute-start(f32[392,128]{1,0:T(8,128)S(1)} %get-tuple-element.18), channel_id=1, source_target_pairs={{0,4},{4,0},{8,12},{12,8},{16,20},{20,16},{24,28},{28,24},{1,5},{5... | collective-permute-start | bytes 602120 | tf_op jit(solution)/shard_map/ppermute | solution.py:331
  2.7 15.0 %collective-permute-start.1 = (f32[392,128]{1,0:T(8,128)S(1)}, f32[392,128]{1,0:T(8,128)S(1)}, u32[]{:S(2)}, u32[]{:S(2)}) collective-permute-start(f32[392,128]{1,0:T(8,128)S(1)} %get-tuple-element.19), channel_id=1, source_target_pairs={{4,8},{12,16},{20,24},{8,4},{16,12},{24,20},{5,9},{13,17},{21,25},... | collective-permute-start | bytes 602120 | tf_op jit(solution)/shard_map/ppermute | solution.py:330
  3.3 6.0 %collective-permute-start.2 = (f32[2,5,32,128]{3,2,1,0:T(8,128)S(1)}, f32[2,5,32,128]{3,2,1,0:T(8,128)S(1)}, u32[]{:S(2)}, u32[]{:S(2)}) collective-permute-start(f32[2,5,32,128]{3,2,1,0:T(8,128)S(1)} %get-tuple-element.20), channel_id=1, source_target_pairs={{0,1},{1,0},{2,3},{3,2},{4,5},{5,4},{6,7},{7,6},{8,9},{9,8},{10,11... | collective-permute-start | bytes 491528 | tf_op jit(solution)/shard_map/ppermute | solution.py:340
  6.0 9.2 %collective-permute-start.3 = (f32[2,5,32,128]{3,2,1,0:T(8,128)S(1)}, f32[2,5,32,128]{3,2,1,0:T(8,128)S(1)}, u32[]{:S(2)}, u32[]{:S(2)}) collective-permute-start(f32[2,5,32,128]{3,2,1,0:T(8,128)S(1)} %get-tuple-element.21), channel_id=1, source_target_pairs={{0,3},{1,2},{2,1},{3,0},{4,7},{5,6},{6,5},{7,4},{8,11},{9,10},{10,... | collective-permute-start | bytes 491528 | tf_op jit(solution)/shard_map/ppermute | solution.py:340
  15.2 8.1 %collective-permute-start.4 = (f32[384,128]{1,0:T(8,128)S(1)}, f32[384,128]{1,0:T(8,128)S(1)}, u32[]{:S(2)}, u32[]{:S(2)}) collective-permute-start(f32[384,128]{1,0:T(8,128)S(1)} %get-tuple-element.22), channel_id=1, source_target_pairs={{0,4},{4,0},{8,12},{12,8},{16,20},{20,16},{24,28},{28,24},{1,5},{5... | collective-permute-start | bytes 589832 | tf_op jit(solution)/shard_map/ppermute | solution.py:331
  16.9 6.3 %collective-permute-start.5 = (f32[384,128]{1,0:T(8,128)S(1)}, f32[384,128]{1,0:T(8,128)S(1)}, u32[]{:S(2)}, u32[]{:S(2)}) collective-permute-start(f32[384,128]{1,0:T(8,128)S(1)} %get-tuple-element.23), channel_id=1, source_target_pairs={{4,8},{12,16},{20,24},{8,4},{16,12},{24,20},{5,9},{13,17},{21,25},... | collective-permute-start | bytes 589832 | tf_op jit(solution)/shard_map/ppermute | solution.py:330
  18.3 8.0 %collective-permute-start.6 = (f32[2,5,32,128]{3,2,1,0:T(8,128)S(1)}, f32[2,5,32,128]{3,2,1,0:T(8,128)S(1)}, u32[]{:S(2)}, u32[]{:S(2)}) collective-permute-start(f32[2,5,32,128]{3,2,1,0:T(8,128)S(1)} %smooth.6), channel_id=1, source_target_pairs={{0,2},{1,3},{2,0},{3,1},{4,6},{5,7},{6,4},{7,5},{8,10},{9,11},{10,... | collective-permute-start | bytes 491528 | tf_op jit(solution)/shard_map/ppermute | solution.py:340
  28.4 5.0 %collective-permute-start.7 = (f32[4,2,16,600]{3,2,1,0:T(8,128)S(1)}, f32[4,2,16,600]{3,2,1,0:T(8,128)S(1)}, u32[]{:S(2)}, u32[]{:S(2)}) collective-permute-start(f32[4,2,16,600]{3,2,1,0:T(8,128)S(1)} %get-tuple-element.28), channel_id=1, source_target_pairs={{0,4},{4,0},{8,12},{12,8},{16,20},{20,16},{24,28},{28,24},{1,5},{5... | collective-permute-start | bytes 921608 | tf_op jit(solution)/shard_map/ppermute | solution.py:357
  33.5 8.2 %collective-permute-start.8 = (f32[2,2,16,600]{3,2,1,0:T(8,128)S(1)}, f32[2,2,16,600]{3,2,1,0:T(8,128)S(1)}, u32[]{:S(2)}, u32[]{:S(2)}) collective-permute-start(f32[2,2,16,600]{3,2,1,0:T(8,128)S(1)} %slice.17), channel_id=1, source_target_pairs={{0,8},{4,20},{8,0},{12,28},{16,24},{20,4},{24,16},{28,12},{1,9},{5... | collective-permute-start | bytes 460808 | tf_op jit(solution)/shard_map/ppermute | solution.py:361
  41.8 4.5 %collective-permute-start.9 = (f32[1,2,16,600]{3,2,1,0:T(8,128)S(1)}, f32[1,2,16,600]{3,2,1,0:T(8,128)S(1)}, u32[]{:S(2)}, u32[]{:S(2)}) collective-permute-start(f32[1,2,16,600]{3,2,1,0:T(8,128)S(1)} %slice.19), channel_id=1, source_target_pairs={{0,16},{4,12},{8,24},{12,4},{16,0},{20,28},{24,8},{28,20},{1,17},{... | collective-permute-start | bytes 230408 | tf_op jit(solution)/shard_map/ppermute | solution.py:361

commit v5 on v4

--- a/solution.py
+++ b/solution.py
@@ -216,8 +216,11 @@
     rim = PASSES - 1
     even = even_strip()
     part = math.gcd(vectors, 2 * GROUP)
+    strip = lax.axis_index("seabed")
+    inside = (strip > 0) & (strip < lax.axis_size("seabed") - 1)
 
     def rims(one, other):
+        other = pick(inside, other, jnp.zeros_like(other))
         return pick(even, one, other), pick(even, other, one)
 
     at_c = slice(rim_base, rim_base + rim)
@@ -267,9 +270,7 @@
                 if paired:
                     owner = (lax.axis_index("freq") ^ index) * owners_in + o
                     apart = owner ^ lax.axis_index("seabed")
-                    x, y = (apart >> 1) & 1, apart >> 2
-                    early, late = jnp.where(owner % 2 == 0, x, y), jnp.where(owner % 2 == 0, y, x)
-                    place = (apart & 1) * 4 + early * 2 + late
+                    place = (apart & 1) * (held.shape[1] // 2) + (apart >> 1)
                 else:
                     place = index * owners_in + o
                 for b in range(2):
@@ -325,7 +326,7 @@
 
 
 def neighbours(pair, cross, strips):
-    inner = [(i, i + 1) for i in range(1, strips - 1, 2)]
+    inner = [(i, (i + 1) % strips) for i in range(1, strips, 2)]
     inner = inner + [(b, a) for a, b in inner]
     cross = lax.ppermute(cross, "seabed", inner)
     pair = lax.ppermute(pair, "seabed", xor_pairs(strips, 1))
@@ -354,16 +355,15 @@
     third = relax(third, edge, 0)
     first = relax(first, edge, 1)
     keep, send = combine([[own, first, second, third]], split, 2, True)
-    total = keep + lax.ppermute(send, "seabed", xor_pairs(strips, 1))
-    for hop in range(2):
-        half = total.shape[0] // 2
-        apart = [(i, i ^ (2 if i % 2 == hop else 4)) for i in range(strips)]
-        total = total[:half] + lax.ppermute(total[half:], "seabed", apart)
-    return total[0]
+    chips = keep + lax.ppermute(send, "seabed", xor_pairs(strips, 1))
+    total = chips[0]
+    for d in range(1, strips // 2):
+        total = total + lax.ppermute(chips[d], "seabed", xor_pairs(strips, 2 * d))
+    return total
 
 
 def plain_shards(field, coefficient, split_of, table, freq_count, strips):
-    vectors, rows = field.shape[:2]
+    _, rows = field.shape[:2]
     spectrum, _, _ = transform(field, table, coefficient, freq_count, ())
     spectrum = jnp.stack(spectrum)
     spectrum = lax.all_to_all(spectrum, "freq", split_axis=0, concat_axis=0, tiled=True)
@@ -375,8 +375,8 @@
     coefficients = (coefficient, *neighbours(pair_c, cross_c, strips))
     edge = neighbours(*edges(chunks), strips)
     chunks = [smooth(c, *edge, i, coefficients, 0) for i, c in enumerate(chunks)]
-    owners_in = vectors * freq_count // strips
-    (partial,) = combine([chunks], split_of(), vectors // owners_in, False)
+    owners_in = strips // freq_count
+    (partial,) = combine([chunks], split_of(), owners_in, False)
     got = lax.all_to_all(partial, "seabed", split_axis=0, concat_axis=0, tiled=True)
     return got.sum(0)
 

time: 47.1 us -> 42.5 us (0.902)
  starting transfers between devices: 21.5 us -> 15.3 us
  waiting for transfers between devices: 15.6 us -> 17.3 us
    ppermute x3 -> x4, starting transfers between devices: 10.6 us -> 3.64 us  [the longest x3 3.55 us: paired_shards(): total = total + lax.ppermute(chips[d], 'seabed', xor_pairs(strips, 2 * d))]
    ppermute x2, starting transfers between devices: 1.32 us -> 5.18 us  [neighbours(): cross = lax.ppermute(cross, 'seabed', inner)]
    ppermute x3, waiting for transfers between devices: 8.42 us -> 10.7 us  [swap(): return lax.ppermute(chunk, 'freq', xor_pairs(freq_count, m))]
    ppermute x2, starting transfers between devices: 2.32 us -> 0.63 us  [neighbours(): pair = lax.ppermute(pair, 'seabed', xor_pairs(strips, 1))]
    ppermute x3, starting transfers between devices: 7.33 us -> 5.87 us  [swap(): return lax.ppermute(chunk, 'freq', xor_pairs(freq_count, m))]
    ppermute x3 -> x4, waiting for transfers between devices: 7.17 us -> 6.08 us  [the longest x3 4.47 us: paired_shards(): total = total + lax.ppermute(chips[d], 'seabed', xor_pairs(strips, 2 * d))]
    ppermute x2, waiting for transfers between devices: 0.01 us -> 0.5 us  [neighbours(): cross = lax.ppermute(cross, 'seabed', inner)]
  transfers between devices with their start and end apart: 10 -> 11, of which waited for: 6 -> 8; matrix products, arithmetic and copies ran while one was open for 0% -> 0% of each run, Pallas kernels for 10% -> 11%
where the time goes in v5:
time: 42.5 us; the launch traced here: 42.4 us
  waiting for transfers between devices  17.3 us (41%)
  starting transfers between devices  15.3 us (36%)
  Pallas kernels  8.9 us (21%)
  local copies, waits for them, and re-layouts  0.7 us (2%)
    ppermute x3, waiting for transfers between devices, swap(): return lax.ppermute(chunk, 'freq', xor_pairs(freq_count, m))  10.7 us
    ppermute x3, starting transfers between devices, swap(): return lax.ppermute(chunk, 'freq', xor_pairs(freq_count, m))  5.87 us
    ppermute x2, starting transfers between devices, neighbours(): cross = lax.ppermute(cross, 'seabed', inner)  5.18 us
    ppermute x3, waiting for transfers between devices, paired_shards(): total = total + lax.ppermute(chips[d], 'seabed', xor_pairs(strips, 2 * d))  4.47 us
    ppermute x3, starting transfers between devices, paired_shards(): total = total + lax.ppermute(chips[d], 'seabed', xor_pairs(strips, 2 * d))  3.55 us
    pallas_call x4, Pallas kernels, smooth(): pl.pallas_call(functools.partial(smooth_kernel, base, rim_base), out_shap...  2.62 us
    pallas_call x1, Pallas kernels, transform(): pl.pallas_call(functools.partial(transform_kernel, slots, edged), out_sha...  2.1 us
    pallas_call x1, Pallas kernels, split_transfer(): pl.pallas_call(split_kernel, out_shape=[jax.ShapeDtypeStruct(transfer.sha...  2.09 us
  transfers between devices with their start and end apart: 11, of which 8 were waited for; matrix products, arithmetic and copies ran while one was open for 0% of the time, Pallas kernels for 11%

profile of v5, /device:TPU:0, one launch (start us, length us, event | category | flops | bytes accessed | tf_op | source)
XLA Modules:
  0.0 42.4 jit_solution(571564967645187644)
XLA Ops:
  0.0 2.1 %transform.1 = (f32[2,5,32,128]{3,2,1,0:T(8,128)S(1)}, f32[2,5,32,128]{3,2,1,0:T(8,128)S(1)}, f32[2,5,32,128]{3,2,1,0:T(8,128)S(1)}, f32[2,5,32,128]{3,2,1,0:T(8...) custom-call(bf16[32,5,32,128]{3,2,1,0:T(8,128)(2,1)} %bitcast.23, f32[4,16,256]{2,1,0:T(8,128)} %constant.2.clone.table_hbm, ...), custom_call_target="tpu_custom_call" | custom-call | flops 167772160 | bytes 1966080 | tf_op jit(solution)/shard_map/transform/pallas_call | solution.py:132
  2.1 0.6 %collective-permute-start = (f32[392,128]{1,0:T(8,128)S(1)}, f32[392,128]{1,0:T(8,128)S(1)}, u32[]{:S(2)}, u32[]{:S(2)}) collective-permute-start(f32[392,128]{1,0:T(8,128)S(1)} %get-tuple-element.18), channel_id=1, source_target_pairs={{0,4},{4,0},{8,12},{12,8},{16,20},{20,16},{24,28},{28,24},{1,5},{5... | collective-permute-start | bytes 602120 | tf_op jit(solution)/shard_map/ppermute | solution.py:332
  2.7 3.5 %collective-permute-start.1 = (f32[392,128]{1,0:T(8,128)S(1)}, f32[392,128]{1,0:T(8,128)S(1)}, u32[]{:S(2)}, u32[]{:S(2)}) collective-permute-start(f32[392,128]{1,0:T(8,128)S(1)} %get-tuple-element.19), channel_id=1, source_target_pairs={{4,8},{12,16},{20,24},{28,0},{8,4},{16,12},{24,20},{0,28},{5,9},{1... | collective-permute-start | bytes 602120 | tf_op jit(solution)/shard_map/ppermute | solution.py:331
  6.2 1.6 %collective-permute-start.2 = (f32[2,5,32,128]{3,2,1,0:T(8,128)S(1)}, f32[2,5,32,128]{3,2,1,0:T(8,128)S(1)}, u32[]{:S(2)}, u32[]{:S(2)}) collective-permute-start(f32[2,5,32,128]{3,2,1,0:T(8,128)S(1)} %get-tuple-element.20), channel_id=1, source_target_pairs={{0,1},{1,0},{2,3},{3,2},{4,5},{5,4},{6,7},{7,6},{8,9},{9,8},{10,11... | collective-permute-start | bytes 491528 | tf_op jit(solution)/shard_map/ppermute | solution.py:341
  7.8 2.5 %collective-permute-start.3 = (f32[2,5,32,128]{3,2,1,0:T(8,128)S(1)}, f32[2,5,32,128]{3,2,1,0:T(8,128)S(1)}, u32[]{:S(2)}, u32[]{:S(2)}) collective-permute-start(f32[2,5,32,128]{3,2,1,0:T(8,128)S(1)} %get-tuple-element.21), channel_id=1, source_target_pairs={{0,3},{1,2},{2,1},{3,0},{4,7},{5,6},{6,5},{7,4},{8,11},{9,10},{10,... | collective-permute-start | bytes 491528 | tf_op jit(solution)/shard_map/ppermute | solution.py:341
  10.3 1.8 %collective-permute-done.2.refs_1_.chunk = f32[2,5,32,128]{3,2,1,0:T(8,128)S(1)} collective-permute-done((f32[2,5,32,128]{3,2,1,0:T(8,128)S(1)}, f32[2,5,32,128]{3,2,1,0:T(8,128)S(1)}, u32[]{:S(2)}, u32[]{:S(2)}) %collective-permute-start.2) | collective-permute-done | bytes 163872 | tf_op jit(solution)/shard_map/ppermute | solution.py:341
  12.0 4.9 %collective-permute-done.3.refs_0_.chunk = f32[2,5,32,128]{3,2,1,0:T(8,128)S(1)} collective-permute-done((f32[2,5,32,128]{3,2,1,0:T(8,128)S(1)}, f32[2,5,32,128]{3,2,1,0:T(8,128)S(1)}, u32[]{:S(2)}, u32[]{:S(2)}) %collective-permute-start.3) | collective-permute-done | bytes 163872 | tf_op jit(solution)/shard_map/ppermute | solution.py:341
  17.1 1.6 %collective-permute-start.5 = (f32[384,128]{1,0:T(8,128)S(1)}, f32[384,128]{1,0:T(8,128)S(1)}, u32[]{:S(2)}, u32[]{:S(2)}) collective-permute-start(f32[384,128]{1,0:T(8,128)S(1)} %get-tuple-element.23), channel_id=1, source_target_pairs={{4,8},{12,16},{20,24},{28,0},{8,4},{16,12},{24,20},{0,28},{5,9},{1... | collective-permute-start | bytes 589832 | tf_op jit(solution)/shard_map/ppermute | solution.py:331
  18.7 0.7 %smooth.6 = f32[2,5,32,128]{3,2,1,0:T(8,128)S(1)} custom-call(f32[2,5,32,128]{3,2,1,0:T(8,128)S(1)} %get-tuple-element.24.chunk, f32[392,128]{1,0:T(8,128)S(1)} %collective-permute-done.pair.pair_c, f32[392,128]{1,0:T(8,128)S(1)} %collective-permute-done.1.cross.cross_c, f32[5,128]{1,0:T(8,128)S(1)} %copy-done, ...), custom_call_target="tpu_custom_call" | custom-call | flops 1228800 | bytes 409600 | tf_op jit(solution)/shard_map/smooth/pallas_call | solution.py:250
  19.4 1.8 %collective-permute-start.6 = (f32[2,5,32,128]{3,2,1,0:T(8,128)S(1)}, f32[2,5,32,128]{3,2,1,0:T(8,128)S(1)}, u32[]{:S(2)}, u32[]{:S(2)}) collective-permute-start(f32[2,5,32,128]{3,2,1,0:T(8,128)S(1)} %smooth.6), channel_id=1, source_target_pairs={{0,2},{1,3},{2,0},{3,1},{4,6},{5,7},{6,4},{7,5},{8,10},{9,11},{10,... | collective-permute-start | bytes 491528 | tf_op jit(solution)/shard_map/ppermute | solution.py:341
  21.2 2.1 %split_transfer.1 = (bf16[2,600,640]{2,1,0:T(8,128)(2,1)S(1)}, bf16[2,600,640]{2,1,0:T(8,128)(2,1)S(1)}) custom-call(f32[2,600,640]{2,1,0:T(8,128)} %bitcast.22), custom_call_target="tpu_custom_call" | custom-call | flops 1536000 | bytes 6144000 | tf_op jit(solution)/shard_map/split_transfer/pallas_call | solution.py:164
  23.3 0.7 %smooth.4.refs_0_ = f32[2,5,32,128]{3,2,1,0:T(8,128)S(1)} custom-call(f32[2,5,32,128]{3,2,1,0:T(8,128)S(1)} %get-tuple-element.17.chunk, f32[392,128]{1,0:T(8,128)S(1)} %collective-permute-done.pair.pair_c, f32[392,128]{1,0:T(8,128)S(1)} %collective-permute-done.1.cross.cross_c, f32[5,128]{1,0:T(8,128)S(1)} %copy-done, ...), custom_call_target="tpu_custom_call" | custom-call | flops 1228800 | bytes 409600 | tf_op jit(solution)/shard_map/smooth/pallas_call | solution.py:250
  24.5 0.7 %smooth.7.refs_3_ = f32[2,5,32,128]{3,2,1,0:T(8,128)S(1)} custom-call(f32[2,5,32,128]{3,2,1,0:T(8,128)S(1)} %collective-permute-done.3.refs_0_.chunk, f32[384,128]{1,0:T(8,128)S(1)} %collective-permute-done.4.pair, f32[384,128]{1,0:T(8,128)S(1)} %collective-permute-done.5.cross, f32[5,128]{1,0:T(8,128)S(1)} %copy-done, ...), custom_call_target="tpu_custom_call" | custom-call | flops 1228800 | bytes 409600 | tf_op jit(solution)/shard_map/smooth/pallas_call | solution.py:250
  25.2 0.7 %smooth.5.refs_1_ = f32[2,5,32,128]{3,2,1,0:T(8,128)S(1)} custom-call(f32[2,5,32,128]{3,2,1,0:T(8,128)S(1)} %collective-permute-done.2.refs_1_.chunk, f32[384,128]{1,0:T(8,128)S(1)} %collective-permute-done.4.pair, f32[384,128]{1,0:T(8,128)S(1)} %collective-permute-done.5.cross, f32[5,128]{1,0:T(8,128)S(1)} %copy-done, ...), custom_call_target="tpu_custom_call" | custom-call | flops 1228800 | bytes 409600 | tf_op jit(solution)/shard_map/smooth/pallas_call | solution.py:250
  25.8 4.0 %collective-permute-done.6.refs_2_ = f32[2,5,32,128]{3,2,1,0:T(8,128)S(1)} collective-permute-done((f32[2,5,32,128]{3,2,1,0:T(8,128)S(1)}, f32[2,5,32,128]{3,2,1,0:T(8,128)S(1)}, u32[]{:S(2)}, u32[]{:S(2)}) %collective-permute-start.6) | collective-permute-done | bytes 163872 | tf_op jit(solution)/shard_map/ppermute | solution.py:341
  29.8 2.1 %combine.1 = (f32[4,2,16,600]{3,2,1,0:T(8,128)S(1)}, f32[4,2,16,600]{3,2,1,0:T(8,128)S(1)}) custom-call(f32[2,5,32,128]{3,2,1,0:T(8,128)S(1)} %smooth.4.refs_0_, f32[2,5,32,128]{3,2,1,0:T(8,128)S(1)} %smooth.5.refs_1_, f32[2,5,32,128]{3,2,1,0:T(8,128)S(1)} %collective-permute-done.6.refs_2_, f32[2,5,32,128]{3,2,1,0:T(8,128)S(1)} %smooth.7.refs_3_, ...), custom_call_target="tpu_custom_call" | custom-call | flops 1179648000 | bytes 4956160 | tf_op jit(solution)/shard_map/combine/pallas_call | solution.py:311
  32.0 1.6 %collective-permute-done.7 = f32[4,2,16,600]{3,2,1,0:T(8,128)S(1)} collective-permute-done((f32[4,2,16,600]{3,2,1,0:T(8,128)S(1)}, f32[4,2,16,600]{3,2,1,0:T(8,128)S(1)}, u32[]{:S(2)}, u32[]{:S(2)}) %collective-permute-start.7) | collective-permute-done | bytes 307232 | tf_op jit(solution)/shard_map/ppermute | solution.py:358
  33.6 1.6 %collective-permute-start.8 = (f32[2,16,600]{2,1,0:T(8,128)S(1)}, f32[2,16,600]{2,1,0:T(8,128)S(1)}, u32[]{:S(2)}, u32[]{:S(2)}) collective-permute-start(f32[2,16,600]{2,1,0:T(8,128)S(1)} %get-tuple-element.29), channel_id=1, source_target_pairs={{0,8},{4,12},{8,0},{12,4},{16,24},{20,28},{24,16},{28,20},{1,9},{5... | collective-permute-start | bytes 230408 | tf_op jit(solution)/shard_map/ppermute | solution.py:361
  35.2 0.8 %collective-permute-start.10 = (f32[2,16,600]{2,1,0:T(8,128)S(1)}, f32[2,16,600]{2,1,0:T(8,128)S(1)}, u32[]{:S(2)}, u32[]{:S(2)}) collective-permute-start(f32[2,16,600]{2,1,0:T(8,128)S(1)} %get-tuple-element.30), channel_id=1, source_target_pairs={{0,24},{4,28},{8,16},{12,20},{16,8},{20,12},{24,0},{28,4},{1,25},{... | collective-permute-start | bytes 230408 | tf_op jit(solution)/shard_map/ppermute | solution.py:361
  36.0 1.2 %collective-permute-start.9 = (f32[2,16,600]{2,1,0:T(8,128)S(1)}, f32[2,16,600]{2,1,0:T(8,128)S(1)}, u32[]{:S(2)}, u32[]{:S(2)}) collective-permute-start(f32[2,16,600]{2,1,0:T(8,128)S(1)} %get-tuple-element.31), channel_id=1, source_target_pairs={{0,16},{4,20},{8,24},{12,28},{16,0},{20,4},{24,8},{28,12},{1,17},{... | collective-permute-start | bytes 230408 | tf_op jit(solution)/shard_map/ppermute | solution.py:361
  37.2 1.4 %collective-permute-done.8 = f32[2,16,600]{2,1,0:T(8,128)S(1)} collective-permute-done((f32[2,16,600]{2,1,0:T(8,128)S(1)}, f32[2,16,600]{2,1,0:T(8,128)S(1)}, u32[]{:S(2)}, u32[]{:S(2)}) %collective-permute-start.8) | collective-permute-done | bytes 76832 | tf_op jit(solution)/shard_map/ppermute | solution.py:361
  38.6 2.0 %collective-permute-done.10 = f32[2,16,600]{2,1,0:T(8,128)S(1)} collective-permute-done((f32[2,16,600]{2,1,0:T(8,128)S(1)}, f32[2,16,600]{2,1,0:T(8,128)S(1)}, u32[]{:S(2)}, u32[]{:S(2)}) %collective-permute-start.10) | collective-permute-done | bytes 76832 | tf_op jit(solution)/shard_map/ppermute | solution.py:361
  40.5 1.1 %collective-permute-done.9 = f32[2,16,600]{2,1,0:T(8,128)S(1)} collective-permute-done((f32[2,16,600]{2,1,0:T(8,128)S(1)}, f32[2,16,600]{2,1,0:T(8,128)S(1)}, u32[]{:S(2)}, u32[]{:S(2)}) %collective-permute-start.9) | collective-permute-done | bytes 76832 | tf_op jit(solution)/shard_map/ppermute | solution.py:361
  41.7 0.7 %copy.5 = f32[16,1,2,600]{3,2,1,0:T(2,128)} copy(f32[16,1,2,600]{3,0,2,1:T(8,128)S(1)} %fusion.3) | data formatting | bytes 153600 | tf_op jit(solution)/shard_map/broadcast_in_dim | solution.py:407
  (12 shorter events, 0.8 us)
Async XLA Ops:
  0.0 18.7 %copy-start = (f32[5,128]{1,0:T(8,128)S(1)}, f32[5,128]{1,0:T(8,128)}, u32[]{:S(2)}) copy-start(f32[5,128]{1,0:T(8,128)} %own_c.7) | copy-start | bytes 7684
  2.1 16.6 %collective-permute-start = (f32[392,128]{1,0:T(8,128)S(1)}, f32[392,128]{1,0:T(8,128)S(1)}, u32[]{:S(2)}, u32[]{:S(2)}) collective-permute-start(f32[392,128]{1,0:T(8,128)S(1)} %get-tuple-element.18), channel_id=1, source_target_pairs={{0,4},{4,0},{8,12},{12,8},{16,20},{20,16},{24,28},{28,24},{1,5},{5... | collective-permute-start | bytes 602120 | tf_op jit(solution)/shard_map/ppermute | solution.py:332
  2.7 16.1 %collective-permute-start.1 = (f32[392,128]{1,0:T(8,128)S(1)}, f32[392,128]{1,0:T(8,128)S(1)}, u32[]{:S(2)}, u32[]{:S(2)}) collective-permute-start(f32[392,128]{1,0:T(8,128)S(1)} %get-tuple-element.19), channel_id=1, source_target_pairs={{4,8},{12,16},{20,24},{28,0},{8,4},{16,12},{24,20},{0,28},{5,9},{1... | collective-permute-start | bytes 602120 | tf_op jit(solution)/shard_map/ppermute | solution.py:331
  6.2 5.8 %collective-permute-start.2 = (f32[2,5,32,128]{3,2,1,0:T(8,128)S(1)}, f32[2,5,32,128]{3,2,1,0:T(8,128)S(1)}, u32[]{:S(2)}, u32[]{:S(2)}) collective-permute-start(f32[2,5,32,128]{3,2,1,0:T(8,128)S(1)} %get-tuple-element.20), channel_id=1, source_target_pairs={{0,1},{1,0},{2,3},{3,2},{4,5},{5,4},{6,7},{7,6},{8,9},{9,8},{10,11... | collective-permute-start | bytes 491528 | tf_op jit(solution)/shard_map/ppermute | solution.py:341
  7.8 9.2 %collective-permute-start.3 = (f32[2,5,32,128]{3,2,1,0:T(8,128)S(1)}, f32[2,5,32,128]{3,2,1,0:T(8,128)S(1)}, u32[]{:S(2)}, u32[]{:S(2)}) collective-permute-start(f32[2,5,32,128]{3,2,1,0:T(8,128)S(1)} %get-tuple-element.21), channel_id=1, source_target_pairs={{0,3},{1,2},{2,1},{3,0},{4,7},{5,6},{6,5},{7,4},{8,11},{9,10},{10,... | collective-permute-start | bytes 491528 | tf_op jit(solution)/shard_map/ppermute | solution.py:341
  17.0 7.0 %collective-permute-start.4 = (f32[384,128]{1,0:T(8,128)S(1)}, f32[384,128]{1,0:T(8,128)S(1)}, u32[]{:S(2)}, u32[]{:S(2)}) collective-permute-start(f32[384,128]{1,0:T(8,128)S(1)} %get-tuple-element.22), channel_id=1, source_target_pairs={{0,4},{4,0},{8,12},{12,8},{16,20},{20,16},{24,28},{28,24},{1,5},{5... | collective-permute-start | bytes 589832 | tf_op jit(solution)/shard_map/ppermute | solution.py:332
  17.1 7.4 %collective-permute-start.5 = (f32[384,128]{1,0:T(8,128)S(1)}, f32[384,128]{1,0:T(8,128)S(1)}, u32[]{:S(2)}, u32[]{:S(2)}) collective-permute-start(f32[384,128]{1,0:T(8,128)S(1)} %get-tuple-element.23), channel_id=1, source_target_pairs={{4,8},{12,16},{20,24},{28,0},{8,4},{16,12},{24,20},{0,28},{5,9},{1... | collective-permute-start | bytes 589832 | tf_op jit(solution)/shard_map/ppermute | solution.py:331
  19.4 10.4 %collective-permute-start.6 = (f32[2,5,32,128]{3,2,1,0:T(8,128)S(1)}, f32[2,5,32,128]{3,2,1,0:T(8,128)S(1)}, u32[]{:S(2)}, u32[]{:S(2)}) collective-permute-start(f32[2,5,32,128]{3,2,1,0:T(8,128)S(1)} %smooth.6), channel_id=1, source_target_pairs={{0,2},{1,3},{2,0},{3,1},{4,6},{5,7},{6,4},{7,5},{8,10},{9,11},{10,... | collective-permute-start | bytes 491528 | tf_op jit(solution)/shard_map/ppermute | solution.py:341
  31.9 1.7 %collective-permute-start.7 = (f32[4,2,16,600]{3,2,1,0:T(8,128)S(1)}, f32[4,2,16,600]{3,2,1,0:T(8,128)S(1)}, u32[]{:S(2)}, u32[]{:S(2)}) collective-permute-start(f32[4,2,16,600]{3,2,1,0:T(8,128)S(1)} %get-tuple-element.28), channel_id=1, source_target_pairs={{0,4},{4,0},{8,12},{12,8},{16,20},{20,16},{24,28},{28,24},{1,5},{5... | collective-permute-start | bytes 921608 | tf_op jit(solution)/shard_map/ppermute | solution.py:358
  33.6 4.9 %collective-permute-start.8 = (f32[2,16,600]{2,1,0:T(8,128)S(1)}, f32[2,16,600]{2,1,0:T(8,128)S(1)}, u32[]{:S(2)}, u32[]{:S(2)}) collective-permute-start(f32[2,16,600]{2,1,0:T(8,128)S(1)} %get-tuple-element.29), channel_id=1, source_target_pairs={{0,8},{4,12},{8,0},{12,4},{16,24},{20,28},{24,16},{28,20},{1,9},{5... | collective-permute-start | bytes 230408 | tf_op jit(solution)/shard_map/ppermute | solution.py:361
  35.2 5.3 %collective-permute-start.10 = (f32[2,16,600]{2,1,0:T(8,128)S(1)}, f32[2,16,600]{2,1,0:T(8,128)S(1)}, u32[]{:S(2)}, u32[]{:S(2)}) collective-permute-start(f32[2,16,600]{2,1,0:T(8,128)S(1)} %get-tuple-element.30), channel_id=1, source_target_pairs={{0,24},{4,28},{8,16},{12,20},{16,8},{20,12},{24,0},{28,4},{1,25},{... | collective-permute-start | bytes 230408 | tf_op jit(solution)/shard_map/ppermute | solution.py:361
  36.0 5.7 %collective-permute-start.9 = (f32[2,16,600]{2,1,0:T(8,128)S(1)}, f32[2,16,600]{2,1,0:T(8,128)S(1)}, u32[]{:S(2)}, u32[]{:S(2)}) collective-permute-start(f32[2,16,600]{2,1,0:T(8,128)S(1)} %get-tuple-element.31), channel_id=1, source_target_pairs={{0,16},{4,20},{8,24},{12,28},{16,0},{20,4},{24,8},{28,12},{1,17},{... | collective-permute-start | bytes 230408 | tf_op jit(solution)/shard_map/ppermute | solution.py:361

commit v6 on v5

--- a/solution.py
+++ b/solution.py
@@ -256,30 +256,23 @@
     )(chunk, pair, cross, *coefficients)
 
 
-def combine_kernel(chunks_in, owners_in, paired, *refs):
-    refs = list(refs)
-    phases = [[refs.pop(0) for _ in range(count)] for count in chunks_in]
-    t_high, t_low = refs.pop(0), refs.pop(0)
-    outs, held = refs[:-1], refs[-1]
-    rows, vectors, width = phases[0][0].shape[1:]
-    each = vectors // owners_in
-    for phase, chunks in enumerate(phases):
-        inner = slice(phase * each, (phase + 1) * each)
-        for index, ref in enumerate(chunks):
-            for o in range(owners_in):
-                if paired:
-                    owner = (lax.axis_index("freq") ^ index) * owners_in + o
-                    apart = owner ^ lax.axis_index("seabed")
-                    place = (apart & 1) * (held.shape[1] // 2) + (apart >> 1)
-                else:
-                    place = index * owners_in + o
-                for b in range(2):
-                    for r in range(rows):
-                        held[b, place, inner, r * width : (r + 1) * width] = ref[
-                            b, r, o * each : (o + 1) * each
-                        ]
-    places, owned, cells = held.shape[1:]
-    lhs_high, lhs_low = split_bf16(held[...].reshape(2 * places * owned, cells))
+def place_of(index, o, owners_in):
+    owner = (lax.axis_index("freq") ^ index) * owners_in + o
+    apart = owner ^ lax.axis_index("seabed")
+    return apart & 1, apart >> 1
+
+
+def combine_kernel(indices, owners_in, paired, absent, *refs):
+    count = len(indices)
+    chunks, (t_high, t_low), (out, held) = refs[:count], refs[count : count + 2], refs[-2:]
+    _, rows, vectors, width = chunks[0].shape
+    owned = vectors // owners_in
+    for at, ref in enumerate(chunks):
+        for b in range(2):
+            for r in range(rows):
+                held[b, at, :, r * width : (r + 1) * width] = ref[b, r]
+    half = count * vectors
+    lhs_high, lhs_low = split_bf16(held[...].reshape(2 * half, rows * width))
 
     def times(a):
         def dot(x, w):
@@ -289,36 +282,63 @@
 
         return (dot(lhs_low, t_high[a]) + dot(lhs_high, t_low[a])) + dot(lhs_high, t_high[a])
 
-    half = places * owned
     by_real, by_imag = times(0), times(1)
     real = by_real[:half] - by_imag[half:]
     imag = by_imag[:half] + by_real[half:]
-    sensors = real.shape[-1]
-    share = places // len(outs)
-    for e, out in enumerate(outs):
-        at = slice(e * share * owned, (e + 1) * share * owned)
-        out[:, 0] = real[at].reshape(share, owned, sensors)
-        out[:, 1] = imag[at].reshape(share, owned, sensors)
-
-
-def combine(phases, split, owners_in, paired):
+
+    def place(index, o):
+        if not paired:
+            return index * owners_in + o
+        core, chip = place_of(index, o, owners_in)
+        return core * (out.shape[0] // 2) + (chip if out.shape[0] > 2 else 0)
+
+    for at, index in enumerate(indices):
+        for o in range(owners_in):
+            span = slice((at * owners_in + o) * owned, (at * owners_in + o + 1) * owned)
+            out[place(index, o), 0] = real[span]
+            out[place(index, o), 1] = imag[span]
+    for index in absent:
+        for o in range(owners_in):
+            out[place(index, o)] = jnp.zeros(out.shape[1:], out.dtype)
+
+
+def combine(chunks, split, owners_in, places, paired, absent=()):
     t_high, t_low = split
     sensors, cells = t_high.shape[1:]
-    places = len(phases[0]) * owners_in
-    owned = sum(p[0].shape[2] for p in phases) // owners_in
-    vectors = places * owned
-    outs = 2 if paired else 1
+    indices = sorted(chunks)
+    _, _, vectors, _ = chunks[indices[0]].shape
+    owned = vectors // owners_in
+    whole = len(indices) * vectors
     return pl.pallas_call(
-        functools.partial(combine_kernel, [len(p) for p in phases], owners_in, paired),
-        out_shape=[jax.ShapeDtypeStruct((places // outs, 2, owned, sensors), jnp.float32)] * outs,
-        scratch_shapes=[pltpu.VMEM((2, places, owned, cells), jnp.float32)],
+        functools.partial(combine_kernel, indices, owners_in, paired, absent),
+        out_shape=jax.ShapeDtypeStruct((places, 2, owned, sensors), jnp.float32),
+        scratch_shapes=[pltpu.VMEM((2, len(indices), vectors, cells), jnp.float32)],
         compiler_params=params(),
         cost_estimate=cost(
-            24 * vectors * sensors * cells,
-            8 * sensors * cells + 8 * vectors * cells + 16 * vectors * sensors,
+            24 * whole * sensors * cells,
+            8 * sensors * cells + 8 * whole * cells + 16 * whole * sensors,
         ),
         name="combine",
-    )(*[c for p in phases for c in p], t_high, t_low)
+    )(*[chunks[i] for i in indices], t_high, t_low)
+
+
+def merge_kernel(late, owners_in, most, most_moved, tail, tail_moved, *outs):
+    _, chip = place_of(late, 0, owners_in)
+    final = tail[0] + tail_moved[0]
+    for d, out in enumerate(outs):
+        here = pick(chip == d, final, jnp.zeros_like(final))
+        out[...] = (most[d] + most_moved[d]) + here
+
+
+def merge(late, owners_in, most, most_moved, tail, tail_moved):
+    shape = jax.ShapeDtypeStruct(most.shape[1:], jnp.float32)
+    return pl.pallas_call(
+        functools.partial(merge_kernel, late, owners_in),
+        out_shape=[shape] * most_moved.shape[0],
+        compiler_params=params(),
+        cost_estimate=cost(4 * most.size, 12 * most.size),
+        name="merge",
+    )(most, most_moved, tail, tail_moved)
 
 
 def xor_pairs(count, apart):
@@ -343,19 +363,27 @@
     def relax(chunk, edge, slot):
         return smooth(chunk, *edge, slot, coefficients, rim_base)
 
+    first = swap(1, chunks[1])
     third = swap(3, chunks[3])
     edge = neighbours(pair, cross, strips)
-    first = swap(1, chunks[1])
     split = split_of()
     coefficients = (coefficient, *edge)
     rim_base = edge_base(2, 0, 0, vectors)
+    first_edge = neighbours(*edges([first]), strips)
     second = swap(2, relax(chunks[2], edge, 0))
     own = relax(chunks[0], edge, 1)
-    edge = neighbours(*edges([third, first]), strips)
-    third = relax(third, edge, 0)
-    first = relax(first, edge, 1)
-    keep, send = combine([[own, first, second, third]], split, 2, True)
-    chips = keep + lax.ppermute(send, "seabed", xor_pairs(strips, 1))
+    third_edge = neighbours(*edges([third]), strips)
+    first = relax(first, first_edge, 0)
+    third = relax(third, third_edge, 0)
+    most = combine({0: own, 1: first, 3: third}, split, 2, strips, True, (2,))
+
+    def to_core(partial):
+        send = partial[partial.shape[0] // 2 :]
+        return lax.ppermute(send, "seabed", xor_pairs(strips, 1))
+
+    most_moved = to_core(most)
+    tail = combine({2: second}, split, 2, 2, True)
+    chips = merge(2, 2, most, most_moved, tail, to_core(tail))
     total = chips[0]
     for d in range(1, strips // 2):
         total = total + lax.ppermute(chips[d], "seabed", xor_pairs(strips, 2 * d))
@@ -376,7 +404,7 @@
     edge = neighbours(*edges(chunks), strips)
     chunks = [smooth(c, *edge, i, coefficients, 0) for i, c in enumerate(chunks)]
     owners_in = strips // freq_count
-    (partial,) = combine([chunks], split_of(), owners_in, False)
+    partial = combine(dict(enumerate(chunks)), split_of(), owners_in, strips, False)
     got = lax.all_to_all(partial, "seabed", split_axis=0, concat_axis=0, tiled=True)
     return got.sum(0)
 

time: 42.5 us -> 47.5 us (1.12)
  starting transfers between devices: 15.3 us -> 19.6 us
  Pallas kernels: 8.9 us -> 10.3 us
  waiting for transfers between devices: 17.3 us -> 16.6 us
    ppermute x2 -> x3, starting transfers between devices: 5.18 us -> 7.46 us  [neighbours(): cross = lax.ppermute(cross, 'seabed', inner)]
    ppermute x3, starting transfers between devices: 5.87 us -> 7.67 us  [swap(): return lax.ppermute(chunk, 'freq', xor_pairs(freq_count, m))]
    pallas_call x1 -> x3, Pallas kernels: 2.06 us -> 3.49 us  [the longest x2 3.45 us: combine(): pl.pallas_call(functools.partial(combine_kernel, indices, owners_in, pair...]
    ppermute x3, waiting for transfers between devices: 10.7 us -> 11.7 us  [swap(): return lax.ppermute(chunk, 'freq', xor_pairs(freq_count, m))]
    ppermute x3, waiting for transfers between devices: 4.47 us -> 3.55 us  [paired_shards(): total = total + lax.ppermute(chips[d], 'seabed', xor_pairs(strips, 2 * d))]
    ppermute x2 -> x3, waiting for transfers between devices: 0.5 us -> 0.01 us  [neighbours(): cross = lax.ppermute(cross, 'seabed', inner)]
    ppermute x1 -> x2, waiting for transfers between devices: 1.61 us -> 1.27 us  [to_core(): return lax.ppermute(send, 'seabed', xor_pairs(strips, 1))]
  transfers between devices with their start and end apart: 11 -> 14, of which waited for: 8 -> 7; matrix products, arithmetic and copies ran while one was open for 0% -> 0% of each run, Pallas kernels for 11% -> 12%
where the time goes in v6:
time: 47.5 us; the launch traced here: 47.3 us
  starting transfers between devices  19.6 us (41%)
  waiting for transfers between devices  16.6 us (35%)
  Pallas kernels  10.3 us (22%)
  local copies, waits for them, and re-layouts  0.71 us (1%)
    ppermute x3, waiting for transfers between devices, swap(): return lax.ppermute(chunk, 'freq', xor_pairs(freq_count, m))  11.7 us
    ppermute x3, starting transfers between devices, swap(): return lax.ppermute(chunk, 'freq', xor_pairs(freq_count, m))  7.67 us
    ppermute x3, starting transfers between devices, neighbours(): cross = lax.ppermute(cross, 'seabed', inner)  7.46 us
    ppermute x3, starting transfers between devices, paired_shards(): total = total + lax.ppermute(chips[d], 'seabed', xor_pairs(strips, 2 * d))  3.55 us
    ppermute x3, waiting for transfers between devices, paired_shards(): total = total + lax.ppermute(chips[d], 'seabed', xor_pairs(strips, 2 * d))  3.55 us
    pallas_call x2, Pallas kernels, combine(): pl.pallas_call(functools.partial(combine_kernel, indices, owners_in, pair...  3.45 us
    pallas_call x4, Pallas kernels, smooth(): pl.pallas_call(functools.partial(smooth_kernel, base, rim_base), out_shap...  2.63 us
    pallas_call x1, Pallas kernels, split_transfer(): pl.pallas_call(split_kernel, out_shape=[jax.ShapeDtypeStruct(transfer.sha...  2.1 us
  transfers between devices with their start and end apart: 14, of which 7 were waited for; matrix products, arithmetic and copies ran while one was open for 0% of the time, Pallas kernels for 12%

profile of v6, /device:TPU:0, one launch (start us, length us, event | category | flops | bytes accessed | tf_op | source)
XLA Modules:
  0.0 47.3 jit_solution(9133068309822608216)
XLA Ops:
  0.0 2.1 %transform.1 = (f32[2,5,32,128]{3,2,1,0:T(8,128)S(1)}, f32[2,5,32,128]{3,2,1,0:T(8,128)S(1)}, f32[2,5,32,128]{3,2,1,0:T(8,128)S(1)}, f32[2,5,32,128]{3,2,1,0:T(8...) custom-call(bf16[32,5,32,128]{3,2,1,0:T(8,128)(2,1)} %bitcast.7, f32[4,16,256]{2,1,0:T(8,128)} %constant.2.clone.table_hbm, ...), custom_call_target="tpu_custom_call" | custom-call | flops 167772160 | bytes 1966080 | tf_op jit(solution)/shard_map/transform/pallas_call | solution.py:132
  2.1 0.6 %collective-permute-start = (f32[392,128]{1,0:T(8,128)S(1)}, f32[392,128]{1,0:T(8,128)S(1)}, u32[]{:S(2)}, u32[]{:S(2)}) collective-permute-start(f32[392,128]{1,0:T(8,128)S(1)} %get-tuple-element.22), channel_id=1, source_target_pairs={{0,4},{4,0},{8,12},{12,8},{16,20},{20,16},{24,28},{28,24},{1,5},{5... | collective-permute-start | bytes 602120 | tf_op jit(solution)/shard_map/ppermute | solution.py:352
  2.6 4.7 %collective-permute-start.5 = (f32[2,5,32,128]{3,2,1,0:T(8,128)S(1)}, f32[2,5,32,128]{3,2,1,0:T(8,128)S(1)}, u32[]{:S(2)}, u32[]{:S(2)}) collective-permute-start(f32[2,5,32,128]{3,2,1,0:T(8,128)S(1)} %get-tuple-element.27), channel_id=1, source_target_pairs={{0,3},{1,2},{2,1},{3,0},{4,7},{5,6},{6,5},{7,4},{8,11},{9,10},{10,... | collective-permute-start | bytes 491528 | tf_op jit(solution)/shard_map/ppermute | solution.py:361
  7.3 2.2 %collective-permute-start.1 = (f32[392,128]{1,0:T(8,128)S(1)}, f32[392,128]{1,0:T(8,128)S(1)}, u32[]{:S(2)}, u32[]{:S(2)}) collective-permute-start(f32[392,128]{1,0:T(8,128)S(1)} %get-tuple-element.23), channel_id=1, source_target_pairs={{4,8},{12,16},{20,24},{28,0},{8,4},{16,12},{24,20},{0,28},{5,9},{1... | collective-permute-start | bytes 602120 | tf_op jit(solution)/shard_map/ppermute | solution.py:351
  9.5 2.9 %collective-permute-done.5.refs_0_.chunk = f32[2,5,32,128]{3,2,1,0:T(8,128)S(1)} collective-permute-done((f32[2,5,32,128]{3,2,1,0:T(8,128)S(1)}, f32[2,5,32,128]{3,2,1,0:T(8,128)S(1)}, u32[]{:S(2)}, u32[]{:S(2)}) %collective-permute-start.5) | collective-permute-done | bytes 163872 | tf_op jit(solution)/shard_map/ppermute | solution.py:361
  12.5 2.7 %collective-permute-start.7 = (f32[192,128]{1,0:T(8,128)S(1)}, f32[192,128]{1,0:T(8,128)S(1)}, u32[]{:S(2)}, u32[]{:S(2)}) collective-permute-start(f32[192,128]{1,0:T(8,128)S(1)} %get-tuple-element.29), channel_id=1, source_target_pairs={{4,8},{12,16},{20,24},{28,0},{8,4},{16,12},{24,20},{0,28},{5,9},{1... | collective-permute-start | bytes 294920 | tf_op jit(solution)/shard_map/ppermute | solution.py:351
  15.8 2.5 %collective-permute-start.4 = (f32[192,128]{1,0:T(8,128)S(1)}, f32[192,128]{1,0:T(8,128)S(1)}, u32[]{:S(2)}, u32[]{:S(2)}) collective-permute-start(f32[192,128]{1,0:T(8,128)S(1)} %get-tuple-element.26), channel_id=1, source_target_pairs={{4,8},{12,16},{20,24},{28,0},{8,4},{16,12},{24,20},{0,28},{5,9},{1... | collective-permute-start | bytes 294920 | tf_op jit(solution)/shard_map/ppermute | solution.py:351
  18.4 2.1 %split_transfer.1 = (bf16[2,600,640]{2,1,0:T(8,128)(2,1)S(1)}, bf16[2,600,640]{2,1,0:T(8,128)(2,1)S(1)}) custom-call(f32[2,600,640]{2,1,0:T(8,128)} %bitcast.6), custom_call_target="tpu_custom_call" | custom-call | flops 1536000 | bytes 6144000 | tf_op jit(solution)/shard_map/split_transfer/pallas_call | solution.py:164
  20.5 0.7 %smooth.4.refs_0_ = f32[2,5,32,128]{3,2,1,0:T(8,128)S(1)} custom-call(f32[2,5,32,128]{3,2,1,0:T(8,128)S(1)} %get-tuple-element.21.chunk, f32[392,128]{1,0:T(8,128)S(1)} %collective-permute-done.pair.pair_c, f32[392,128]{1,0:T(8,128)S(1)} %collective-permute-done.1.cross.cross_c, f32[5,128]{1,0:T(8,128)S(1)} %copy-done, ...), custom_call_target="tpu_custom_call" | custom-call | flops 1228800 | bytes 409600 | tf_op jit(solution)/shard_map/smooth/pallas_call | solution.py:250
  21.2 0.7 %smooth.6.refs_2_ = f32[2,5,32,128]{3,2,1,0:T(8,128)S(1)} custom-call(f32[2,5,32,128]{3,2,1,0:T(8,128)S(1)} %collective-permute-done.5.refs_0_.chunk, f32[192,128]{1,0:T(8,128)S(1)} %collective-permute-done.6.pair, f32[192,128]{1,0:T(8,128)S(1)} %collective-permute-done.7.cross, f32[5,128]{1,0:T(8,128)S(1)} %copy-done, ...), custom_call_target="tpu_custom_call" | custom-call | flops 1228800 | bytes 409600 | tf_op jit(solution)/shard_map/smooth/pallas_call | solution.py:250
  21.9 0.7 %smooth.5.refs_1_ = f32[2,5,32,128]{3,2,1,0:T(8,128)S(1)} custom-call(f32[2,5,32,128]{3,2,1,0:T(8,128)S(1)} %collective-permute-done.2.refs_0_.chunk, f32[192,128]{1,0:T(8,128)S(1)} %collective-permute-done.3.pair, f32[192,128]{1,0:T(8,128)S(1)} %collective-permute-done.4.cross, f32[5,128]{1,0:T(8,128)S(1)} %copy-done, ...), custom_call_target="tpu_custom_call" | custom-call | flops 1228800 | bytes 409600 | tf_op jit(solution)/shard_map/smooth/pallas_call | solution.py:250
  22.5 1.9 %combine.2.most = f32[8,2,16,600]{3,2,1,0:T(8,128)S(1)} custom-call(f32[2,5,32,128]{3,2,1,0:T(8,128)S(1)} %smooth.4.refs_0_, f32[2,5,32,128]{3,2,1,0:T(8,128)S(1)} %smooth.5.refs_1_, f32[2,5,32,128]{3,2,1,0:T(8,128)S(1)} %smooth.6.refs_2_, bf16[2,600,640]{2,1,0:T(8,128)(2,1)S(1)} %get-tuple-element.30.refs_3_.refs_1_, ...), custom_call_target="tpu_custom_call" | custom-call | flops 884736000 | bytes 4485120 | tf_op jit(solution)/shard_map/combine/pallas_call | solution.py:312
  24.6 0.7 %smooth.7 = f32[2,5,32,128]{3,2,1,0:T(8,128)S(1)} custom-call(f32[2,5,32,128]{3,2,1,0:T(8,128)S(1)} %get-tuple-element.32.chunk, f32[392,128]{1,0:T(8,128)S(1)} %collective-permute-done.pair.pair_c, f32[392,128]{1,0:T(8,128)S(1)} %collective-permute-done.1.cross.cross_c, f32[5,128]{1,0:T(8,128)S(1)} %copy-done, ...), custom_call_target="tpu_custom_call" | custom-call | flops 1228800 | bytes 409600 | tf_op jit(solution)/shard_map/smooth/pallas_call | solution.py:250
  25.2 3.0 %collective-permute-start.9 = (f32[2,5,32,128]{3,2,1,0:T(8,128)S(1)}, f32[2,5,32,128]{3,2,1,0:T(8,128)S(1)}, u32[]{:S(2)}, u32[]{:S(2)}) collective-permute-start(f32[2,5,32,128]{3,2,1,0:T(8,128)S(1)} %smooth.7), channel_id=1, source_target_pairs={{0,2},{1,3},{2,0},{3,1},{4,6},{5,7},{6,4},{7,5},{8,10},{9,11},{10,... | collective-permute-start | bytes 491528 | tf_op jit(solution)/shard_map/ppermute | solution.py:361
  28.2 8.4 %collective-permute-done.9.refs_0_ = f32[2,5,32,128]{3,2,1,0:T(8,128)S(1)} collective-permute-done((f32[2,5,32,128]{3,2,1,0:T(8,128)S(1)}, f32[2,5,32,128]{3,2,1,0:T(8,128)S(1)}, u32[]{:S(2)}, u32[]{:S(2)}) %collective-permute-start.9) | collective-permute-done | bytes 163872 | tf_op jit(solution)/shard_map/ppermute | solution.py:361
  36.6 1.5 %combine.3.tail = f32[2,2,16,600]{3,2,1,0:T(8,128)S(1)} custom-call(f32[2,5,32,128]{3,2,1,0:T(8,128)S(1)} %collective-permute-done.9.refs_0_, bf16[2,600,640]{2,1,0:T(8,128)(2,1)S(1)} %get-tuple-element.30.refs_3_.refs_1_, bf16[2,600,640]{2,1,0:T(8,128)(2,1)S(1)} %get-tuple-element.31.refs_4_.refs_2_), custom_call_target="tpu_custom_call" | custom-call | flops 294912000 | bytes 3543040 | tf_op jit(solution)/shard_map/combine/pallas_call | solution.py:312
  38.2 1.3 %collective-permute-done.10.tail_moved = f32[1,2,16,600]{3,2,1,0:T(8,128)S(1)} collective-permute-done((f32[1,2,16,600]{3,2,1,0:T(8,128)S(1)}, f32[1,2,16,600]{3,2,1,0:T(8,128)S(1)}, u32[]{:S(2)}, u32[]{:S(2)}) %collective-permute-start.10) | collective-permute-done | bytes 76832 | tf_op jit(solution)/shard_map/ppermute | solution.py:382
  39.5 0.7 %collective-permute-start.11 = (f32[2,16,600]{2,1,0:T(8,128)S(1)}, f32[2,16,600]{2,1,0:T(8,128)S(1)}, u32[]{:S(2)}, u32[]{:S(2)}) collective-permute-start(f32[2,16,600]{2,1,0:T(8,128)S(1)} %get-tuple-element.34), channel_id=1, source_target_pairs={{0,8},{4,12},{8,0},{12,4},{16,24},{20,28},{24,16},{28,20},{1,9},{5... | collective-permute-start | bytes 230408 | tf_op jit(solution)/shard_map/ppermute | solution.py:389
  40.3 1.0 %collective-permute-start.12 = (f32[2,16,600]{2,1,0:T(8,128)S(1)}, f32[2,16,600]{2,1,0:T(8,128)S(1)}, u32[]{:S(2)}, u32[]{:S(2)}) collective-permute-start(f32[2,16,600]{2,1,0:T(8,128)S(1)} %get-tuple-element.35), channel_id=1, source_target_pairs={{0,16},{4,20},{8,24},{12,28},{16,0},{20,4},{24,8},{28,12},{1,17},{... | collective-permute-start | bytes 230408 | tf_op jit(solution)/shard_map/ppermute | solution.py:389
  41.3 1.8 %collective-permute-start.13 = (f32[2,16,600]{2,1,0:T(8,128)S(1)}, f32[2,16,600]{2,1,0:T(8,128)S(1)}, u32[]{:S(2)}, u32[]{:S(2)}) collective-permute-start(f32[2,16,600]{2,1,0:T(8,128)S(1)} %get-tuple-element.36), channel_id=1, source_target_pairs={{0,24},{4,28},{8,16},{12,20},{16,8},{20,12},{24,0},{28,4},{1,25},{... | collective-permute-start | bytes 230408 | tf_op jit(solution)/shard_map/ppermute | solution.py:389
  43.1 1.2 %collective-permute-done.11 = f32[2,16,600]{2,1,0:T(8,128)S(1)} collective-permute-done((f32[2,16,600]{2,1,0:T(8,128)S(1)}, f32[2,16,600]{2,1,0:T(8,128)S(1)}, u32[]{:S(2)}, u32[]{:S(2)}) %collective-permute-start.11) | collective-permute-done | bytes 76832 | tf_op jit(solution)/shard_map/ppermute | solution.py:389
  44.3 1.3 %collective-permute-done.12 = f32[2,16,600]{2,1,0:T(8,128)S(1)} collective-permute-done((f32[2,16,600]{2,1,0:T(8,128)S(1)}, f32[2,16,600]{2,1,0:T(8,128)S(1)}, u32[]{:S(2)}, u32[]{:S(2)}) %collective-permute-start.12) | collective-permute-done | bytes 76832 | tf_op jit(solution)/shard_map/ppermute | solution.py:389
  45.6 1.0 %collective-permute-done.13 = f32[2,16,600]{2,1,0:T(8,128)S(1)} collective-permute-done((f32[2,16,600]{2,1,0:T(8,128)S(1)}, f32[2,16,600]{2,1,0:T(8,128)S(1)}, u32[]{:S(2)}, u32[]{:S(2)}) %collective-permute-start.13) | collective-permute-done | bytes 76832 | tf_op jit(solution)/shard_map/ppermute | solution.py:389
  46.6 0.7 %copy.5 = f32[16,1,2,600]{3,2,1,0:T(2,128)} copy(f32[16,1,2,600]{3,0,2,1:T(8,128)S(1)} %add_bitcast_fusion) | data formatting | bytes 153600 | tf_op jit(solution)/shard_map/broadcast_in_dim | solution.py:435
  (21 shorter events, 0.9 us)
Async XLA Ops:
  2.1 13.8 %collective-permute-start = (f32[392,128]{1,0:T(8,128)S(1)}, f32[392,128]{1,0:T(8,128)S(1)}, u32[]{:S(2)}, u32[]{:S(2)}) collective-permute-start(f32[392,128]{1,0:T(8,128)S(1)} %get-tuple-element.22), channel_id=1, source_target_pairs={{0,4},{4,0},{8,12},{12,8},{16,20},{20,16},{24,28},{28,24},{1,5},{5... | collective-permute-start | bytes 602120 | tf_op jit(solution)/shard_map/ppermute | solution.py:352
  2.6 9.8 %collective-permute-start.5 = (f32[2,5,32,128]{3,2,1,0:T(8,128)S(1)}, f32[2,5,32,128]{3,2,1,0:T(8,128)S(1)}, u32[]{:S(2)}, u32[]{:S(2)}) collective-permute-start(f32[2,5,32,128]{3,2,1,0:T(8,128)S(1)} %get-tuple-element.27), channel_id=1, source_target_pairs={{0,3},{1,2},{2,1},{3,0},{4,7},{5,6},{6,5},{7,4},{8,11},{9,10},{10,... | collective-permute-start | bytes 491528 | tf_op jit(solution)/shard_map/ppermute | solution.py:361
  7.3 8.4 %collective-permute-start.2 = (f32[2,5,32,128]{3,2,1,0:T(8,128)S(1)}, f32[2,5,32,128]{3,2,1,0:T(8,128)S(1)}, u32[]{:S(2)}, u32[]{:S(2)}) collective-permute-start(f32[2,5,32,128]{3,2,1,0:T(8,128)S(1)} %get-tuple-element.24), channel_id=1, source_target_pairs={{0,1},{1,0},{2,3},{3,2},{4,5},{5,4},{6,7},{7,6},{8,9},{9,8},{10,11... | collective-permute-start | bytes 491528 | tf_op jit(solution)/shard_map/ppermute | solution.py:361
  7.3 13.2 %collective-permute-start.1 = (f32[392,128]{1,0:T(8,128)S(1)}, f32[392,128]{1,0:T(8,128)S(1)}, u32[]{:S(2)}, u32[]{:S(2)}) collective-permute-start(f32[392,128]{1,0:T(8,128)S(1)} %get-tuple-element.23), channel_id=1, source_target_pairs={{4,8},{12,16},{20,24},{28,0},{8,4},{16,12},{24,20},{0,28},{5,9},{1... | collective-permute-start | bytes 602120 | tf_op jit(solution)/shard_map/ppermute | solution.py:351
  12.4 8.7 %collective-permute-start.6 = (f32[192,128]{1,0:T(8,128)S(1)}, f32[192,128]{1,0:T(8,128)S(1)}, u32[]{:S(2)}, u32[]{:S(2)}) collective-permute-start(f32[192,128]{1,0:T(8,128)S(1)} %get-tuple-element.28), channel_id=1, source_target_pairs={{0,4},{4,0},{8,12},{12,8},{16,20},{20,16},{24,28},{28,24},{1,5},{5... | collective-permute-start | bytes 294920 | tf_op jit(solution)/shard_map/ppermute | solution.py:352
  12.5 8.7 %collective-permute-start.7 = (f32[192,128]{1,0:T(8,128)S(1)}, f32[192,128]{1,0:T(8,128)S(1)}, u32[]{:S(2)}, u32[]{:S(2)}) collective-permute-start(f32[192,128]{1,0:T(8,128)S(1)} %get-tuple-element.29), channel_id=1, source_target_pairs={{4,8},{12,16},{20,24},{28,0},{8,4},{16,12},{24,20},{0,28},{5,9},{1... | collective-permute-start | bytes 294920 | tf_op jit(solution)/shard_map/ppermute | solution.py:351
  15.7 6.1 %collective-permute-start.3 = (f32[192,128]{1,0:T(8,128)S(1)}, f32[192,128]{1,0:T(8,128)S(1)}, u32[]{:S(2)}, u32[]{:S(2)}) collective-permute-start(f32[192,128]{1,0:T(8,128)S(1)} %get-tuple-element.25), channel_id=1, source_target_pairs={{0,4},{4,0},{8,12},{12,8},{16,20},{20,16},{24,28},{28,24},{1,5},{5... | collective-permute-start | bytes 294920 | tf_op jit(solution)/shard_map/ppermute | solution.py:352
  15.8 6.0 %collective-permute-start.4 = (f32[192,128]{1,0:T(8,128)S(1)}, f32[192,128]{1,0:T(8,128)S(1)}, u32[]{:S(2)}, u32[]{:S(2)}) collective-permute-start(f32[192,128]{1,0:T(8,128)S(1)} %get-tuple-element.26), channel_id=1, source_target_pairs={{4,8},{12,16},{20,24},{28,0},{8,4},{16,12},{24,20},{0,28},{5,9},{1... | collective-permute-start | bytes 294920 | tf_op jit(solution)/shard_map/ppermute | solution.py:351
  18.4 2.1 %copy-start = (f32[5,128]{1,0:T(8,128)S(1)}, f32[5,128]{1,0:T(8,128)}, u32[]{:S(2)}) copy-start(f32[5,128]{1,0:T(8,128)} %own_c.7) | copy-start | bytes 7684
  24.5 15.0 %collective-permute-start.8 = (f32[4,2,16,600]{3,2,1,0:T(8,128)S(1)}, f32[4,2,16,600]{3,2,1,0:T(8,128)S(1)}, u32[]{:S(2)}, u32[]{:S(2)}) collective-permute-start(f32[4,2,16,600]{3,2,1,0:T(8,128)S(1)} %slice.8), channel_id=1, source_target_pairs={{0,4},{4,0},{8,12},{12,8},{16,20},{20,16},{24,28},{28,24},{1,5},{5... | collective-permute-start | bytes 921608 | tf_op jit(solution)/shard_map/ppermute | solution.py:382
  25.2 11.3 %collective-permute-start.9 = (f32[2,5,32,128]{3,2,1,0:T(8,128)S(1)}, f32[2,5,32,128]{3,2,1,0:T(8,128)S(1)}, u32[]{:S(2)}, u32[]{:S(2)}) collective-permute-start(f32[2,5,32,128]{3,2,1,0:T(8,128)S(1)} %smooth.7), channel_id=1, source_target_pairs={{0,2},{1,3},{2,0},{3,1},{4,6},{5,7},{6,4},{7,5},{8,10},{9,11},{10,... | collective-permute-start | bytes 491528 | tf_op jit(solution)/shard_map/ppermute | solution.py:361
  38.1 1.3 %collective-permute-start.10 = (f32[1,2,16,600]{3,2,1,0:T(8,128)S(1)}, f32[1,2,16,600]{3,2,1,0:T(8,128)S(1)}, u32[]{:S(2)}, u32[]{:S(2)}) collective-permute-start(f32[1,2,16,600]{3,2,1,0:T(8,128)S(1)} %slice.9), channel_id=1, source_target_pairs={{0,4},{4,0},{8,12},{12,8},{16,20},{20,16},{24,28},{28,24},{1,5},{5... | collective-permute-start | bytes 230408 | tf_op jit(solution)/shard_map/ppermute | solution.py:382
  39.5 4.7 %collective-permute-start.11 = (f32[2,16,600]{2,1,0:T(8,128)S(1)}, f32[2,16,600]{2,1,0:T(8,128)S(1)}, u32[]{:S(2)}, u32[]{:S(2)}) collective-permute-start(f32[2,16,600]{2,1,0:T(8,128)S(1)} %get-tuple-element.34), channel_id=1, source_target_pairs={{0,8},{4,12},{8,0},{12,4},{16,24},{20,28},{24,16},{28,20},{1,9},{5... | collective-permute-start | bytes 230408 | tf_op jit(solution)/shard_map/ppermute | solution.py:389
  40.3 5.3 %collective-permute-start.12 = (f32[2,16,600]{2,1,0:T(8,128)S(1)}, f32[2,16,600]{2,1,0:T(8,128)S(1)}, u32[]{:S(2)}, u32[]{:S(2)}) collective-permute-start(f32[2,16,600]{2,1,0:T(8,128)S(1)} %get-tuple-element.35), channel_id=1, source_target_pairs={{0,16},{4,20},{8,24},{12,28},{16,0},{20,4},{24,8},{28,12},{1,17},{... | collective-permute-start | bytes 230408 | tf_op jit(solution)/shard_map/ppermute | solution.py:389
  41.3 5.3 %collective-permute-start.13 = (f32[2,16,600]{2,1,0:T(8,128)S(1)}, f32[2,16,600]{2,1,0:T(8,128)S(1)}, u32[]{:S(2)}, u32[]{:S(2)}) collective-permute-start(f32[2,16,600]{2,1,0:T(8,128)S(1)} %get-tuple-element.36), channel_id=1, source_target_pairs={{0,24},{4,28},{8,16},{12,20},{16,8},{20,12},{24,0},{28,4},{1,25},{... | collective-permute-start | bytes 230408 | tf_op jit(solution)/shard_map/ppermute | solution.py:389

commit v7 on v6

--- a/solution.py
+++ b/solution.py
@@ -153,19 +153,17 @@
 
 
 def split_kernel(x_ref, high_ref, low_ref):
-    high, low = split_bf16(x_ref[...])
-    high_ref[...] = high
-    low_ref[...] = low
+    high_ref[0], low_ref[0] = split_bf16(jnp.transpose(x_ref[0]))
 
 
 def split_transfer(transfer):
     parts, sensors, cells = transfer.shape
-    block = pl.BlockSpec((1, sensors, cells), lambda a: (a, 0, 0))
+    block = pl.BlockSpec((1, cells, sensors), lambda a: (a, 0, 0))
     return pl.pallas_call(
         split_kernel,
-        out_shape=[jax.ShapeDtypeStruct(transfer.shape, jnp.bfloat16)] * 2,
+        out_shape=[jax.ShapeDtypeStruct((parts, cells, sensors), jnp.bfloat16)] * 2,
         grid=(parts,),
-        in_specs=[block],
+        in_specs=[pl.BlockSpec((1, sensors, cells), lambda a: (a, 0, 0))],
         out_specs=[block, block],
         compiler_params=params(),
         cost_estimate=cost(2 * transfer.size, 8 * transfer.size),
@@ -277,7 +275,7 @@
     def times(a):
         def dot(x, w):
             return lax.dot_general(
-                x, w, (((1,), (1,)), ((), ())), preferred_element_type=jnp.float32
+                x, w, (((1,), (0,)), ((), ())), preferred_element_type=jnp.float32
             )
 
         return (dot(lhs_low, t_high[a]) + dot(lhs_high, t_low[a])) + dot(lhs_high, t_high[a])
@@ -304,7 +302,7 @@
 
 def combine(chunks, split, owners_in, places, paired, absent=()):
     t_high, t_low = split
-    sensors, cells = t_high.shape[1:]
+    cells, sensors = t_high.shape[1:]
     indices = sorted(chunks)
     _, _, vectors, _ = chunks[indices[0]].shape
     owned = vectors // owners_in
@@ -355,7 +353,7 @@
 
 def paired_shards(field, coefficient, split_of, table, freq_count, strips):
     vectors = field.shape[0]
-    chunks, pair, cross = transform(field, table, coefficient, freq_count, (2, 0))
+    chunks, pair, cross = transform(field, table, coefficient, freq_count, (2,))
 
     def swap(m, chunk):
         return lax.ppermute(chunk, "freq", xor_pairs(freq_count, m))
@@ -368,12 +366,12 @@
     edge = neighbours(pair, cross, strips)
     split = split_of()
     coefficients = (coefficient, *edge)
-    rim_base = edge_base(2, 0, 0, vectors)
-    first_edge = neighbours(*edges([first]), strips)
+    rim_base = edge_base(1, 0, 0, vectors)
+    mid_edge = neighbours(*edges([chunks[0], first]), strips)
     second = swap(2, relax(chunks[2], edge, 0))
-    own = relax(chunks[0], edge, 1)
+    own = relax(chunks[0], mid_edge, 0)
     third_edge = neighbours(*edges([third]), strips)
-    first = relax(first, first_edge, 0)
+    first = relax(first, mid_edge, 1)
     third = relax(third, third_edge, 0)
     most = combine({0: own, 1: first, 3: third}, split, 2, strips, True, (2,))
 

time: 47.5 us -> 47.3 us (level)
  the two profiles are of different devices: /device:TPU:0 before, /device:TPU:24 now
where the time goes in v7:
time: 47.3 us; the launch traced here: 47.2 us
  waiting for transfers between devices  25.5 us (54%)
  starting transfers between devices  11.2 us (24%)
  Pallas kernels  9.63 us (20%)
  local copies, waits for them, and re-layouts  0.72 us (2%)
    ppermute x3, waiting for transfers between devices, swap(): return lax.ppermute(chunk, 'freq', xor_pairs(freq_count, m))  16 us
    ppermute x3, starting transfers between devices, neighbours(): cross = lax.ppermute(cross, 'seabed', inner)  5.26 us
    ppermute x3, waiting for transfers between devices, paired_shards(): total = total + lax.ppermute(chips[d], 'seabed', xor_pairs(strips, 2 * d))  4.26 us
    ppermute x3, waiting for transfers between devices, neighbours(): cross = lax.ppermute(cross, 'seabed', inner)  3.97 us
    ppermute x3, starting transfers between devices, paired_shards(): total = total + lax.ppermute(chips[d], 'seabed', xor_pairs(strips, 2 * d))  3.55 us
    pallas_call x4, Pallas kernels, smooth(): pl.pallas_call(functools.partial(smooth_kernel, base, rim_base), out_shap...  2.62 us
    pallas_call x1, Pallas kernels, split_transfer(): pl.pallas_call(split_kernel, out_shape=[jax.ShapeDtypeStruct((parts, cell...  2.44 us
    pallas_call x2, Pallas kernels, combine(): pl.pallas_call(functools.partial(combine_kernel, indices, owners_in, pair...  2.4 us
  transfers between devices with their start and end apart: 14, of which 7 were waited for; matrix products, arithmetic and copies ran while one was open for 0% of the time, Pallas kernels for 10%

profile of v7, /device:TPU:24, one launch (start us, length us, event | category | flops | bytes accessed | tf_op | source)
XLA Modules:
  0.0 47.2 jit_solution(6955930238623427150)
XLA Ops:
  0.0 2.1 %transform.1 = (f32[2,5,32,128]{3,2,1,0:T(8,128)S(1)}, f32[2,5,32,128]{3,2,1,0:T(8,128)S(1)}, f32[2,5,32,128]{3,2,1,0:T(8,128)S(1)}, f32[2,5,32,128]{3,2,1,0:T(8...) custom-call(bf16[32,5,32,128]{3,2,1,0:T(8,128)(2,1)} %bitcast.7, f32[4,16,256]{2,1,0:T(8,128)} %constant.2.clone.table_hbm, ...), custom_call_target="tpu_custom_call" | custom-call | flops 167772160 | bytes 1966080 | tf_op jit(solution)/shard_map/transform/pallas_call | solution.py:132
  2.1 0.5 %collective-permute-start = (f32[2,5,32,128]{3,2,1,0:T(8,128)S(1)}, f32[2,5,32,128]{3,2,1,0:T(8,128)S(1)}, u32[]{:S(2)}, u32[]{:S(2)}) collective-permute-start(f32[2,5,32,128]{3,2,1,0:T(8,128)S(1)} %get-tuple-element.22), channel_id=1, source_target_pairs={{0,1},{1,0},{2,3},{3,2},{4,5},{5,4},{6,7},{7,6},{8,9},{9,8},{10,11... | collective-permute-start | bytes 491528 | tf_op jit(solution)/shard_map/ppermute | solution.py:359
  2.6 1.4 %collective-permute-start.5 = (f32[2,5,32,128]{3,2,1,0:T(8,128)S(1)}, f32[2,5,32,128]{3,2,1,0:T(8,128)S(1)}, u32[]{:S(2)}, u32[]{:S(2)}) collective-permute-start(f32[2,5,32,128]{3,2,1,0:T(8,128)S(1)} %get-tuple-element.27), channel_id=1, source_target_pairs={{0,3},{1,2},{2,1},{3,0},{4,7},{5,6},{6,5},{7,4},{8,11},{9,10},{10,... | collective-permute-start | bytes 491528 | tf_op jit(solution)/shard_map/ppermute | solution.py:359
  3.9 7.7 %collective-permute-done.refs_1_.chunk = f32[2,5,32,128]{3,2,1,0:T(8,128)S(1)} collective-permute-done((f32[2,5,32,128]{3,2,1,0:T(8,128)S(1)}, f32[2,5,32,128]{3,2,1,0:T(8,128)S(1)}, u32[]{:S(2)}, u32[]{:S(2)}) %collective-permute-start) | collective-permute-done | bytes 163872 | tf_op jit(solution)/shard_map/ppermute | solution.py:359
  11.7 2.5 %collective-permute-start.2 = (f32[384,128]{1,0:T(8,128)S(1)}, f32[384,128]{1,0:T(8,128)S(1)}, u32[]{:S(2)}, u32[]{:S(2)}) collective-permute-start(f32[384,128]{1,0:T(8,128)S(1)} %get-tuple-element.24), channel_id=1, source_target_pairs={{4,8},{12,16},{20,24},{28,0},{8,4},{16,12},{24,20},{0,28},{5,9},{1... | collective-permute-start | bytes 589832 | tf_op jit(solution)/shard_map/ppermute | solution.py:349
  14.6 2.5 %collective-permute-start.7 = (f32[192,128]{1,0:T(8,128)S(1)}, f32[192,128]{1,0:T(8,128)S(1)}, u32[]{:S(2)}, u32[]{:S(2)}) collective-permute-start(f32[192,128]{1,0:T(8,128)S(1)} %get-tuple-element.29), channel_id=1, source_target_pairs={{4,8},{12,16},{20,24},{28,0},{8,4},{16,12},{24,20},{0,28},{5,9},{1... | collective-permute-start | bytes 294920 | tf_op jit(solution)/shard_map/ppermute | solution.py:349
  17.1 2.4 %split_transfer.1 = (bf16[2,640,600]{2,1,0:T(8,128)(2,1)S(1)}, bf16[2,640,600]{2,1,0:T(8,128)(2,1)S(1)}) custom-call(f32[2,600,640]{2,1,0:T(8,128)} %bitcast.6), custom_call_target="tpu_custom_call" | custom-call | flops 1536000 | bytes 6144000 | tf_op jit(solution)/shard_map/split_transfer/pallas_call | solution.py:162
  19.6 1.9 %collective-permute-done.4.cross_c.cross = f32[200,128]{1,0:T(8,128)S(1)} collective-permute-done((f32[200,128]{1,0:T(8,128)S(1)}, f32[200,128]{1,0:T(8,128)S(1)}, u32[]{:S(2)}, u32[]{:S(2)}) %collective-permute-start.4) | collective-permute-done | bytes 102432 | tf_op jit(solution)/shard_map/ppermute | solution.py:349
  21.4 2.1 %collective-permute-done.7.cross = f32[192,128]{1,0:T(8,128)S(1)} collective-permute-done((f32[192,128]{1,0:T(8,128)S(1)}, f32[192,128]{1,0:T(8,128)S(1)}, u32[]{:S(2)}, u32[]{:S(2)}) %collective-permute-start.7) | collective-permute-done | bytes 98336 | tf_op jit(solution)/shard_map/ppermute | solution.py:349
  23.5 0.7 %smooth.6.refs_2_ = f32[2,5,32,128]{3,2,1,0:T(8,128)S(1)} custom-call(f32[2,5,32,128]{3,2,1,0:T(8,128)S(1)} %collective-permute-done.5.refs_0_.chunk, f32[192,128]{1,0:T(8,128)S(1)} %collective-permute-done.6.pair, f32[192,128]{1,0:T(8,128)S(1)} %collective-permute-done.7.cross, f32[5,128]{1,0:T(8,128)S(1)} %copy-done, ...), custom_call_target="tpu_custom_call" | custom-call | flops 1228800 | bytes 409600 | tf_op jit(solution)/shard_map/smooth/pallas_call | solution.py:248
  24.2 0.7 %smooth.5.refs_1_ = f32[2,5,32,128]{3,2,1,0:T(8,128)S(1)} custom-call(f32[2,5,32,128]{3,2,1,0:T(8,128)S(1)} %collective-permute-done.refs_1_.chunk, f32[384,128]{1,0:T(8,128)S(1)} %collective-permute-done.1.pair, f32[384,128]{1,0:T(8,128)S(1)} %collective-permute-done.2.cross, f32[5,128]{1,0:T(8,128)S(1)} %copy-done, ...), custom_call_target="tpu_custom_call" | custom-call | flops 1228800 | bytes 409600 | tf_op jit(solution)/shard_map/smooth/pallas_call | solution.py:248
  24.9 0.7 %smooth.4.refs_0_ = f32[2,5,32,128]{3,2,1,0:T(8,128)S(1)} custom-call(f32[2,5,32,128]{3,2,1,0:T(8,128)S(1)} %get-tuple-element.21.refs_0_.chunk, f32[384,128]{1,0:T(8,128)S(1)} %collective-permute-done.1.pair, f32[384,128]{1,0:T(8,128)S(1)} %collective-permute-done.2.cross, f32[5,128]{1,0:T(8,128)S(1)} %copy-done, ...), custom_call_target="tpu_custom_call" | custom-call | flops 1228800 | bytes 409600 | tf_op jit(solution)/shard_map/smooth/pallas_call | solution.py:248
  25.5 1.5 %combine.2.most = f32[8,2,16,600]{3,2,1,0:T(8,128)S(1)} custom-call(f32[2,5,32,128]{3,2,1,0:T(8,128)S(1)} %smooth.4.refs_0_, f32[2,5,32,128]{3,2,1,0:T(8,128)S(1)} %smooth.5.refs_1_, f32[2,5,32,128]{3,2,1,0:T(8,128)S(1)} %smooth.6.refs_2_, bf16[2,640,600]{2,1,0:T(8,128)(2,1)S(1)} %get-tuple-element.30.refs_3_.refs_1_, ...), custom_call_target="tpu_custom_call" | custom-call | flops 884736000 | bytes 4485120 | tf_op jit(solution)/shard_map/combine/pallas_call | solution.py:310
  27.1 0.2 collective-permute-start.8
  27.3 0.7 %smooth.7 = f32[2,5,32,128]{3,2,1,0:T(8,128)S(1)} custom-call(f32[2,5,32,128]{3,2,1,0:T(8,128)S(1)} %get-tuple-element.32.chunk, f32[200,128]{1,0:T(8,128)S(1)} %collective-permute-done.3.pair_c.pair, f32[200,128]{1,0:T(8,128)S(1)} %collective-permute-done.4.cross_c.cross, f32[5,128]{1,0:T(8,128)S(1)} %copy-done, ...), custom_call_target="tpu_custom_call" | custom-call | flops 1228800 | bytes 409600 | tf_op jit(solution)/shard_map/smooth/pallas_call | solution.py:248
  28.0 8.4 %collective-permute-done.9.refs_0_ = f32[2,5,32,128]{3,2,1,0:T(8,128)S(1)} collective-permute-done((f32[2,5,32,128]{3,2,1,0:T(8,128)S(1)}, f32[2,5,32,128]{3,2,1,0:T(8,128)S(1)}, u32[]{:S(2)}, u32[]{:S(2)}) %collective-permute-start.9) | collective-permute-done | bytes 163872 | tf_op jit(solution)/shard_map/ppermute | solution.py:359
  36.4 0.9 %combine.3.tail = f32[2,2,16,600]{3,2,1,0:T(8,128)S(1)} custom-call(f32[2,5,32,128]{3,2,1,0:T(8,128)S(1)} %collective-permute-done.9.refs_0_, bf16[2,640,600]{2,1,0:T(8,128)(2,1)S(1)} %get-tuple-element.30.refs_3_.refs_1_, bf16[2,640,600]{2,1,0:T(8,128)(2,1)S(1)} %get-tuple-element.31.refs_4_.refs_2_), custom_call_target="tpu_custom_call" | custom-call | flops 294912000 | bytes 3543040 | tf_op jit(solution)/shard_map/combine/pallas_call | solution.py:310
  37.4 1.2 %collective-permute-done.10.tail_moved = f32[1,2,16,600]{3,2,1,0:T(8,128)S(1)} collective-permute-done((f32[1,2,16,600]{3,2,1,0:T(8,128)S(1)}, f32[1,2,16,600]{3,2,1,0:T(8,128)S(1)}, u32[]{:S(2)}, u32[]{:S(2)}) %collective-permute-start.10) | collective-permute-done | bytes 76832 | tf_op jit(solution)/shard_map/ppermute | solution.py:380
  38.7 1.6 %collective-permute-start.11 = (f32[2,16,600]{2,1,0:T(8,128)S(1)}, f32[2,16,600]{2,1,0:T(8,128)S(1)}, u32[]{:S(2)}, u32[]{:S(2)}) collective-permute-start(f32[2,16,600]{2,1,0:T(8,128)S(1)} %get-tuple-element.34), channel_id=1, source_target_pairs={{0,8},{4,12},{8,0},{12,4},{16,24},{20,28},{24,16},{28,20},{1,9},{5... | collective-permute-start | bytes 230408 | tf_op jit(solution)/shard_map/ppermute | solution.py:387
  40.3 0.7 %collective-permute-start.12 = (f32[2,16,600]{2,1,0:T(8,128)S(1)}, f32[2,16,600]{2,1,0:T(8,128)S(1)}, u32[]{:S(2)}, u32[]{:S(2)}) collective-permute-start(f32[2,16,600]{2,1,0:T(8,128)S(1)} %get-tuple-element.35), channel_id=1, source_target_pairs={{0,16},{4,20},{8,24},{12,28},{16,0},{20,4},{24,8},{28,12},{1,17},{... | collective-permute-start | bytes 230408 | tf_op jit(solution)/shard_map/ppermute | solution.py:387
  41.0 1.3 %collective-permute-start.13 = (f32[2,16,600]{2,1,0:T(8,128)S(1)}, f32[2,16,600]{2,1,0:T(8,128)S(1)}, u32[]{:S(2)}, u32[]{:S(2)}) collective-permute-start(f32[2,16,600]{2,1,0:T(8,128)S(1)} %get-tuple-element.36), channel_id=1, source_target_pairs={{0,24},{4,28},{8,16},{12,20},{16,8},{20,12},{24,0},{28,4},{1,25},{... | collective-permute-start | bytes 230408 | tf_op jit(solution)/shard_map/ppermute | solution.py:387
  42.2 1.0 %collective-permute-done.11 = f32[2,16,600]{2,1,0:T(8,128)S(1)} collective-permute-done((f32[2,16,600]{2,1,0:T(8,128)S(1)}, f32[2,16,600]{2,1,0:T(8,128)S(1)}, u32[]{:S(2)}, u32[]{:S(2)}) %collective-permute-start.11) | collective-permute-done | bytes 76832 | tf_op jit(solution)/shard_map/ppermute | solution.py:387
  43.2 3.2 %collective-permute-done.12 = f32[2,16,600]{2,1,0:T(8,128)S(1)} collective-permute-done((f32[2,16,600]{2,1,0:T(8,128)S(1)}, f32[2,16,600]{2,1,0:T(8,128)S(1)}, u32[]{:S(2)}, u32[]{:S(2)}) %collective-permute-start.12) | collective-permute-done | bytes 76832 | tf_op jit(solution)/shard_map/ppermute | solution.py:387
  46.5 0.7 %copy.5 = f32[16,1,2,600]{3,2,1,0:T(2,128)} copy(f32[16,1,2,600]{3,0,2,1:T(8,128)S(1)} %add_bitcast_fusion) | data formatting | bytes 153600 | tf_op jit(solution)/shard_map/broadcast_in_dim | solution.py:433
  (21 shorter events, 0.7 us)
Async XLA Ops:
  2.1 9.5 %collective-permute-start = (f32[2,5,32,128]{3,2,1,0:T(8,128)S(1)}, f32[2,5,32,128]{3,2,1,0:T(8,128)S(1)}, u32[]{:S(2)}, u32[]{:S(2)}) collective-permute-start(f32[2,5,32,128]{3,2,1,0:T(8,128)S(1)} %get-tuple-element.22), channel_id=1, source_target_pairs={{0,1},{1,0},{2,3},{3,2},{4,5},{5,4},{6,7},{7,6},{8,9},{9,8},{10,11... | collective-permute-start | bytes 491528 | tf_op jit(solution)/shard_map/ppermute | solution.py:359
  2.6 11.9 %collective-permute-start.5 = (f32[2,5,32,128]{3,2,1,0:T(8,128)S(1)}, f32[2,5,32,128]{3,2,1,0:T(8,128)S(1)}, u32[]{:S(2)}, u32[]{:S(2)}) collective-permute-start(f32[2,5,32,128]{3,2,1,0:T(8,128)S(1)} %get-tuple-element.27), channel_id=1, source_target_pairs={{0,3},{1,2},{2,1},{3,0},{4,7},{5,6},{6,5},{7,4},{8,11},{9,10},{10,... | collective-permute-start | bytes 491528 | tf_op jit(solution)/shard_map/ppermute | solution.py:359
  3.9 10.6 %collective-permute-start.3 = (f32[200,128]{1,0:T(8,128)S(1)}, f32[200,128]{1,0:T(8,128)S(1)}, u32[]{:S(2)}, u32[]{:S(2)}) collective-permute-start(f32[200,128]{1,0:T(8,128)S(1)} %get-tuple-element.25), channel_id=1, source_target_pairs={{0,4},{4,0},{8,12},{12,8},{16,20},{20,16},{24,28},{28,24},{1,5},{5... | collective-permute-start | bytes 307208 | tf_op jit(solution)/shard_map/ppermute | solution.py:350
  11.6 11.9 %copy-start = (f32[5,128]{1,0:T(8,128)S(1)}, f32[5,128]{1,0:T(8,128)}, u32[]{:S(2)}) copy-start(f32[5,128]{1,0:T(8,128)} %own_c.7) | copy-start | bytes 7684
  11.7 12.5 %collective-permute-start.1 = (f32[384,128]{1,0:T(8,128)S(1)}, f32[384,128]{1,0:T(8,128)S(1)}, u32[]{:S(2)}, u32[]{:S(2)}) collective-permute-start(f32[384,128]{1,0:T(8,128)S(1)} %get-tuple-element.23), channel_id=1, source_target_pairs={{0,4},{4,0},{8,12},{12,8},{16,20},{20,16},{24,28},{28,24},{1,5},{5... | collective-permute-start | bytes 589832 | tf_op jit(solution)/shard_map/ppermute | solution.py:350
  11.7 12.5 %collective-permute-start.2 = (f32[384,128]{1,0:T(8,128)S(1)}, f32[384,128]{1,0:T(8,128)S(1)}, u32[]{:S(2)}, u32[]{:S(2)}) collective-permute-start(f32[384,128]{1,0:T(8,128)S(1)} %get-tuple-element.24), channel_id=1, source_target_pairs={{4,8},{12,16},{20,24},{28,0},{8,4},{16,12},{24,20},{0,28},{5,9},{1... | collective-permute-start | bytes 589832 | tf_op jit(solution)/shard_map/ppermute | solution.py:349
  14.3 7.1 %collective-permute-start.4 = (f32[200,128]{1,0:T(8,128)S(1)}, f32[200,128]{1,0:T(8,128)S(1)}, u32[]{:S(2)}, u32[]{:S(2)}) collective-permute-start(f32[200,128]{1,0:T(8,128)S(1)} %get-tuple-element.26), channel_id=1, source_target_pairs={{4,8},{12,16},{20,24},{28,0},{8,4},{16,12},{24,20},{0,28},{5,9},{1... | collective-permute-start | bytes 307208 | tf_op jit(solution)/shard_map/ppermute | solution.py:349
  14.5 7.0 %collective-permute-start.6 = (f32[192,128]{1,0:T(8,128)S(1)}, f32[192,128]{1,0:T(8,128)S(1)}, u32[]{:S(2)}, u32[]{:S(2)}) collective-permute-start(f32[192,128]{1,0:T(8,128)S(1)} %get-tuple-element.28), channel_id=1, source_target_pairs={{0,4},{4,0},{8,12},{12,8},{16,20},{20,16},{24,28},{28,24},{1,5},{5... | collective-permute-start | bytes 294920 | tf_op jit(solution)/shard_map/ppermute | solution.py:350
  14.6 9.0 %collective-permute-start.7 = (f32[192,128]{1,0:T(8,128)S(1)}, f32[192,128]{1,0:T(8,128)S(1)}, u32[]{:S(2)}, u32[]{:S(2)}) collective-permute-start(f32[192,128]{1,0:T(8,128)S(1)} %get-tuple-element.29), channel_id=1, source_target_pairs={{4,8},{12,16},{20,24},{28,0},{8,4},{16,12},{24,20},{0,28},{5,9},{1... | collective-permute-start | bytes 294920 | tf_op jit(solution)/shard_map/ppermute | solution.py:349
  27.1 11.5 %collective-permute-start.8 = (f32[4,2,16,600]{3,2,1,0:T(8,128)S(1)}, f32[4,2,16,600]{3,2,1,0:T(8,128)S(1)}, u32[]{:S(2)}, u32[]{:S(2)}) collective-permute-start(f32[4,2,16,600]{3,2,1,0:T(8,128)S(1)} %slice.8), channel_id=1, source_target_pairs={{0,4},{4,0},{8,12},{12,8},{16,20},{20,16},{24,28},{28,24},{1,5},{5... | collective-permute-start | bytes 921608 | tf_op jit(solution)/shard_map/ppermute | solution.py:380
  27.9 8.5 %collective-permute-start.9 = (f32[2,5,32,128]{3,2,1,0:T(8,128)S(1)}, f32[2,5,32,128]{3,2,1,0:T(8,128)S(1)}, u32[]{:S(2)}, u32[]{:S(2)}) collective-permute-start(f32[2,5,32,128]{3,2,1,0:T(8,128)S(1)} %smooth.7), channel_id=1, source_target_pairs={{0,2},{1,3},{2,0},{3,1},{4,6},{5,7},{6,4},{7,5},{8,10},{9,11},{10,... | collective-permute-start | bytes 491528 | tf_op jit(solution)/shard_map/ppermute | solution.py:359
  37.3 1.3 %collective-permute-start.10 = (f32[1,2,16,600]{3,2,1,0:T(8,128)S(1)}, f32[1,2,16,600]{3,2,1,0:T(8,128)S(1)}, u32[]{:S(2)}, u32[]{:S(2)}) collective-permute-start(f32[1,2,16,600]{3,2,1,0:T(8,128)S(1)} %slice.9), channel_id=1, source_target_pairs={{0,4},{4,0},{8,12},{12,8},{16,20},{20,16},{24,28},{28,24},{1,5},{5... | collective-permute-start | bytes 230408 | tf_op jit(solution)/shard_map/ppermute | solution.py:380
  38.7 4.6 %collective-permute-start.11 = (f32[2,16,600]{2,1,0:T(8,128)S(1)}, f32[2,16,600]{2,1,0:T(8,128)S(1)}, u32[]{:S(2)}, u32[]{:S(2)}) collective-permute-start(f32[2,16,600]{2,1,0:T(8,128)S(1)} %get-tuple-element.34), channel_id=1, source_target_pairs={{0,8},{4,12},{8,0},{12,4},{16,24},{20,28},{24,16},{28,20},{1,9},{5... | collective-permute-start | bytes 230408 | tf_op jit(solution)/shard_map/ppermute | solution.py:387
  40.3 6.2 %collective-permute-start.12 = (f32[2,16,600]{2,1,0:T(8,128)S(1)}, f32[2,16,600]{2,1,0:T(8,128)S(1)}, u32[]{:S(2)}, u32[]{:S(2)}) collective-permute-start(f32[2,16,600]{2,1,0:T(8,128)S(1)} %get-tuple-element.35), channel_id=1, source_target_pairs={{0,16},{4,20},{8,24},{12,28},{16,0},{20,4},{24,8},{28,12},{1,17},{... | collective-permute-start | bytes 230408 | tf_op jit(solution)/shard_map/ppermute | solution.py:387
  41.0 5.5 %collective-permute-start.13 = (f32[2,16,600]{2,1,0:T(8,128)S(1)}, f32[2,16,600]{2,1,0:T(8,128)S(1)}, u32[]{:S(2)}, u32[]{:S(2)}) collective-permute-start(f32[2,16,600]{2,1,0:T(8,128)S(1)} %get-tuple-element.36), channel_id=1, source_target_pairs={{0,24},{4,28},{8,16},{12,20},{16,8},{20,12},{24,0},{28,4},{1,25},{... | collective-permute-start | bytes 230408 | tf_op jit(solution)/shard_map/ppermute | solution.py:387

commit v8 on v7

--- a/solution.py
+++ b/solution.py
@@ -288,7 +288,7 @@
         if not paired:
             return index * owners_in + o
         core, chip = place_of(index, o, owners_in)
-        return core * (out.shape[0] // 2) + (chip if out.shape[0] > 2 else 0)
+        return core * (out.shape[0] // 2) + (chip if absent else indices.index(index))
 
     for at, index in enumerate(indices):
         for o in range(owners_in):
@@ -321,11 +321,13 @@
 
 
 def merge_kernel(late, owners_in, most, most_moved, tail, tail_moved, *outs):
-    _, chip = place_of(late, 0, owners_in)
-    final = tail[0] + tail_moved[0]
+    chips = [place_of(index, 0, owners_in)[1] for index in late]
+    final = [tail[i] + tail_moved[i] for i in range(len(late))]
     for d, out in enumerate(outs):
-        here = pick(chip == d, final, jnp.zeros_like(final))
-        out[...] = (most[d] + most_moved[d]) + here
+        value = most[d] + most_moved[d]
+        for chip, add in zip(chips, final):
+            value = value + pick(chip == d, add, jnp.zeros_like(add))
+        out[...] = value
 
 
 def merge(late, owners_in, most, most_moved, tail, tail_moved):
@@ -367,21 +369,21 @@
     split = split_of()
     coefficients = (coefficient, *edge)
     rim_base = edge_base(1, 0, 0, vectors)
+    second = swap(2, relax(chunks[2], edge, 0))
     mid_edge = neighbours(*edges([chunks[0], first]), strips)
-    second = swap(2, relax(chunks[2], edge, 0))
     own = relax(chunks[0], mid_edge, 0)
     third_edge = neighbours(*edges([third]), strips)
     first = relax(first, mid_edge, 1)
     third = relax(third, third_edge, 0)
-    most = combine({0: own, 1: first, 3: third}, split, 2, strips, True, (2,))
+    most = combine({0: own, 1: first}, split, 2, strips, True, (2, 3))
 
     def to_core(partial):
         send = partial[partial.shape[0] // 2 :]
         return lax.ppermute(send, "seabed", xor_pairs(strips, 1))
 
     most_moved = to_core(most)
-    tail = combine({2: second}, split, 2, 2, True)
-    chips = merge(2, 2, most, most_moved, tail, to_core(tail))
+    tail = combine({2: second, 3: third}, split, 2, strips // 2, True)
+    chips = merge((2, 3), 2, most, most_moved, tail, to_core(tail))
     total = chips[0]
     for d in range(1, strips // 2):
         total = total + lax.ppermute(chips[d], "seabed", xor_pairs(strips, 2 * d))

time: 47.3 us -> 42.8 us (0.905)
  the two profiles are of different devices: /device:TPU:24 before, /device:TPU:0 now
where the time goes in v8:
time: 42.8 us; the launch traced here: 42.7 us
  starting transfers between devices  16.2 us (38%)
  waiting for transfers between devices  16.1 us (38%)
  Pallas kernels  9.51 us (22%)
  local copies, waits for them, and re-layouts  0.72 us (2%)
    ppermute x3, starting transfers between devices, swap(): return lax.ppermute(chunk, 'freq', xor_pairs(freq_count, m))  7.1 us
    ppermute x3, waiting for transfers between devices, swap(): return lax.ppermute(chunk, 'freq', xor_pairs(freq_count, m))  5.26 us
    ppermute x3, waiting for transfers between devices, neighbours(): cross = lax.ppermute(cross, 'seabed', inner)  5.15 us
    ppermute x3, starting transfers between devices, neighbours(): cross = lax.ppermute(cross, 'seabed', inner)  5.12 us
    ppermute x3, waiting for transfers between devices, paired_shards(): total = total + lax.ppermute(chips[d], 'seabed', xor_pairs(strips, 2 * d))  3.67 us
    ppermute x3, starting transfers between devices, paired_shards(): total = total + lax.ppermute(chips[d], 'seabed', xor_pairs(strips, 2 * d))  3.55 us
    pallas_call x4, Pallas kernels, smooth(): pl.pallas_call(functools.partial(smooth_kernel, base, rim_base), out_shap...  2.62 us
    pallas_call x1, Pallas kernels, split_transfer(): pl.pallas_call(split_kernel, out_shape=[jax.ShapeDtypeStruct((parts, cell...  2.44 us
  transfers between devices with their start and end apart: 14, of which 9 were waited for; matrix products, arithmetic and copies ran while one was open for 0% of the time, Pallas kernels for 17%

profile of v8, /device:TPU:0, one launch (start us, length us, event | category | flops | bytes accessed | tf_op | source)
XLA Modules:
  0.0 42.7 jit_solution(14699167368068710792)
XLA Ops:
  0.0 2.1 %transform.1 = (f32[2,5,32,128]{3,2,1,0:T(8,128)S(1)}, f32[2,5,32,128]{3,2,1,0:T(8,128)S(1)}, f32[2,5,32,128]{3,2,1,0:T(8,128)S(1)}, f32[2,5,32,128]{3,2,1,0:T(8...) custom-call(bf16[32,5,32,128]{3,2,1,0:T(8,128)(2,1)} %bitcast.7, f32[4,16,256]{2,1,0:T(8,128)} %constant.2.clone.table_hbm, ...), custom_call_target="tpu_custom_call" | custom-call | flops 167772160 | bytes 1966080 | tf_op jit(solution)/shard_map/transform/pallas_call | solution.py:132
  2.1 3.1 %collective-permute-start = (f32[2,5,32,128]{3,2,1,0:T(8,128)S(1)}, f32[2,5,32,128]{3,2,1,0:T(8,128)S(1)}, u32[]{:S(2)}, u32[]{:S(2)}) collective-permute-start(f32[2,5,32,128]{3,2,1,0:T(8,128)S(1)} %get-tuple-element.22), channel_id=1, source_target_pairs={{0,1},{1,0},{2,3},{3,2},{4,5},{5,4},{6,7},{7,6},{8,9},{9,8},{10,11... | collective-permute-start | bytes 491528 | tf_op jit(solution)/shard_map/ppermute | solution.py:361
  5.2 4.2 %collective-permute-done.refs_1_.chunk = f32[2,5,32,128]{3,2,1,0:T(8,128)S(1)} collective-permute-done((f32[2,5,32,128]{3,2,1,0:T(8,128)S(1)}, f32[2,5,32,128]{3,2,1,0:T(8,128)S(1)}, u32[]{:S(2)}, u32[]{:S(2)}) %collective-permute-start) | collective-permute-done | bytes 163872 | tf_op jit(solution)/shard_map/ppermute | solution.py:361
  9.5 2.7 %collective-permute-start.2 = (f32[384,128]{1,0:T(8,128)S(1)}, f32[384,128]{1,0:T(8,128)S(1)}, u32[]{:S(2)}, u32[]{:S(2)}) collective-permute-start(f32[384,128]{1,0:T(8,128)S(1)} %get-tuple-element.24), channel_id=1, source_target_pairs={{4,8},{12,16},{20,24},{28,0},{8,4},{16,12},{24,20},{0,28},{5,9},{1... | collective-permute-start | bytes 589832 | tf_op jit(solution)/shard_map/ppermute | solution.py:351
  12.3 3.6 %collective-permute-start.7 = (f32[2,5,32,128]{3,2,1,0:T(8,128)S(1)}, f32[2,5,32,128]{3,2,1,0:T(8,128)S(1)}, u32[]{:S(2)}, u32[]{:S(2)}) collective-permute-start(f32[2,5,32,128]{3,2,1,0:T(8,128)S(1)} %get-tuple-element.30), channel_id=1, source_target_pairs={{0,3},{1,2},{2,1},{3,0},{4,7},{5,6},{6,5},{7,4},{8,11},{9,10},{10,... | collective-permute-start | bytes 491528 | tf_op jit(solution)/shard_map/ppermute | solution.py:361
  15.9 0.6 %collective-permute-start.4 = (f32[200,128]{1,0:T(8,128)S(1)}, f32[200,128]{1,0:T(8,128)S(1)}, u32[]{:S(2)}, u32[]{:S(2)}) collective-permute-start(f32[200,128]{1,0:T(8,128)S(1)} %get-tuple-element.26), channel_id=1, source_target_pairs={{4,8},{12,16},{20,24},{28,0},{8,4},{16,12},{24,20},{0,28},{5,9},{1... | collective-permute-start | bytes 307208 | tf_op jit(solution)/shard_map/ppermute | solution.py:351
  16.5 0.7 %collective-permute-done.3.pair_c.pair = f32[200,128]{1,0:T(8,128)S(1)} collective-permute-done((f32[200,128]{1,0:T(8,128)S(1)}, f32[200,128]{1,0:T(8,128)S(1)}, u32[]{:S(2)}, u32[]{:S(2)}) %collective-permute-start.3) | collective-permute-done | bytes 102432 | tf_op jit(solution)/shard_map/ppermute | solution.py:352
  17.2 4.5 %collective-permute-done.4.cross_c.cross = f32[200,128]{1,0:T(8,128)S(1)} collective-permute-done((f32[200,128]{1,0:T(8,128)S(1)}, f32[200,128]{1,0:T(8,128)S(1)}, u32[]{:S(2)}, u32[]{:S(2)}) %collective-permute-start.4) | collective-permute-done | bytes 102432 | tf_op jit(solution)/shard_map/ppermute | solution.py:351
  21.7 0.7 %smooth.6 = f32[2,5,32,128]{3,2,1,0:T(8,128)S(1)} custom-call(f32[2,5,32,128]{3,2,1,0:T(8,128)S(1)} %get-tuple-element.29.chunk, f32[200,128]{1,0:T(8,128)S(1)} %collective-permute-done.3.pair_c.pair, f32[200,128]{1,0:T(8,128)S(1)} %collective-permute-done.4.cross_c.cross, f32[5,128]{1,0:T(8,128)S(1)} %copy-done, ...), custom_call_target="tpu_custom_call" | custom-call | flops 1228800 | bytes 409600 | tf_op jit(solution)/shard_map/smooth/pallas_call | solution.py:248
  22.7 2.4 %split_transfer.1 = (bf16[2,640,600]{2,1,0:T(8,128)(2,1)S(1)}, bf16[2,640,600]{2,1,0:T(8,128)(2,1)S(1)}) custom-call(f32[2,600,640]{2,1,0:T(8,128)} %bitcast.6), custom_call_target="tpu_custom_call" | custom-call | flops 1536000 | bytes 6144000 | tf_op jit(solution)/shard_map/split_transfer/pallas_call | solution.py:162
  25.3 1.8 %collective-permute-start.9 = (f32[192,128]{1,0:T(8,128)S(1)}, f32[192,128]{1,0:T(8,128)S(1)}, u32[]{:S(2)}, u32[]{:S(2)}) collective-permute-start(f32[192,128]{1,0:T(8,128)S(1)} %get-tuple-element.32), channel_id=1, source_target_pairs={{4,8},{12,16},{20,24},{28,0},{8,4},{16,12},{24,20},{0,28},{5,9},{1... | collective-permute-start | bytes 294920 | tf_op jit(solution)/shard_map/ppermute | solution.py:351
  27.1 0.7 %smooth.5.refs_1_ = f32[2,5,32,128]{3,2,1,0:T(8,128)S(1)} custom-call(f32[2,5,32,128]{3,2,1,0:T(8,128)S(1)} %collective-permute-done.refs_1_.chunk, f32[384,128]{1,0:T(8,128)S(1)} %collective-permute-done.1.pair, f32[384,128]{1,0:T(8,128)S(1)} %collective-permute-done.2.cross, f32[5,128]{1,0:T(8,128)S(1)} %copy-done, ...), custom_call_target="tpu_custom_call" | custom-call | flops 1228800 | bytes 409600 | tf_op jit(solution)/shard_map/smooth/pallas_call | solution.py:248
  27.7 0.7 %smooth.4.refs_0_ = f32[2,5,32,128]{3,2,1,0:T(8,128)S(1)} custom-call(f32[2,5,32,128]{3,2,1,0:T(8,128)S(1)} %get-tuple-element.21.refs_0_.chunk, f32[384,128]{1,0:T(8,128)S(1)} %collective-permute-done.1.pair, f32[384,128]{1,0:T(8,128)S(1)} %collective-permute-done.2.cross, f32[5,128]{1,0:T(8,128)S(1)} %copy-done, ...), custom_call_target="tpu_custom_call" | custom-call | flops 1228800 | bytes 409600 | tf_op jit(solution)/shard_map/smooth/pallas_call | solution.py:248
  28.4 1.1 %combine.2.most = f32[8,2,16,600]{3,2,1,0:T(8,128)S(1)} custom-call(f32[2,5,32,128]{3,2,1,0:T(8,128)S(1)} %smooth.4.refs_0_, f32[2,5,32,128]{3,2,1,0:T(8,128)S(1)} %smooth.5.refs_1_, bf16[2,640,600]{2,1,0:T(8,128)(2,1)S(1)} %get-tuple-element.27.refs_2_, bf16[2,640,600]{2,1,0:T(8,128)(2,1)S(1)} %get-tuple-element.28.refs_3_), custom_call_target="tpu_custom_call" | custom-call | flops 589824000 | bytes 4014080 | tf_op jit(solution)/shard_map/combine/pallas_call | solution.py:310
  30.4 0.7 %smooth.7.refs_1_ = f32[2,5,32,128]{3,2,1,0:T(8,128)S(1)} custom-call(f32[2,5,32,128]{3,2,1,0:T(8,128)S(1)} %collective-permute-done.7.refs_0_.chunk, f32[192,128]{1,0:T(8,128)S(1)} %collective-permute-done.8.pair, f32[192,128]{1,0:T(8,128)S(1)} %collective-permute-done.9.cross, f32[5,128]{1,0:T(8,128)S(1)} %copy-done, ...), custom_call_target="tpu_custom_call" | custom-call | flops 1228800 | bytes 409600 | tf_op jit(solution)/shard_map/smooth/pallas_call | solution.py:248
  31.0 1.1 %collective-permute-done.6.refs_0_ = f32[2,5,32,128]{3,2,1,0:T(8,128)S(1)} collective-permute-done((f32[2,5,32,128]{3,2,1,0:T(8,128)S(1)}, f32[2,5,32,128]{3,2,1,0:T(8,128)S(1)}, u32[]{:S(2)}, u32[]{:S(2)}) %collective-permute-start.6) | collective-permute-done | bytes 163872 | tf_op jit(solution)/shard_map/ppermute | solution.py:361
  32.1 1.1 %combine.3.tail = f32[4,2,16,600]{3,2,1,0:T(8,128)S(1)} custom-call(f32[2,5,32,128]{3,2,1,0:T(8,128)S(1)} %collective-permute-done.6.refs_0_, f32[2,5,32,128]{3,2,1,0:T(8,128)S(1)} %smooth.7.refs_1_, bf16[2,640,600]{2,1,0:T(8,128)(2,1)S(1)} %get-tuple-element.27.refs_2_, bf16[2,640,600]{2,1,0:T(8,128)(2,1)S(1)} %get-tuple-element.28.refs_3_), custom_call_target="tpu_custom_call" | custom-call | flops 589824000 | bytes 4014080 | tf_op jit(solution)/shard_map/combine/pallas_call | solution.py:310
  33.3 1.4 %collective-permute-done.10.tail_moved = f32[2,2,16,600]{3,2,1,0:T(8,128)S(1)} collective-permute-done((f32[2,2,16,600]{3,2,1,0:T(8,128)S(1)}, f32[2,2,16,600]{3,2,1,0:T(8,128)S(1)}, u32[]{:S(2)}, u32[]{:S(2)}) %collective-permute-start.10) | collective-permute-done | bytes 153632 | tf_op jit(solution)/shard_map/ppermute | solution.py:382
  34.7 0.6 %collective-permute-start.11 = (f32[2,16,600]{2,1,0:T(8,128)S(1)}, f32[2,16,600]{2,1,0:T(8,128)S(1)}, u32[]{:S(2)}, u32[]{:S(2)}) collective-permute-start(f32[2,16,600]{2,1,0:T(8,128)S(1)} %get-tuple-element.34), channel_id=1, source_target_pairs={{0,8},{4,12},{8,0},{12,4},{16,24},{20,28},{24,16},{28,20},{1,9},{5... | collective-permute-start | bytes 230408 | tf_op jit(solution)/shard_map/ppermute | solution.py:389
  35.4 1.2 %collective-permute-start.12 = (f32[2,16,600]{2,1,0:T(8,128)S(1)}, f32[2,16,600]{2,1,0:T(8,128)S(1)}, u32[]{:S(2)}, u32[]{:S(2)}) collective-permute-start(f32[2,16,600]{2,1,0:T(8,128)S(1)} %get-tuple-element.35), channel_id=1, source_target_pairs={{0,16},{4,20},{8,24},{12,28},{16,0},{20,4},{24,8},{28,12},{1,17},{... | collective-permute-start | bytes 230408 | tf_op jit(solution)/shard_map/ppermute | solution.py:389
  36.6 1.7 %collective-permute-start.13 = (f32[2,16,600]{2,1,0:T(8,128)S(1)}, f32[2,16,600]{2,1,0:T(8,128)S(1)}, u32[]{:S(2)}, u32[]{:S(2)}) collective-permute-start(f32[2,16,600]{2,1,0:T(8,128)S(1)} %get-tuple-element.36), channel_id=1, source_target_pairs={{0,24},{4,28},{8,16},{12,20},{16,8},{20,12},{24,0},{28,4},{1,25},{... | collective-permute-start | bytes 230408 | tf_op jit(solution)/shard_map/ppermute | solution.py:389
  38.3 1.1 %collective-permute-done.11 = f32[2,16,600]{2,1,0:T(8,128)S(1)} collective-permute-done((f32[2,16,600]{2,1,0:T(8,128)S(1)}, f32[2,16,600]{2,1,0:T(8,128)S(1)}, u32[]{:S(2)}, u32[]{:S(2)}) %collective-permute-start.11) | collective-permute-done | bytes 76832 | tf_op jit(solution)/shard_map/ppermute | solution.py:389
  39.8 2.1 %collective-permute-done.13 = f32[2,16,600]{2,1,0:T(8,128)S(1)} collective-permute-done((f32[2,16,600]{2,1,0:T(8,128)S(1)}, f32[2,16,600]{2,1,0:T(8,128)S(1)}, u32[]{:S(2)}, u32[]{:S(2)}) %collective-permute-start.13) | collective-permute-done | bytes 76832 | tf_op jit(solution)/shard_map/ppermute | solution.py:389
  42.0 0.7 %copy.5 = f32[16,1,2,600]{3,2,1,0:T(2,128)} copy(f32[16,1,2,600]{3,0,2,1:T(8,128)S(1)} %add_bitcast_fusion) | data formatting | bytes 153600 | tf_op jit(solution)/shard_map/broadcast_in_dim | solution.py:435
  (21 shorter events, 2.1 us)
Async XLA Ops:
  0.0 21.7 %copy-start = (f32[5,128]{1,0:T(8,128)S(1)}, f32[5,128]{1,0:T(8,128)}, u32[]{:S(2)}) copy-start(f32[5,128]{1,0:T(8,128)} %own_c.7) | copy-start | bytes 7684
  2.1 7.3 %collective-permute-start = (f32[2,5,32,128]{3,2,1,0:T(8,128)S(1)}, f32[2,5,32,128]{3,2,1,0:T(8,128)S(1)}, u32[]{:S(2)}, u32[]{:S(2)}) collective-permute-start(f32[2,5,32,128]{3,2,1,0:T(8,128)S(1)} %get-tuple-element.22), channel_id=1, source_target_pairs={{0,1},{1,0},{2,3},{3,2},{4,5},{5,4},{6,7},{7,6},{8,9},{9,8},{10,11... | collective-permute-start | bytes 491528 | tf_op jit(solution)/shard_map/ppermute | solution.py:361
  9.5 17.6 %collective-permute-start.1 = (f32[384,128]{1,0:T(8,128)S(1)}, f32[384,128]{1,0:T(8,128)S(1)}, u32[]{:S(2)}, u32[]{:S(2)}) collective-permute-start(f32[384,128]{1,0:T(8,128)S(1)} %get-tuple-element.23), channel_id=1, source_target_pairs={{0,4},{4,0},{8,12},{12,8},{16,20},{20,16},{24,28},{28,24},{1,5},{5... | collective-permute-start | bytes 589832 | tf_op jit(solution)/shard_map/ppermute | solution.py:352
  9.5 17.5 %collective-permute-start.2 = (f32[384,128]{1,0:T(8,128)S(1)}, f32[384,128]{1,0:T(8,128)S(1)}, u32[]{:S(2)}, u32[]{:S(2)}) collective-permute-start(f32[384,128]{1,0:T(8,128)S(1)} %get-tuple-element.24), channel_id=1, source_target_pairs={{4,8},{12,16},{20,24},{28,0},{8,4},{16,12},{24,20},{0,28},{5,9},{1... | collective-permute-start | bytes 589832 | tf_op jit(solution)/shard_map/ppermute | solution.py:351
  12.3 12.9 %collective-permute-start.7 = (f32[2,5,32,128]{3,2,1,0:T(8,128)S(1)}, f32[2,5,32,128]{3,2,1,0:T(8,128)S(1)}, u32[]{:S(2)}, u32[]{:S(2)}) collective-permute-start(f32[2,5,32,128]{3,2,1,0:T(8,128)S(1)} %get-tuple-element.30), channel_id=1, source_target_pairs={{0,3},{1,2},{2,1},{3,0},{4,7},{5,6},{6,5},{7,4},{8,11},{9,10},{10,... | collective-permute-start | bytes 491528 | tf_op jit(solution)/shard_map/ppermute | solution.py:361
  15.9 1.3 %collective-permute-start.3 = (f32[200,128]{1,0:T(8,128)S(1)}, f32[200,128]{1,0:T(8,128)S(1)}, u32[]{:S(2)}, u32[]{:S(2)}) collective-permute-start(f32[200,128]{1,0:T(8,128)S(1)} %get-tuple-element.25), channel_id=1, source_target_pairs={{0,4},{4,0},{8,12},{12,8},{16,20},{20,16},{24,28},{28,24},{1,5},{5... | collective-permute-start | bytes 307208 | tf_op jit(solution)/shard_map/ppermute | solution.py:352
  15.9 5.8 %collective-permute-start.4 = (f32[200,128]{1,0:T(8,128)S(1)}, f32[200,128]{1,0:T(8,128)S(1)}, u32[]{:S(2)}, u32[]{:S(2)}) collective-permute-start(f32[200,128]{1,0:T(8,128)S(1)} %get-tuple-element.26), channel_id=1, source_target_pairs={{4,8},{12,16},{20,24},{28,0},{8,4},{16,12},{24,20},{0,28},{5,9},{1... | collective-permute-start | bytes 307208 | tf_op jit(solution)/shard_map/ppermute | solution.py:351
  22.3 9.7 %collective-permute-start.6 = (f32[2,5,32,128]{3,2,1,0:T(8,128)S(1)}, f32[2,5,32,128]{3,2,1,0:T(8,128)S(1)}, u32[]{:S(2)}, u32[]{:S(2)}) collective-permute-start(f32[2,5,32,128]{3,2,1,0:T(8,128)S(1)} %smooth.6), channel_id=1, source_target_pairs={{0,2},{1,3},{2,0},{3,1},{4,6},{5,7},{6,4},{7,5},{8,10},{9,11},{10,... | collective-permute-start | bytes 491528 | tf_op jit(solution)/shard_map/ppermute | solution.py:361
  25.2 4.5 %collective-permute-start.8 = (f32[192,128]{1,0:T(8,128)S(1)}, f32[192,128]{1,0:T(8,128)S(1)}, u32[]{:S(2)}, u32[]{:S(2)}) collective-permute-start(f32[192,128]{1,0:T(8,128)S(1)} %get-tuple-element.31), channel_id=1, source_target_pairs={{0,4},{4,0},{8,12},{12,8},{16,20},{20,16},{24,28},{28,24},{1,5},{5... | collective-permute-start | bytes 294920 | tf_op jit(solution)/shard_map/ppermute | solution.py:352
  25.3 5.1 %collective-permute-start.9 = (f32[192,128]{1,0:T(8,128)S(1)}, f32[192,128]{1,0:T(8,128)S(1)}, u32[]{:S(2)}, u32[]{:S(2)}) collective-permute-start(f32[192,128]{1,0:T(8,128)S(1)} %get-tuple-element.32), channel_id=1, source_target_pairs={{4,8},{12,16},{20,24},{28,0},{8,4},{16,12},{24,20},{0,28},{5,9},{1... | collective-permute-start | bytes 294920 | tf_op jit(solution)/shard_map/ppermute | solution.py:351
  29.5 5.1 %collective-permute-start.5 = (f32[4,2,16,600]{3,2,1,0:T(8,128)S(1)}, f32[4,2,16,600]{3,2,1,0:T(8,128)S(1)}, u32[]{:S(2)}, u32[]{:S(2)}) collective-permute-start(f32[4,2,16,600]{3,2,1,0:T(8,128)S(1)} %slice.8), channel_id=1, source_target_pairs={{0,4},{4,0},{8,12},{12,8},{16,20},{20,16},{24,28},{28,24},{1,5},{5... | collective-permute-start | bytes 921608 | tf_op jit(solution)/shard_map/ppermute | solution.py:382
  33.2 1.5 %collective-permute-start.10 = (f32[2,2,16,600]{3,2,1,0:T(8,128)S(1)}, f32[2,2,16,600]{3,2,1,0:T(8,128)S(1)}, u32[]{:S(2)}, u32[]{:S(2)}) collective-permute-start(f32[2,2,16,600]{3,2,1,0:T(8,128)S(1)} %slice.9), channel_id=1, source_target_pairs={{0,4},{4,0},{8,12},{12,8},{16,20},{20,16},{24,28},{28,24},{1,5},{5... | collective-permute-start | bytes 460808 | tf_op jit(solution)/shard_map/ppermute | solution.py:382
  34.7 4.6 %collective-permute-start.11 = (f32[2,16,600]{2,1,0:T(8,128)S(1)}, f32[2,16,600]{2,1,0:T(8,128)S(1)}, u32[]{:S(2)}, u32[]{:S(2)}) collective-permute-start(f32[2,16,600]{2,1,0:T(8,128)S(1)} %get-tuple-element.34), channel_id=1, source_target_pairs={{0,8},{4,12},{8,0},{12,4},{16,24},{20,28},{24,16},{28,20},{1,9},{5... | collective-permute-start | bytes 230408 | tf_op jit(solution)/shard_map/ppermute | solution.py:389
  35.4 4.4 %collective-permute-start.12 = (f32[2,16,600]{2,1,0:T(8,128)S(1)}, f32[2,16,600]{2,1,0:T(8,128)S(1)}, u32[]{:S(2)}, u32[]{:S(2)}) collective-permute-start(f32[2,16,600]{2,1,0:T(8,128)S(1)} %get-tuple-element.35), channel_id=1, source_target_pairs={{0,16},{4,20},{8,24},{12,28},{16,0},{20,4},{24,8},{28,12},{1,17},{... | collective-permute-start | bytes 230408 | tf_op jit(solution)/shard_map/ppermute | solution.py:389
  36.6 5.3 %collective-permute-start.13 = (f32[2,16,600]{2,1,0:T(8,128)S(1)}, f32[2,16,600]{2,1,0:T(8,128)S(1)}, u32[]{:S(2)}, u32[]{:S(2)}) collective-permute-start(f32[2,16,600]{2,1,0:T(8,128)S(1)} %get-tuple-element.36), channel_id=1, source_target_pairs={{0,24},{4,28},{8,16},{12,20},{16,8},{20,12},{24,0},{28,4},{1,25},{... | collective-permute-start | bytes 230408 | tf_op jit(solution)/shard_map/ppermute | solution.py:389

commit v9 on v8

--- a/solution.py
+++ b/solution.py
@@ -63,8 +63,8 @@
 
 
 def transform_kernel(slots, edged, field_hbm, table_hbm, own_hbm, *refs):
-    outs, (pair, cross) = refs[:slots], refs[slots : slots + 2]
-    field, table, own_c, field_sem, table_sem, own_sem = refs[slots + 2 :]
+    outs, pair, crosses = refs[:slots], refs[slots], refs[slots + 1 : -6]
+    field, table, own_c, field_sem, table_sem, own_sem = refs[-6:]
     vectors, rows, steps, width = field.shape
     blocks = vectors // GROUP
     even = even_strip()
@@ -82,12 +82,11 @@
         get(i).start()
     get_own.wait()
     rim = PASSES - 1
-    base = edge_base(len(edged), 0, 0, vectors)
     last_c, first_c = own_c[rows - rim :], own_c[:rim]
-    pad = jnp.zeros((pair.shape[0] - base - rim, width), jnp.float32)
-    for ref, one, other in ((pair, last_c, first_c), (cross, first_c, last_c)):
+    for ref, one, other in ((pair, last_c, first_c), (crosses[0], first_c, last_c)):
+        base = ref.shape[0] - GROUP
         ref[base : base + rim] = pick(even, one, other)
-        ref[base + rim :] = pad
+        ref[base + rim :] = jnp.zeros((GROUP - rim, width), jnp.float32)
     get_table.wait()
     short = table[...]
     shape = (short.shape[0], GROUP, short.shape[1])
@@ -120,20 +119,24 @@
                     first = values[at : at + GROUP, r * width : (r + 1) * width]
                     to = edge_base(edged.index(slot), b, r, vectors) + i * GROUP
                     pair[to : to + GROUP] = pick(even, last, first)
-                    cross[to : to + GROUP] = pick(even, first, last)
+                    to = edge_base(0, b, r, vectors) + i * GROUP
+                    crosses[edged.index(slot)][to : to + GROUP] = pick(even, first, last)
 
 
 def transform(field, table, coefficient, slots, edged):
     vectors, rows, steps, width = field.shape
     chunk = jax.ShapeDtypeStruct((2, rows, vectors, width), jnp.float32)
-    edge = jax.ShapeDtypeStruct((edge_base(len(edged), 0, 0, vectors) + GROUP, width), jnp.float32)
+    size = edge_base(1, 0, 0, vectors)
+    pair = (len(edged) * size + GROUP, width)
+    crosses = [(size * bool(edged) + GROUP, width)] + [(size, width)] * (len(edged) - 1)
+    edges = [jax.ShapeDtypeStruct(shape, jnp.float32) for shape in (pair, *crosses)]
     hbm = pl.BlockSpec(memory_space=pltpu.HBM)
     vmem = pl.BlockSpec(memory_space=pltpu.VMEM)
-    *chunks, pair, cross = pl.pallas_call(
+    outs = pl.pallas_call(
         functools.partial(transform_kernel, slots, edged),
-        out_shape=[chunk] * slots + [edge] * 2,
+        out_shape=[chunk] * slots + edges,
         in_specs=[hbm, hbm, hbm],
-        out_specs=[vmem] * (slots + 2),
+        out_specs=[vmem] * (slots + len(edges)),
         scratch_shapes=[
             pltpu.VMEM(field.shape, field.dtype),
             pltpu.VMEM(table.shape[1:], table.dtype),
@@ -149,7 +152,7 @@
         ),
         name="transform",
     )(*map(in_hbm, (field, table, coefficient)))
-    return chunks, pair, cross
+    return outs[:slots], outs[slots], outs[slots + 1 :]
 
 
 def split_kernel(x_ref, high_ref, low_ref):
@@ -185,31 +188,39 @@
     return out
 
 
-def edges_kernel(count, *refs):
-    chunks, (pair, cross) = refs[:count], refs[count:]
+def edges_kernel(count, crossing, *refs):
+    chunks, outs = refs[:count], refs[count:]
     _, rows, vectors, _ = chunks[0].shape
     even = even_strip().astype(jnp.int32)
-    for index, chunk in enumerate(chunks):
-        for ref, start in ((pair, even), (cross, 1 - even)):
-            for b in range(2):
-                for r in range(PASSES):
-                    at = edge_base(index, b, r, vectors)
-                    ref[at : at + vectors] = chunk[b, start * (rows - PASSES) + r]
-
-
-def edges(chunks):
+
+    def put(ref, slot, chunk, last):
+        for b in range(2):
+            for r in range(PASSES):
+                at = edge_base(slot, b, r, vectors)
+                ref[at : at + vectors] = chunk[b, last * (rows - PASSES) + r]
+
+    if crossing:
+        for slot, index in enumerate(crossing):
+            put(outs[-1], slot, chunks[index], 1 - even)
+    if len(outs) > 1 or not crossing:
+        for index, chunk in enumerate(chunks):
+            put(outs[0], index, chunk, even)
+
+
+def edges(chunks, crossing, pair=True):
     _, _, vectors, width = chunks[0].shape
-    shape = (edge_base(len(chunks), 0, 0, vectors), width)
+    counts = [len(chunks)] * pair + [len(crossing)] * bool(crossing)
+    shapes = [(edge_base(n, 0, 0, vectors), width) for n in counts]
     return pl.pallas_call(
-        functools.partial(edges_kernel, len(chunks)),
-        out_shape=[jax.ShapeDtypeStruct(shape, jnp.float32)] * 2,
-        compiler_params=params(),
-        cost_estimate=cost(0, 16 * shape[0] * width),
+        functools.partial(edges_kernel, len(chunks), crossing),
+        out_shape=[jax.ShapeDtypeStruct(shape, jnp.float32) for shape in shapes],
+        compiler_params=params(),
+        cost_estimate=cost(0, 16 * shapes[0][0] * width),
         name="edges",
     )(*chunks)
 
 
-def smooth_kernel(base, rim_base, chunk, pair, cross, own_c, pair_c, cross_c, out):
+def smooth_kernel(pair_slot, cross_slot, chunk, pair, cross, own_c, pair_c, cross_c, out):
     _, rows, vectors, width = chunk.shape
     rim = PASSES - 1
     even = even_strip()
@@ -221,8 +232,11 @@
         other = pick(inside, other, jnp.zeros_like(other))
         return pick(even, one, other), pick(even, other, one)
 
-    at_c = slice(rim_base, rim_base + rim)
-    high_c, low_c = rims(pair_c[at_c], cross_c[at_c])
+    def rim_of(ref):
+        base = ref.shape[0] - GROUP
+        return ref[base : base + rim]
+
+    high_c, low_c = rims(rim_of(pair_c), rim_of(cross_c))
     coefficients = [low_c[i : i + 1] for i in range(rim)]
     coefficients += [own_c[i : i + 1] for i in range(rows)]
     coefficients += [high_c[i : i + 1] for i in range(rim)]
@@ -232,8 +246,9 @@
             span = slice(start, start + part)
             low, high = [], []
             for r in range(PASSES):
-                at = base + edge_base(0, b, r, vectors) + start
-                above, below = rims(pair[at : at + part], cross[at : at + part])
+                at = edge_base(pair_slot, b, r, vectors) + start
+                to = edge_base(cross_slot, b, r, vectors) + start
+                above, below = rims(pair[at : at + part], cross[to : to + part])
                 high.append(above)
                 low.append(below)
             values = low + [chunk[b, r, span] for r in range(rows)] + high
@@ -243,10 +258,9 @@
                 out[b, r, span] = values[r]
 
 
-def smooth(chunk, pair, cross, slot, coefficients, rim_base):
-    base = edge_base(slot, 0, 0, chunk.shape[2])
+def smooth(chunk, pair, pair_slot, cross, cross_slot, coefficients):
     return pl.pallas_call(
-        functools.partial(smooth_kernel, base, rim_base),
+        functools.partial(smooth_kernel, pair_slot, cross_slot),
         out_shape=jax.ShapeDtypeStruct(chunk.shape, jnp.float32),
         compiler_params=params(),
         cost_estimate=cost(30 * chunk.size, 10 * chunk.size),
@@ -345,36 +359,40 @@
     return [(i, i ^ apart) for i in range(count)]
 
 
-def neighbours(pair, cross, strips):
+def to_pair(edge, strips):
+    return lax.ppermute(edge, "seabed", xor_pairs(strips, 1))
+
+
+def to_cross(edge, strips):
     inner = [(i, (i + 1) % strips) for i in range(1, strips, 2)]
-    inner = inner + [(b, a) for a, b in inner]
-    cross = lax.ppermute(cross, "seabed", inner)
-    pair = lax.ppermute(pair, "seabed", xor_pairs(strips, 1))
-    return pair, cross
+    return lax.ppermute(edge, "seabed", inner + [(b, a) for a, b in inner])
 
 
 def paired_shards(field, coefficient, split_of, table, freq_count, strips):
-    vectors = field.shape[0]
-    chunks, pair, cross = transform(field, table, coefficient, freq_count, (2,))
+    chunks, pair, crosses = transform(field, table, coefficient, freq_count, (2, 0))
 
     def swap(m, chunk):
         return lax.ppermute(chunk, "freq", xor_pairs(freq_count, m))
 
-    def relax(chunk, edge, slot):
-        return smooth(chunk, *edge, slot, coefficients, rim_base)
+    def relax(chunk, pair, pair_slot, cross):
+        return smooth(chunk, pair, pair_slot, cross, 0, coefficients)
 
     first = swap(1, chunks[1])
     third = swap(3, chunks[3])
-    edge = neighbours(pair, cross, strips)
+    cross2 = to_cross(crosses[0], strips)
+    pair = to_pair(pair, strips)
+    cross0 = to_cross(crosses[1], strips)
+    coefficients = (coefficient, pair, cross2)
     split = split_of()
-    coefficients = (coefficient, *edge)
-    rim_base = edge_base(1, 0, 0, vectors)
-    second = swap(2, relax(chunks[2], edge, 0))
-    mid_edge = neighbours(*edges([chunks[0], first]), strips)
-    own = relax(chunks[0], mid_edge, 0)
-    third_edge = neighbours(*edges([third]), strips)
-    first = relax(first, mid_edge, 1)
-    third = relax(third, third_edge, 0)
+    second = swap(2, relax(chunks[2], pair, 0, cross2))
+    own = relax(chunks[0], pair, 1, cross0)
+    (cross1,) = edges([first], (0,), False)
+    cross1 = to_cross(cross1, strips)
+    pair, cross3 = edges([first, third], (1,))
+    cross3 = to_cross(cross3, strips)
+    pair = to_pair(pair, strips)
+    first = relax(first, pair, 0, cross1)
+    third = relax(third, pair, 1, cross3)
     most = combine({0: own, 1: first}, split, 2, strips, True, (2, 3))
 
     def to_core(partial):
@@ -391,18 +409,16 @@
 
 
 def plain_shards(field, coefficient, split_of, table, freq_count, strips):
-    _, rows = field.shape[:2]
-    spectrum, _, _ = transform(field, table, coefficient, freq_count, ())
+    spectrum, pair_c, (cross_c,) = transform(field, table, coefficient, freq_count, ())
     spectrum = jnp.stack(spectrum)
     spectrum = lax.all_to_all(spectrum, "freq", split_axis=0, concat_axis=0, tiled=True)
     chunks = list(spectrum)
-    rim = PASSES - 1
-    even = even_strip()
-    first_c, last_c = coefficient[:rim], coefficient[rows - rim :]
-    pair_c, cross_c = pick(even, last_c, first_c), pick(even, first_c, last_c)
-    coefficients = (coefficient, *neighbours(pair_c, cross_c, strips))
-    edge = neighbours(*edges(chunks), strips)
-    chunks = [smooth(c, *edge, i, coefficients, 0) for i, c in enumerate(chunks)]
+    pair_c = to_pair(pair_c, strips)
+    cross_c = to_cross(cross_c, strips)
+    coefficients = (coefficient, pair_c, cross_c)
+    pair, cross = edges(chunks, tuple(range(len(chunks))))
+    pair, cross = to_pair(pair, strips), to_cross(cross, strips)
+    chunks = [smooth(c, pair, i, cross, i, coefficients) for i, c in enumerate(chunks)]
     owners_in = strips // freq_count
     partial = combine(dict(enumerate(chunks)), split_of(), owners_in, strips, False)
     got = lax.all_to_all(partial, "seabed", split_axis=0, concat_axis=0, tiled=True)

time: 42.8 us -> 44.1 us (1.030)
  starting transfers between devices: 16.2 us -> 19.2 us
  waiting for transfers between devices: 16.1 us -> 14.4 us
    ppermute x6, waiting for transfers between devices: 5.81 us -> 0.88 us  [the longest x4 0.88 us: to_cross(): return lax.ppermute(edge, 'seabed', inner + [(b, a) for a, b in inner])]
    ppermute x6, starting transfers between devices: 5.27 us -> 7.92 us  [the longest x4 7.85 us: to_cross(): return lax.ppermute(edge, 'seabed', inner + [(b, a) for a, b in inner])]
    ppermute x3, waiting for transfers between devices: 5.26 us -> 7.53 us  [swap(): return lax.ppermute(chunk, 'freq', xor_pairs(freq_count, m))]
    ppermute x3, waiting for transfers between devices: 3.67 us -> 4.77 us  [paired_shards(): total = total + lax.ppermute(chips[d], 'seabed', xor_pairs(strips, 2 * d))]
  transfers between devices with their start and end apart: 14 -> 14, of which waited for: 9 -> 8; matrix products, arithmetic and copies ran while one was open for 0% -> 0% of each run, Pallas kernels for 17% -> 17%
where the time goes in v9:
time: 44.1 us; the launch traced here: 44 us
  starting transfers between devices  19.2 us (44%)
  waiting for transfers between devices  14.4 us (33%)
  Pallas kernels  9.52 us (22%)
  local copies, waits for them, and re-layouts  0.72 us (2%)
    ppermute x4, starting transfers between devices, to_cross(): return lax.ppermute(edge, 'seabed', inner + [(b, a) for a, b in inner])  7.85 us
    ppermute x3, waiting for transfers between devices, swap(): return lax.ppermute(chunk, 'freq', xor_pairs(freq_count, m))  7.53 us
    ppermute x3, starting transfers between devices, swap(): return lax.ppermute(chunk, 'freq', xor_pairs(freq_count, m))  7.41 us
    ppermute x3, waiting for transfers between devices, paired_shards(): total = total + lax.ppermute(chips[d], 'seabed', xor_pairs(strips, 2 * d))  4.77 us
    ppermute x3, starting transfers between devices, paired_shards(): total = total + lax.ppermute(chips[d], 'seabed', xor_pairs(strips, 2 * d))  3.55 us
    pallas_call x4, Pallas kernels, smooth(): pl.pallas_call(functools.partial(smooth_kernel, pair_slot, cross_slot), o...  2.61 us
    pallas_call x1, Pallas kernels, split_transfer(): pl.pallas_call(split_kernel, out_shape=[jax.ShapeDtypeStruct((parts, cell...  2.44 us
    pallas_call x2, Pallas kernels, combine(): pl.pallas_call(functools.partial(combine_kernel, indices, owners_in, pair...  2.26 us
  transfers between devices with their start and end apart: 14, of which 8 were waited for; matrix products, arithmetic and copies ran while one was open for 0% of the time, Pallas kernels for 17%

profile of v9, /device:TPU:0, one launch (start us, length us, event | category | flops | bytes accessed | tf_op | source)
XLA Modules:
  0.0 44.0 jit_solution(4537797490636228642)
XLA Ops:
  0.0 2.1 %transform.1 = (f32[2,5,32,128]{3,2,1,0:T(8,128)S(1)}, f32[2,5,32,128]{3,2,1,0:T(8,128)S(1)}, f32[2,5,32,128]{3,2,1,0:T(8,128)S(1)}, f32[2,5,32,128]{3,2,1,0:T(8...) custom-call(bf16[32,5,32,128]{3,2,1,0:T(8,128)(2,1)} %bitcast.7, ...), custom_call_target="tpu_custom_call" | custom-call | flops 167772160 | bytes 1966080 | tf_op jit(solution)/shard_map/transform/pallas_call | solution.py:135
  2.1 3.1 %collective-permute-start.3 = (f32[2,5,32,128]{3,2,1,0:T(8,128)S(1)}, f32[2,5,32,128]{3,2,1,0:T(8,128)S(1)}, u32[]{:S(2)}, u32[]{:S(2)}) collective-permute-start(f32[2,5,32,128]{3,2,1,0:T(8,128)S(1)} %get-tuple-element.24), channel_id=1, source_target_pairs={{0,1},{1,0},{2,3},{3,2},{4,5},{5,4},{6,7},{7,6},{8,9},{9,8},{10,11... | collective-permute-start | bytes 491528 | tf_op jit(solution)/shard_map/ppermute | solution.py:375
  5.2 2.5 %collective-permute-start.4 = (f32[2,5,32,128]{3,2,1,0:T(8,128)S(1)}, f32[2,5,32,128]{3,2,1,0:T(8,128)S(1)}, u32[]{:S(2)}, u32[]{:S(2)}) collective-permute-start(f32[2,5,32,128]{3,2,1,0:T(8,128)S(1)} %get-tuple-element.25), channel_id=1, source_target_pairs={{0,3},{1,2},{2,1},{3,0},{4,7},{5,6},{6,5},{7,4},{8,11},{9,10},{10,... | collective-permute-start | bytes 491528 | tf_op jit(solution)/shard_map/ppermute | solution.py:375
  7.7 2.1 %collective-permute-done.3.refs_0_.chunk = f32[2,5,32,128]{3,2,1,0:T(8,128)S(1)} collective-permute-done((f32[2,5,32,128]{3,2,1,0:T(8,128)S(1)}, f32[2,5,32,128]{3,2,1,0:T(8,128)S(1)}, u32[]{:S(2)}, u32[]{:S(2)}) %collective-permute-start.3) | collective-permute-done | bytes 163872 | tf_op jit(solution)/shard_map/ppermute | solution.py:375
  9.8 5.4 %collective-permute-done.4.refs_1_.chunk = f32[2,5,32,128]{3,2,1,0:T(8,128)S(1)} collective-permute-done((f32[2,5,32,128]{3,2,1,0:T(8,128)S(1)}, f32[2,5,32,128]{3,2,1,0:T(8,128)S(1)}, u32[]{:S(2)}, u32[]{:S(2)}) %collective-permute-start.4) | collective-permute-done | bytes 163872 | tf_op jit(solution)/shard_map/ppermute | solution.py:375
  15.3 2.6 %collective-permute-start.2 = (f32[200,128]{1,0:T(8,128)S(1)}, f32[200,128]{1,0:T(8,128)S(1)}, u32[]{:S(2)}, u32[]{:S(2)}) collective-permute-start(f32[200,128]{1,0:T(8,128)S(1)} %get-tuple-element.23), channel_id=1, source_target_pairs={{4,8},{12,16},{20,24},{28,0},{8,4},{16,12},{24,20},{0,28},{5,9},{1... | collective-permute-start | bytes 307208 | tf_op jit(solution)/shard_map/ppermute | solution.py:368
  18.1 2.5 %collective-permute-start.6 = (f32[192,128]{1,0:T(8,128)S(1)}, f32[192,128]{1,0:T(8,128)S(1)}, u32[]{:S(2)}, u32[]{:S(2)}) collective-permute-start(f32[192,128]{1,0:T(8,128)S(1)} %edges.3), channel_id=1, source_target_pairs={{4,8},{12,16},{20,24},{28,0},{8,4},{16,12},{24,20},{0,28},{5,9},{1... | collective-permute-start | bytes 294920 | tf_op jit(solution)/shard_map/ppermute | solution.py:368
  21.2 0.7 %smooth.6 = f32[2,5,32,128]{3,2,1,0:T(8,128)S(1)} custom-call(f32[2,5,32,128]{3,2,1,0:T(8,128)S(1)} %get-tuple-element.29.chunk, f32[392,128]{1,0:T(8,128)S(1)} %collective-permute-done.pair.pair_c, f32[200,128]{1,0:T(8,128)S(1)} %collective-permute-done.2.cross_c.cross, f32[5,128]{1,0:T(8,128)S(1)} %copy-done, ...), custom_call_target="tpu_custom_call" | custom-call | flops 1228800 | bytes 409600 | tf_op jit(solution)/shard_map/smooth/pallas_call | solution.py:262
  21.8 1.8 %collective-permute-start.8 = (f32[2,5,32,128]{3,2,1,0:T(8,128)S(1)}, f32[2,5,32,128]{3,2,1,0:T(8,128)S(1)}, u32[]{:S(2)}, u32[]{:S(2)}) collective-permute-start(f32[2,5,32,128]{3,2,1,0:T(8,128)S(1)} %smooth.6), channel_id=1, source_target_pairs={{0,2},{1,3},{2,0},{3,1},{4,6},{5,7},{6,4},{7,5},{8,10},{9,11},{10,... | collective-permute-start | bytes 491528 | tf_op jit(solution)/shard_map/ppermute | solution.py:375
  23.6 2.4 %split_transfer.1 = (bf16[2,640,600]{2,1,0:T(8,128)(2,1)S(1)}, bf16[2,640,600]{2,1,0:T(8,128)(2,1)S(1)}) custom-call(f32[2,600,640]{2,1,0:T(8,128)} %bitcast.6), custom_call_target="tpu_custom_call" | custom-call | flops 1536000 | bytes 6144000 | tf_op jit(solution)/shard_map/split_transfer/pallas_call | solution.py:165
  26.1 2.6 %collective-permute-start.9 = (f32[192,128]{1,0:T(8,128)S(1)}, f32[192,128]{1,0:T(8,128)S(1)}, u32[]{:S(2)}, u32[]{:S(2)}) collective-permute-start(f32[192,128]{1,0:T(8,128)S(1)} %get-tuple-element.30), channel_id=1, source_target_pairs={{4,8},{12,16},{20,24},{28,0},{8,4},{16,12},{24,20},{0,28},{5,9},{1... | collective-permute-start | bytes 294920 | tf_op jit(solution)/shard_map/ppermute | solution.py:368
  28.7 0.7 %smooth.4.refs_0_ = f32[2,5,32,128]{3,2,1,0:T(8,128)S(1)} custom-call(f32[2,5,32,128]{3,2,1,0:T(8,128)S(1)} %get-tuple-element.20.chunk, f32[392,128]{1,0:T(8,128)S(1)} %collective-permute-done.pair.pair_c, f32[192,128]{1,0:T(8,128)S(1)} %collective-permute-done.1.cross, f32[5,128]{1,0:T(8,128)S(1)} %copy-done, ...), custom_call_target="tpu_custom_call" | custom-call | flops 1228800 | bytes 409600 | tf_op jit(solution)/shard_map/smooth/pallas_call | solution.py:262
  29.4 0.7 %smooth.5.refs_1_ = f32[2,5,32,128]{3,2,1,0:T(8,128)S(1)} custom-call(f32[2,5,32,128]{3,2,1,0:T(8,128)S(1)} %collective-permute-done.3.refs_0_.chunk, f32[384,128]{1,0:T(8,128)S(1)} %collective-permute-done.5.pair, f32[192,128]{1,0:T(8,128)S(1)} %collective-permute-done.6.cross, f32[5,128]{1,0:T(8,128)S(1)} %copy-done, ...), custom_call_target="tpu_custom_call" | custom-call | flops 1228800 | bytes 409600 | tf_op jit(solution)/shard_map/smooth/pallas_call | solution.py:262
  30.0 1.1 %combine.2.most = f32[8,2,16,600]{3,2,1,0:T(8,128)S(1)} custom-call(f32[2,5,32,128]{3,2,1,0:T(8,128)S(1)} %smooth.4.refs_0_, f32[2,5,32,128]{3,2,1,0:T(8,128)S(1)} %smooth.5.refs_1_, bf16[2,640,600]{2,1,0:T(8,128)(2,1)S(1)} %get-tuple-element.27.refs_2_, bf16[2,640,600]{2,1,0:T(8,128)(2,1)S(1)} %get-tuple-element.28.refs_3_), custom_call_target="tpu_custom_call" | custom-call | flops 589824000 | bytes 4014080 | tf_op jit(solution)/shard_map/combine/pallas_call | solution.py:324
  31.6 0.7 %smooth.7.refs_1_ = f32[2,5,32,128]{3,2,1,0:T(8,128)S(1)} custom-call(f32[2,5,32,128]{3,2,1,0:T(8,128)S(1)} %collective-permute-done.4.refs_1_.chunk, f32[384,128]{1,0:T(8,128)S(1)} %collective-permute-done.5.pair, f32[192,128]{1,0:T(8,128)S(1)} %collective-permute-done.9.cross, f32[5,128]{1,0:T(8,128)S(1)} %copy-done, ...), custom_call_target="tpu_custom_call" | custom-call | flops 1228800 | bytes 409600 | tf_op jit(solution)/shard_map/smooth/pallas_call | solution.py:262
  32.3 1.1 %combine.3.tail = f32[4,2,16,600]{3,2,1,0:T(8,128)S(1)} custom-call(f32[2,5,32,128]{3,2,1,0:T(8,128)S(1)} %collective-permute-done.8.refs_0_, f32[2,5,32,128]{3,2,1,0:T(8,128)S(1)} %smooth.7.refs_1_, bf16[2,640,600]{2,1,0:T(8,128)(2,1)S(1)} %get-tuple-element.27.refs_2_, bf16[2,640,600]{2,1,0:T(8,128)(2,1)S(1)} %get-tuple-element.28.refs_3_), custom_call_target="tpu_custom_call" | custom-call | flops 589824000 | bytes 4014080 | tf_op jit(solution)/shard_map/combine/pallas_call | solution.py:324
  33.7 1.2 %collective-permute-done.10.tail_moved = f32[2,2,16,600]{3,2,1,0:T(8,128)S(1)} collective-permute-done((f32[2,2,16,600]{3,2,1,0:T(8,128)S(1)}, f32[2,2,16,600]{3,2,1,0:T(8,128)S(1)}, u32[]{:S(2)}, u32[]{:S(2)}) %collective-permute-start.10) | collective-permute-done | bytes 153632 | tf_op jit(solution)/shard_map/ppermute | solution.py:400
  35.0 1.3 %collective-permute-start.11 = (f32[2,16,600]{2,1,0:T(8,128)S(1)}, f32[2,16,600]{2,1,0:T(8,128)S(1)}, u32[]{:S(2)}, u32[]{:S(2)}) collective-permute-start(f32[2,16,600]{2,1,0:T(8,128)S(1)} %get-tuple-element.32), channel_id=1, source_target_pairs={{0,8},{4,12},{8,0},{12,4},{16,24},{20,28},{24,16},{28,20},{1,9},{5... | collective-permute-start | bytes 230408 | tf_op jit(solution)/shard_map/ppermute | solution.py:407
  36.3 1.7 %collective-permute-start.12 = (f32[2,16,600]{2,1,0:T(8,128)S(1)}, f32[2,16,600]{2,1,0:T(8,128)S(1)}, u32[]{:S(2)}, u32[]{:S(2)}) collective-permute-start(f32[2,16,600]{2,1,0:T(8,128)S(1)} %get-tuple-element.33), channel_id=1, source_target_pairs={{0,16},{4,20},{8,24},{12,28},{16,0},{20,4},{24,8},{28,12},{1,17},{... | collective-permute-start | bytes 230408 | tf_op jit(solution)/shard_map/ppermute | solution.py:407
  37.9 0.6 %collective-permute-start.13 = (f32[2,16,600]{2,1,0:T(8,128)S(1)}, f32[2,16,600]{2,1,0:T(8,128)S(1)}, u32[]{:S(2)}, u32[]{:S(2)}) collective-permute-start(f32[2,16,600]{2,1,0:T(8,128)S(1)} %get-tuple-element.34), channel_id=1, source_target_pairs={{0,24},{4,28},{8,16},{12,20},{16,8},{20,12},{24,0},{28,4},{1,25},{... | collective-permute-start | bytes 230408 | tf_op jit(solution)/shard_map/ppermute | solution.py:407
  38.5 1.1 %collective-permute-done.11 = f32[2,16,600]{2,1,0:T(8,128)S(1)} collective-permute-done((f32[2,16,600]{2,1,0:T(8,128)S(1)}, f32[2,16,600]{2,1,0:T(8,128)S(1)}, u32[]{:S(2)}, u32[]{:S(2)}) %collective-permute-start.11) | collective-permute-done | bytes 76832 | tf_op jit(solution)/shard_map/ppermute | solution.py:407
  39.6 2.1 %collective-permute-done.12 = f32[2,16,600]{2,1,0:T(8,128)S(1)} collective-permute-done((f32[2,16,600]{2,1,0:T(8,128)S(1)}, f32[2,16,600]{2,1,0:T(8,128)S(1)}, u32[]{:S(2)}, u32[]{:S(2)}) %collective-permute-start.12) | collective-permute-done | bytes 76832 | tf_op jit(solution)/shard_map/ppermute | solution.py:407
  41.7 1.6 %collective-permute-done.13 = f32[2,16,600]{2,1,0:T(8,128)S(1)} collective-permute-done((f32[2,16,600]{2,1,0:T(8,128)S(1)}, f32[2,16,600]{2,1,0:T(8,128)S(1)}, u32[]{:S(2)}, u32[]{:S(2)}) %collective-permute-start.13) | collective-permute-done | bytes 76832 | tf_op jit(solution)/shard_map/ppermute | solution.py:407
  43.3 0.7 %copy.5 = f32[16,1,2,600]{3,2,1,0:T(2,128)} copy(f32[16,1,2,600]{3,0,2,1:T(8,128)S(1)} %add_bitcast_fusion) | data formatting | bytes 153600 | tf_op jit(solution)/shard_map/broadcast_in_dim | solution.py:451
  (21 shorter events, 1.6 us)
Async XLA Ops:
  0.0 21.2 %copy-start = (f32[5,128]{1,0:T(8,128)S(1)}, f32[5,128]{1,0:T(8,128)}, u32[]{:S(2)}) copy-start(f32[5,128]{1,0:T(8,128)} %own_c.7) | copy-start | bytes 7684
  2.1 7.7 %collective-permute-start.3 = (f32[2,5,32,128]{3,2,1,0:T(8,128)S(1)}, f32[2,5,32,128]{3,2,1,0:T(8,128)S(1)}, u32[]{:S(2)}, u32[]{:S(2)}) collective-permute-start(f32[2,5,32,128]{3,2,1,0:T(8,128)S(1)} %get-tuple-element.24), channel_id=1, source_target_pairs={{0,1},{1,0},{2,3},{3,2},{4,5},{5,4},{6,7},{7,6},{8,9},{9,8},{10,11... | collective-permute-start | bytes 491528 | tf_op jit(solution)/shard_map/ppermute | solution.py:375
  5.2 10.0 %collective-permute-start.4 = (f32[2,5,32,128]{3,2,1,0:T(8,128)S(1)}, f32[2,5,32,128]{3,2,1,0:T(8,128)S(1)}, u32[]{:S(2)}, u32[]{:S(2)}) collective-permute-start(f32[2,5,32,128]{3,2,1,0:T(8,128)S(1)} %get-tuple-element.25), channel_id=1, source_target_pairs={{0,3},{1,2},{2,1},{3,0},{4,7},{5,6},{6,5},{7,4},{8,11},{9,10},{10,... | collective-permute-start | bytes 491528 | tf_op jit(solution)/shard_map/ppermute | solution.py:375
  7.7 13.5 %collective-permute-start = (f32[392,128]{1,0:T(8,128)S(1)}, f32[392,128]{1,0:T(8,128)S(1)}, u32[]{:S(2)}, u32[]{:S(2)}) collective-permute-start(f32[392,128]{1,0:T(8,128)S(1)} %get-tuple-element.21), channel_id=1, source_target_pairs={{0,4},{4,0},{8,12},{12,8},{16,20},{20,16},{24,28},{28,24},{1,5},{5... | collective-permute-start | bytes 602120 | tf_op jit(solution)/shard_map/ppermute | solution.py:363
  15.3 14.1 %collective-permute-start.5 = (f32[384,128]{1,0:T(8,128)S(1)}, f32[384,128]{1,0:T(8,128)S(1)}, u32[]{:S(2)}, u32[]{:S(2)}) collective-permute-start(f32[384,128]{1,0:T(8,128)S(1)} %get-tuple-element.26), channel_id=1, source_target_pairs={{0,4},{4,0},{8,12},{12,8},{16,20},{20,16},{24,28},{28,24},{1,5},{5... | collective-permute-start | bytes 589832 | tf_op jit(solution)/shard_map/ppermute | solution.py:363
  15.3 5.8 %collective-permute-start.2 = (f32[200,128]{1,0:T(8,128)S(1)}, f32[200,128]{1,0:T(8,128)S(1)}, u32[]{:S(2)}, u32[]{:S(2)}) collective-permute-start(f32[200,128]{1,0:T(8,128)S(1)} %get-tuple-element.23), channel_id=1, source_target_pairs={{4,8},{12,16},{20,24},{28,0},{8,4},{16,12},{24,20},{0,28},{5,9},{1... | collective-permute-start | bytes 307208 | tf_op jit(solution)/shard_map/ppermute | solution.py:368
  17.9 10.8 %collective-permute-start.1 = (f32[192,128]{1,0:T(8,128)S(1)}, f32[192,128]{1,0:T(8,128)S(1)}, u32[]{:S(2)}, u32[]{:S(2)}) collective-permute-start(f32[192,128]{1,0:T(8,128)S(1)} %get-tuple-element.22), channel_id=1, source_target_pairs={{4,8},{12,16},{20,24},{28,0},{8,4},{16,12},{24,20},{0,28},{5,9},{1... | collective-permute-start | bytes 294920 | tf_op jit(solution)/shard_map/ppermute | solution.py:368
  18.1 11.3 %collective-permute-start.6 = (f32[192,128]{1,0:T(8,128)S(1)}, f32[192,128]{1,0:T(8,128)S(1)}, u32[]{:S(2)}, u32[]{:S(2)}) collective-permute-start(f32[192,128]{1,0:T(8,128)S(1)} %edges.3), channel_id=1, source_target_pairs={{4,8},{12,16},{20,24},{28,0},{8,4},{16,12},{24,20},{0,28},{5,9},{1... | collective-permute-start | bytes 294920 | tf_op jit(solution)/shard_map/ppermute | solution.py:368
  21.8 10.4 %collective-permute-start.8 = (f32[2,5,32,128]{3,2,1,0:T(8,128)S(1)}, f32[2,5,32,128]{3,2,1,0:T(8,128)S(1)}, u32[]{:S(2)}, u32[]{:S(2)}) collective-permute-start(f32[2,5,32,128]{3,2,1,0:T(8,128)S(1)} %smooth.6), channel_id=1, source_target_pairs={{0,2},{1,3},{2,0},{3,1},{4,6},{5,7},{6,4},{7,5},{8,10},{9,11},{10,... | collective-permute-start | bytes 491528 | tf_op jit(solution)/shard_map/ppermute | solution.py:375
  26.1 5.5 %collective-permute-start.9 = (f32[192,128]{1,0:T(8,128)S(1)}, f32[192,128]{1,0:T(8,128)S(1)}, u32[]{:S(2)}, u32[]{:S(2)}) collective-permute-start(f32[192,128]{1,0:T(8,128)S(1)} %get-tuple-element.30), channel_id=1, source_target_pairs={{4,8},{12,16},{20,24},{28,0},{8,4},{16,12},{24,20},{0,28},{5,9},{1... | collective-permute-start | bytes 294920 | tf_op jit(solution)/shard_map/ppermute | solution.py:368
  31.2 3.7 %collective-permute-start.7 = (f32[4,2,16,600]{3,2,1,0:T(8,128)S(1)}, f32[4,2,16,600]{3,2,1,0:T(8,128)S(1)}, u32[]{:S(2)}, u32[]{:S(2)}) collective-permute-start(f32[4,2,16,600]{3,2,1,0:T(8,128)S(1)} %slice.8), channel_id=1, source_target_pairs={{0,4},{4,0},{8,12},{12,8},{16,20},{20,16},{24,28},{28,24},{1,5},{5... | collective-permute-start | bytes 921608 | tf_op jit(solution)/shard_map/ppermute | solution.py:400
  33.4 1.5 %collective-permute-start.10 = (f32[2,2,16,600]{3,2,1,0:T(8,128)S(1)}, f32[2,2,16,600]{3,2,1,0:T(8,128)S(1)}, u32[]{:S(2)}, u32[]{:S(2)}) collective-permute-start(f32[2,2,16,600]{3,2,1,0:T(8,128)S(1)} %slice.9), channel_id=1, source_target_pairs={{0,4},{4,0},{8,12},{12,8},{16,20},{20,16},{24,28},{28,24},{1,5},{5... | collective-permute-start | bytes 460808 | tf_op jit(solution)/shard_map/ppermute | solution.py:400
  35.0 4.6 %collective-permute-start.11 = (f32[2,16,600]{2,1,0:T(8,128)S(1)}, f32[2,16,600]{2,1,0:T(8,128)S(1)}, u32[]{:S(2)}, u32[]{:S(2)}) collective-permute-start(f32[2,16,600]{2,1,0:T(8,128)S(1)} %get-tuple-element.32), channel_id=1, source_target_pairs={{0,8},{4,12},{8,0},{12,4},{16,24},{20,28},{24,16},{28,20},{1,9},{5... | collective-permute-start | bytes 230408 | tf_op jit(solution)/shard_map/ppermute | solution.py:407
  36.3 5.4 %collective-permute-start.12 = (f32[2,16,600]{2,1,0:T(8,128)S(1)}, f32[2,16,600]{2,1,0:T(8,128)S(1)}, u32[]{:S(2)}, u32[]{:S(2)}) collective-permute-start(f32[2,16,600]{2,1,0:T(8,128)S(1)} %get-tuple-element.33), channel_id=1, source_target_pairs={{0,16},{4,20},{8,24},{12,28},{16,0},{20,4},{24,8},{28,12},{1,17},{... | collective-permute-start | bytes 230408 | tf_op jit(solution)/shard_map/ppermute | solution.py:407
  37.9 5.3 %collective-permute-start.13 = (f32[2,16,600]{2,1,0:T(8,128)S(1)}, f32[2,16,600]{2,1,0:T(8,128)S(1)}, u32[]{:S(2)}, u32[]{:S(2)}) collective-permute-start(f32[2,16,600]{2,1,0:T(8,128)S(1)} %get-tuple-element.34), channel_id=1, source_target_pairs={{0,24},{4,28},{8,16},{12,20},{16,8},{20,12},{24,0},{28,4},{1,25},{... | collective-permute-start | bytes 230408 | tf_op jit(solution)/shard_map/ppermute | solution.py:407

commit v10 on v9

--- a/solution.py
+++ b/solution.py
@@ -111,24 +111,25 @@
                 for r in range(rows):
                     piece = values[at : at + GROUP, r * width : (r + 1) * width]
                     outs[slot][b, r, span] = piece
-                if slot not in edged:
+                if slot not in sum(edged, ()):
                     continue
+                group = [slot in g for g in edged].index(True)
                 for r in range(PASSES):
                     row = (rows - PASSES + r) * width
                     last = values[at : at + GROUP, row : row + width]
                     first = values[at : at + GROUP, r * width : (r + 1) * width]
-                    to = edge_base(edged.index(slot), b, r, vectors) + i * GROUP
+                    to = edge_base(sum(edged, ()).index(slot), b, r, vectors) + i * GROUP
                     pair[to : to + GROUP] = pick(even, last, first)
-                    to = edge_base(0, b, r, vectors) + i * GROUP
-                    crosses[edged.index(slot)][to : to + GROUP] = pick(even, first, last)
+                    to = edge_base(edged[group].index(slot), b, r, vectors) + i * GROUP
+                    crosses[group][to : to + GROUP] = pick(even, first, last)
 
 
 def transform(field, table, coefficient, slots, edged):
     vectors, rows, steps, width = field.shape
     chunk = jax.ShapeDtypeStruct((2, rows, vectors, width), jnp.float32)
     size = edge_base(1, 0, 0, vectors)
-    pair = (len(edged) * size + GROUP, width)
-    crosses = [(size * bool(edged) + GROUP, width)] + [(size, width)] * (len(edged) - 1)
+    pair = (sum(map(len, edged)) * size + GROUP, width)
+    crosses = [(len(g) * size + GROUP * (i == 0), width) for i, g in enumerate(edged)]
     edges = [jax.ShapeDtypeStruct(shape, jnp.float32) for shape in (pair, *crosses)]
     hbm = pl.BlockSpec(memory_space=pltpu.HBM)
     vmem = pl.BlockSpec(memory_space=pltpu.VMEM)
@@ -369,39 +370,36 @@
 
 
 def paired_shards(field, coefficient, split_of, table, freq_count, strips):
-    chunks, pair, crosses = transform(field, table, coefficient, freq_count, (2, 0))
+    chunks, pair, crosses = transform(field, table, coefficient, freq_count, ((2,), (0, 1)))
 
     def swap(m, chunk):
         return lax.ppermute(chunk, "freq", xor_pairs(freq_count, m))
 
-    def relax(chunk, pair, pair_slot, cross):
-        return smooth(chunk, pair, pair_slot, cross, 0, coefficients)
-
-    first = swap(1, chunks[1])
+    def relax(chunk, pair, pair_slot, cross, cross_slot):
+        return smooth(chunk, pair, pair_slot, cross, cross_slot, coefficients)
+
     third = swap(3, chunks[3])
     cross2 = to_cross(crosses[0], strips)
     pair = to_pair(pair, strips)
-    cross0 = to_cross(crosses[1], strips)
+    cross01 = to_cross(crosses[1], strips)
     coefficients = (coefficient, pair, cross2)
     split = split_of()
-    second = swap(2, relax(chunks[2], pair, 0, cross2))
-    own = relax(chunks[0], pair, 1, cross0)
-    (cross1,) = edges([first], (0,), False)
-    cross1 = to_cross(cross1, strips)
-    pair, cross3 = edges([first, third], (1,))
+    second = swap(2, relax(chunks[2], pair, 0, cross2, 0))
+    pair3, cross3 = edges([third], (0,))
     cross3 = to_cross(cross3, strips)
-    pair = to_pair(pair, strips)
-    first = relax(first, pair, 0, cross1)
-    third = relax(third, pair, 1, cross3)
-    most = combine({0: own, 1: first}, split, 2, strips, True, (2, 3))
+    pair3 = to_pair(pair3, strips)
+    first = swap(1, relax(chunks[1], pair, 2, cross01, 1))
+    own = relax(chunks[0], pair, 1, cross01, 0)
+    third = relax(third, pair3, 0, cross3, 0)
+    most = combine({0: own, 3: third}, split, 2, strips, True, (1, 2))
 
     def to_core(partial):
         send = partial[partial.shape[0] // 2 :]
         return lax.ppermute(send, "seabed", xor_pairs(strips, 1))
 
     most_moved = to_core(most)
-    tail = combine({2: second, 3: third}, split, 2, strips // 2, True)
-    chips = merge((2, 3), 2, most, most_moved, tail, to_core(tail))
+    tail = combine({1: first, 2: second}, split, 2, strips // 2, True)
+    chips = merge((1, 2), 2, most, most_moved, tail, to_core(tail))
     total = chips[0]
     for d in range(1, strips // 2):
         total = total + lax.ppermute(chips[d], "seabed", xor_pairs(strips, 2 * d))
@@ -409,7 +407,7 @@
 
 
 def plain_shards(field, coefficient, split_of, table, freq_count, strips):
-    spectrum, pair_c, (cross_c,) = transform(field, table, coefficient, freq_count, ())
+    spectrum, pair_c, (cross_c,) = transform(field, table, coefficient, freq_count, ((),))
     spectrum = jnp.stack(spectrum)
     spectrum = lax.all_to_all(spectrum, "freq", split_axis=0, concat_axis=0, tiled=True)
     chunks = list(spectrum)
@@ -440,14 +438,7 @@
     table = transform_operand(steps, freq_count, order)
     field = jnp.transpose(uplift, (0, 2, 1, 3))
     run = paired_shards if paired else plain_shards
-    total = run(
-        field,
-        coefficient,
-        lambda: split_transfer(transfer[0]),
-        table,
-        freq_count,
-        strips,
-    )
+    total = run(field, coefficient, lambda: split_transfer(transfer[0]), table, freq_count, strips)
     return jnp.transpose(total, (1, 0, 2))[:, None]
 
 

time: 44.1 us -> 42 us (0.952)
  starting transfers between devices: 19.2 us -> 16.2 us
  local copies, waits for them, and re-layouts: 0.72 us -> 1.4 us
    ppermute x4 -> x3, starting transfers between devices: 7.85 us -> 5.19 us  [to_cross(): return lax.ppermute(edge, 'seabed', inner + [(b, a) for a, b in inner])]
    ppermute x3, waiting for transfers between devices: 7.53 us -> 5.56 us  [swap(): return lax.ppermute(chunk, 'freq', xor_pairs(freq_count, m))]
    ppermute x4 -> x3, waiting for transfers between devices: 0.88 us -> 2.37 us  [to_cross(): return lax.ppermute(edge, 'seabed', inner + [(b, a) for a, b in inner])]
    ppermute x3, starting transfers between devices: 7.41 us -> 6.59 us  [swap(): return lax.ppermute(chunk, 'freq', xor_pairs(freq_count, m))]
    unnamed x2, local copies, waits for them, and re-layouts: 0.01 us -> 0.69 us
    ppermute x3, waiting for transfers between devices: 4.77 us -> 5.34 us  [paired_shards(): total = total + lax.ppermute(chips[d], 'seabed', xor_pairs(strips, 2 * d))]
    ppermute x2, starting transfers between devices: 0.07 us -> 0.63 us  [to_pair(): return lax.ppermute(edge, 'seabed', xor_pairs(strips, 1))]
  transfers between devices with their start and end apart: 14 -> 13, of which waited for: 8 -> 8; matrix products, arithmetic and copies ran while one was open for 0% -> 0% of each run, Pallas kernels for 17% -> 17%
where the time goes in v10:
time: 42 us; the launch traced here: 41.8 us
  starting transfers between devices  16.2 us (39%)
  waiting for transfers between devices  14.6 us (35%)
  Pallas kernels  9.43 us (22%)
  local copies, waits for them, and re-layouts  1.4 us (3%)
    ppermute x3, starting transfers between devices, swap(): return lax.ppermute(chunk, 'freq', xor_pairs(freq_count, m))  6.59 us
    ppermute x3, waiting for transfers between devices, swap(): return lax.ppermute(chunk, 'freq', xor_pairs(freq_count, m))  5.56 us
    ppermute x3, waiting for transfers between devices, paired_shards(): total = total + lax.ppermute(chips[d], 'seabed', xor_pairs(strips, 2 * d))  5.34 us
    ppermute x3, starting transfers between devices, to_cross(): return lax.ppermute(edge, 'seabed', inner + [(b, a) for a, b in inner])  5.19 us
    ppermute x3, starting transfers between devices, paired_shards(): total = total + lax.ppermute(chips[d], 'seabed', xor_pairs(strips, 2 * d))  3.61 us
    pallas_call x4, Pallas kernels, smooth(): pl.pallas_call(functools.partial(smooth_kernel, pair_slot, cross_slot), o...  2.62 us
    pallas_call x1, Pallas kernels, split_transfer(): pl.pallas_call(split_kernel, out_shape=[jax.ShapeDtypeStruct((parts, cell...  2.44 us
    ppermute x3, waiting for transfers between devices, to_cross(): return lax.ppermute(edge, 'seabed', inner + [(b, a) for a, b in inner])  2.37 us
  transfers between devices with their start and end apart: 13, of which 8 were waited for; matrix products, arithmetic and copies ran while one was open for 0% of the time, Pallas kernels for 17%

profile of v10, /device:TPU:0, one launch (start us, length us, event | category | flops | bytes accessed | tf_op | source)
XLA Modules:
  0.0 41.8 jit_solution(17112673265146111373)
XLA Ops:
  0.0 2.1 %transform.1 = (f32[2,5,32,128]{3,2,1,0:T(8,128)S(1)}, f32[2,5,32,128]{3,2,1,0:T(8,128)S(1)}, f32[2,5,32,128]{3,2,1,0:T(8,128)S(1)}, f32[2,5,32,128]{3,2,1,0:T(8...) custom-call(bf16[32,5,32,128]{3,2,1,0:T(8,128)(2,1)} %bitcast.7, ...), custom_call_target="tpu_custom_call" | custom-call | flops 167772160 | bytes 1966080 | tf_op jit(solution)/shard_map/transform/pallas_call | solution.py:136
  2.6 4.7 %collective-permute-start.3 = (f32[2,5,32,128]{3,2,1,0:T(8,128)S(1)}, f32[2,5,32,128]{3,2,1,0:T(8,128)S(1)}, u32[]{:S(2)}, u32[]{:S(2)}) collective-permute-start(f32[2,5,32,128]{3,2,1,0:T(8,128)S(1)} %get-tuple-element.24), channel_id=1, source_target_pairs={{0,3},{1,2},{2,1},{3,0},{4,7},{5,6},{6,5},{7,4},{8,11},{9,10},{10,... | collective-permute-start | bytes 491528 | tf_op jit(solution)/shard_map/ppermute | solution.py:376
  7.3 2.2 %collective-permute-start.1 = (f32[384,128]{1,0:T(8,128)S(1)}, f32[384,128]{1,0:T(8,128)S(1)}, u32[]{:S(2)}, u32[]{:S(2)}) collective-permute-start(f32[384,128]{1,0:T(8,128)S(1)} %get-tuple-element.22), channel_id=1, source_target_pairs={{4,8},{12,16},{20,24},{28,0},{8,4},{16,12},{24,20},{0,28},{5,9},{1... | collective-permute-start | bytes 589832 | tf_op jit(solution)/shard_map/ppermute | solution.py:369
  10.0 2.2 %collective-permute-done.3.refs_0_.chunk = f32[2,5,32,128]{3,2,1,0:T(8,128)S(1)} collective-permute-done((f32[2,5,32,128]{3,2,1,0:T(8,128)S(1)}, f32[2,5,32,128]{3,2,1,0:T(8,128)S(1)}, u32[]{:S(2)}, u32[]{:S(2)}) %collective-permute-start.3) | collective-permute-done | bytes 163872 | tf_op jit(solution)/shard_map/ppermute | solution.py:376
  12.3 2.5 %collective-permute-start.5 = (f32[192,128]{1,0:T(8,128)S(1)}, f32[192,128]{1,0:T(8,128)S(1)}, u32[]{:S(2)}, u32[]{:S(2)}) collective-permute-start(f32[192,128]{1,0:T(8,128)S(1)} %get-tuple-element.26), channel_id=1, source_target_pairs={{4,8},{12,16},{20,24},{28,0},{8,4},{16,12},{24,20},{0,28},{5,9},{1... | collective-permute-start | bytes 294920 | tf_op jit(solution)/shard_map/ppermute | solution.py:369
  14.9 2.4 %collective-permute-done.2.cross_c.cross = f32[200,128]{1,0:T(8,128)S(1)} collective-permute-done((f32[200,128]{1,0:T(8,128)S(1)}, f32[200,128]{1,0:T(8,128)S(1)}, u32[]{:S(2)}, u32[]{:S(2)}) %collective-permute-start.2) | collective-permute-done | bytes 102432 | tf_op jit(solution)/shard_map/ppermute | solution.py:369
  17.2 0.7 %copy-done = f32[5,128]{1,0:T(8,128)S(1)} copy-done((f32[5,128]{1,0:T(8,128)S(1)}, f32[5,128]{1,0:T(8,128)}, u32[]{:S(2)}) %copy-start) | copy-done | bytes 2584
  17.9 0.7 %smooth.6 = f32[2,5,32,128]{3,2,1,0:T(8,128)S(1)} custom-call(f32[2,5,32,128]{3,2,1,0:T(8,128)S(1)} %get-tuple-element.29.chunk, f32[584,128]{1,0:T(8,128)S(1)} %collective-permute-done.pair.pair_c, f32[384,128]{1,0:T(8,128)S(1)} %collective-permute-done.1.cross, f32[5,128]{1,0:T(8,128)S(1)} %copy-done, f32[584,128]{1,0:T(8,128)S(1)} %collective-permute-done.pair.pair_c, ...), custom_call_target="tpu_custom_call" | custom-call | flops 1228800 | bytes 409600 | tf_op jit(solution)/shard_map/smooth/pallas_call | solution.py:263
  18.6 0.8 %collective-permute-start.7 = (f32[2,5,32,128]{3,2,1,0:T(8,128)S(1)}, f32[2,5,32,128]{3,2,1,0:T(8,128)S(1)}, u32[]{:S(2)}, u32[]{:S(2)}) collective-permute-start(f32[2,5,32,128]{3,2,1,0:T(8,128)S(1)} %smooth.6), channel_id=1, source_target_pairs={{0,1},{1,0},{2,3},{3,2},{4,5},{5,4},{6,7},{7,6},{8,9},{9,8},{10,11... | collective-permute-start | bytes 491528 | tf_op jit(solution)/shard_map/ppermute | solution.py:376
  19.4 0.7 %smooth.7 = f32[2,5,32,128]{3,2,1,0:T(8,128)S(1)} custom-call(f32[2,5,32,128]{3,2,1,0:T(8,128)S(1)} %get-tuple-element.30.chunk, f32[584,128]{1,0:T(8,128)S(1)} %collective-permute-done.pair.pair_c, f32[200,128]{1,0:T(8,128)S(1)} %collective-permute-done.2.cross_c.cross, f32[5,128]{1,0:T(8,128)S(1)} %copy-done, ...), custom_call_target="tpu_custom_call" | custom-call | flops 1228800 | bytes 409600 | tf_op jit(solution)/shard_map/smooth/pallas_call | solution.py:263
  20.1 1.1 %collective-permute-start.8 = (f32[2,5,32,128]{3,2,1,0:T(8,128)S(1)}, f32[2,5,32,128]{3,2,1,0:T(8,128)S(1)}, u32[]{:S(2)}, u32[]{:S(2)}) collective-permute-start(f32[2,5,32,128]{3,2,1,0:T(8,128)S(1)} %smooth.7), channel_id=1, source_target_pairs={{0,2},{1,3},{2,0},{3,1},{4,6},{5,7},{6,4},{7,5},{8,10},{9,11},{10,... | collective-permute-start | bytes 491528 | tf_op jit(solution)/shard_map/ppermute | solution.py:376
  21.1 2.4 %split_transfer.1 = (bf16[2,640,600]{2,1,0:T(8,128)(2,1)S(1)}, bf16[2,640,600]{2,1,0:T(8,128)(2,1)S(1)}) custom-call(f32[2,600,640]{2,1,0:T(8,128)} %bitcast.6), custom_call_target="tpu_custom_call" | custom-call | flops 1536000 | bytes 6144000 | tf_op jit(solution)/shard_map/split_transfer/pallas_call | solution.py:166
  23.6 0.7 %smooth.4.refs_0_ = f32[2,5,32,128]{3,2,1,0:T(8,128)S(1)} custom-call(f32[2,5,32,128]{3,2,1,0:T(8,128)S(1)} %get-tuple-element.20.chunk, f32[584,128]{1,0:T(8,128)S(1)} %collective-permute-done.pair.pair_c, f32[384,128]{1,0:T(8,128)S(1)} %collective-permute-done.1.cross, f32[5,128]{1,0:T(8,128)S(1)} %copy-done, ...), custom_call_target="tpu_custom_call" | custom-call | flops 1228800 | bytes 409600 | tf_op jit(solution)/shard_map/smooth/pallas_call | solution.py:263
  24.3 0.7 %smooth.5.refs_1_ = f32[2,5,32,128]{3,2,1,0:T(8,128)S(1)} custom-call(f32[2,5,32,128]{3,2,1,0:T(8,128)S(1)} %collective-permute-done.3.refs_0_.chunk, f32[192,128]{1,0:T(8,128)S(1)} %collective-permute-done.4.pair, f32[192,128]{1,0:T(8,128)S(1)} %collective-permute-done.5.cross, f32[5,128]{1,0:T(8,128)S(1)} %copy-done, ...), custom_call_target="tpu_custom_call" | custom-call | flops 1228800 | bytes 409600 | tf_op jit(solution)/shard_map/smooth/pallas_call | solution.py:263
  24.9 1.1 %combine.2.most = f32[8,2,16,600]{3,2,1,0:T(8,128)S(1)} custom-call(f32[2,5,32,128]{3,2,1,0:T(8,128)S(1)} %smooth.4.refs_0_, f32[2,5,32,128]{3,2,1,0:T(8,128)S(1)} %smooth.5.refs_1_, bf16[2,640,600]{2,1,0:T(8,128)(2,1)S(1)} %get-tuple-element.27.refs_2_, bf16[2,640,600]{2,1,0:T(8,128)(2,1)S(1)} %get-tuple-element.28.refs_3_), custom_call_target="tpu_custom_call" | custom-call | flops 589824000 | bytes 4014080 | tf_op jit(solution)/shard_map/combine/pallas_call | solution.py:325
  26.5 2.9 %collective-permute-done.8.refs_1_ = f32[2,5,32,128]{3,2,1,0:T(8,128)S(1)} collective-permute-done((f32[2,5,32,128]{3,2,1,0:T(8,128)S(1)}, f32[2,5,32,128]{3,2,1,0:T(8,128)S(1)}, u32[]{:S(2)}, u32[]{:S(2)}) %collective-permute-start.8) | collective-permute-done | bytes 163872 | tf_op jit(solution)/shard_map/ppermute | solution.py:376
  29.5 1.1 %combine.3.tail = f32[4,2,16,600]{3,2,1,0:T(8,128)S(1)} custom-call(f32[2,5,32,128]{3,2,1,0:T(8,128)S(1)} %collective-permute-done.7.refs_0_, f32[2,5,32,128]{3,2,1,0:T(8,128)S(1)} %collective-permute-done.8.refs_1_, bf16[2,640,600]{2,1,0:T(8,128)(2,1)S(1)} %get-tuple-element.27.refs_2_, bf16[2,640,600]{2,1,0:T(8,128)(2,1)S(1)} %get-tuple-element.28.refs_3_), custom_call_target="tpu_custom_call" | custom-call | flops 589824000 | bytes 4014080 | tf_op jit(solution)/shard_map/combine/pallas_call | solution.py:325
  30.7 1.4 %collective-permute-done.9.tail_moved = f32[2,2,16,600]{3,2,1,0:T(8,128)S(1)} collective-permute-done((f32[2,2,16,600]{3,2,1,0:T(8,128)S(1)}, f32[2,2,16,600]{3,2,1,0:T(8,128)S(1)}, u32[]{:S(2)}, u32[]{:S(2)}) %collective-permute-start.9) | collective-permute-done | bytes 153632 | tf_op jit(solution)/shard_map/ppermute | solution.py:398
  32.1 1.3 %collective-permute-start.10 = (f32[2,16,600]{2,1,0:T(8,128)S(1)}, f32[2,16,600]{2,1,0:T(8,128)S(1)}, u32[]{:S(2)}, u32[]{:S(2)}) collective-permute-start(f32[2,16,600]{2,1,0:T(8,128)S(1)} %get-tuple-element.32), channel_id=1, source_target_pairs={{0,8},{4,12},{8,0},{12,4},{16,24},{20,28},{24,16},{28,20},{1,9},{5... | collective-permute-start | bytes 230408 | tf_op jit(solution)/shard_map/ppermute | solution.py:405
  33.4 2.3 %collective-permute-start.11 = (f32[2,16,600]{2,1,0:T(8,128)S(1)}, f32[2,16,600]{2,1,0:T(8,128)S(1)}, u32[]{:S(2)}, u32[]{:S(2)}) collective-permute-start(f32[2,16,600]{2,1,0:T(8,128)S(1)} %get-tuple-element.33), channel_id=1, source_target_pairs={{0,16},{4,20},{8,24},{12,28},{16,0},{20,4},{24,8},{28,12},{1,17},{... | collective-permute-start | bytes 230408 | tf_op jit(solution)/shard_map/ppermute | solution.py:405
  35.8 0.9 %collective-permute-done.10 = f32[2,16,600]{2,1,0:T(8,128)S(1)} collective-permute-done((f32[2,16,600]{2,1,0:T(8,128)S(1)}, f32[2,16,600]{2,1,0:T(8,128)S(1)}, u32[]{:S(2)}, u32[]{:S(2)}) %collective-permute-start.10) | collective-permute-done | bytes 76832 | tf_op jit(solution)/shard_map/ppermute | solution.py:405
  36.7 2.6 %collective-permute-done.11 = f32[2,16,600]{2,1,0:T(8,128)S(1)} collective-permute-done((f32[2,16,600]{2,1,0:T(8,128)S(1)}, f32[2,16,600]{2,1,0:T(8,128)S(1)}, u32[]{:S(2)}, u32[]{:S(2)}) %collective-permute-start.11) | collective-permute-done | bytes 76832 | tf_op jit(solution)/shard_map/ppermute | solution.py:405
  39.3 1.8 %collective-permute-done.12 = f32[2,16,600]{2,1,0:T(8,128)S(1)} collective-permute-done((f32[2,16,600]{2,1,0:T(8,128)S(1)}, f32[2,16,600]{2,1,0:T(8,128)S(1)}, u32[]{:S(2)}, u32[]{:S(2)}) %collective-permute-start.12) | collective-permute-done | bytes 76832 | tf_op jit(solution)/shard_map/ppermute | solution.py:405
  41.1 0.7 %copy.5 = f32[16,1,2,600]{3,2,1,0:T(2,128)} copy(f32[16,1,2,600]{3,0,2,1:T(8,128)S(1)} %add_bitcast_fusion) | data formatting | bytes 153600 | tf_op jit(solution)/shard_map/broadcast_in_dim | solution.py:442
  (18 shorter events, 1.7 us)
Async XLA Ops:
  2.1 15.2 %collective-permute-start = (f32[584,128]{1,0:T(8,128)S(1)}, f32[584,128]{1,0:T(8,128)S(1)}, u32[]{:S(2)}, u32[]{:S(2)}) collective-permute-start(f32[584,128]{1,0:T(8,128)S(1)} %get-tuple-element.21), channel_id=1, source_target_pairs={{0,4},{4,0},{8,12},{12,8},{16,20},{20,16},{24,28},{28,24},{1,5},{5... | collective-permute-start | bytes 897032 | tf_op jit(solution)/shard_map/ppermute | solution.py:364
  2.6 9.6 %collective-permute-start.3 = (f32[2,5,32,128]{3,2,1,0:T(8,128)S(1)}, f32[2,5,32,128]{3,2,1,0:T(8,128)S(1)}, u32[]{:S(2)}, u32[]{:S(2)}) collective-permute-start(f32[2,5,32,128]{3,2,1,0:T(8,128)S(1)} %get-tuple-element.24), channel_id=1, source_target_pairs={{0,3},{1,2},{2,1},{3,0},{4,7},{5,6},{6,5},{7,4},{8,11},{9,10},{10,... | collective-permute-start | bytes 491528 | tf_op jit(solution)/shard_map/ppermute | solution.py:376
  7.3 9.9 %collective-permute-start.1 = (f32[384,128]{1,0:T(8,128)S(1)}, f32[384,128]{1,0:T(8,128)S(1)}, u32[]{:S(2)}, u32[]{:S(2)}) collective-permute-start(f32[384,128]{1,0:T(8,128)S(1)} %get-tuple-element.22), channel_id=1, source_target_pairs={{4,8},{12,16},{20,24},{28,0},{8,4},{16,12},{24,20},{0,28},{5,9},{1... | collective-permute-start | bytes 589832 | tf_op jit(solution)/shard_map/ppermute | solution.py:369
  9.5 7.7 %collective-permute-start.2 = (f32[200,128]{1,0:T(8,128)S(1)}, f32[200,128]{1,0:T(8,128)S(1)}, u32[]{:S(2)}, u32[]{:S(2)}) collective-permute-start(f32[200,128]{1,0:T(8,128)S(1)} %get-tuple-element.23), channel_id=1, source_target_pairs={{4,8},{12,16},{20,24},{28,0},{8,4},{16,12},{24,20},{0,28},{5,9},{1... | collective-permute-start | bytes 307208 | tf_op jit(solution)/shard_map/ppermute | solution.py:369
  12.2 12.0 %collective-permute-start.4 = (f32[192,128]{1,0:T(8,128)S(1)}, f32[192,128]{1,0:T(8,128)S(1)}, u32[]{:S(2)}, u32[]{:S(2)}) collective-permute-start(f32[192,128]{1,0:T(8,128)S(1)} %get-tuple-element.25), channel_id=1, source_target_pairs={{0,4},{4,0},{8,12},{12,8},{16,20},{20,16},{24,28},{28,24},{1,5},{5... | collective-permute-start | bytes 294920 | tf_op jit(solution)/shard_map/ppermute | solution.py:364
  12.3 12.0 %collective-permute-start.5 = (f32[192,128]{1,0:T(8,128)S(1)}, f32[192,128]{1,0:T(8,128)S(1)}, u32[]{:S(2)}, u32[]{:S(2)}) collective-permute-start(f32[192,128]{1,0:T(8,128)S(1)} %get-tuple-element.26), channel_id=1, source_target_pairs={{4,8},{12,16},{20,24},{28,0},{8,4},{16,12},{24,20},{0,28},{5,9},{1... | collective-permute-start | bytes 294920 | tf_op jit(solution)/shard_map/ppermute | solution.py:369
  17.2 0.7 %copy-start = (f32[5,128]{1,0:T(8,128)S(1)}, f32[5,128]{1,0:T(8,128)}, u32[]{:S(2)}) copy-start(f32[5,128]{1,0:T(8,128)} %own_c.7) | copy-start | bytes 7684
  18.6 8.0 %collective-permute-start.7 = (f32[2,5,32,128]{3,2,1,0:T(8,128)S(1)}, f32[2,5,32,128]{3,2,1,0:T(8,128)S(1)}, u32[]{:S(2)}, u32[]{:S(2)}) collective-permute-start(f32[2,5,32,128]{3,2,1,0:T(8,128)S(1)} %smooth.6), channel_id=1, source_target_pairs={{0,1},{1,0},{2,3},{3,2},{4,5},{5,4},{6,7},{7,6},{8,9},{9,8},{10,11... | collective-permute-start | bytes 491528 | tf_op jit(solution)/shard_map/ppermute | solution.py:376
  20.1 9.4 %collective-permute-start.8 = (f32[2,5,32,128]{3,2,1,0:T(8,128)S(1)}, f32[2,5,32,128]{3,2,1,0:T(8,128)S(1)}, u32[]{:S(2)}, u32[]{:S(2)}) collective-permute-start(f32[2,5,32,128]{3,2,1,0:T(8,128)S(1)} %smooth.7), channel_id=1, source_target_pairs={{0,2},{1,3},{2,0},{3,1},{4,6},{5,7},{6,4},{7,5},{8,10},{9,11},{10,... | collective-permute-start | bytes 491528 | tf_op jit(solution)/shard_map/ppermute | solution.py:376
  26.1 4.6 %collective-permute-start.6 = (f32[4,2,16,600]{3,2,1,0:T(8,128)S(1)}, f32[4,2,16,600]{3,2,1,0:T(8,128)S(1)}, u32[]{:S(2)}, u32[]{:S(2)}) collective-permute-start(f32[4,2,16,600]{3,2,1,0:T(8,128)S(1)} %slice.8), channel_id=1, source_target_pairs={{0,4},{4,0},{8,12},{12,8},{16,20},{20,16},{24,28},{28,24},{1,5},{5... | collective-permute-start | bytes 921608 | tf_op jit(solution)/shard_map/ppermute | solution.py:398
  30.6 1.5 %collective-permute-start.9 = (f32[2,2,16,600]{3,2,1,0:T(8,128)S(1)}, f32[2,2,16,600]{3,2,1,0:T(8,128)S(1)}, u32[]{:S(2)}, u32[]{:S(2)}) collective-permute-start(f32[2,2,16,600]{3,2,1,0:T(8,128)S(1)} %slice.9), channel_id=1, source_target_pairs={{0,4},{4,0},{8,12},{12,8},{16,20},{20,16},{24,28},{28,24},{1,5},{5... | collective-permute-start | bytes 460808 | tf_op jit(solution)/shard_map/ppermute | solution.py:398
  32.1 4.6 %collective-permute-start.10 = (f32[2,16,600]{2,1,0:T(8,128)S(1)}, f32[2,16,600]{2,1,0:T(8,128)S(1)}, u32[]{:S(2)}, u32[]{:S(2)}) collective-permute-start(f32[2,16,600]{2,1,0:T(8,128)S(1)} %get-tuple-element.32), channel_id=1, source_target_pairs={{0,8},{4,12},{8,0},{12,4},{16,24},{20,28},{24,16},{28,20},{1,9},{5... | collective-permute-start | bytes 230408 | tf_op jit(solution)/shard_map/ppermute | solution.py:405
  33.4 5.9 %collective-permute-start.11 = (f32[2,16,600]{2,1,0:T(8,128)S(1)}, f32[2,16,600]{2,1,0:T(8,128)S(1)}, u32[]{:S(2)}, u32[]{:S(2)}) collective-permute-start(f32[2,16,600]{2,1,0:T(8,128)S(1)} %get-tuple-element.33), channel_id=1, source_target_pairs={{0,16},{4,20},{8,24},{12,28},{16,0},{20,4},{24,8},{28,12},{1,17},{... | collective-permute-start | bytes 230408 | tf_op jit(solution)/shard_map/ppermute | solution.py:405
  35.8 5.3 %collective-permute-start.12 = (f32[2,16,600]{2,1,0:T(8,128)S(1)}, f32[2,16,600]{2,1,0:T(8,128)S(1)}, u32[]{:S(2)}, u32[]{:S(2)}) collective-permute-start(f32[2,16,600]{2,1,0:T(8,128)S(1)} %get-tuple-element.34), channel_id=1, source_target_pairs={{0,24},{4,28},{8,16},{12,20},{16,8},{20,12},{24,0},{28,4},{1,25},{... | collective-permute-start | bytes 230408 | tf_op jit(solution)/shard_map/ppermute | solution.py:405

commit v11 on v10

--- a/solution.py
+++ b/solution.py
@@ -64,22 +64,17 @@
 
 def transform_kernel(slots, edged, field_hbm, table_hbm, own_hbm, *refs):
     outs, pair, crosses = refs[:slots], refs[slots], refs[slots + 1 : -6]
-    field, table, own_c, field_sem, table_sem, own_sem = refs[-6:]
+    own_c, field, table, field_sem, table_sem, own_sem = refs[-6:]
     vectors, rows, steps, width = field.shape
     blocks = vectors // GROUP
     even = even_strip()
     source = lax.axis_index("freq") if table_hbm.shape[0] > 1 else 0
+    get_field = pltpu.make_async_copy(field_hbm, field, field_sem)
+    get_field.start()
     get_table = pltpu.make_async_copy(table_hbm.at[source], table, table_sem)
     get_table.start()
     get_own = pltpu.make_async_copy(own_hbm, own_c, own_sem)
     get_own.start()
-
-    def get(i):
-        at = pl.ds(i * GROUP, GROUP)
-        return pltpu.make_async_copy(field_hbm.at[at], field.at[at], field_sem.at[i])
-
-    for i in range(blocks):
-        get(i).start()
     get_own.wait()
     rim = PASSES - 1
     last_c, first_c = own_c[rows - rim :], own_c[:rim]
@@ -96,8 +91,8 @@
         (column >= mine * steps) & (column < (mine + 1) * steps), short[:, None], 0.0
     )
     full = full.reshape(-1, short.shape[1]).astype(jnp.bfloat16)
+    get_field.wait()
     for i in range(blocks):
-        get(i).wait()
         span = slice(i * GROUP, (i + 1) * GROUP)
         data = jnp.concatenate(
             [field[span, r].reshape(GROUP * steps, width) for r in range(rows)], axis=1
@@ -130,7 +125,7 @@
     size = edge_base(1, 0, 0, vectors)
     pair = (sum(map(len, edged)) * size + GROUP, width)
     crosses = [(len(g) * size + GROUP * (i == 0), width) for i, g in enumerate(edged)]
-    edges = [jax.ShapeDtypeStruct(shape, jnp.float32) for shape in (pair, *crosses)]
+    edges = [jax.ShapeDtypeStruct(shape, jnp.float32) for shape in (pair, *crosses, coefficient.shape)]
     hbm = pl.BlockSpec(memory_space=pltpu.HBM)
     vmem = pl.BlockSpec(memory_space=pltpu.VMEM)
     outs = pl.pallas_call(
@@ -141,8 +136,7 @@
         scratch_shapes=[
             pltpu.VMEM(field.shape, field.dtype),
             pltpu.VMEM(table.shape[1:], table.dtype),
-            pltpu.VMEM(coefficient.shape, coefficient.dtype),
-            pltpu.SemaphoreType.DMA((vectors // GROUP,)),
+            pltpu.SemaphoreType.DMA(()),
             pltpu.SemaphoreType.DMA(()),
             pltpu.SemaphoreType.DMA(()),
         ],
@@ -153,7 +147,7 @@
         ),
         name="transform",
     )(*map(in_hbm, (field, table, coefficient)))
-    return outs[:slots], outs[slots], outs[slots + 1 :]
+    return outs[:slots], outs[slots], outs[slots + 1 : -1], outs[-1]
 
 
 def split_kernel(x_ref, high_ref, low_ref):
@@ -370,7 +364,7 @@
 
 
 def paired_shards(field, coefficient, split_of, table, freq_count, strips):
-    chunks, pair, crosses = transform(field, table, coefficient, freq_count, ((2,), (0, 1)))
+    chunks, pair, crosses, coefficient = transform(field, table, coefficient, freq_count, ((2,), (1,), (0,)))
 
     def swap(m, chunk):
         return lax.ppermute(chunk, "freq", xor_pairs(freq_count, m))
@@ -381,15 +375,16 @@
     third = swap(3, chunks[3])
     cross2 = to_cross(crosses[0], strips)
     pair = to_pair(pair, strips)
-    cross01 = to_cross(crosses[1], strips)
+    cross1 = to_cross(crosses[1], strips)
+    cross0 = to_cross(crosses[2], strips)
     coefficients = (coefficient, pair, cross2)
     split = split_of()
     second = swap(2, relax(chunks[2], pair, 0, cross2, 0))
     pair3, cross3 = edges([third], (0,))
     cross3 = to_cross(cross3, strips)
     pair3 = to_pair(pair3, strips)
-    first = swap(1, relax(chunks[1], pair, 2, cross01, 1))
-    own = relax(chunks[0], pair, 1, cross01, 0)
+    first = swap(1, relax(chunks[1], pair, 1, cross1, 0))
+    own = relax(chunks[0], pair, 2, cross0, 0)
     third = relax(third, pair3, 0, cross3, 0)
     most = combine({0: own, 3: third}, split, 2, strips, True, (1, 2))
 
@@ -407,7 +402,7 @@
 
 
 def plain_shards(field, coefficient, split_of, table, freq_count, strips):
-    spectrum, pair_c, (cross_c,) = transform(field, table, coefficient, freq_count, ((),))
+    spectrum, pair_c, (cross_c,), coefficient = transform(field, table, coefficient, freq_count, ((),))
     spectrum = jnp.stack(spectrum)
     spectrum = lax.all_to_all(spectrum, "freq", split_axis=0, concat_axis=0, tiled=True)
     chunks = list(spectrum)

time: 42 us -> 40.4 us (0.962)
  waiting for transfers between devices: 14.6 us -> 11.6 us
  starting transfers between devices: 16.2 us -> 18.6 us
  local copies, waits for them, and re-layouts: 1.4 us -> 0.71 us
    ppermute x3 -> x4, waiting for transfers between devices: 2.37 us -> 0.01 us  [to_cross(): return lax.ppermute(edge, 'seabed', inner + [(b, a) for a, b in inner])]
    ppermute x3, starting transfers between devices: 6.59 us -> 8.6 us  [swap(): return lax.ppermute(chunk, 'freq', xor_pairs(freq_count, m))]
    unnamed x2 -> x0, local copies, waits for them, and re-layouts: 0.69 us -> none
    ppermute x3, waiting for transfers between devices: 5.56 us -> 4.89 us  [swap(): return lax.ppermute(chunk, 'freq', xor_pairs(freq_count, m))]
    ppermute x3 -> x4, starting transfers between devices: 5.19 us -> 5.7 us  [to_cross(): return lax.ppermute(edge, 'seabed', inner + [(b, a) for a, b in inner])]
  transfers between devices with their start and end apart: 13 -> 14, of which waited for: 8 -> 7; matrix products, arithmetic and copies ran while one was open for 0% -> 0% of each run, Pallas kernels for 17% -> 18%
where the time goes in v11:
time: 40.4 us; the launch traced here: 40.2 us
  starting transfers between devices  18.6 us (46%)
  waiting for transfers between devices  11.6 us (29%)
  Pallas kernels  9.11 us (23%)
  local copies, waits for them, and re-layouts  0.71 us (2%)
    ppermute x3, starting transfers between devices, swap(): return lax.ppermute(chunk, 'freq', xor_pairs(freq_count, m))  8.6 us
    ppermute x4, starting transfers between devices, to_cross(): return lax.ppermute(edge, 'seabed', inner + [(b, a) for a, b in inner])  5.7 us
    ppermute x3, waiting for transfers between devices, paired_shards(): total = total + lax.ppermute(chips[d], 'seabed', xor_pairs(strips, 2 * d))  5.32 us
    ppermute x3, waiting for transfers between devices, swap(): return lax.ppermute(chunk, 'freq', xor_pairs(freq_count, m))  4.89 us
    ppermute x3, starting transfers between devices, paired_shards(): total = total + lax.ppermute(chips[d], 'seabed', xor_pairs(strips, 2 * d))  3.55 us
    pallas_call x4, Pallas kernels, smooth(): pl.pallas_call(functools.partial(smooth_kernel, pair_slot, cross_slot), o...  2.62 us
    pallas_call x1, Pallas kernels, split_transfer(): pl.pallas_call(split_kernel, out_shape=[jax.ShapeDtypeStruct((parts, cell...  2.45 us
    pallas_call x2, Pallas kernels, combine(): pl.pallas_call(functools.partial(combine_kernel, indices, owners_in, pair...  2.23 us
  transfers between devices with their start and end apart: 14, of which 7 were waited for; matrix products, arithmetic and copies ran while one was open for 0% of the time, Pallas kernels for 18%

profile of v11, /device:TPU:0, one launch (start us, length us, event | category | flops | bytes accessed | tf_op | source)
XLA Modules:
  0.0 40.2 jit_solution(18365220092634015075)
XLA Ops:
  0.0 1.7 %transform.1 = (f32[2,5,32,128]{3,2,1,0:T(8,128)S(1)}, f32[2,5,32,128]{3,2,1,0:T(8,128)S(1)}, f32[2,5,32,128]{3,2,1,0:T(8,128)S(1)}, f32[2,5,32,128]{3,2,1,0:T(8...) custom-call(bf16[32,5,32,128]{3,2,1,0:T(8,128)(2,1)} %bitcast.7, ...), custom_call_target="tpu_custom_call" | custom-call | flops 167772160 | bytes 1966080 | tf_op jit(solution)/shard_map/transform/pallas_call | solution.py:131
  1.7 0.6 %collective-permute-start = (f32[584,128]{1,0:T(8,128)S(1)}, f32[584,128]{1,0:T(8,128)S(1)}, u32[]{:S(2)}, u32[]{:S(2)}) collective-permute-start(f32[584,128]{1,0:T(8,128)S(1)} %get-tuple-element.23), channel_id=1, source_target_pairs={{0,4},{4,0},{8,12},{12,8},{16,20},{20,16},{24,28},{28,24},{1,5},{5... | collective-permute-start | bytes 897032 | tf_op jit(solution)/shard_map/ppermute | solution.py:358
  2.3 4.7 %collective-permute-start.3 = (f32[2,5,32,128]{3,2,1,0:T(8,128)S(1)}, f32[2,5,32,128]{3,2,1,0:T(8,128)S(1)}, u32[]{:S(2)}, u32[]{:S(2)}) collective-permute-start(f32[2,5,32,128]{3,2,1,0:T(8,128)S(1)} %get-tuple-element.27), channel_id=1, source_target_pairs={{0,3},{1,2},{2,1},{3,0},{4,7},{5,6},{6,5},{7,4},{8,11},{9,10},{10,... | collective-permute-start | bytes 491528 | tf_op jit(solution)/shard_map/ppermute | solution.py:370
  7.0 2.2 %collective-permute-start.2 = (f32[200,128]{1,0:T(8,128)S(1)}, f32[200,128]{1,0:T(8,128)S(1)}, u32[]{:S(2)}, u32[]{:S(2)}) collective-permute-start(f32[200,128]{1,0:T(8,128)S(1)} %get-tuple-element.26), channel_id=1, source_target_pairs={{4,8},{12,16},{20,24},{28,0},{8,4},{16,12},{24,20},{0,28},{5,9},{1... | collective-permute-start | bytes 307208 | tf_op jit(solution)/shard_map/ppermute | solution.py:363
  9.6 2.2 %collective-permute-done.3.refs_0_.chunk = f32[2,5,32,128]{3,2,1,0:T(8,128)S(1)} collective-permute-done((f32[2,5,32,128]{3,2,1,0:T(8,128)S(1)}, f32[2,5,32,128]{3,2,1,0:T(8,128)S(1)}, u32[]{:S(2)}, u32[]{:S(2)}) %collective-permute-start.3) | collective-permute-done | bytes 163872 | tf_op jit(solution)/shard_map/ppermute | solution.py:370
  11.9 2.5 %collective-permute-start.5 = (f32[192,128]{1,0:T(8,128)S(1)}, f32[192,128]{1,0:T(8,128)S(1)}, u32[]{:S(2)}, u32[]{:S(2)}) collective-permute-start(f32[192,128]{1,0:T(8,128)S(1)} %get-tuple-element.29), channel_id=1, source_target_pairs={{4,8},{12,16},{20,24},{28,0},{8,4},{16,12},{24,20},{0,28},{5,9},{1... | collective-permute-start | bytes 294920 | tf_op jit(solution)/shard_map/ppermute | solution.py:363
  14.5 0.5 %collective-permute-start.1 = (f32[192,128]{1,0:T(8,128)S(1)}, f32[192,128]{1,0:T(8,128)S(1)}, u32[]{:S(2)}, u32[]{:S(2)}) collective-permute-start(f32[192,128]{1,0:T(8,128)S(1)} %get-tuple-element.24), channel_id=1, source_target_pairs={{4,8},{12,16},{20,24},{28,0},{8,4},{16,12},{24,20},{0,28},{5,9},{1... | collective-permute-start | bytes 294920 | tf_op jit(solution)/shard_map/ppermute | solution.py:363
  15.0 0.7 %smooth.7 = f32[2,5,32,128]{3,2,1,0:T(8,128)S(1)} custom-call(f32[2,5,32,128]{3,2,1,0:T(8,128)S(1)} %get-tuple-element.34.chunk, f32[584,128]{1,0:T(8,128)S(1)} %collective-permute-done.pair.pair_c, f32[200,128]{1,0:T(8,128)S(1)} %collective-permute-done.2.cross_c.cross, f32[5,128]{1,0:T(8,128)S(1)} %get-tuple-element.25.own_c, ...), custom_call_target="tpu_custom_call" | custom-call | flops 1228800 | bytes 409600 | tf_op jit(solution)/shard_map/smooth/pallas_call | solution.py:257
  15.7 3.9 %collective-permute-start.9 = (f32[2,5,32,128]{3,2,1,0:T(8,128)S(1)}, f32[2,5,32,128]{3,2,1,0:T(8,128)S(1)}, u32[]{:S(2)}, u32[]{:S(2)}) collective-permute-start(f32[2,5,32,128]{3,2,1,0:T(8,128)S(1)} %smooth.7), channel_id=1, source_target_pairs={{0,2},{1,3},{2,0},{3,1},{4,6},{5,7},{6,4},{7,5},{8,10},{9,11},{10,... | collective-permute-start | bytes 491528 | tf_op jit(solution)/shard_map/ppermute | solution.py:370
  19.5 0.7 %smooth.6 = f32[2,5,32,128]{3,2,1,0:T(8,128)S(1)} custom-call(f32[2,5,32,128]{3,2,1,0:T(8,128)S(1)} %get-tuple-element.32.chunk, f32[584,128]{1,0:T(8,128)S(1)} %collective-permute-done.pair.pair_c, f32[192,128]{1,0:T(8,128)S(1)} %collective-permute-done.7.cross, f32[5,128]{1,0:T(8,128)S(1)} %get-tuple-element.25.own_c, ...), custom_call_target="tpu_custom_call" | custom-call | flops 1228800 | bytes 409600 | tf_op jit(solution)/shard_map/smooth/pallas_call | solution.py:257
  20.3 2.5 %split_transfer.1 = (bf16[2,640,600]{2,1,0:T(8,128)(2,1)S(1)}, bf16[2,640,600]{2,1,0:T(8,128)(2,1)S(1)}) custom-call(f32[2,600,640]{2,1,0:T(8,128)} %bitcast.6), custom_call_target="tpu_custom_call" | custom-call | flops 1536000 | bytes 6144000 | tf_op jit(solution)/shard_map/split_transfer/pallas_call | solution.py:160
  22.8 0.7 %smooth.5.refs_1_ = f32[2,5,32,128]{3,2,1,0:T(8,128)S(1)} custom-call(f32[2,5,32,128]{3,2,1,0:T(8,128)S(1)} %collective-permute-done.3.refs_0_.chunk, f32[192,128]{1,0:T(8,128)S(1)} %collective-permute-done.4.pair, f32[192,128]{1,0:T(8,128)S(1)} %collective-permute-done.5.cross, f32[5,128]{1,0:T(8,128)S(1)} %get-tuple-element.25.own_c, ...), custom_call_target="tpu_custom_call" | custom-call | flops 1228800 | bytes 409600 | tf_op jit(solution)/shard_map/smooth/pallas_call | solution.py:257
  23.4 0.7 %smooth.4.refs_0_ = f32[2,5,32,128]{3,2,1,0:T(8,128)S(1)} custom-call(f32[2,5,32,128]{3,2,1,0:T(8,128)S(1)} %get-tuple-element.22.chunk, f32[584,128]{1,0:T(8,128)S(1)} %collective-permute-done.pair.pair_c, f32[192,128]{1,0:T(8,128)S(1)} %collective-permute-done.1.cross, f32[5,128]{1,0:T(8,128)S(1)} %get-tuple-element.25.own_c, ...), custom_call_target="tpu_custom_call" | custom-call | flops 1228800 | bytes 409600 | tf_op jit(solution)/shard_map/smooth/pallas_call | solution.py:257
  24.1 1.1 %combine.2.most = f32[8,2,16,600]{3,2,1,0:T(8,128)S(1)} custom-call(f32[2,5,32,128]{3,2,1,0:T(8,128)S(1)} %smooth.4.refs_0_, f32[2,5,32,128]{3,2,1,0:T(8,128)S(1)} %smooth.5.refs_1_, bf16[2,640,600]{2,1,0:T(8,128)(2,1)S(1)} %get-tuple-element.30.refs_2_, bf16[2,640,600]{2,1,0:T(8,128)(2,1)S(1)} %get-tuple-element.31.refs_3_), custom_call_target="tpu_custom_call" | custom-call | flops 589824000 | bytes 4014080 | tf_op jit(solution)/shard_map/combine/pallas_call | solution.py:319
  25.3 1.7 %collective-permute-done.9.refs_1_ = f32[2,5,32,128]{3,2,1,0:T(8,128)S(1)} collective-permute-done((f32[2,5,32,128]{3,2,1,0:T(8,128)S(1)}, f32[2,5,32,128]{3,2,1,0:T(8,128)S(1)}, u32[]{:S(2)}, u32[]{:S(2)}) %collective-permute-start.9) | collective-permute-done | bytes 163872 | tf_op jit(solution)/shard_map/ppermute | solution.py:370
  27.0 0.9 %collective-permute-done.8.refs_0_ = f32[2,5,32,128]{3,2,1,0:T(8,128)S(1)} collective-permute-done((f32[2,5,32,128]{3,2,1,0:T(8,128)S(1)}, f32[2,5,32,128]{3,2,1,0:T(8,128)S(1)}, u32[]{:S(2)}, u32[]{:S(2)}) %collective-permute-start.8) | collective-permute-done | bytes 163872 | tf_op jit(solution)/shard_map/ppermute | solution.py:370
  28.0 1.1 %combine.3.tail = f32[4,2,16,600]{3,2,1,0:T(8,128)S(1)} custom-call(f32[2,5,32,128]{3,2,1,0:T(8,128)S(1)} %collective-permute-done.8.refs_0_, f32[2,5,32,128]{3,2,1,0:T(8,128)S(1)} %collective-permute-done.9.refs_1_, bf16[2,640,600]{2,1,0:T(8,128)(2,1)S(1)} %get-tuple-element.30.refs_2_, bf16[2,640,600]{2,1,0:T(8,128)(2,1)S(1)} %get-tuple-element.31.refs_3_), custom_call_target="tpu_custom_call" | custom-call | flops 589824000 | bytes 4014080 | tf_op jit(solution)/shard_map/combine/pallas_call | solution.py:319
  29.2 1.4 %collective-permute-done.10.tail_moved = f32[2,2,16,600]{3,2,1,0:T(8,128)S(1)} collective-permute-done((f32[2,2,16,600]{3,2,1,0:T(8,128)S(1)}, f32[2,2,16,600]{3,2,1,0:T(8,128)S(1)}, u32[]{:S(2)}, u32[]{:S(2)}) %collective-permute-start.10) | collective-permute-done | bytes 153632 | tf_op jit(solution)/shard_map/ppermute | solution.py:393
  30.6 2.0 %collective-permute-start.11 = (f32[2,16,600]{2,1,0:T(8,128)S(1)}, f32[2,16,600]{2,1,0:T(8,128)S(1)}, u32[]{:S(2)}, u32[]{:S(2)}) collective-permute-start(f32[2,16,600]{2,1,0:T(8,128)S(1)} %get-tuple-element.36), channel_id=1, source_target_pairs={{0,8},{4,12},{8,0},{12,4},{16,24},{20,28},{24,16},{28,20},{1,9},{5... | collective-permute-start | bytes 230408 | tf_op jit(solution)/shard_map/ppermute | solution.py:400
  32.6 1.5 %collective-permute-start.12 = (f32[2,16,600]{2,1,0:T(8,128)S(1)}, f32[2,16,600]{2,1,0:T(8,128)S(1)}, u32[]{:S(2)}, u32[]{:S(2)}) collective-permute-start(f32[2,16,600]{2,1,0:T(8,128)S(1)} %get-tuple-element.37), channel_id=1, source_target_pairs={{0,16},{4,20},{8,24},{12,28},{16,0},{20,4},{24,8},{28,12},{1,17},{... | collective-permute-start | bytes 230408 | tf_op jit(solution)/shard_map/ppermute | solution.py:400
  34.2 1.2 %collective-permute-done.11 = f32[2,16,600]{2,1,0:T(8,128)S(1)} collective-permute-done((f32[2,16,600]{2,1,0:T(8,128)S(1)}, f32[2,16,600]{2,1,0:T(8,128)S(1)}, u32[]{:S(2)}, u32[]{:S(2)}) %collective-permute-start.11) | collective-permute-done | bytes 76832 | tf_op jit(solution)/shard_map/ppermute | solution.py:400
  35.4 2.5 %collective-permute-done.12 = f32[2,16,600]{2,1,0:T(8,128)S(1)} collective-permute-done((f32[2,16,600]{2,1,0:T(8,128)S(1)}, f32[2,16,600]{2,1,0:T(8,128)S(1)}, u32[]{:S(2)}, u32[]{:S(2)}) %collective-permute-start.12) | collective-permute-done | bytes 76832 | tf_op jit(solution)/shard_map/ppermute | solution.py:400
  37.9 1.6 %collective-permute-done.13 = f32[2,16,600]{2,1,0:T(8,128)S(1)} collective-permute-done((f32[2,16,600]{2,1,0:T(8,128)S(1)}, f32[2,16,600]{2,1,0:T(8,128)S(1)}, u32[]{:S(2)}, u32[]{:S(2)}) %collective-permute-start.13) | collective-permute-done | bytes 76832 | tf_op jit(solution)/shard_map/ppermute | solution.py:400
  39.5 0.7 %copy.5 = f32[16,1,2,600]{3,2,1,0:T(2,128)} copy(f32[16,1,2,600]{3,0,2,1:T(8,128)S(1)} %add_bitcast_fusion) | data formatting | bytes 153600 | tf_op jit(solution)/shard_map/broadcast_in_dim | solution.py:437
  (18 shorter events, 0.9 us)
Async XLA Ops:
  1.7 13.3 %collective-permute-start = (f32[584,128]{1,0:T(8,128)S(1)}, f32[584,128]{1,0:T(8,128)S(1)}, u32[]{:S(2)}, u32[]{:S(2)}) collective-permute-start(f32[584,128]{1,0:T(8,128)S(1)} %get-tuple-element.23), channel_id=1, source_target_pairs={{0,4},{4,0},{8,12},{12,8},{16,20},{20,16},{24,28},{28,24},{1,5},{5... | collective-permute-start | bytes 897032 | tf_op jit(solution)/shard_map/ppermute | solution.py:358
  2.3 9.6 %collective-permute-start.3 = (f32[2,5,32,128]{3,2,1,0:T(8,128)S(1)}, f32[2,5,32,128]{3,2,1,0:T(8,128)S(1)}, u32[]{:S(2)}, u32[]{:S(2)}) collective-permute-start(f32[2,5,32,128]{3,2,1,0:T(8,128)S(1)} %get-tuple-element.27), channel_id=1, source_target_pairs={{0,3},{1,2},{2,1},{3,0},{4,7},{5,6},{6,5},{7,4},{8,11},{9,10},{10,... | collective-permute-start | bytes 491528 | tf_op jit(solution)/shard_map/ppermute | solution.py:370
  7.0 7.5 %collective-permute-start.2 = (f32[200,128]{1,0:T(8,128)S(1)}, f32[200,128]{1,0:T(8,128)S(1)}, u32[]{:S(2)}, u32[]{:S(2)}) collective-permute-start(f32[200,128]{1,0:T(8,128)S(1)} %get-tuple-element.26), channel_id=1, source_target_pairs={{4,8},{12,16},{20,24},{28,0},{8,4},{16,12},{24,20},{0,28},{5,9},{1... | collective-permute-start | bytes 307208 | tf_op jit(solution)/shard_map/ppermute | solution.py:363
  9.2 10.4 %collective-permute-start.7 = (f32[192,128]{1,0:T(8,128)S(1)}, f32[192,128]{1,0:T(8,128)S(1)}, u32[]{:S(2)}, u32[]{:S(2)}) collective-permute-start(f32[192,128]{1,0:T(8,128)S(1)} %get-tuple-element.33), channel_id=1, source_target_pairs={{4,8},{12,16},{20,24},{28,0},{8,4},{16,12},{24,20},{0,28},{5,9},{1... | collective-permute-start | bytes 294920 | tf_op jit(solution)/shard_map/ppermute | solution.py:363
  11.9 10.9 %collective-permute-start.4 = (f32[192,128]{1,0:T(8,128)S(1)}, f32[192,128]{1,0:T(8,128)S(1)}, u32[]{:S(2)}, u32[]{:S(2)}) collective-permute-start(f32[192,128]{1,0:T(8,128)S(1)} %get-tuple-element.28), channel_id=1, source_target_pairs={{0,4},{4,0},{8,12},{12,8},{16,20},{20,16},{24,28},{28,24},{1,5},{5... | collective-permute-start | bytes 294920 | tf_op jit(solution)/shard_map/ppermute | solution.py:358
  11.9 10.8 %collective-permute-start.5 = (f32[192,128]{1,0:T(8,128)S(1)}, f32[192,128]{1,0:T(8,128)S(1)}, u32[]{:S(2)}, u32[]{:S(2)}) collective-permute-start(f32[192,128]{1,0:T(8,128)S(1)} %get-tuple-element.29), channel_id=1, source_target_pairs={{4,8},{12,16},{20,24},{28,0},{8,4},{16,12},{24,20},{0,28},{5,9},{1... | collective-permute-start | bytes 294920 | tf_op jit(solution)/shard_map/ppermute | solution.py:363
  14.5 8.9 %collective-permute-start.1 = (f32[192,128]{1,0:T(8,128)S(1)}, f32[192,128]{1,0:T(8,128)S(1)}, u32[]{:S(2)}, u32[]{:S(2)}) collective-permute-start(f32[192,128]{1,0:T(8,128)S(1)} %get-tuple-element.24), channel_id=1, source_target_pairs={{4,8},{12,16},{20,24},{28,0},{8,4},{16,12},{24,20},{0,28},{5,9},{1... | collective-permute-start | bytes 294920 | tf_op jit(solution)/shard_map/ppermute | solution.py:363
  15.7 11.4 %collective-permute-start.9 = (f32[2,5,32,128]{3,2,1,0:T(8,128)S(1)}, f32[2,5,32,128]{3,2,1,0:T(8,128)S(1)}, u32[]{:S(2)}, u32[]{:S(2)}) collective-permute-start(f32[2,5,32,128]{3,2,1,0:T(8,128)S(1)} %smooth.7), channel_id=1, source_target_pairs={{0,2},{1,3},{2,0},{3,1},{4,6},{5,7},{6,4},{7,5},{8,10},{9,11},{10,... | collective-permute-start | bytes 491528 | tf_op jit(solution)/shard_map/ppermute | solution.py:370
  20.2 7.8 %collective-permute-start.8 = (f32[2,5,32,128]{3,2,1,0:T(8,128)S(1)}, f32[2,5,32,128]{3,2,1,0:T(8,128)S(1)}, u32[]{:S(2)}, u32[]{:S(2)}) collective-permute-start(f32[2,5,32,128]{3,2,1,0:T(8,128)S(1)} %smooth.6), channel_id=1, source_target_pairs={{0,1},{1,0},{2,3},{3,2},{4,5},{5,4},{6,7},{7,6},{8,9},{9,8},{10,11... | collective-permute-start | bytes 491528 | tf_op jit(solution)/shard_map/ppermute | solution.py:370
  25.2 3.9 %collective-permute-start.6 = (f32[4,2,16,600]{3,2,1,0:T(8,128)S(1)}, f32[4,2,16,600]{3,2,1,0:T(8,128)S(1)}, u32[]{:S(2)}, u32[]{:S(2)}) collective-permute-start(f32[4,2,16,600]{3,2,1,0:T(8,128)S(1)} %slice.8), channel_id=1, source_target_pairs={{0,4},{4,0},{8,12},{12,8},{16,20},{20,16},{24,28},{28,24},{1,5},{5... | collective-permute-start | bytes 921608 | tf_op jit(solution)/shard_map/ppermute | solution.py:393
  29.1 1.5 %collective-permute-start.10 = (f32[2,2,16,600]{3,2,1,0:T(8,128)S(1)}, f32[2,2,16,600]{3,2,1,0:T(8,128)S(1)}, u32[]{:S(2)}, u32[]{:S(2)}) collective-permute-start(f32[2,2,16,600]{3,2,1,0:T(8,128)S(1)} %slice.9), channel_id=1, source_target_pairs={{0,4},{4,0},{8,12},{12,8},{16,20},{20,16},{24,28},{28,24},{1,5},{5... | collective-permute-start | bytes 460808 | tf_op jit(solution)/shard_map/ppermute | solution.py:393
  30.6 4.8 %collective-permute-start.11 = (f32[2,16,600]{2,1,0:T(8,128)S(1)}, f32[2,16,600]{2,1,0:T(8,128)S(1)}, u32[]{:S(2)}, u32[]{:S(2)}) collective-permute-start(f32[2,16,600]{2,1,0:T(8,128)S(1)} %get-tuple-element.36), channel_id=1, source_target_pairs={{0,8},{4,12},{8,0},{12,4},{16,24},{20,28},{24,16},{28,20},{1,9},{5... | collective-permute-start | bytes 230408 | tf_op jit(solution)/shard_map/ppermute | solution.py:400
  32.6 5.3 %collective-permute-start.12 = (f32[2,16,600]{2,1,0:T(8,128)S(1)}, f32[2,16,600]{2,1,0:T(8,128)S(1)}, u32[]{:S(2)}, u32[]{:S(2)}) collective-permute-start(f32[2,16,600]{2,1,0:T(8,128)S(1)} %get-tuple-element.37), channel_id=1, source_target_pairs={{0,16},{4,20},{8,24},{12,28},{16,0},{20,4},{24,8},{28,12},{1,17},{... | collective-permute-start | bytes 230408 | tf_op jit(solution)/shard_map/ppermute | solution.py:400
  34.2 5.3 %collective-permute-start.13 = (f32[2,16,600]{2,1,0:T(8,128)S(1)}, f32[2,16,600]{2,1,0:T(8,128)S(1)}, u32[]{:S(2)}, u32[]{:S(2)}) collective-permute-start(f32[2,16,600]{2,1,0:T(8,128)S(1)} %get-tuple-element.38), channel_id=1, source_target_pairs={{0,24},{4,28},{8,16},{12,20},{16,8},{20,12},{24,0},{28,4},{1,25},{... | collective-permute-start | bytes 230408 | tf_op jit(solution)/shard_map/ppermute | solution.py:400

commit v12 on v9

--- a/solution.py
+++ b/solution.py
@@ -64,22 +64,17 @@
 
 def transform_kernel(slots, edged, field_hbm, table_hbm, own_hbm, *refs):
     outs, pair, crosses = refs[:slots], refs[slots], refs[slots + 1 : -6]
-    field, table, own_c, field_sem, table_sem, own_sem = refs[-6:]
+    own_c, field, table, field_sem, table_sem, own_sem = refs[-6:]
     vectors, rows, steps, width = field.shape
     blocks = vectors // GROUP
     even = even_strip()
     source = lax.axis_index("freq") if table_hbm.shape[0] > 1 else 0
+    get_field = pltpu.make_async_copy(field_hbm, field, field_sem)
+    get_field.start()
     get_table = pltpu.make_async_copy(table_hbm.at[source], table, table_sem)
     get_table.start()
     get_own = pltpu.make_async_copy(own_hbm, own_c, own_sem)
     get_own.start()
-
-    def get(i):
-        at = pl.ds(i * GROUP, GROUP)
-        return pltpu.make_async_copy(field_hbm.at[at], field.at[at], field_sem.at[i])
-
-    for i in range(blocks):
-        get(i).start()
     get_own.wait()
     rim = PASSES - 1
     last_c, first_c = own_c[rows - rim :], own_c[:rim]
@@ -96,8 +91,8 @@
         (column >= mine * steps) & (column < (mine + 1) * steps), short[:, None], 0.0
     )
     full = full.reshape(-1, short.shape[1]).astype(jnp.bfloat16)
+    get_field.wait()
     for i in range(blocks):
-        get(i).wait()
         span = slice(i * GROUP, (i + 1) * GROUP)
         data = jnp.concatenate(
             [field[span, r].reshape(GROUP * steps, width) for r in range(rows)], axis=1
@@ -111,25 +106,26 @@
                 for r in range(rows):
                     piece = values[at : at + GROUP, r * width : (r + 1) * width]
                     outs[slot][b, r, span] = piece
-                if slot not in edged:
+                if slot not in sum(edged, ()):
                     continue
+                group = [slot in g for g in edged].index(True)
                 for r in range(PASSES):
                     row = (rows - PASSES + r) * width
                     last = values[at : at + GROUP, row : row + width]
                     first = values[at : at + GROUP, r * width : (r + 1) * width]
-                    to = edge_base(edged.index(slot), b, r, vectors) + i * GROUP
+                    to = edge_base(sum(edged, ()).index(slot), b, r, vectors) + i * GROUP
                     pair[to : to + GROUP] = pick(even, last, first)
-                    to = edge_base(0, b, r, vectors) + i * GROUP
-                    crosses[edged.index(slot)][to : to + GROUP] = pick(even, first, last)
+                    to = edge_base(edged[group].index(slot), b, r, vectors) + i * GROUP
+                    crosses[group][to : to + GROUP] = pick(even, first, last)
 
 
 def transform(field, table, coefficient, slots, edged):
     vectors, rows, steps, width = field.shape
     chunk = jax.ShapeDtypeStruct((2, rows, vectors, width), jnp.float32)
     size = edge_base(1, 0, 0, vectors)
-    pair = (len(edged) * size + GROUP, width)
-    crosses = [(size * bool(edged) + GROUP, width)] + [(size, width)] * (len(edged) - 1)
-    edges = [jax.ShapeDtypeStruct(shape, jnp.float32) for shape in (pair, *crosses)]
+    pair = (sum(map(len, edged)) * size + GROUP, width)
+    crosses = [(len(g) * size + GROUP * (i == 0), width) for i, g in enumerate(edged)]
+    edges = [jax.ShapeDtypeStruct(shape, jnp.float32) for shape in (pair, *crosses, coefficient.shape)]
     hbm = pl.BlockSpec(memory_space=pltpu.HBM)
     vmem = pl.BlockSpec(memory_space=pltpu.VMEM)
     outs = pl.pallas_call(
@@ -140,8 +136,7 @@
         scratch_shapes=[
             pltpu.VMEM(field.shape, field.dtype),
             pltpu.VMEM(table.shape[1:], table.dtype),
-            pltpu.VMEM(coefficient.shape, coefficient.dtype),
-            pltpu.SemaphoreType.DMA((vectors // GROUP,)),
+            pltpu.SemaphoreType.DMA(()),
             pltpu.SemaphoreType.DMA(()),
             pltpu.SemaphoreType.DMA(()),
         ],
@@ -152,7 +147,7 @@
         ),
         name="transform",
     )(*map(in_hbm, (field, table, coefficient)))
-    return outs[:slots], outs[slots], outs[slots + 1 :]
+    return outs[:slots], outs[slots], outs[slots + 1 : -1], outs[-1]
 
 
 def split_kernel(x_ref, high_ref, low_ref):
@@ -285,6 +280,7 @@
                 held[b, at, :, r * width : (r + 1) * width] = ref[b, r]
     half = count * vectors
     lhs_high, lhs_low = split_bf16(held[...].reshape(2 * half, rows * width))
+    lhs_both = jnp.concatenate([lhs_high, lhs_low], axis=0)
 
     def times(a):
         def dot(x, w):
@@ -292,7 +288,8 @@
                 x, w, (((1,), (0,)), ((), ())), preferred_element_type=jnp.float32
             )
 
-        return (dot(lhs_low, t_high[a]) + dot(lhs_high, t_low[a])) + dot(lhs_high, t_high[a])
+        by_high = dot(lhs_both, t_high[a])
+        return (by_high[2 * half :] + dot(lhs_high, t_low[a])) + by_high[: 2 * half]
 
     by_real, by_imag = times(0), times(1)
     real = by_real[:half] - by_imag[half:]
@@ -369,7 +366,9 @@
 
 
 def paired_shards(field, coefficient, split_of, table, freq_count, strips):
-    chunks, pair, crosses = transform(field, table, coefficient, freq_count, (2, 0))
+    chunks, pair, crosses, coefficient = transform(
+        field, table, coefficient, freq_count, ((2,), (0,))
+    )
 
     def swap(m, chunk):
         return lax.ppermute(chunk, "freq", xor_pairs(freq_count, m))
@@ -409,7 +408,9 @@
 
 
 def plain_shards(field, coefficient, split_of, table, freq_count, strips):
-    spectrum, pair_c, (cross_c,) = transform(field, table, coefficient, freq_count, ())
+    spectrum, pair_c, (cross_c,), coefficient = transform(
+        field, table, coefficient, freq_count, ((),)
+    )
     spectrum = jnp.stack(spectrum)
     spectrum = lax.all_to_all(spectrum, "freq", split_axis=0, concat_axis=0, tiled=True)
     chunks = list(spectrum)

time: 44.1 us -> 43.8 us (level)
  Pallas kernels: 9.52 us -> 9.03 us
where the time goes in v12:
time: 43.8 us; the launch traced here: 43.5 us
  starting transfers between devices  19.2 us (44%)
  waiting for transfers between devices  14.5 us (33%)
  Pallas kernels  9.03 us (21%)
  local copies, waits for them, and re-layouts  0.71 us (2%)
    ppermute x4, starting transfers between devices, to_cross(): return lax.ppermute(edge, 'seabed', inner + [(b, a) for a, b in inner])  7.84 us
    ppermute x3, waiting for transfers between devices, swap(): return lax.ppermute(chunk, 'freq', xor_pairs(freq_count, m))  7.52 us
    ppermute x3, starting transfers between devices, swap(): return lax.ppermute(chunk, 'freq', xor_pairs(freq_count, m))  7.42 us
    ppermute x3, waiting for transfers between devices, paired_shards(): total = total + lax.ppermute(chips[d], 'seabed', xor_pairs(strips, 2 * d))  4.77 us
    ppermute x3, starting transfers between devices, paired_shards(): total = total + lax.ppermute(chips[d], 'seabed', xor_pairs(strips, 2 * d))  3.55 us
    pallas_call x4, Pallas kernels, smooth(): pl.pallas_call(functools.partial(smooth_kernel, pair_slot, cross_slot), o...  2.61 us
    pallas_call x1, Pallas kernels, split_transfer(): pl.pallas_call(split_kernel, out_shape=[jax.ShapeDtypeStruct((parts, cell...  2.44 us
    pallas_call x2, Pallas kernels, combine(): pl.pallas_call(functools.partial(combine_kernel, indices, owners_in, pair...  2.13 us
  transfers between devices with their start and end apart: 14, of which 8 were waited for; matrix products, arithmetic and copies ran while one was open for 0% of the time, Pallas kernels for 17%

profile of v12, /device:TPU:0, one launch (start us, length us, event | category | flops | bytes accessed | tf_op | source)
XLA Modules:
  0.0 43.5 jit_solution(14212675245408365568)
XLA Ops:
  0.0 1.7 %transform.1 = (f32[2,5,32,128]{3,2,1,0:T(8,128)S(1)}, f32[2,5,32,128]{3,2,1,0:T(8,128)S(1)}, f32[2,5,32,128]{3,2,1,0:T(8,128)S(1)}, f32[2,5,32,128]{3,2,1,0:T(8...) custom-call(bf16[32,5,32,128]{3,2,1,0:T(8,128)(2,1)} %bitcast.7, ...), custom_call_target="tpu_custom_call" | custom-call | flops 167772160 | bytes 1966080 | tf_op jit(solution)/shard_map/transform/pallas_call | solution.py:131
  1.7 3.1 %collective-permute-start.3 = (f32[2,5,32,128]{3,2,1,0:T(8,128)S(1)}, f32[2,5,32,128]{3,2,1,0:T(8,128)S(1)}, u32[]{:S(2)}, u32[]{:S(2)}) collective-permute-start(f32[2,5,32,128]{3,2,1,0:T(8,128)S(1)} %get-tuple-element.26), channel_id=1, source_target_pairs={{0,1},{1,0},{2,3},{3,2},{4,5},{5,4},{6,7},{7,6},{8,9},{9,8},{10,11... | collective-permute-start | bytes 491528 | tf_op jit(solution)/shard_map/ppermute | solution.py:374
  4.9 2.5 %collective-permute-start.4 = (f32[2,5,32,128]{3,2,1,0:T(8,128)S(1)}, f32[2,5,32,128]{3,2,1,0:T(8,128)S(1)}, u32[]{:S(2)}, u32[]{:S(2)}) collective-permute-start(f32[2,5,32,128]{3,2,1,0:T(8,128)S(1)} %get-tuple-element.27), channel_id=1, source_target_pairs={{0,3},{1,2},{2,1},{3,0},{4,7},{5,6},{6,5},{7,4},{8,11},{9,10},{10,... | collective-permute-start | bytes 491528 | tf_op jit(solution)/shard_map/ppermute | solution.py:374
  7.3 2.1 %collective-permute-done.3.refs_0_.chunk = f32[2,5,32,128]{3,2,1,0:T(8,128)S(1)} collective-permute-done((f32[2,5,32,128]{3,2,1,0:T(8,128)S(1)}, f32[2,5,32,128]{3,2,1,0:T(8,128)S(1)}, u32[]{:S(2)}, u32[]{:S(2)}) %collective-permute-start.3) | collective-permute-done | bytes 163872 | tf_op jit(solution)/shard_map/ppermute | solution.py:374
  9.5 5.4 %collective-permute-done.4.refs_1_.chunk = f32[2,5,32,128]{3,2,1,0:T(8,128)S(1)} collective-permute-done((f32[2,5,32,128]{3,2,1,0:T(8,128)S(1)}, f32[2,5,32,128]{3,2,1,0:T(8,128)S(1)}, u32[]{:S(2)}, u32[]{:S(2)}) %collective-permute-start.4) | collective-permute-done | bytes 163872 | tf_op jit(solution)/shard_map/ppermute | solution.py:374
  15.0 2.5 %collective-permute-start.2 = (f32[200,128]{1,0:T(8,128)S(1)}, f32[200,128]{1,0:T(8,128)S(1)}, u32[]{:S(2)}, u32[]{:S(2)}) collective-permute-start(f32[200,128]{1,0:T(8,128)S(1)} %get-tuple-element.25), channel_id=1, source_target_pairs={{4,8},{12,16},{20,24},{28,0},{8,4},{16,12},{24,20},{0,28},{5,9},{1... | collective-permute-start | bytes 307208 | tf_op jit(solution)/shard_map/ppermute | solution.py:365
  17.7 2.5 %collective-permute-start.6 = (f32[192,128]{1,0:T(8,128)S(1)}, f32[192,128]{1,0:T(8,128)S(1)}, u32[]{:S(2)}, u32[]{:S(2)}) collective-permute-start(f32[192,128]{1,0:T(8,128)S(1)} %edges.3), channel_id=1, source_target_pairs={{4,8},{12,16},{20,24},{28,0},{8,4},{16,12},{24,20},{0,28},{5,9},{1... | collective-permute-start | bytes 294920 | tf_op jit(solution)/shard_map/ppermute | solution.py:365
  20.8 0.7 %smooth.6 = f32[2,5,32,128]{3,2,1,0:T(8,128)S(1)} custom-call(f32[2,5,32,128]{3,2,1,0:T(8,128)S(1)} %get-tuple-element.31.chunk, f32[392,128]{1,0:T(8,128)S(1)} %collective-permute-done.pair.pair_c, f32[200,128]{1,0:T(8,128)S(1)} %collective-permute-done.2.cross_c.cross, f32[5,128]{1,0:T(8,128)S(1)} %get-tuple-element.24.own_c, ...), custom_call_target="tpu_custom_call" | custom-call | flops 1228800 | bytes 409600 | tf_op jit(solution)/shard_map/smooth/pallas_call | solution.py:257
  21.5 1.8 %collective-permute-start.8 = (f32[2,5,32,128]{3,2,1,0:T(8,128)S(1)}, f32[2,5,32,128]{3,2,1,0:T(8,128)S(1)}, u32[]{:S(2)}, u32[]{:S(2)}) collective-permute-start(f32[2,5,32,128]{3,2,1,0:T(8,128)S(1)} %smooth.6), channel_id=1, source_target_pairs={{0,2},{1,3},{2,0},{3,1},{4,6},{5,7},{6,4},{7,5},{8,10},{9,11},{10,... | collective-permute-start | bytes 491528 | tf_op jit(solution)/shard_map/ppermute | solution.py:374
  23.3 2.4 %split_transfer.1 = (bf16[2,640,600]{2,1,0:T(8,128)(2,1)S(1)}, bf16[2,640,600]{2,1,0:T(8,128)(2,1)S(1)}) custom-call(f32[2,600,640]{2,1,0:T(8,128)} %bitcast.6), custom_call_target="tpu_custom_call" | custom-call | flops 1536000 | bytes 6144000 | tf_op jit(solution)/shard_map/split_transfer/pallas_call | solution.py:160
  25.7 2.6 %collective-permute-start.9 = (f32[192,128]{1,0:T(8,128)S(1)}, f32[192,128]{1,0:T(8,128)S(1)}, u32[]{:S(2)}, u32[]{:S(2)}) collective-permute-start(f32[192,128]{1,0:T(8,128)S(1)} %get-tuple-element.32), channel_id=1, source_target_pairs={{4,8},{12,16},{20,24},{28,0},{8,4},{16,12},{24,20},{0,28},{5,9},{1... | collective-permute-start | bytes 294920 | tf_op jit(solution)/shard_map/ppermute | solution.py:365
  28.3 0.7 %smooth.4.refs_0_ = f32[2,5,32,128]{3,2,1,0:T(8,128)S(1)} custom-call(f32[2,5,32,128]{3,2,1,0:T(8,128)S(1)} %get-tuple-element.21.chunk, f32[392,128]{1,0:T(8,128)S(1)} %collective-permute-done.pair.pair_c, f32[192,128]{1,0:T(8,128)S(1)} %collective-permute-done.1.cross, f32[5,128]{1,0:T(8,128)S(1)} %get-tuple-element.24.own_c, ...), custom_call_target="tpu_custom_call" | custom-call | flops 1228800 | bytes 409600 | tf_op jit(solution)/shard_map/smooth/pallas_call | solution.py:257
  29.0 0.7 %smooth.5.refs_1_ = f32[2,5,32,128]{3,2,1,0:T(8,128)S(1)} custom-call(f32[2,5,32,128]{3,2,1,0:T(8,128)S(1)} %collective-permute-done.3.refs_0_.chunk, f32[384,128]{1,0:T(8,128)S(1)} %collective-permute-done.5.pair, f32[192,128]{1,0:T(8,128)S(1)} %collective-permute-done.6.cross, f32[5,128]{1,0:T(8,128)S(1)} %get-tuple-element.24.own_c, ...), custom_call_target="tpu_custom_call" | custom-call | flops 1228800 | bytes 409600 | tf_op jit(solution)/shard_map/smooth/pallas_call | solution.py:257
  29.7 1.1 %combine.2.most = f32[8,2,16,600]{3,2,1,0:T(8,128)S(1)} custom-call(f32[2,5,32,128]{3,2,1,0:T(8,128)S(1)} %smooth.4.refs_0_, f32[2,5,32,128]{3,2,1,0:T(8,128)S(1)} %smooth.5.refs_1_, bf16[2,640,600]{2,1,0:T(8,128)(2,1)S(1)} %get-tuple-element.29.refs_2_, bf16[2,640,600]{2,1,0:T(8,128)(2,1)S(1)} %get-tuple-element.30.refs_3_), custom_call_target="tpu_custom_call" | custom-call | flops 589824000 | bytes 4014080 | tf_op jit(solution)/shard_map/combine/pallas_call | solution.py:321
  31.2 0.7 %smooth.7.refs_1_ = f32[2,5,32,128]{3,2,1,0:T(8,128)S(1)} custom-call(f32[2,5,32,128]{3,2,1,0:T(8,128)S(1)} %collective-permute-done.4.refs_1_.chunk, f32[384,128]{1,0:T(8,128)S(1)} %collective-permute-done.5.pair, f32[192,128]{1,0:T(8,128)S(1)} %collective-permute-done.9.cross, f32[5,128]{1,0:T(8,128)S(1)} %get-tuple-element.24.own_c, ...), custom_call_target="tpu_custom_call" | custom-call | flops 1228800 | bytes 409600 | tf_op jit(solution)/shard_map/smooth/pallas_call | solution.py:257
  31.9 1.1 %combine.3.tail = f32[4,2,16,600]{3,2,1,0:T(8,128)S(1)} custom-call(f32[2,5,32,128]{3,2,1,0:T(8,128)S(1)} %collective-permute-done.8.refs_0_, f32[2,5,32,128]{3,2,1,0:T(8,128)S(1)} %smooth.7.refs_1_, bf16[2,640,600]{2,1,0:T(8,128)(2,1)S(1)} %get-tuple-element.29.refs_2_, bf16[2,640,600]{2,1,0:T(8,128)(2,1)S(1)} %get-tuple-element.30.refs_3_), custom_call_target="tpu_custom_call" | custom-call | flops 589824000 | bytes 4014080 | tf_op jit(solution)/shard_map/combine/pallas_call | solution.py:321
  33.2 1.3 %collective-permute-done.10.tail_moved = f32[2,2,16,600]{3,2,1,0:T(8,128)S(1)} collective-permute-done((f32[2,2,16,600]{3,2,1,0:T(8,128)S(1)}, f32[2,2,16,600]{3,2,1,0:T(8,128)S(1)}, u32[]{:S(2)}, u32[]{:S(2)}) %collective-permute-start.10) | collective-permute-done | bytes 153632 | tf_op jit(solution)/shard_map/ppermute | solution.py:399
  34.5 1.3 %collective-permute-start.11 = (f32[2,16,600]{2,1,0:T(8,128)S(1)}, f32[2,16,600]{2,1,0:T(8,128)S(1)}, u32[]{:S(2)}, u32[]{:S(2)}) collective-permute-start(f32[2,16,600]{2,1,0:T(8,128)S(1)} %get-tuple-element.34), channel_id=1, source_target_pairs={{0,8},{4,12},{8,0},{12,4},{16,24},{20,28},{24,16},{28,20},{1,9},{5... | collective-permute-start | bytes 230408 | tf_op jit(solution)/shard_map/ppermute | solution.py:406
  35.8 1.7 %collective-permute-start.12 = (f32[2,16,600]{2,1,0:T(8,128)S(1)}, f32[2,16,600]{2,1,0:T(8,128)S(1)}, u32[]{:S(2)}, u32[]{:S(2)}) collective-permute-start(f32[2,16,600]{2,1,0:T(8,128)S(1)} %get-tuple-element.35), channel_id=1, source_target_pairs={{0,16},{4,20},{8,24},{12,28},{16,0},{20,4},{24,8},{28,12},{1,17},{... | collective-permute-start | bytes 230408 | tf_op jit(solution)/shard_map/ppermute | solution.py:406
  37.5 0.6 %collective-permute-start.13 = (f32[2,16,600]{2,1,0:T(8,128)S(1)}, f32[2,16,600]{2,1,0:T(8,128)S(1)}, u32[]{:S(2)}, u32[]{:S(2)}) collective-permute-start(f32[2,16,600]{2,1,0:T(8,128)S(1)} %get-tuple-element.36), channel_id=1, source_target_pairs={{0,24},{4,28},{8,16},{12,20},{16,8},{20,12},{24,0},{28,4},{1,25},{... | collective-permute-start | bytes 230408 | tf_op jit(solution)/shard_map/ppermute | solution.py:406
  38.1 1.0 %collective-permute-done.11 = f32[2,16,600]{2,1,0:T(8,128)S(1)} collective-permute-done((f32[2,16,600]{2,1,0:T(8,128)S(1)}, f32[2,16,600]{2,1,0:T(8,128)S(1)}, u32[]{:S(2)}, u32[]{:S(2)}) %collective-permute-start.11) | collective-permute-done | bytes 76832 | tf_op jit(solution)/shard_map/ppermute | solution.py:406
  39.1 2.2 %collective-permute-done.12 = f32[2,16,600]{2,1,0:T(8,128)S(1)} collective-permute-done((f32[2,16,600]{2,1,0:T(8,128)S(1)}, f32[2,16,600]{2,1,0:T(8,128)S(1)}, u32[]{:S(2)}, u32[]{:S(2)}) %collective-permute-start.12) | collective-permute-done | bytes 76832 | tf_op jit(solution)/shard_map/ppermute | solution.py:406
  41.2 1.6 %collective-permute-done.13 = f32[2,16,600]{2,1,0:T(8,128)S(1)} collective-permute-done((f32[2,16,600]{2,1,0:T(8,128)S(1)}, f32[2,16,600]{2,1,0:T(8,128)S(1)}, u32[]{:S(2)}, u32[]{:S(2)}) %collective-permute-start.13) | collective-permute-done | bytes 76832 | tf_op jit(solution)/shard_map/ppermute | solution.py:406
  42.9 0.7 %copy.5 = f32[16,1,2,600]{3,2,1,0:T(2,128)} copy(f32[16,1,2,600]{3,0,2,1:T(8,128)S(1)} %add_bitcast_fusion) | data formatting | bytes 153600 | tf_op jit(solution)/shard_map/broadcast_in_dim | solution.py:452
  (19 shorter events, 1.6 us)
Async XLA Ops:
  1.7 7.7 %collective-permute-start.3 = (f32[2,5,32,128]{3,2,1,0:T(8,128)S(1)}, f32[2,5,32,128]{3,2,1,0:T(8,128)S(1)}, u32[]{:S(2)}, u32[]{:S(2)}) collective-permute-start(f32[2,5,32,128]{3,2,1,0:T(8,128)S(1)} %get-tuple-element.26), channel_id=1, source_target_pairs={{0,1},{1,0},{2,3},{3,2},{4,5},{5,4},{6,7},{7,6},{8,9},{9,8},{10,11... | collective-permute-start | bytes 491528 | tf_op jit(solution)/shard_map/ppermute | solution.py:374
  4.9 10.0 %collective-permute-start.4 = (f32[2,5,32,128]{3,2,1,0:T(8,128)S(1)}, f32[2,5,32,128]{3,2,1,0:T(8,128)S(1)}, u32[]{:S(2)}, u32[]{:S(2)}) collective-permute-start(f32[2,5,32,128]{3,2,1,0:T(8,128)S(1)} %get-tuple-element.27), channel_id=1, source_target_pairs={{0,3},{1,2},{2,1},{3,0},{4,7},{5,6},{6,5},{7,4},{8,11},{9,10},{10,... | collective-permute-start | bytes 491528 | tf_op jit(solution)/shard_map/ppermute | solution.py:374
  7.3 13.5 %collective-permute-start = (f32[392,128]{1,0:T(8,128)S(1)}, f32[392,128]{1,0:T(8,128)S(1)}, u32[]{:S(2)}, u32[]{:S(2)}) collective-permute-start(f32[392,128]{1,0:T(8,128)S(1)} %get-tuple-element.22), channel_id=1, source_target_pairs={{0,4},{4,0},{8,12},{12,8},{16,20},{20,16},{24,28},{28,24},{1,5},{5... | collective-permute-start | bytes 602120 | tf_op jit(solution)/shard_map/ppermute | solution.py:360
  14.9 14.1 %collective-permute-start.5 = (f32[384,128]{1,0:T(8,128)S(1)}, f32[384,128]{1,0:T(8,128)S(1)}, u32[]{:S(2)}, u32[]{:S(2)}) collective-permute-start(f32[384,128]{1,0:T(8,128)S(1)} %get-tuple-element.28), channel_id=1, source_target_pairs={{0,4},{4,0},{8,12},{12,8},{16,20},{20,16},{24,28},{28,24},{1,5},{5... | collective-permute-start | bytes 589832 | tf_op jit(solution)/shard_map/ppermute | solution.py:360
  15.0 5.8 %collective-permute-start.2 = (f32[200,128]{1,0:T(8,128)S(1)}, f32[200,128]{1,0:T(8,128)S(1)}, u32[]{:S(2)}, u32[]{:S(2)}) collective-permute-start(f32[200,128]{1,0:T(8,128)S(1)} %get-tuple-element.25), channel_id=1, source_target_pairs={{4,8},{12,16},{20,24},{28,0},{8,4},{16,12},{24,20},{0,28},{5,9},{1... | collective-permute-start | bytes 307208 | tf_op jit(solution)/shard_map/ppermute | solution.py:365
  17.5 10.8 %collective-permute-start.1 = (f32[192,128]{1,0:T(8,128)S(1)}, f32[192,128]{1,0:T(8,128)S(1)}, u32[]{:S(2)}, u32[]{:S(2)}) collective-permute-start(f32[192,128]{1,0:T(8,128)S(1)} %get-tuple-element.23), channel_id=1, source_target_pairs={{4,8},{12,16},{20,24},{28,0},{8,4},{16,12},{24,20},{0,28},{5,9},{1... | collective-permute-start | bytes 294920 | tf_op jit(solution)/shard_map/ppermute | solution.py:365
  17.7 11.3 %collective-permute-start.6 = (f32[192,128]{1,0:T(8,128)S(1)}, f32[192,128]{1,0:T(8,128)S(1)}, u32[]{:S(2)}, u32[]{:S(2)}) collective-permute-start(f32[192,128]{1,0:T(8,128)S(1)} %edges.3), channel_id=1, source_target_pairs={{4,8},{12,16},{20,24},{28,0},{8,4},{16,12},{24,20},{0,28},{5,9},{1... | collective-permute-start | bytes 294920 | tf_op jit(solution)/shard_map/ppermute | solution.py:365
  21.5 10.4 %collective-permute-start.8 = (f32[2,5,32,128]{3,2,1,0:T(8,128)S(1)}, f32[2,5,32,128]{3,2,1,0:T(8,128)S(1)}, u32[]{:S(2)}, u32[]{:S(2)}) collective-permute-start(f32[2,5,32,128]{3,2,1,0:T(8,128)S(1)} %smooth.6), channel_id=1, source_target_pairs={{0,2},{1,3},{2,0},{3,1},{4,6},{5,7},{6,4},{7,5},{8,10},{9,11},{10,... | collective-permute-start | bytes 491528 | tf_op jit(solution)/shard_map/ppermute | solution.py:374
  25.7 5.5 %collective-permute-start.9 = (f32[192,128]{1,0:T(8,128)S(1)}, f32[192,128]{1,0:T(8,128)S(1)}, u32[]{:S(2)}, u32[]{:S(2)}) collective-permute-start(f32[192,128]{1,0:T(8,128)S(1)} %get-tuple-element.32), channel_id=1, source_target_pairs={{4,8},{12,16},{20,24},{28,0},{8,4},{16,12},{24,20},{0,28},{5,9},{1... | collective-permute-start | bytes 294920 | tf_op jit(solution)/shard_map/ppermute | solution.py:365
  30.8 3.7 %collective-permute-start.7 = (f32[4,2,16,600]{3,2,1,0:T(8,128)S(1)}, f32[4,2,16,600]{3,2,1,0:T(8,128)S(1)}, u32[]{:S(2)}, u32[]{:S(2)}) collective-permute-start(f32[4,2,16,600]{3,2,1,0:T(8,128)S(1)} %slice.8), channel_id=1, source_target_pairs={{0,4},{4,0},{8,12},{12,8},{16,20},{20,16},{24,28},{28,24},{1,5},{5... | collective-permute-start | bytes 921608 | tf_op jit(solution)/shard_map/ppermute | solution.py:399
  33.0 1.5 %collective-permute-start.10 = (f32[2,2,16,600]{3,2,1,0:T(8,128)S(1)}, f32[2,2,16,600]{3,2,1,0:T(8,128)S(1)}, u32[]{:S(2)}, u32[]{:S(2)}) collective-permute-start(f32[2,2,16,600]{3,2,1,0:T(8,128)S(1)} %slice.9), channel_id=1, source_target_pairs={{0,4},{4,0},{8,12},{12,8},{16,20},{20,16},{24,28},{28,24},{1,5},{5... | collective-permute-start | bytes 460808 | tf_op jit(solution)/shard_map/ppermute | solution.py:399
  34.5 4.6 %collective-permute-start.11 = (f32[2,16,600]{2,1,0:T(8,128)S(1)}, f32[2,16,600]{2,1,0:T(8,128)S(1)}, u32[]{:S(2)}, u32[]{:S(2)}) collective-permute-start(f32[2,16,600]{2,1,0:T(8,128)S(1)} %get-tuple-element.34), channel_id=1, source_target_pairs={{0,8},{4,12},{8,0},{12,4},{16,24},{20,28},{24,16},{28,20},{1,9},{5... | collective-permute-start | bytes 230408 | tf_op jit(solution)/shard_map/ppermute | solution.py:406
  35.8 5.4 %collective-permute-start.12 = (f32[2,16,600]{2,1,0:T(8,128)S(1)}, f32[2,16,600]{2,1,0:T(8,128)S(1)}, u32[]{:S(2)}, u32[]{:S(2)}) collective-permute-start(f32[2,16,600]{2,1,0:T(8,128)S(1)} %get-tuple-element.35), channel_id=1, source_target_pairs={{0,16},{4,20},{8,24},{12,28},{16,0},{20,4},{24,8},{28,12},{1,17},{... | collective-permute-start | bytes 230408 | tf_op jit(solution)/shard_map/ppermute | solution.py:406
  37.5 5.3 %collective-permute-start.13 = (f32[2,16,600]{2,1,0:T(8,128)S(1)}, f32[2,16,600]{2,1,0:T(8,128)S(1)}, u32[]{:S(2)}, u32[]{:S(2)}) collective-permute-start(f32[2,16,600]{2,1,0:T(8,128)S(1)} %get-tuple-element.36), channel_id=1, source_target_pairs={{0,24},{4,28},{8,16},{12,20},{16,8},{20,12},{24,0},{28,4},{1,25},{... | collective-permute-start | bytes 230408 | tf_op jit(solution)/shard_map/ppermute | solution.py:406

commit v13 on v12

--- a/solution.py
+++ b/solution.py
@@ -151,20 +151,20 @@
 
 
 def split_kernel(x_ref, high_ref, low_ref):
-    high_ref[0], low_ref[0] = split_bf16(jnp.transpose(x_ref[0]))
-
-
-def split_transfer(transfer):
-    parts, sensors, cells = transfer.shape
-    block = pl.BlockSpec((1, cells, sensors), lambda a: (a, 0, 0))
+    high_ref[...], low_ref[...] = split_bf16(jnp.transpose(x_ref[0]))
+
+
+def split_transfer(transfer, part):
+    _, sensors, cells = transfer.shape
+    block = pl.BlockSpec((cells, sensors), lambda i: (0, 0))
     return pl.pallas_call(
         split_kernel,
-        out_shape=[jax.ShapeDtypeStruct((parts, cells, sensors), jnp.bfloat16)] * 2,
-        grid=(parts,),
-        in_specs=[pl.BlockSpec((1, sensors, cells), lambda a: (a, 0, 0))],
+        out_shape=[jax.ShapeDtypeStruct((cells, sensors), jnp.bfloat16)] * 2,
+        grid=(1,),
+        in_specs=[pl.BlockSpec((1, sensors, cells), lambda i: (part, 0, 0))],
         out_specs=[block, block],
         compiler_params=params(),
-        cost_estimate=cost(2 * transfer.size, 8 * transfer.size),
+        cost_estimate=cost(2 * sensors * cells, 8 * sensors * cells),
         name="split_transfer",
     )(in_hbm(transfer))
 
@@ -271,7 +271,7 @@
 
 def combine_kernel(indices, owners_in, paired, absent, *refs):
     count = len(indices)
-    chunks, (t_high, t_low), (out, held) = refs[:count], refs[count : count + 2], refs[-2:]
+    chunks, transfer, (out, held) = refs[:count], refs[count : count + 4], refs[-2:]
     _, rows, vectors, width = chunks[0].shape
     owned = vectors // owners_in
     for at, ref in enumerate(chunks):
@@ -282,16 +282,16 @@
     lhs_high, lhs_low = split_bf16(held[...].reshape(2 * half, rows * width))
     lhs_both = jnp.concatenate([lhs_high, lhs_low], axis=0)
 
-    def times(a):
+    def times(t_high, t_low):
         def dot(x, w):
             return lax.dot_general(
                 x, w, (((1,), (0,)), ((), ())), preferred_element_type=jnp.float32
             )
 
-        by_high = dot(lhs_both, t_high[a])
-        return (by_high[2 * half :] + dot(lhs_high, t_low[a])) + by_high[: 2 * half]
-
-    by_real, by_imag = times(0), times(1)
+        by_high = dot(lhs_both, t_high[...])
+        return (by_high[2 * half :] + dot(lhs_high, t_low[...])) + by_high[: 2 * half]
+
+    by_real, by_imag = times(*transfer[:2]), times(*transfer[2:])
     real = by_real[:half] - by_imag[half:]
     imag = by_imag[:half] + by_real[half:]
 
@@ -312,8 +312,7 @@
 
 
 def combine(chunks, split, owners_in, places, paired, absent=()):
-    t_high, t_low = split
-    cells, sensors = t_high.shape[1:]
+    cells, sensors = split[0].shape
     indices = sorted(chunks)
     _, _, vectors, _ = chunks[indices[0]].shape
     owned = vectors // owners_in
@@ -328,7 +327,7 @@
             8 * sensors * cells + 8 * whole * cells + 16 * whole * sensors,
         ),
         name="combine",
-    )(*[chunks[i] for i in indices], t_high, t_low)
+    )(*[chunks[i] for i in indices], *split)
 
 
 def merge_kernel(late, owners_in, most, most_moved, tail, tail_moved, *outs):
@@ -382,7 +381,8 @@
     pair = to_pair(pair, strips)
     cross0 = to_cross(crosses[1], strips)
     coefficients = (coefficient, pair, cross2)
-    split = split_of()
+    real = split_of(0)
+    split = (*real, *split_of(1))
     second = swap(2, relax(chunks[2], pair, 0, cross2))
     own = relax(chunks[0], pair, 1, cross0)
     (cross1,) = edges([first], (0,), False)
@@ -421,7 +421,7 @@
     pair, cross = to_pair(pair, strips), to_cross(cross, strips)
     chunks = [smooth(c, pair, i, cross, i, coefficients) for i, c in enumerate(chunks)]
     owners_in = strips // freq_count
-    partial = combine(dict(enumerate(chunks)), split_of(), owners_in, strips, False)
+    partial = combine(dict(enumerate(chunks)), (*split_of(0), *split_of(1)), owners_in, strips, False)
     got = lax.all_to_all(partial, "seabed", split_axis=0, concat_axis=0, tiled=True)
     return got.sum(0)
 
@@ -444,7 +444,7 @@
     total = run(
         field,
         coefficient,
-        lambda: split_transfer(transfer[0]),
+        lambda part: split_transfer(transfer[0], part),
         table,
         freq_count,
         strips,

time: 43.8 us -> 44.8 us (1.023)
  Pallas kernels: 9.03 us -> 10.4 us
    pallas_call x1 -> x2, Pallas kernels: 2.44 us -> 3.81 us  [split_transfer(): pl.pallas_call(split_kernel, out_shape=[jax.ShapeDtypeStruct((cells, sens...]
  transfers between devices with their start and end apart: 14 -> 14, of which waited for: 8 -> 8; matrix products, arithmetic and copies ran while one was open for 0% -> 0% of each run, Pallas kernels for 17% -> 19%
where the time goes in v13:
time: 44.8 us; the launch traced here: 44.6 us
  starting transfers between devices  19.2 us (43%)
  waiting for transfers between devices  14.2 us (32%)
  Pallas kernels  10.4 us (23%)
  local copies, waits for them, and re-layouts  0.71 us (2%)
    ppermute x4, starting transfers between devices, to_cross(): return lax.ppermute(edge, 'seabed', inner + [(b, a) for a, b in inner])  7.84 us
    ppermute x3, waiting for transfers between devices, swap(): return lax.ppermute(chunk, 'freq', xor_pairs(freq_count, m))  7.52 us
    ppermute x3, starting transfers between devices, swap(): return lax.ppermute(chunk, 'freq', xor_pairs(freq_count, m))  7.42 us
    ppermute x3, waiting for transfers between devices, paired_shards(): total = total + lax.ppermute(chips[d], 'seabed', xor_pairs(strips, 2 * d))  4.47 us
    pallas_call x2, Pallas kernels, split_transfer(): pl.pallas_call(split_kernel, out_shape=[jax.ShapeDtypeStruct((cells, sens...  3.81 us
    ppermute x3, starting transfers between devices, paired_shards(): total = total + lax.ppermute(chips[d], 'seabed', xor_pairs(strips, 2 * d))  3.55 us
    pallas_call x4, Pallas kernels, smooth(): pl.pallas_call(functools.partial(smooth_kernel, pair_slot, cross_slot), o...  2.62 us
    pallas_call x2, Pallas kernels, combine(): pl.pallas_call(functools.partial(combine_kernel, indices, owners_in, pair...  2.14 us
  transfers between devices with their start and end apart: 14, of which 8 were waited for; matrix products, arithmetic and copies ran while one was open for 0% of the time, Pallas kernels for 19%

profile of v13, /device:TPU:0, one launch (start us, length us, event | category | flops | bytes accessed | tf_op | source)
XLA Modules:
  0.0 44.6 jit_solution(1598746140114853694)
XLA Ops:
  0.0 1.7 %transform.1 = (f32[2,5,32,128]{3,2,1,0:T(8,128)S(1)}, f32[2,5,32,128]{3,2,1,0:T(8,128)S(1)}, f32[2,5,32,128]{3,2,1,0:T(8,128)S(1)}, f32[2,5,32,128]{3,2,1,0:T(8...) custom-call(bf16[32,5,32,128]{3,2,1,0:T(8,128)(2,1)} %bitcast.8, ...), custom_call_target="tpu_custom_call" | custom-call | flops 167772160 | bytes 1966080 | tf_op jit(solution)/shard_map/transform/pallas_call | solution.py:131
  1.7 3.1 %collective-permute-start.3 = (f32[2,5,32,128]{3,2,1,0:T(8,128)S(1)}, f32[2,5,32,128]{3,2,1,0:T(8,128)S(1)}, u32[]{:S(2)}, u32[]{:S(2)}) collective-permute-start(f32[2,5,32,128]{3,2,1,0:T(8,128)S(1)} %get-tuple-element.28), channel_id=1, source_target_pairs={{0,1},{1,0},{2,3},{3,2},{4,5},{5,4},{6,7},{7,6},{8,9},{9,8},{10,11... | collective-permute-start | bytes 491528 | tf_op jit(solution)/shard_map/ppermute | solution.py:373
  4.9 2.5 %collective-permute-start.4 = (f32[2,5,32,128]{3,2,1,0:T(8,128)S(1)}, f32[2,5,32,128]{3,2,1,0:T(8,128)S(1)}, u32[]{:S(2)}, u32[]{:S(2)}) collective-permute-start(f32[2,5,32,128]{3,2,1,0:T(8,128)S(1)} %get-tuple-element.29), channel_id=1, source_target_pairs={{0,3},{1,2},{2,1},{3,0},{4,7},{5,6},{6,5},{7,4},{8,11},{9,10},{10,... | collective-permute-start | bytes 491528 | tf_op jit(solution)/shard_map/ppermute | solution.py:373
  7.3 2.1 %collective-permute-done.3.refs_0_.chunk = f32[2,5,32,128]{3,2,1,0:T(8,128)S(1)} collective-permute-done((f32[2,5,32,128]{3,2,1,0:T(8,128)S(1)}, f32[2,5,32,128]{3,2,1,0:T(8,128)S(1)}, u32[]{:S(2)}, u32[]{:S(2)}) %collective-permute-start.3) | collective-permute-done | bytes 163872 | tf_op jit(solution)/shard_map/ppermute | solution.py:373
  9.4 5.4 %collective-permute-done.4.refs_1_.chunk = f32[2,5,32,128]{3,2,1,0:T(8,128)S(1)} collective-permute-done((f32[2,5,32,128]{3,2,1,0:T(8,128)S(1)}, f32[2,5,32,128]{3,2,1,0:T(8,128)S(1)}, u32[]{:S(2)}, u32[]{:S(2)}) %collective-permute-start.4) | collective-permute-done | bytes 163872 | tf_op jit(solution)/shard_map/ppermute | solution.py:373
  15.0 2.5 %collective-permute-start.2 = (f32[200,128]{1,0:T(8,128)S(1)}, f32[200,128]{1,0:T(8,128)S(1)}, u32[]{:S(2)}, u32[]{:S(2)}) collective-permute-start(f32[200,128]{1,0:T(8,128)S(1)} %get-tuple-element.27), channel_id=1, source_target_pairs={{4,8},{12,16},{20,24},{28,0},{8,4},{16,12},{24,20},{0,28},{5,9},{1... | collective-permute-start | bytes 307208 | tf_op jit(solution)/shard_map/ppermute | solution.py:364
  17.7 2.5 %collective-permute-start.6 = (f32[192,128]{1,0:T(8,128)S(1)}, f32[192,128]{1,0:T(8,128)S(1)}, u32[]{:S(2)}, u32[]{:S(2)}) collective-permute-start(f32[192,128]{1,0:T(8,128)S(1)} %edges.3), channel_id=1, source_target_pairs={{4,8},{12,16},{20,24},{28,0},{8,4},{16,12},{24,20},{0,28},{5,9},{1... | collective-permute-start | bytes 294920 | tf_op jit(solution)/shard_map/ppermute | solution.py:364
  20.8 0.7 %smooth.6 = f32[2,5,32,128]{3,2,1,0:T(8,128)S(1)} custom-call(f32[2,5,32,128]{3,2,1,0:T(8,128)S(1)} %get-tuple-element.35.chunk, f32[392,128]{1,0:T(8,128)S(1)} %collective-permute-done.pair.pair_c, f32[200,128]{1,0:T(8,128)S(1)} %collective-permute-done.2.cross_c.cross, f32[5,128]{1,0:T(8,128)S(1)} %get-tuple-element.26.own_c, ...), custom_call_target="tpu_custom_call" | custom-call | flops 1228800 | bytes 409600 | tf_op jit(solution)/shard_map/smooth/pallas_call | solution.py:257
  21.4 1.8 %collective-permute-start.8 = (f32[2,5,32,128]{3,2,1,0:T(8,128)S(1)}, f32[2,5,32,128]{3,2,1,0:T(8,128)S(1)}, u32[]{:S(2)}, u32[]{:S(2)}) collective-permute-start(f32[2,5,32,128]{3,2,1,0:T(8,128)S(1)} %smooth.6), channel_id=1, source_target_pairs={{0,2},{1,3},{2,0},{3,1},{4,6},{5,7},{6,4},{7,5},{8,10},{9,11},{10,... | collective-permute-start | bytes 491528 | tf_op jit(solution)/shard_map/ppermute | solution.py:373
  23.3 1.9 %split_transfer.3 = (bf16[640,600]{1,0:T(8,128)(2,1)S(1)}, bf16[640,600]{1,0:T(8,128)(2,1)S(1)}) custom-call(f32[2,600,640]{2,1,0:T(8,128)} %bitcast.6), custom_call_target="tpu_custom_call" | custom-call | flops 768000 | bytes 3072000 | tf_op jit(solution)/shard_map/split_transfer/pallas_call | solution.py:160
  25.2 1.9 %split_transfer.2 = (bf16[640,600]{1,0:T(8,128)(2,1)S(1)}, bf16[640,600]{1,0:T(8,128)(2,1)S(1)}) custom-call(f32[2,600,640]{2,1,0:T(8,128)} %bitcast.7), custom_call_target="tpu_custom_call" | custom-call | flops 768000 | bytes 3072000 | tf_op jit(solution)/shard_map/split_transfer/pallas_call | solution.py:160
  27.1 2.6 %collective-permute-start.9 = (f32[192,128]{1,0:T(8,128)S(1)}, f32[192,128]{1,0:T(8,128)S(1)}, u32[]{:S(2)}, u32[]{:S(2)}) collective-permute-start(f32[192,128]{1,0:T(8,128)S(1)} %get-tuple-element.36), channel_id=1, source_target_pairs={{4,8},{12,16},{20,24},{28,0},{8,4},{16,12},{24,20},{0,28},{5,9},{1... | collective-permute-start | bytes 294920 | tf_op jit(solution)/shard_map/ppermute | solution.py:364
  29.7 0.7 %smooth.4.refs_0_ = f32[2,5,32,128]{3,2,1,0:T(8,128)S(1)} custom-call(f32[2,5,32,128]{3,2,1,0:T(8,128)S(1)} %get-tuple-element.23.chunk, f32[392,128]{1,0:T(8,128)S(1)} %collective-permute-done.pair.pair_c, f32[192,128]{1,0:T(8,128)S(1)} %collective-permute-done.1.cross, f32[5,128]{1,0:T(8,128)S(1)} %get-tuple-element.26.own_c, ...), custom_call_target="tpu_custom_call" | custom-call | flops 1228800 | bytes 409600 | tf_op jit(solution)/shard_map/smooth/pallas_call | solution.py:257
  30.4 0.7 %smooth.5.refs_1_ = f32[2,5,32,128]{3,2,1,0:T(8,128)S(1)} custom-call(f32[2,5,32,128]{3,2,1,0:T(8,128)S(1)} %collective-permute-done.3.refs_0_.chunk, f32[384,128]{1,0:T(8,128)S(1)} %collective-permute-done.5.pair, f32[192,128]{1,0:T(8,128)S(1)} %collective-permute-done.6.cross, f32[5,128]{1,0:T(8,128)S(1)} %get-tuple-element.26.own_c, ...), custom_call_target="tpu_custom_call" | custom-call | flops 1228800 | bytes 409600 | tf_op jit(solution)/shard_map/smooth/pallas_call | solution.py:257
  31.0 1.1 %combine.2.most = f32[8,2,16,600]{3,2,1,0:T(8,128)S(1)} custom-call(f32[2,5,32,128]{3,2,1,0:T(8,128)S(1)} %smooth.4.refs_0_, f32[2,5,32,128]{3,2,1,0:T(8,128)S(1)} %smooth.5.refs_1_, bf16[640,600]{1,0:T(8,128)(2,1)S(1)} %get-tuple-element.31.refs_2_, bf16[640,600]{1,0:T(8,128)(2,1)S(1)} %get-tuple-element.32.refs_3_, ...), custom_call_target="tpu_custom_call" | custom-call | flops 589824000 | bytes 4014080 | tf_op jit(solution)/shard_map/combine/pallas_call | solution.py:320
  33.3 1.1 %combine.3.tail = f32[4,2,16,600]{3,2,1,0:T(8,128)S(1)} custom-call(f32[2,5,32,128]{3,2,1,0:T(8,128)S(1)} %collective-permute-done.8.refs_0_, f32[2,5,32,128]{3,2,1,0:T(8,128)S(1)} %smooth.7.refs_1_, bf16[640,600]{1,0:T(8,128)(2,1)S(1)} %get-tuple-element.31.refs_2_, bf16[640,600]{1,0:T(8,128)(2,1)S(1)} %get-tuple-element.32.refs_3_, ...), custom_call_target="tpu_custom_call" | custom-call | flops 589824000 | bytes 4014080 | tf_op jit(solution)/shard_map/combine/pallas_call | solution.py:320
  34.5 1.3 %collective-permute-done.10.tail_moved = f32[2,2,16,600]{3,2,1,0:T(8,128)S(1)} collective-permute-done((f32[2,2,16,600]{3,2,1,0:T(8,128)S(1)}, f32[2,2,16,600]{3,2,1,0:T(8,128)S(1)}, u32[]{:S(2)}, u32[]{:S(2)}) %collective-permute-start.10) | collective-permute-done | bytes 153632 | tf_op jit(solution)/shard_map/ppermute | solution.py:399
  35.9 1.2 %collective-permute-start.11 = (f32[2,16,600]{2,1,0:T(8,128)S(1)}, f32[2,16,600]{2,1,0:T(8,128)S(1)}, u32[]{:S(2)}, u32[]{:S(2)}) collective-permute-start(f32[2,16,600]{2,1,0:T(8,128)S(1)} %get-tuple-element.38), channel_id=1, source_target_pairs={{0,8},{4,12},{8,0},{12,4},{16,24},{20,28},{24,16},{28,20},{1,9},{5... | collective-permute-start | bytes 230408 | tf_op jit(solution)/shard_map/ppermute | solution.py:406
  37.1 1.5 %collective-permute-start.12 = (f32[2,16,600]{2,1,0:T(8,128)S(1)}, f32[2,16,600]{2,1,0:T(8,128)S(1)}, u32[]{:S(2)}, u32[]{:S(2)}) collective-permute-start(f32[2,16,600]{2,1,0:T(8,128)S(1)} %get-tuple-element.39), channel_id=1, source_target_pairs={{0,16},{4,20},{8,24},{12,28},{16,0},{20,4},{24,8},{28,12},{1,17},{... | collective-permute-start | bytes 230408 | tf_op jit(solution)/shard_map/ppermute | solution.py:406
  38.6 0.9 %collective-permute-start.13 = (f32[2,16,600]{2,1,0:T(8,128)S(1)}, f32[2,16,600]{2,1,0:T(8,128)S(1)}, u32[]{:S(2)}, u32[]{:S(2)}) collective-permute-start(f32[2,16,600]{2,1,0:T(8,128)S(1)} %get-tuple-element.40), channel_id=1, source_target_pairs={{0,24},{4,28},{8,16},{12,20},{16,8},{20,12},{24,0},{28,4},{1,25},{... | collective-permute-start | bytes 230408 | tf_op jit(solution)/shard_map/ppermute | solution.py:406
  39.4 1.0 %collective-permute-done.11 = f32[2,16,600]{2,1,0:T(8,128)S(1)} collective-permute-done((f32[2,16,600]{2,1,0:T(8,128)S(1)}, f32[2,16,600]{2,1,0:T(8,128)S(1)}, u32[]{:S(2)}, u32[]{:S(2)}) %collective-permute-start.11) | collective-permute-done | bytes 76832 | tf_op jit(solution)/shard_map/ppermute | solution.py:406
  40.4 1.9 %collective-permute-done.12 = f32[2,16,600]{2,1,0:T(8,128)S(1)} collective-permute-done((f32[2,16,600]{2,1,0:T(8,128)S(1)}, f32[2,16,600]{2,1,0:T(8,128)S(1)}, u32[]{:S(2)}, u32[]{:S(2)}) %collective-permute-start.12) | collective-permute-done | bytes 76832 | tf_op jit(solution)/shard_map/ppermute | solution.py:406
  42.3 1.6 %collective-permute-done.13 = f32[2,16,600]{2,1,0:T(8,128)S(1)} collective-permute-done((f32[2,16,600]{2,1,0:T(8,128)S(1)}, f32[2,16,600]{2,1,0:T(8,128)S(1)}, u32[]{:S(2)}, u32[]{:S(2)}) %collective-permute-start.13) | collective-permute-done | bytes 76832 | tf_op jit(solution)/shard_map/ppermute | solution.py:406
  43.9 0.7 %copy.5 = f32[16,1,2,600]{3,2,1,0:T(2,128)} copy(f32[16,1,2,600]{3,0,2,1:T(8,128)S(1)} %add_bitcast_fusion) | data formatting | bytes 153600 | tf_op jit(solution)/shard_map/broadcast_in_dim | solution.py:452
  (20 shorter events, 2.3 us)
Async XLA Ops:
  1.7 7.7 %collective-permute-start.3 = (f32[2,5,32,128]{3,2,1,0:T(8,128)S(1)}, f32[2,5,32,128]{3,2,1,0:T(8,128)S(1)}, u32[]{:S(2)}, u32[]{:S(2)}) collective-permute-start(f32[2,5,32,128]{3,2,1,0:T(8,128)S(1)} %get-tuple-element.28), channel_id=1, source_target_pairs={{0,1},{1,0},{2,3},{3,2},{4,5},{5,4},{6,7},{7,6},{8,9},{9,8},{10,11... | collective-permute-start | bytes 491528 | tf_op jit(solution)/shard_map/ppermute | solution.py:373
  4.9 10.0 %collective-permute-start.4 = (f32[2,5,32,128]{3,2,1,0:T(8,128)S(1)}, f32[2,5,32,128]{3,2,1,0:T(8,128)S(1)}, u32[]{:S(2)}, u32[]{:S(2)}) collective-permute-start(f32[2,5,32,128]{3,2,1,0:T(8,128)S(1)} %get-tuple-element.29), channel_id=1, source_target_pairs={{0,3},{1,2},{2,1},{3,0},{4,7},{5,6},{6,5},{7,4},{8,11},{9,10},{10,... | collective-permute-start | bytes 491528 | tf_op jit(solution)/shard_map/ppermute | solution.py:373
  7.3 13.5 %collective-permute-start = (f32[392,128]{1,0:T(8,128)S(1)}, f32[392,128]{1,0:T(8,128)S(1)}, u32[]{:S(2)}, u32[]{:S(2)}) collective-permute-start(f32[392,128]{1,0:T(8,128)S(1)} %get-tuple-element.24), channel_id=1, source_target_pairs={{0,4},{4,0},{8,12},{12,8},{16,20},{20,16},{24,28},{28,24},{1,5},{5... | collective-permute-start | bytes 602120 | tf_op jit(solution)/shard_map/ppermute | solution.py:359
  14.9 15.5 %collective-permute-start.5 = (f32[384,128]{1,0:T(8,128)S(1)}, f32[384,128]{1,0:T(8,128)S(1)}, u32[]{:S(2)}, u32[]{:S(2)}) collective-permute-start(f32[384,128]{1,0:T(8,128)S(1)} %get-tuple-element.30), channel_id=1, source_target_pairs={{0,4},{4,0},{8,12},{12,8},{16,20},{20,16},{24,28},{28,24},{1,5},{5... | collective-permute-start | bytes 589832 | tf_op jit(solution)/shard_map/ppermute | solution.py:359
  15.0 5.8 %collective-permute-start.2 = (f32[200,128]{1,0:T(8,128)S(1)}, f32[200,128]{1,0:T(8,128)S(1)}, u32[]{:S(2)}, u32[]{:S(2)}) collective-permute-start(f32[200,128]{1,0:T(8,128)S(1)} %get-tuple-element.27), channel_id=1, source_target_pairs={{4,8},{12,16},{20,24},{28,0},{8,4},{16,12},{24,20},{0,28},{5,9},{1... | collective-permute-start | bytes 307208 | tf_op jit(solution)/shard_map/ppermute | solution.py:364
  17.5 12.2 %collective-permute-start.1 = (f32[192,128]{1,0:T(8,128)S(1)}, f32[192,128]{1,0:T(8,128)S(1)}, u32[]{:S(2)}, u32[]{:S(2)}) collective-permute-start(f32[192,128]{1,0:T(8,128)S(1)} %get-tuple-element.25), channel_id=1, source_target_pairs={{4,8},{12,16},{20,24},{28,0},{8,4},{16,12},{24,20},{0,28},{5,9},{1... | collective-permute-start | bytes 294920 | tf_op jit(solution)/shard_map/ppermute | solution.py:364
  17.7 12.7 %collective-permute-start.6 = (f32[192,128]{1,0:T(8,128)S(1)}, f32[192,128]{1,0:T(8,128)S(1)}, u32[]{:S(2)}, u32[]{:S(2)}) collective-permute-start(f32[192,128]{1,0:T(8,128)S(1)} %edges.3), channel_id=1, source_target_pairs={{4,8},{12,16},{20,24},{28,0},{8,4},{16,12},{24,20},{0,28},{5,9},{1... | collective-permute-start | bytes 294920 | tf_op jit(solution)/shard_map/ppermute | solution.py:364
  21.4 11.8 %collective-permute-start.8 = (f32[2,5,32,128]{3,2,1,0:T(8,128)S(1)}, f32[2,5,32,128]{3,2,1,0:T(8,128)S(1)}, u32[]{:S(2)}, u32[]{:S(2)}) collective-permute-start(f32[2,5,32,128]{3,2,1,0:T(8,128)S(1)} %smooth.6), channel_id=1, source_target_pairs={{0,2},{1,3},{2,0},{3,1},{4,6},{5,7},{6,4},{7,5},{8,10},{9,11},{10,... | collective-permute-start | bytes 491528 | tf_op jit(solution)/shard_map/ppermute | solution.py:373
  27.1 5.5 %collective-permute-start.9 = (f32[192,128]{1,0:T(8,128)S(1)}, f32[192,128]{1,0:T(8,128)S(1)}, u32[]{:S(2)}, u32[]{:S(2)}) collective-permute-start(f32[192,128]{1,0:T(8,128)S(1)} %get-tuple-element.36), channel_id=1, source_target_pairs={{4,8},{12,16},{20,24},{28,0},{8,4},{16,12},{24,20},{0,28},{5,9},{1... | collective-permute-start | bytes 294920 | tf_op jit(solution)/shard_map/ppermute | solution.py:364
  32.1 3.7 %collective-permute-start.7 = (f32[4,2,16,600]{3,2,1,0:T(8,128)S(1)}, f32[4,2,16,600]{3,2,1,0:T(8,128)S(1)}, u32[]{:S(2)}, u32[]{:S(2)}) collective-permute-start(f32[4,2,16,600]{3,2,1,0:T(8,128)S(1)} %slice.8), channel_id=1, source_target_pairs={{0,4},{4,0},{8,12},{12,8},{16,20},{20,16},{24,28},{28,24},{1,5},{5... | collective-permute-start | bytes 921608 | tf_op jit(solution)/shard_map/ppermute | solution.py:399
  34.3 1.5 %collective-permute-start.10 = (f32[2,2,16,600]{3,2,1,0:T(8,128)S(1)}, f32[2,2,16,600]{3,2,1,0:T(8,128)S(1)}, u32[]{:S(2)}, u32[]{:S(2)}) collective-permute-start(f32[2,2,16,600]{3,2,1,0:T(8,128)S(1)} %slice.9), channel_id=1, source_target_pairs={{0,4},{4,0},{8,12},{12,8},{16,20},{20,16},{24,28},{28,24},{1,5},{5... | collective-permute-start | bytes 460808 | tf_op jit(solution)/shard_map/ppermute | solution.py:399
  35.9 4.6 %collective-permute-start.11 = (f32[2,16,600]{2,1,0:T(8,128)S(1)}, f32[2,16,600]{2,1,0:T(8,128)S(1)}, u32[]{:S(2)}, u32[]{:S(2)}) collective-permute-start(f32[2,16,600]{2,1,0:T(8,128)S(1)} %get-tuple-element.38), channel_id=1, source_target_pairs={{0,8},{4,12},{8,0},{12,4},{16,24},{20,28},{24,16},{28,20},{1,9},{5... | collective-permute-start | bytes 230408 | tf_op jit(solution)/shard_map/ppermute | solution.py:406
  37.1 5.3 %collective-permute-start.12 = (f32[2,16,600]{2,1,0:T(8,128)S(1)}, f32[2,16,600]{2,1,0:T(8,128)S(1)}, u32[]{:S(2)}, u32[]{:S(2)}) collective-permute-start(f32[2,16,600]{2,1,0:T(8,128)S(1)} %get-tuple-element.39), channel_id=1, source_target_pairs={{0,16},{4,20},{8,24},{12,28},{16,0},{20,4},{24,8},{28,12},{1,17},{... | collective-permute-start | bytes 230408 | tf_op jit(solution)/shard_map/ppermute | solution.py:406
  38.6 5.3 %collective-permute-start.13 = (f32[2,16,600]{2,1,0:T(8,128)S(1)}, f32[2,16,600]{2,1,0:T(8,128)S(1)}, u32[]{:S(2)}, u32[]{:S(2)}) collective-permute-start(f32[2,16,600]{2,1,0:T(8,128)S(1)} %get-tuple-element.40), channel_id=1, source_target_pairs={{0,24},{4,28},{8,16},{12,20},{16,8},{20,12},{24,0},{28,4},{1,25},{... | collective-permute-start | bytes 230408 | tf_op jit(solution)/shard_map/ppermute | solution.py:406

commit v14 on v13

--- a/solution.py
+++ b/solution.py
@@ -385,22 +385,22 @@
     split = (*real, *split_of(1))
     second = swap(2, relax(chunks[2], pair, 0, cross2))
     own = relax(chunks[0], pair, 1, cross0)
-    (cross1,) = edges([first], (0,), False)
+    (cross3,) = edges([third], (0,), False)
+    cross3 = to_cross(cross3, strips)
+    pair, cross1 = edges([third, first], (1,))
     cross1 = to_cross(cross1, strips)
-    pair, cross3 = edges([first, third], (1,))
-    cross3 = to_cross(cross3, strips)
     pair = to_pair(pair, strips)
-    first = relax(first, pair, 0, cross1)
-    third = relax(third, pair, 1, cross3)
-    most = combine({0: own, 1: first}, split, 2, strips, True, (2, 3))
+    third = relax(third, pair, 0, cross3)
+    first = relax(first, pair, 1, cross1)
+    most = combine({0: own, 3: third}, split, 2, strips, True, (1, 2))
 
     def to_core(partial):
         send = partial[partial.shape[0] // 2 :]
         return lax.ppermute(send, "seabed", xor_pairs(strips, 1))
 
     most_moved = to_core(most)
-    tail = combine({2: second, 3: third}, split, 2, strips // 2, True)
-    chips = merge((2, 3), 2, most, most_moved, tail, to_core(tail))
+    tail = combine({1: first, 2: second}, split, 2, strips // 2, True)
+    chips = merge((1, 2), 2, most, most_moved, tail, to_core(tail))
     total = chips[0]
     for d in range(1, strips // 2):
         total = total + lax.ppermute(chips[d], "seabed", xor_pairs(strips, 2 * d))

time: 44.8 us -> 43.5 us (0.971)
  starting transfers between devices: 19.2 us -> 17.6 us
    ppermute x3, starting transfers between devices: 7.42 us -> 5.84 us  [swap(): return lax.ppermute(chunk, 'freq', xor_pairs(freq_count, m))]
  transfers between devices with their start and end apart: 14 -> 14, of which waited for: 8 -> 8; matrix products, arithmetic and copies ran while one was open for 0% -> 0% of each run, Pallas kernels for 19% -> 20%
where the time goes in v14:
time: 43.5 us; the launch traced here: 43.3 us
  starting transfers between devices  17.6 us (40%)
  waiting for transfers between devices  14.5 us (33%)
  Pallas kernels  10.4 us (24%)
  local copies, waits for them, and re-layouts  0.71 us (2%)
    ppermute x4, starting transfers between devices, to_cross(): return lax.ppermute(edge, 'seabed', inner + [(b, a) for a, b in inner])  7.84 us
    ppermute x3, waiting for transfers between devices, swap(): return lax.ppermute(chunk, 'freq', xor_pairs(freq_count, m))  7.81 us
    ppermute x3, starting transfers between devices, swap(): return lax.ppermute(chunk, 'freq', xor_pairs(freq_count, m))  5.84 us
    ppermute x3, waiting for transfers between devices, paired_shards(): total = total + lax.ppermute(chips[d], 'seabed', xor_pairs(strips, 2 * d))  4.47 us
    pallas_call x2, Pallas kernels, split_transfer(): pl.pallas_call(split_kernel, out_shape=[jax.ShapeDtypeStruct((cells, sens...  3.81 us
    ppermute x3, starting transfers between devices, paired_shards(): total = total + lax.ppermute(chips[d], 'seabed', xor_pairs(strips, 2 * d))  3.55 us
    pallas_call x4, Pallas kernels, smooth(): pl.pallas_call(functools.partial(smooth_kernel, pair_slot, cross_slot), o...  2.62 us
    pallas_call x2, Pallas kernels, combine(): pl.pallas_call(functools.partial(combine_kernel, indices, owners_in, pair...  2.14 us
  transfers between devices with their start and end apart: 14, of which 8 were waited for; matrix products, arithmetic and copies ran while one was open for 0% of the time, Pallas kernels for 20%

profile of v14, /device:TPU:0, one launch (start us, length us, event | category | flops | bytes accessed | tf_op | source)
XLA Modules:
  0.0 43.3 jit_solution(144379169497414266)
XLA Ops:
  0.0 1.7 %transform.1 = (f32[2,5,32,128]{3,2,1,0:T(8,128)S(1)}, f32[2,5,32,128]{3,2,1,0:T(8,128)S(1)}, f32[2,5,32,128]{3,2,1,0:T(8,128)S(1)}, f32[2,5,32,128]{3,2,1,0:T(8...) custom-call(bf16[32,5,32,128]{3,2,1,0:T(8,128)(2,1)} %bitcast.8, ...), custom_call_target="tpu_custom_call" | custom-call | flops 167772160 | bytes 1966080 | tf_op jit(solution)/shard_map/transform/pallas_call | solution.py:131
  1.7 5.1 %collective-permute-start.3 = (f32[2,5,32,128]{3,2,1,0:T(8,128)S(1)}, f32[2,5,32,128]{3,2,1,0:T(8,128)S(1)}, u32[]{:S(2)}, u32[]{:S(2)}) collective-permute-start(f32[2,5,32,128]{3,2,1,0:T(8,128)S(1)} %get-tuple-element.28), channel_id=1, source_target_pairs={{0,3},{1,2},{2,1},{3,0},{4,7},{5,6},{6,5},{7,4},{8,11},{9,10},{10,... | collective-permute-start | bytes 491528 | tf_op jit(solution)/shard_map/ppermute | solution.py:373
  6.9 5.1 %collective-permute-done.3.refs_0_.chunk = f32[2,5,32,128]{3,2,1,0:T(8,128)S(1)} collective-permute-done((f32[2,5,32,128]{3,2,1,0:T(8,128)S(1)}, f32[2,5,32,128]{3,2,1,0:T(8,128)S(1)}, u32[]{:S(2)}, u32[]{:S(2)}) %collective-permute-start.3) | collective-permute-done | bytes 163872 | tf_op jit(solution)/shard_map/ppermute | solution.py:373
  12.0 2.7 %collective-permute-done.4.refs_1_.chunk = f32[2,5,32,128]{3,2,1,0:T(8,128)S(1)} collective-permute-done((f32[2,5,32,128]{3,2,1,0:T(8,128)S(1)}, f32[2,5,32,128]{3,2,1,0:T(8,128)S(1)}, u32[]{:S(2)}, u32[]{:S(2)}) %collective-permute-start.4) | collective-permute-done | bytes 163872 | tf_op jit(solution)/shard_map/ppermute | solution.py:373
  14.8 2.5 %collective-permute-start.2 = (f32[200,128]{1,0:T(8,128)S(1)}, f32[200,128]{1,0:T(8,128)S(1)}, u32[]{:S(2)}, u32[]{:S(2)}) collective-permute-start(f32[200,128]{1,0:T(8,128)S(1)} %get-tuple-element.27), channel_id=1, source_target_pairs={{4,8},{12,16},{20,24},{28,0},{8,4},{16,12},{24,20},{0,28},{5,9},{1... | collective-permute-start | bytes 307208 | tf_op jit(solution)/shard_map/ppermute | solution.py:364
  17.5 2.5 %collective-permute-start.6 = (f32[192,128]{1,0:T(8,128)S(1)}, f32[192,128]{1,0:T(8,128)S(1)}, u32[]{:S(2)}, u32[]{:S(2)}) collective-permute-start(f32[192,128]{1,0:T(8,128)S(1)} %edges.3), channel_id=1, source_target_pairs={{4,8},{12,16},{20,24},{28,0},{8,4},{16,12},{24,20},{0,28},{5,9},{1... | collective-permute-start | bytes 294920 | tf_op jit(solution)/shard_map/ppermute | solution.py:364
  20.6 0.7 %smooth.7 = f32[2,5,32,128]{3,2,1,0:T(8,128)S(1)} custom-call(f32[2,5,32,128]{3,2,1,0:T(8,128)S(1)} %get-tuple-element.36.chunk, f32[392,128]{1,0:T(8,128)S(1)} %collective-permute-done.pair.pair_c, f32[200,128]{1,0:T(8,128)S(1)} %collective-permute-done.2.cross_c.cross, f32[5,128]{1,0:T(8,128)S(1)} %get-tuple-element.26.own_c, ...), custom_call_target="tpu_custom_call" | custom-call | flops 1228800 | bytes 409600 | tf_op jit(solution)/shard_map/smooth/pallas_call | solution.py:257
  21.3 0.7 %collective-permute-start.9 = (f32[2,5,32,128]{3,2,1,0:T(8,128)S(1)}, f32[2,5,32,128]{3,2,1,0:T(8,128)S(1)}, u32[]{:S(2)}, u32[]{:S(2)}) collective-permute-start(f32[2,5,32,128]{3,2,1,0:T(8,128)S(1)} %smooth.7), channel_id=1, source_target_pairs={{0,2},{1,3},{2,0},{3,1},{4,6},{5,7},{6,4},{7,5},{8,10},{9,11},{10,... | collective-permute-start | bytes 491528 | tf_op jit(solution)/shard_map/ppermute | solution.py:373
  22.0 1.9 %split_transfer.3 = (bf16[640,600]{1,0:T(8,128)(2,1)S(1)}, bf16[640,600]{1,0:T(8,128)(2,1)S(1)}) custom-call(f32[2,600,640]{2,1,0:T(8,128)} %bitcast.6), custom_call_target="tpu_custom_call" | custom-call | flops 768000 | bytes 3072000 | tf_op jit(solution)/shard_map/split_transfer/pallas_call | solution.py:160
  23.9 1.9 %split_transfer.2 = (bf16[640,600]{1,0:T(8,128)(2,1)S(1)}, bf16[640,600]{1,0:T(8,128)(2,1)S(1)}) custom-call(f32[2,600,640]{2,1,0:T(8,128)} %bitcast.7), custom_call_target="tpu_custom_call" | custom-call | flops 768000 | bytes 3072000 | tf_op jit(solution)/shard_map/split_transfer/pallas_call | solution.py:160
  25.8 2.6 %collective-permute-start.8 = (f32[192,128]{1,0:T(8,128)S(1)}, f32[192,128]{1,0:T(8,128)S(1)}, u32[]{:S(2)}, u32[]{:S(2)}) collective-permute-start(f32[192,128]{1,0:T(8,128)S(1)} %get-tuple-element.35), channel_id=1, source_target_pairs={{4,8},{12,16},{20,24},{28,0},{8,4},{16,12},{24,20},{0,28},{5,9},{1... | collective-permute-start | bytes 294920 | tf_op jit(solution)/shard_map/ppermute | solution.py:364
  28.4 0.7 %smooth.4.refs_0_ = f32[2,5,32,128]{3,2,1,0:T(8,128)S(1)} custom-call(f32[2,5,32,128]{3,2,1,0:T(8,128)S(1)} %get-tuple-element.23.chunk, f32[392,128]{1,0:T(8,128)S(1)} %collective-permute-done.pair.pair_c, f32[192,128]{1,0:T(8,128)S(1)} %collective-permute-done.1.cross, f32[5,128]{1,0:T(8,128)S(1)} %get-tuple-element.26.own_c, ...), custom_call_target="tpu_custom_call" | custom-call | flops 1228800 | bytes 409600 | tf_op jit(solution)/shard_map/smooth/pallas_call | solution.py:257
  29.1 0.7 %smooth.5.refs_1_ = f32[2,5,32,128]{3,2,1,0:T(8,128)S(1)} custom-call(f32[2,5,32,128]{3,2,1,0:T(8,128)S(1)} %collective-permute-done.3.refs_0_.chunk, f32[384,128]{1,0:T(8,128)S(1)} %collective-permute-done.5.pair, f32[192,128]{1,0:T(8,128)S(1)} %collective-permute-done.6.cross, f32[5,128]{1,0:T(8,128)S(1)} %get-tuple-element.26.own_c, ...), custom_call_target="tpu_custom_call" | custom-call | flops 1228800 | bytes 409600 | tf_op jit(solution)/shard_map/smooth/pallas_call | solution.py:257
  29.7 1.1 %combine.2.most = f32[8,2,16,600]{3,2,1,0:T(8,128)S(1)} custom-call(f32[2,5,32,128]{3,2,1,0:T(8,128)S(1)} %smooth.4.refs_0_, f32[2,5,32,128]{3,2,1,0:T(8,128)S(1)} %smooth.5.refs_1_, bf16[640,600]{1,0:T(8,128)(2,1)S(1)} %get-tuple-element.31.refs_2_, bf16[640,600]{1,0:T(8,128)(2,1)S(1)} %get-tuple-element.32.refs_3_, ...), custom_call_target="tpu_custom_call" | custom-call | flops 589824000 | bytes 4014080 | tf_op jit(solution)/shard_map/combine/pallas_call | solution.py:320
  31.3 0.7 %smooth.6.refs_0_ = f32[2,5,32,128]{3,2,1,0:T(8,128)S(1)} custom-call(f32[2,5,32,128]{3,2,1,0:T(8,128)S(1)} %collective-permute-done.4.refs_1_.chunk, f32[384,128]{1,0:T(8,128)S(1)} %collective-permute-done.5.pair, f32[192,128]{1,0:T(8,128)S(1)} %collective-permute-done.8.cross, f32[5,128]{1,0:T(8,128)S(1)} %get-tuple-element.26.own_c, ...), custom_call_target="tpu_custom_call" | custom-call | flops 1228800 | bytes 409600 | tf_op jit(solution)/shard_map/smooth/pallas_call | solution.py:257
  32.0 1.1 %combine.3.tail = f32[4,2,16,600]{3,2,1,0:T(8,128)S(1)} custom-call(f32[2,5,32,128]{3,2,1,0:T(8,128)S(1)} %smooth.6.refs_0_, f32[2,5,32,128]{3,2,1,0:T(8,128)S(1)} %collective-permute-done.9.refs_1_, bf16[640,600]{1,0:T(8,128)(2,1)S(1)} %get-tuple-element.31.refs_2_, bf16[640,600]{1,0:T(8,128)(2,1)S(1)} %get-tuple-element.32.refs_3_, ...), custom_call_target="tpu_custom_call" | custom-call | flops 589824000 | bytes 4014080 | tf_op jit(solution)/shard_map/combine/pallas_call | solution.py:320
  33.2 1.3 %collective-permute-done.10.tail_moved = f32[2,2,16,600]{3,2,1,0:T(8,128)S(1)} collective-permute-done((f32[2,2,16,600]{3,2,1,0:T(8,128)S(1)}, f32[2,2,16,600]{3,2,1,0:T(8,128)S(1)}, u32[]{:S(2)}, u32[]{:S(2)}) %collective-permute-start.10) | collective-permute-done | bytes 153632 | tf_op jit(solution)/shard_map/ppermute | solution.py:399
  34.6 1.2 %collective-permute-start.11 = (f32[2,16,600]{2,1,0:T(8,128)S(1)}, f32[2,16,600]{2,1,0:T(8,128)S(1)}, u32[]{:S(2)}, u32[]{:S(2)}) collective-permute-start(f32[2,16,600]{2,1,0:T(8,128)S(1)} %get-tuple-element.38), channel_id=1, source_target_pairs={{0,8},{4,12},{8,0},{12,4},{16,24},{20,28},{24,16},{28,20},{1,9},{5... | collective-permute-start | bytes 230408 | tf_op jit(solution)/shard_map/ppermute | solution.py:406
  35.8 1.5 %collective-permute-start.12 = (f32[2,16,600]{2,1,0:T(8,128)S(1)}, f32[2,16,600]{2,1,0:T(8,128)S(1)}, u32[]{:S(2)}, u32[]{:S(2)}) collective-permute-start(f32[2,16,600]{2,1,0:T(8,128)S(1)} %get-tuple-element.39), channel_id=1, source_target_pairs={{0,16},{4,20},{8,24},{12,28},{16,0},{20,4},{24,8},{28,12},{1,17},{... | collective-permute-start | bytes 230408 | tf_op jit(solution)/shard_map/ppermute | solution.py:406
  37.3 0.9 %collective-permute-start.13 = (f32[2,16,600]{2,1,0:T(8,128)S(1)}, f32[2,16,600]{2,1,0:T(8,128)S(1)}, u32[]{:S(2)}, u32[]{:S(2)}) collective-permute-start(f32[2,16,600]{2,1,0:T(8,128)S(1)} %get-tuple-element.40), channel_id=1, source_target_pairs={{0,24},{4,28},{8,16},{12,20},{16,8},{20,12},{24,0},{28,4},{1,25},{... | collective-permute-start | bytes 230408 | tf_op jit(solution)/shard_map/ppermute | solution.py:406
  38.1 1.0 %collective-permute-done.11 = f32[2,16,600]{2,1,0:T(8,128)S(1)} collective-permute-done((f32[2,16,600]{2,1,0:T(8,128)S(1)}, f32[2,16,600]{2,1,0:T(8,128)S(1)}, u32[]{:S(2)}, u32[]{:S(2)}) %collective-permute-start.11) | collective-permute-done | bytes 76832 | tf_op jit(solution)/shard_map/ppermute | solution.py:406
  39.1 1.9 %collective-permute-done.12 = f32[2,16,600]{2,1,0:T(8,128)S(1)} collective-permute-done((f32[2,16,600]{2,1,0:T(8,128)S(1)}, f32[2,16,600]{2,1,0:T(8,128)S(1)}, u32[]{:S(2)}, u32[]{:S(2)}) %collective-permute-start.12) | collective-permute-done | bytes 76832 | tf_op jit(solution)/shard_map/ppermute | solution.py:406
  41.0 1.6 %collective-permute-done.13 = f32[2,16,600]{2,1,0:T(8,128)S(1)} collective-permute-done((f32[2,16,600]{2,1,0:T(8,128)S(1)}, f32[2,16,600]{2,1,0:T(8,128)S(1)}, u32[]{:S(2)}, u32[]{:S(2)}) %collective-permute-start.13) | collective-permute-done | bytes 76832 | tf_op jit(solution)/shard_map/ppermute | solution.py:406
  42.6 0.7 %copy.5 = f32[16,1,2,600]{3,2,1,0:T(2,128)} copy(f32[16,1,2,600]{3,0,2,1:T(8,128)S(1)} %add_bitcast_fusion) | data formatting | bytes 153600 | tf_op jit(solution)/shard_map/broadcast_in_dim | solution.py:452
  (20 shorter events, 1.6 us)
Async XLA Ops:
  1.7 10.2 %collective-permute-start.3 = (f32[2,5,32,128]{3,2,1,0:T(8,128)S(1)}, f32[2,5,32,128]{3,2,1,0:T(8,128)S(1)}, u32[]{:S(2)}, u32[]{:S(2)}) collective-permute-start(f32[2,5,32,128]{3,2,1,0:T(8,128)S(1)} %get-tuple-element.28), channel_id=1, source_target_pairs={{0,3},{1,2},{2,1},{3,0},{4,7},{5,6},{6,5},{7,4},{8,11},{9,10},{10,... | collective-permute-start | bytes 491528 | tf_op jit(solution)/shard_map/ppermute | solution.py:373
  6.9 7.8 %collective-permute-start.4 = (f32[2,5,32,128]{3,2,1,0:T(8,128)S(1)}, f32[2,5,32,128]{3,2,1,0:T(8,128)S(1)}, u32[]{:S(2)}, u32[]{:S(2)}) collective-permute-start(f32[2,5,32,128]{3,2,1,0:T(8,128)S(1)} %get-tuple-element.29), channel_id=1, source_target_pairs={{0,1},{1,0},{2,3},{3,2},{4,5},{5,4},{6,7},{7,6},{8,9},{9,8},{10,11... | collective-permute-start | bytes 491528 | tf_op jit(solution)/shard_map/ppermute | solution.py:373
  6.9 13.7 %collective-permute-start = (f32[392,128]{1,0:T(8,128)S(1)}, f32[392,128]{1,0:T(8,128)S(1)}, u32[]{:S(2)}, u32[]{:S(2)}) collective-permute-start(f32[392,128]{1,0:T(8,128)S(1)} %get-tuple-element.24), channel_id=1, source_target_pairs={{0,4},{4,0},{8,12},{12,8},{16,20},{20,16},{24,28},{28,24},{1,5},{5... | collective-permute-start | bytes 602120 | tf_op jit(solution)/shard_map/ppermute | solution.py:359
  14.7 14.3 %collective-permute-start.5 = (f32[384,128]{1,0:T(8,128)S(1)}, f32[384,128]{1,0:T(8,128)S(1)}, u32[]{:S(2)}, u32[]{:S(2)}) collective-permute-start(f32[384,128]{1,0:T(8,128)S(1)} %get-tuple-element.30), channel_id=1, source_target_pairs={{0,4},{4,0},{8,12},{12,8},{16,20},{20,16},{24,28},{28,24},{1,5},{5... | collective-permute-start | bytes 589832 | tf_op jit(solution)/shard_map/ppermute | solution.py:359
  14.8 5.8 %collective-permute-start.2 = (f32[200,128]{1,0:T(8,128)S(1)}, f32[200,128]{1,0:T(8,128)S(1)}, u32[]{:S(2)}, u32[]{:S(2)}) collective-permute-start(f32[200,128]{1,0:T(8,128)S(1)} %get-tuple-element.27), channel_id=1, source_target_pairs={{4,8},{12,16},{20,24},{28,0},{8,4},{16,12},{24,20},{0,28},{5,9},{1... | collective-permute-start | bytes 307208 | tf_op jit(solution)/shard_map/ppermute | solution.py:364
  17.3 11.0 %collective-permute-start.1 = (f32[192,128]{1,0:T(8,128)S(1)}, f32[192,128]{1,0:T(8,128)S(1)}, u32[]{:S(2)}, u32[]{:S(2)}) collective-permute-start(f32[192,128]{1,0:T(8,128)S(1)} %get-tuple-element.25), channel_id=1, source_target_pairs={{4,8},{12,16},{20,24},{28,0},{8,4},{16,12},{24,20},{0,28},{5,9},{1... | collective-permute-start | bytes 294920 | tf_op jit(solution)/shard_map/ppermute | solution.py:364
  17.5 11.5 %collective-permute-start.6 = (f32[192,128]{1,0:T(8,128)S(1)}, f32[192,128]{1,0:T(8,128)S(1)}, u32[]{:S(2)}, u32[]{:S(2)}) collective-permute-start(f32[192,128]{1,0:T(8,128)S(1)} %edges.3), channel_id=1, source_target_pairs={{4,8},{12,16},{20,24},{28,0},{8,4},{16,12},{24,20},{0,28},{5,9},{1... | collective-permute-start | bytes 294920 | tf_op jit(solution)/shard_map/ppermute | solution.py:364
  21.3 10.7 %collective-permute-start.9 = (f32[2,5,32,128]{3,2,1,0:T(8,128)S(1)}, f32[2,5,32,128]{3,2,1,0:T(8,128)S(1)}, u32[]{:S(2)}, u32[]{:S(2)}) collective-permute-start(f32[2,5,32,128]{3,2,1,0:T(8,128)S(1)} %smooth.7), channel_id=1, source_target_pairs={{0,2},{1,3},{2,0},{3,1},{4,6},{5,7},{6,4},{7,5},{8,10},{9,11},{10,... | collective-permute-start | bytes 491528 | tf_op jit(solution)/shard_map/ppermute | solution.py:373
  25.8 5.5 %collective-permute-start.8 = (f32[192,128]{1,0:T(8,128)S(1)}, f32[192,128]{1,0:T(8,128)S(1)}, u32[]{:S(2)}, u32[]{:S(2)}) collective-permute-start(f32[192,128]{1,0:T(8,128)S(1)} %get-tuple-element.35), channel_id=1, source_target_pairs={{4,8},{12,16},{20,24},{28,0},{8,4},{16,12},{24,20},{0,28},{5,9},{1... | collective-permute-start | bytes 294920 | tf_op jit(solution)/shard_map/ppermute | solution.py:364
  30.8 3.7 %collective-permute-start.7 = (f32[4,2,16,600]{3,2,1,0:T(8,128)S(1)}, f32[4,2,16,600]{3,2,1,0:T(8,128)S(1)}, u32[]{:S(2)}, u32[]{:S(2)}) collective-permute-start(f32[4,2,16,600]{3,2,1,0:T(8,128)S(1)} %slice.8), channel_id=1, source_target_pairs={{0,4},{4,0},{8,12},{12,8},{16,20},{20,16},{24,28},{28,24},{1,5},{5... | collective-permute-start | bytes 921608 | tf_op jit(solution)/shard_map/ppermute | solution.py:399
  33.0 1.5 %collective-permute-start.10 = (f32[2,2,16,600]{3,2,1,0:T(8,128)S(1)}, f32[2,2,16,600]{3,2,1,0:T(8,128)S(1)}, u32[]{:S(2)}, u32[]{:S(2)}) collective-permute-start(f32[2,2,16,600]{3,2,1,0:T(8,128)S(1)} %slice.9), channel_id=1, source_target_pairs={{0,4},{4,0},{8,12},{12,8},{16,20},{20,16},{24,28},{28,24},{1,5},{5... | collective-permute-start | bytes 460808 | tf_op jit(solution)/shard_map/ppermute | solution.py:399
  34.6 4.6 %collective-permute-start.11 = (f32[2,16,600]{2,1,0:T(8,128)S(1)}, f32[2,16,600]{2,1,0:T(8,128)S(1)}, u32[]{:S(2)}, u32[]{:S(2)}) collective-permute-start(f32[2,16,600]{2,1,0:T(8,128)S(1)} %get-tuple-element.38), channel_id=1, source_target_pairs={{0,8},{4,12},{8,0},{12,4},{16,24},{20,28},{24,16},{28,20},{1,9},{5... | collective-permute-start | bytes 230408 | tf_op jit(solution)/shard_map/ppermute | solution.py:406
  35.8 5.3 %collective-permute-start.12 = (f32[2,16,600]{2,1,0:T(8,128)S(1)}, f32[2,16,600]{2,1,0:T(8,128)S(1)}, u32[]{:S(2)}, u32[]{:S(2)}) collective-permute-start(f32[2,16,600]{2,1,0:T(8,128)S(1)} %get-tuple-element.39), channel_id=1, source_target_pairs={{0,16},{4,20},{8,24},{12,28},{16,0},{20,4},{24,8},{28,12},{1,17},{... | collective-permute-start | bytes 230408 | tf_op jit(solution)/shard_map/ppermute | solution.py:406
  37.3 5.3 %collective-permute-start.13 = (f32[2,16,600]{2,1,0:T(8,128)S(1)}, f32[2,16,600]{2,1,0:T(8,128)S(1)}, u32[]{:S(2)}, u32[]{:S(2)}) collective-permute-start(f32[2,16,600]{2,1,0:T(8,128)S(1)} %get-tuple-element.40), channel_id=1, source_target_pairs={{0,24},{4,28},{8,16},{12,20},{16,8},{20,12},{24,0},{28,4},{1,25},{... | collective-permute-start | bytes 230408 | tf_op jit(solution)/shard_map/ppermute | solution.py:406
